TPU v7x, 32 devices: a whole 2x2x4 slice. The times are simulated.
32 devices in a mesh: dp: 4 (over y, x), expert: 8 (over z, core).
Axes of the slice: x: 2, y: 2, z: 4, core: 2. Of those that a mesh axis runs over, the one named last changes fastest.
Arguments:
- layer_input: bfloat16 [16384, 1280], P(('dp', 'expert')), may hold values from -6 to 6
- lengths: int32 [32], P(('dp', 'expert')), may hold values from 256 to 512, as said below
- expert_ids: int32 [16384, 7], P(('dp', 'expert')), may hold values from 0 to 14, all different within a row; in each aligned block of 512 rows (0 to 511, 512 to 1023, ...) at most 240 rows name the same one
- norm1: float32 [1280], replicated, may hold values from 0.5 to 1.5
- w_qkv: bfloat16 [1280, 3840], replicated, may hold values from -0.15625 to 0.15625
- w_out: bfloat16 [1280, 1280], replicated, may hold values from -1.25 to 1.25
- norm2: float32 [1280], replicated, may hold values from 0.5 to 1.5
- w_router: bfloat16 [1280, 16], replicated, may hold values from -0.078125 to 0.078125
- w_shared_in: bfloat16 [1280, 1792], replicated, may hold values from -0.15625 to 0.15625
- w_shared_down: bfloat16 [896, 1280], replicated, may hold values from -0.1875 to 0.1875
- w_expert_in: bfloat16 [16, 1280, 1792], P('expert'), may hold values from -0.15625 to 0.15625
- w_expert_down: bfloat16 [16, 896, 1280], P('expert'), may hold values from -1.5 to 1.5
- dout: bfloat16 [16384, 1280], P(('dp', 'expert')), may hold values from -6 to 6
Outputs:
- out: bfloat16 [16384, 1280], P(('dp', 'expert'))
- grad_x: float32 [16384, 1280], P(('dp', 'expert'))
- grad_norm1: float32 [1280], P(('dp', 'expert'))
- grad_qkv: float32 [1280, 3840], P(('dp', 'expert'))
- grad_out: float32 [1280, 1280], P(('dp', 'expert'))
- grad_norm2: float32 [1280], P(('dp', 'expert'))
- grad_router: float32 [1280, 16], P(('dp', 'expert'))
- grad_shared_in: float32 [1280, 1792], P(('dp', 'expert'))
- grad_shared_down: float32 [896, 1280], P(None, ('dp', 'expert'))
- grad_expert_in: float32 [16, 1280, 1792], P('expert', 'dp')
- grad_expert_down: float32 [16, 896, 1280], P('expert', 'dp')
- counts: int32 [16], replicated
Inputs may be any that keep to these rules, and one draw needn't show every extreme that they name: `expert_ids`: each row names 7 different routed experts. Among the rows of one sequence no expert is named more than 240 times, a bound that some block reaches. `lengths`: some sequence has exactly 512 live tokens and some exactly half of 512.
All inputs are finite; a program needn't handle non-finite values.
Results may differ from a plain program's by a relative error of at most 0.015.
Values may be sent and summed in bfloat16 or wider, within the bound.
No kernel may reach another device: no remote copies, remote signals or barrier semaphores. Data moves between devices by JAX's collectives and lax.ppermute only.
A program may use at most 384 MiB of HBM per device.

v0:
```python
import jax
import jax.numpy as jnp
from jax import lax
from jax.sharding import PartitionSpec as P

HEAD_DIM = 128


NORM_EPS = 1e-06
MASK_VALUE = -1e30
QUERY_BLOCK = 512


def silu_parts(gate_in):
    sigmoid_v = jax.nn.sigmoid(gate_in)
    return (gate_in * sigmoid_v, sigmoid_v * (1.0 + gate_in * (1.0 - sigmoid_v)))


def normalize(values_in, gain_vec):
    inverse = lax.rsqrt(jnp.mean(values_in * values_in, axis=-1, keepdims=True) + NORM_EPS)
    return (values_in * inverse * gain_vec, inverse)


def norm_back(incoming, values_in, inverse, gain_vec):
    scaled = values_in * inverse
    grad_gain = jnp.sum(incoming * scaled, axis=0)
    inner_grad = incoming * gain_vec
    grad_values = inverse * (
        inner_grad - scaled * jnp.mean(inner_grad * scaled, axis=-1, keepdims=True)
    )
    return (grad_values, grad_gain)


def rope_tables(seq_slots, head_width):
    half_dim = head_width // 2
    inv_freq = 1.0 / 10000.0 ** (jnp.arange(half_dim, dtype=jnp.float32) * 2.0 / head_width)
    angles = jnp.arange(seq_slots, dtype=jnp.float32)[:, None] * inv_freq[None, :]
    return (jnp.cos(angles)[:, None, :], jnp.sin(angles)[:, None, :])


def rotate(values_in, cosine, sine_t):
    half_dim = values_in.shape[-1] // 2
    first_half = values_in[..., :half_dim]
    second_half = values_in[..., half_dim:]
    return jnp.concatenate(
        [first_half * cosine - second_half * sine_t, first_half * sine_t + second_half * cosine],
        axis=-1,
    )


def score_block(query_block, keys_in, block_start, seq_length, score_scale):
    raw_scores = (
        jnp.einsum("qhd,khd->hqk", query_block, keys_in, preferred_element_type=jnp.float32)
        * score_scale
    )
    query_pos = block_start + jnp.arange(query_block.shape[0], dtype=jnp.int32)[:, None]
    key_pos = jnp.arange(keys_in.shape[0], dtype=jnp.int32)[None, :]
    allowed = (key_pos <= query_pos) & (key_pos < seq_length)
    return jnp.where(allowed[None], raw_scores, MASK_VALUE)


def attention_forward(queries, keys_in, values_in, seq_length):
    seq_slots, heads, head_width = queries.shape
    block_rows = min(QUERY_BLOCK, seq_slots)
    score_scale = head_width ** (-0.5)

    def one_block(block_index):
        block_start = block_index * block_rows
        scores = score_block(queries, keys_in, block_start, seq_length, score_scale)
        highest = jnp.max(scores, axis=-1, keepdims=True)
        weights_exp = jnp.exp(scores - highest)
        totals = jnp.sum(weights_exp, axis=-1, keepdims=True)
        probs_low = (weights_exp / totals).astype(jnp.bfloat16)
        block_out = jnp.einsum(
            "hqk,khd->qhd", probs_low, values_in, preferred_element_type=jnp.float32
        )
        return (block_out, highest + jnp.log(totals))

    block_outs, log_norm = lax.map(one_block, jnp.arange(seq_slots // block_rows))
    return (block_outs.reshape(seq_slots, heads, head_width), log_norm)


def attention_backward(queries, keys_in, values_in, grad_attended, log_norm, seq_length):
    seq_slots, heads, head_width = queries.shape
    block_rows = min(QUERY_BLOCK, seq_slots)
    score_scale = head_width ** (-0.5)

    def one_step(carried, block_in):
        grad_keys, grad_values = carried
        block_index, block_norm = block_in
        block_start = block_index * block_rows
        scores = score_block(queries, keys_in, block_start, seq_length, score_scale)
        probs = jnp.exp(scores - block_norm)
        grad_probs = jnp.einsum(
            "qhd,khd->hqk", grad_attended, values_in, preferred_element_type=jnp.float32
        )
        row_dot = jnp.sum(grad_probs * probs, axis=-1, keepdims=True)
        grad_scores = (probs * (grad_probs - row_dot)).astype(jnp.bfloat16)
        grad_query = (
            jnp.einsum("hqk,khd->qhd", grad_scores, keys_in, preferred_element_type=jnp.float32)
            * score_scale
        )
        grad_keys = (
            grad_keys
            + jnp.einsum("hqk,qhd->khd", grad_scores, queries, preferred_element_type=jnp.float32)
            * score_scale
        )
        grad_values = grad_values + jnp.einsum(
            "hqk,qhd->khd",
            probs.astype(jnp.bfloat16),
            grad_attended,
            preferred_element_type=jnp.float32,
        )
        return ((grad_keys, grad_values), grad_query)

    zeros_kv = jnp.zeros((seq_slots, heads, head_width), jnp.float32)
    (grad_keys, grad_values), grad_queries = lax.scan(
        one_step, (zeros_kv, zeros_kv), (jnp.arange(seq_slots // block_rows), log_norm)
    )
    return (grad_queries.reshape(seq_slots, heads, head_width), grad_keys, grad_values)


def reduce_experts(grad_in_part, grad_down_part):
    return (
        lax.psum_scatter(
            grad_in_part.astype(jnp.bfloat16), "dp", scatter_dimension=1, tiled=True
        ).astype(jnp.float32),
        lax.psum_scatter(
            grad_down_part.astype(jnp.bfloat16), "dp", scatter_dimension=1, tiled=True
        ).astype(jnp.float32),
    )


def per_device(
    layer_input,
    lengths,
    expert_ids,
    norm1,
    w_qkv,
    w_out,
    norm2,
    w_router,
    w_shared_in,
    w_shared_down,
    w_expert_in,
    w_expert_down,
    dout,
):
    seq_slots, width = layer_input.shape
    top_k = expert_ids.shape[1]
    experts = w_router.shape[1]
    local_experts = w_expert_in.shape[0]
    hidden_units = w_shared_down.shape[0]
    heads = width // HEAD_DIM
    capacity = (seq_slots * top_k // (experts - 1) // 8 + 1) * 8
    seq_length = lengths[0]
    live_rows = jnp.arange(seq_slots, dtype=jnp.int32) < seq_length
    live_col = live_rows.astype(jnp.float32)[:, None]
    cosine, sine_t = rope_tables(seq_slots, HEAD_DIM)
    x_full = layer_input.astype(jnp.float32)
    h1_full, inverse_one = normalize(x_full, norm1)
    h1_low = h1_full.astype(jnp.bfloat16)
    proj_qkv = jnp.dot(h1_low, w_qkv, preferred_element_type=jnp.float32).reshape(
        seq_slots, 3, heads, HEAD_DIM
    )
    queries = rotate(proj_qkv[:, 0], cosine, sine_t).astype(jnp.bfloat16)
    keys_in = rotate(proj_qkv[:, 1], cosine, sine_t).astype(jnp.bfloat16)
    values_in = proj_qkv[:, 2].astype(jnp.bfloat16)
    attended, log_norm = attention_forward(queries, keys_in, values_in, seq_length)
    attended_low = attended.reshape(seq_slots, width).astype(jnp.bfloat16)
    branch = jnp.dot(attended_low, w_out, preferred_element_type=jnp.float32)
    x_mid = x_full + live_col * branch
    h2_full, inverse_two = normalize(x_mid, norm2)
    h2_low = h2_full.astype(jnp.bfloat16)
    logits = jnp.dot(h2_low, w_router, preferred_element_type=jnp.float32)
    router_cols = jnp.arange(experts, dtype=jnp.int32) < experts - 1
    logits = jnp.where(router_cols[None, :], logits, MASK_VALUE)
    highest = jnp.max(logits, axis=-1, keepdims=True)
    weights_exp = jnp.exp(logits - highest)
    router_probs = weights_exp / jnp.sum(weights_exp, axis=-1, keepdims=True)
    choose_table = (
        expert_ids[:, :, None] == jnp.arange(experts, dtype=jnp.int32)[None, None, :]
    ).astype(jnp.float32)
    gates = jnp.sum(choose_table * router_probs[:, None, :], axis=-1)
    shared_gu = jnp.dot(h2_low, w_shared_in, preferred_element_type=jnp.float32)
    shared_act, shared_slope = silu_parts(shared_gu[:, :hidden_units])
    shared_up = shared_gu[:, hidden_units:]
    shared_hidden = (shared_act * shared_up).astype(jnp.bfloat16)
    shared_out = jnp.dot(shared_hidden, w_shared_down, preferred_element_type=jnp.float32)
    flat_ids = expert_ids.reshape(-1)
    live_flat = jnp.repeat(live_rows, top_k)
    pick_table = (
        (flat_ids[:, None] == jnp.arange(experts, dtype=jnp.int32)[None, :]) & live_flat[:, None]
    ).astype(jnp.int32)
    slot_rank = jnp.sum((jnp.cumsum(pick_table, axis=0) - pick_table) * pick_table, axis=-1)
    slot_index = jnp.where(live_flat, flat_ids * capacity + slot_rank, experts * capacity)
    slot_source = (
        jnp.full((experts * capacity,), seq_slots * top_k, jnp.int32)
        .at[slot_index]
        .set(jnp.arange(seq_slots * top_k, dtype=jnp.int32), mode="drop")
    )
    send_rows = jnp.take(h2_low, slot_source // top_k, axis=0, mode="fill", fill_value=0).reshape(
        experts, capacity, width
    )
    counts = lax.psum(jnp.sum(pick_table, axis=0), ("dp", "expert"))
    slot_rows = lax.all_to_all(send_rows, "expert", split_axis=0, concat_axis=0, tiled=True)
    slot_count = slot_rows.shape[1]
    grouped = slot_rows.reshape(-1, local_experts, slot_count, width)
    gate_up = jnp.einsum("nscd,sdf->nscf", grouped, w_expert_in, preferred_element_type=jnp.float32)
    activation, unused_slope = silu_parts(gate_up[..., :hidden_units])
    hidden_low = (activation * gate_up[..., hidden_units:]).astype(jnp.bfloat16)
    result_rows = jnp.einsum(
        "nscf,sfd->nscd", hidden_low, w_expert_down, preferred_element_type=jnp.float32
    ).astype(jnp.bfloat16)
    returned_rows = lax.all_to_all(
        result_rows.reshape(-1, slot_count, width),
        "expert",
        split_axis=0,
        concat_axis=0,
        tiled=True,
    )
    kept_gate_up = gate_up.reshape(-1, slot_count, 2 * hidden_units)
    picked = jnp.take(
        returned_rows.reshape(-1, width), slot_index, axis=0, mode="fill", fill_value=0
    ).reshape(seq_slots, top_k, width)
    picked_full = picked.astype(jnp.float32)
    routed_out = jnp.sum(gates[:, :, None] * picked_full, axis=1)
    result = (x_mid + live_col * (shared_out + routed_out)).astype(jnp.bfloat16)
    grad_top = dout.astype(jnp.float32)
    grad_branch = live_col * grad_top
    grad_branch_low = grad_branch.astype(jnp.bfloat16)
    grad_shared_down = jnp.dot(shared_hidden.T, grad_branch_low, preferred_element_type=jnp.float32)
    grad_hidden = jnp.dot(grad_branch_low, w_shared_down.T, preferred_element_type=jnp.float32)
    grad_shared_gu = jnp.concatenate(
        [grad_hidden * shared_up * shared_slope, grad_hidden * shared_act], axis=-1
    ).astype(jnp.bfloat16)
    grad_shared_in = jnp.dot(h2_low.T, grad_shared_gu, preferred_element_type=jnp.float32)
    grad_h2 = jnp.dot(grad_shared_gu, w_shared_in.T, preferred_element_type=jnp.float32)
    grad_picked = (
        (gates[:, :, None] * grad_branch[:, None, :]).astype(jnp.bfloat16).reshape(-1, width)
    )
    grad_gates = jnp.sum(picked_full * grad_branch[:, None, :], axis=-1)
    grad_send = jnp.take(grad_picked, slot_source, axis=0, mode="fill", fill_value=0).reshape(
        experts, capacity, width
    )
    grad_recv = lax.all_to_all(grad_send, "expert", split_axis=0, concat_axis=0, tiled=True)
    owners = grad_recv.shape[0] // local_experts
    grad_result = grad_recv.reshape(owners, local_experts, capacity, width)
    rows_held = slot_rows.reshape(owners, local_experts, capacity, width)
    gate_up_held = kept_gate_up.reshape(owners, local_experts, capacity, 2 * hidden_units)
    expert_act, expert_slope = silu_parts(gate_up_held[..., :hidden_units])
    expert_up = gate_up_held[..., hidden_units:]
    expert_hidden = (expert_act * expert_up).astype(jnp.bfloat16)
    grad_expert_down = jnp.einsum(
        "nscf,nscd->sfd", expert_hidden, grad_result, preferred_element_type=jnp.float32
    )
    grad_expert_hidden = jnp.einsum(
        "nscd,sfd->nscf", grad_result, w_expert_down, preferred_element_type=jnp.float32
    )
    grad_expert_gu = jnp.concatenate(
        [grad_expert_hidden * expert_up * expert_slope, grad_expert_hidden * expert_act], axis=-1
    ).astype(jnp.bfloat16)
    grad_expert_in = jnp.einsum(
        "nscd,nscf->sdf", rows_held, grad_expert_gu, preferred_element_type=jnp.float32
    )
    grad_rows = jnp.einsum(
        "nscf,sdf->nscd", grad_expert_gu, w_expert_in, preferred_element_type=jnp.float32
    ).astype(jnp.bfloat16)
    grad_back = lax.all_to_all(
        grad_rows.reshape(-1, capacity, width), "expert", split_axis=0, concat_axis=0, tiled=True
    )
    grad_slots = jnp.take(
        grad_back.reshape(-1, width), slot_index, axis=0, mode="fill", fill_value=0
    ).reshape(seq_slots, top_k, width)
    grad_h2 = grad_h2 + jnp.sum(grad_slots.astype(jnp.float32), axis=1)
    grad_probs = jnp.sum(choose_table * grad_gates[:, :, None], axis=1)
    grad_logits = (
        router_probs * (grad_probs - jnp.sum(grad_probs * router_probs, axis=-1, keepdims=True))
    ).astype(jnp.bfloat16)
    grad_router = jnp.dot(h2_low.T, grad_logits, preferred_element_type=jnp.float32)
    grad_h2 = grad_h2 + jnp.dot(grad_logits, w_router.T, preferred_element_type=jnp.float32)
    grad_mid_norm, grad_norm2 = norm_back(grad_h2, x_mid, inverse_two, norm2)
    grad_mid = grad_top + grad_mid_norm
    grad_attn_branch = (live_col * grad_mid).astype(jnp.bfloat16)
    grad_out_weight = jnp.dot(attended_low.T, grad_attn_branch, preferred_element_type=jnp.float32)
    grad_attended = (
        jnp.dot(grad_attn_branch, w_out.T, preferred_element_type=jnp.float32)
        .astype(jnp.bfloat16)
        .reshape(seq_slots, heads, HEAD_DIM)
    )
    grad_queries, grad_keys, grad_values = attention_backward(
        queries, keys_in, values_in, grad_attended, log_norm, seq_length
    )
    grad_proj = (
        jnp.stack(
            [
                rotate(grad_queries, cosine, -sine_t),
                rotate(grad_keys, cosine, -sine_t),
                grad_values,
            ],
            axis=1,
        )
        .astype(jnp.bfloat16)
        .reshape(seq_slots, 3 * width)
    )
    grad_qkv_weight = jnp.dot(h1_low.T, grad_proj, preferred_element_type=jnp.float32)
    grad_h1 = jnp.dot(grad_proj, w_qkv.T, preferred_element_type=jnp.float32)
    grad_in_norm, grad_norm1 = norm_back(grad_h1, x_full, inverse_one, norm1)
    grad_input = grad_mid + grad_in_norm
    expert_in_sum, expert_down_sum = reduce_experts(grad_expert_in, grad_expert_down)
    norm1_sum, qkv_sum, out_sum, norm2_sum, router_sum, shared_in_sum, shared_down_sum = (
        lax.psum_scatter(grad_norm1, ("dp", "expert"), scatter_dimension=0, tiled=True),
        lax.psum_scatter(grad_qkv_weight, ("dp", "expert"), scatter_dimension=0, tiled=True),
        lax.psum_scatter(grad_out_weight, ("dp", "expert"), scatter_dimension=0, tiled=True),
        lax.psum_scatter(grad_norm2, ("dp", "expert"), scatter_dimension=0, tiled=True),
        lax.psum_scatter(grad_router, ("dp", "expert"), scatter_dimension=0, tiled=True),
        lax.psum_scatter(grad_shared_in, ("dp", "expert"), scatter_dimension=0, tiled=True),
        lax.psum_scatter(grad_shared_down, ("dp", "expert"), scatter_dimension=1, tiled=True),
    )
    return (
        result,
        grad_input,
        norm1_sum,
        qkv_sum,
        out_sum,
        norm2_sum,
        router_sum,
        shared_in_sum,
        shared_down_sum,
        expert_in_sum,
        expert_down_sum,
        counts,
    )


def solution(mesh):
    return jax.shard_map(
        per_device,
        mesh=mesh,
        in_specs=(
            P(("dp", "expert"), None),
            P(("dp", "expert")),
            P(("dp", "expert"), None),
            P(),
            P(),
            P(),
            P(),
            P(),
            P(),
            P(),
            P("expert", None, None),
            P("expert", None, None),
            P(("dp", "expert"), None),
        ),
        out_specs=(
            P(("dp", "expert"), None),
            P(("dp", "expert"), None),
            P(("dp", "expert")),
            P(("dp", "expert"), None),
            P(("dp", "expert"), None),
            P(("dp", "expert")),
            P(("dp", "expert"), None),
            P(("dp", "expert"), None),
            P(None, ("dp", "expert")),
            P("expert", "dp", None),
            P("expert", "dp", None),
            P(),
        ),
        check_vma=False,
    )
```

profile of v0, /device:TPU:0, one launch (start us, length us, event | category | flops | bytes accessed | tf_op | source)
XLA Modules:
  0.0 1829.5 jit_solution(8007353251317582185)
XLA Ops:
  22.1 8.3 reduce-window.6
  36.7 14.0 scatter_custom_fusion
  52.6 2.4 fusion.72
  55.0 8.8 fusion.63
  63.8 3.3 fusion.86
  68.5 3.2 copy.141
  71.7 3.2 copy.142
  74.9 5.5 subtract_convert_fusion.3
  80.4 3.3 fusion.87
  85.4 2.4 copy-done.1
  87.8 4.6 fusion.44
  92.5 2.3 multiply_reduce_fusion.5
  97.6 21.9 %gather_fusion = bf16[3840,1280]{1,0:T(8,128)(2,1)} fusion(bf16[512,1280]{1,0:T(8,128)(2,1)} %multiply_convert_fusion.4, s32[4096]{0:T(1024)S(1)} %copy-done.57), kind=kCustom, calls=%fused_computation.2 | custom fusion | bytes 19676160 | tf_op jit(solution)/shard_map/jit(_take)/gather | solution.py:202
  119.5 7.0 broadcast_select_fusion.1
  126.5 221.4 %all_to_all.20 = bf16[16,240,1280]{2,1,0:T(8,128)(2,1)S(1)} all-to-all(bf16[16,240,1280]{2,1,0:T(8,128)(2,1)S(1)} %broadcast_select_fusion.1), channel_id=1, replica_groups=mesh['dp'=4,'expert'=8] {'expert'}, dimensions={0} | all-to-all | bytes 19660800 | tf_op jit(solution)/shard_map/all_to_all | solution.py:206
  347.9 21.4 %convolution_bitcast_fusion = f32[8,2,240,1792]{3,2,0,1:T(8,128)} fusion(bf16[8,2,240,1280]{3,2,1,0:T(8,128)(2,1)S(1)} %bitcast.127, bf16[2,1280,1792]{2,1,0:T(8,128)(2,1)S(1)} %bitcast.139), kind=kOutput, calls=%fused_computation.20 | convolution fusion | flops 17616076800 | bytes 46530560 | tf_op jit(solution)/shard_map/nscd,sdf->nscf/dot_general | solution.py:209
  369.3 10.1 multiply_convert_fusion.1
  379.4 2.8 copy-done.20
  382.2 14.8 fusion.16
  397.0 8.1 copy.105
  405.1 5.4 all-to-all-start.1
  412.8 7.5 mul.573
  420.3 19.5 %mul.574 = f32[3584,1280]{1,0:T(8,128)} reshape(f32[512,7,1280]{2,1,0:T(8,128)} %mul.573) | data formatting | bytes 36700160 | tf_op jit(solution)/shard_map/mul | solution.py:240
  443.5 181.8 %all-to-all-done.1 = bf16[16,240,1280]{2,1,0:T(8,128)(2,1)} async-done(((bf16[16,240,1280]{2,1,0:T(8,128)(2,1)}), bf16[16,240,1280]{2,1,0:T(8,128)(2,1)}, u32[]{:S(2)}, u32[]{:S(2)}) %all-to-all-start.1) | async-done | bytes 9830432 | tf_op jit(solution)/shard_map/all_to_all | solution.py:215
  625.3 24.2 %gather_fusion.2 = bf16[3584,1280]{1,0:T(8,128)(2,1)} fusion(bf16[3840,1280]{1,0:T(8,128)(2,1)} %bitcast.17, s32[4096]{0:T(1024)S(1)} %pad_clamp_fusion.1), kind=kCustom, calls=%fused_computation.clone | custom fusion | bytes 18364416 | tf_op jit(solution)/shard_map/jit(_take)/gather | solution.py:223
  649.5 10.8 multiply_reduce_fusion.1
  664.5 11.5 multiply_convert_fusion
  676.1 25.4 %gather_fusion.1 = bf16[3840,1280]{1,0:T(8,128)(2,1)} fusion(bf16[3584,1280]{1,0:T(8,128)(2,1)} %multiply_convert_fusion, s32[4096]{0:T(1024)} %pad_clamp_fusion), kind=kCustom, calls=%fused_computation.3 | custom fusion | bytes 19676160 | tf_op jit(solution)/shard_map/jit(_take)/gather | solution.py:243
  701.4 9.6 broadcast_select_fusion
  711.0 5.2 all-to-all-start.2
  719.3 214.3 %all-to-all-done.2 = bf16[16,240,1280]{2,1,0:T(8,128)(2,1)} async-done(((bf16[16,240,1280]{2,1,0:T(8,128)(2,1)}), bf16[16,240,1280]{2,1,0:T(8,128)(2,1)}, u32[]{:S(2)}, u32[]{:S(2)}) %all-to-all-start.2) | async-done | bytes 9830432 | tf_op jit(solution)/shard_map/all_to_all | solution.py:246
  933.7 15.0 bitcast_convert_fusion.1
  948.7 26.2 %fusion.1 = (bf16[8,2,240,896]{3,2,0,1:T(8,128)(2,1)}, bf16[8,2,240,896]{3,2,0,1:T(8,128)(2,1)}) fusion(f32[8,2,240,1792]{3,2,0,1:T(8,128)} %convolution_bitcast_fusion, bf16[2,896,1280]{2,1,0:T(8,128)(2,1)} %param.26, bf16[8,2,240,1280]{3,2,1,0:T(8,128)(2,1)} %bitcast.19), kind=kOutput, calls=%fused_computation.13 | convolution fusion | flops 8852766720 | bytes 55705600 | tf_op jit(solution)/shard_map/nscd,sfd->nscf/dot_general | solution.py:257
  974.9 25.2 %bitcast_convert_fusion = bf16[2,1280,1792]{2,1,0:T(8,128)(2,1)} fusion(bf16[8,2,240,1280]{3,2,1,0:T(8,128)(2,1)} %bitcast.128, bf16[8,2,240,896]{3,2,0,1:T(8,128)(2,1)} %get-tuple-element.79, bf16[8,2,240,896]{3,2,0,1:T(8,128)(2,1)} %get-tuple-element.78), kind=kOutput, calls=%fused_computation.6 | convolution fusion | flops 17648189440 | bytes 32768000 | tf_op jit(solution)/shard_map/nscd,nscf->sdf/dot_general | solution.py:263
  1000.7 5.4 fusion.89
  1006.1 3.4 multiply_convert_fusion.6
  1010.4 3.9 fusion.54
  1014.4 25.1 %fusion.17 = bf16[8,2,240,1280]{3,2,0,1:T(8,128)(2,1)} fusion(bf16[2,1280,1792]{2,1,0:T(8,128)(2,1)} %param.25, bf16[8,2,240,896]{3,2,0,1:T(8,128)(2,1)} %get-tuple-element.79, bf16[8,2,240,896]{3,2,0,1:T(8,128)(2,1)} %get-tuple-element.78), kind=kOutput, calls=%fused_computation.43 | convolution fusion | flops 17648517120 | bytes 32768000 | tf_op jit(solution)/shard_map/nscf,sdf->nscd/dot_general | solution.py:266
  1039.5 8.5 copy.108
  1048.0 5.2 all-to-all-start.3
  1053.3 8.3 fusion.52
  1061.8 260.2 %all-to-all-done.3 = bf16[16,240,1280]{2,1,0:T(8,128)(2,1)} async-done(((bf16[16,240,1280]{2,1,0:T(8,128)(2,1)}), bf16[16,240,1280]{2,1,0:T(8,128)(2,1)}, u32[]{:S(2)}, u32[]{:S(2)}) %all-to-all-start.3) | async-done | bytes 9830432 | tf_op jit(solution)/shard_map/all_to_all | solution.py:269
  1322.0 24.3 %gather_fusion.3 = bf16[3584,1280]{1,0:T(8,128)(2,1)} fusion(bf16[3840,1280]{1,0:T(8,128)(2,1)} %bitcast.25, s32[4096]{0:T(1024)S(1)} %copy-done.52), kind=kCustom, calls=%fused_computation.1.clone | custom fusion | bytes 18364416 | tf_op jit(solution)/shard_map/jit(_take)/gather | solution.py:272
  1346.3 18.9 %select_convert_fusion = (f32[3584,1280]{1,0:T(8,128)}, f32[3584,1280]{1,0:T(8,128)}) fusion(bf16[3584,1280]{1,0:T(8,128)(2,1)} %gather_fusion.3, pred[3584]{0:T(1024)(128)(4,1)S(1)} %copy-done.61, bf16[3584,1280]{1,0:T(8,128)(2,1)} %gather_fusion.2), kind=kLoop, calls=%fused_computation.36 | loop fusion | flops 18350080 | bytes 55053824 | tf_op jit(solution)/shard_map/convert_element_type | solution.py:275
  1365.1 19.3 %reshape.325 = f32[512,7,1280]{2,1,0:T(8,128)} reshape(f32[3584,1280]{1,0:T(8,128)} %get-tuple-element.98) | data formatting | bytes 36700160 | tf_op jit(solution)/shard_map/convert_element_type | solution.py:275
  1384.4 12.3 reduce_sum.165
  1396.7 6.4 convolution_add_fusion.2
  1406.7 4.7 fusion.85
  1412.2 4.7 convolution_convert_fusion.2
  1417.0 2.6 copy.110
  1419.6 11.3 multiply_reduce_fusion.2
  1430.9 6.3 multiply_convert_fusion.2
  1437.3 2.3 multiply_bitcast_fusion.1
  1448.7 6.3 copy.121
  1455.1 12.4 fusion.61
  1468.1 38.8 %psum.7 = s32[16]{0:T(128)} all-reduce(s32[16]{0:T(128)S(1)} %copy-done.74), channel_id=1, replica_groups=mesh['dp'=4,'expert'=8] {'dp','expert'}, use_global_device_ids=true, to_apply=%region_31.33 | all-reduce | flops 16 | bytes 128 | tf_op jit(solution)/shard_map/psum | solution.py:205
  1508.3 2.9 convert_element_type.161
  1511.2 12.1 fusion.41
  1523.3 41.8 %all-reduce.4 = (f32[1280]{0:T(1024)S(1)}, f32[1280]{0:T(1024)S(1)}) all-reduce(f32[1280]{0:T(1024)S(1)} %get-tuple-element.56, f32[1280]{0:T(1024)S(1)} %get-tuple-element.54), channel_id=2, replica_groups=mesh['dp'=4,'expert'=8] {'dp','expert'}, use_global_device_ids=true, to_apply=%region_20.22.clone | all-reduce | flops 2560 | bytes 20480
  1566.3 19.3 %reshape.324 = f32[512,7,1280]{2,1,0:T(8,128)} reshape(f32[3584,1280]{1,0:T(8,128)} %get-tuple-element.99) | data formatting | bytes 36700160 | tf_op jit(solution)/shard_map/convert_element_type | solution.py:226
  1586.2 28.3 %multiply_reduce_fusion = f32[512,1280]{1,0:T(8,128)S(1)} fusion(f32[512,7,1280]{2,1,0:T(8,128)} %reshape.324, f32[512,7]{1,0:T(8,128)S(1)} %copy-done.28), kind=kLoop, calls=%fused_computation.5 | loop fusion | flops 8519680 | bytes 20985856 | tf_op jit(solution)/shard_map/reduce_sum | solution.py:227
  1614.6 2.6 fusion.35
  1620.4 4.3 convert_element_type.159
  1624.8 197.1 %reduce-scatter.11.cloned.1.call-done = f32[40,3840]{1,0:T(8,128)} async-done(((f32[1280,3840]{1,0:T(8,128)}), f32[40,3840]{1,0:T(8,128)}) %reduce-scatter.11.cloned.1.call-update) | async-done | bytes 614416 | tf_op jit(solution)/shard_map/reduce_scatter | solution.py:313
  (247 shorter events, 62.7 us)
Async XLA Ops:
  8.0 84.4 %copy-start = (bf16[1280,1280]{1,0:T(8,128)(2,1)S(1)}, bf16[1280,1280]{1,0:T(8,128)(2,1)}, u32[]{:S(2)}) copy-start(bf16[1280,1280]{1,0:T(8,128)(2,1)} %param.20) | copy-start | bytes 9830404
  15.3 48.4 %copy-start.44 = (s32[3584]{0:T(1024)}, s32[3584]{0:T(1024)S(1)}, u32[]{:S(2)}) copy-start(s32[3584]{0:T(1024)S(1)} %eq.41) | copy-start | bytes 43012
  55.0 20.0 %copy-start.25 = (f32[512,64]{1,0:T(8,128)}, f32[512,64]{1,0:T(8,128)S(1)}, u32[]{:S(2)}) copy-start(f32[512,64]{1,0:T(8,128)S(1)} %get-tuple-element.102) | copy-start | bytes 393220
  63.8 4.7 copy-start.19
  74.9 5.5 copy-start.33
  83.8 4.0 copy-start.1
  83.8 4.0 copy-start.37
  87.8 4.6 copy-start.53
  87.8 4.6 copy-start.21
  87.8 4.6 copy-start.63
  92.5 3.8 copy-start.55
  97.6 21.9 %copy-start.71 = (pred[16,240]{1,0:T(8,128)(4,1)S(1)}, pred[16,240]{1,0:T(8,128)(4,1)}, u32[]{:S(2)}) copy-start(pred[16,240]{1,0:T(8,128)(4,1)} %broadcast_in_dim.145) | copy-start | bytes 11524
  119.5 228.4 %slice-start.3 = ((s8[9175040]{0:T(1024)(128)(4,1)}), s8[4194304]{0:T(1024)(128)(4,1)S(1)}, s32[]{:S(2)}) async-start(s8[9175040]{0:T(1024)(128)(4,1)} %bitcast.138), calls=%async_computation.20 | async-start | bytes 8388608
  119.5 228.4 %slice-start.4 = ((s8[9175040]{0:T(1024)(128)(4,1)}), s8[4194304]{0:T(1024)(128)(4,1)S(1)}, s32[]{:S(2)}) async-start(s8[9175040]{0:T(1024)(128)(4,1)} %bitcast.138), calls=%async_computation.21 | async-start | bytes 8388608
  126.5 221.4 %slice-start.5 = ((s8[9175040]{0:T(1024)(128)(4,1)}), s8[786432]{0:T(1024)(128)(4,1)S(1)}, s32[]{:S(2)}) async-start(s8[9175040]{0:T(1024)(128)(4,1)} %bitcast.138), calls=%async_computation.22 | async-start | bytes 1572864
  347.9 21.4 %copy-start.18 = (bf16[16,240,1280]{2,1,0:T(8,128)(2,1)}, bf16[16,240,1280]{2,1,0:T(8,128)(2,1)S(1)}, u32[]{:S(2)}) copy-start(bf16[16,240,1280]{2,1,0:T(8,128)(2,1)S(1)} %all_to_all.20) | copy-start | bytes 29491204
  405.1 5.4 copy-start.69
  405.1 220.2 %all-to-all-start.1 = ((bf16[16,240,1280]{2,1,0:T(8,128)(2,1)}), bf16[16,240,1280]{2,1,0:T(8,128)(2,1)}, u32[]{:S(2)}, u32[]{:S(2)}) async-start(bf16[16,240,1280]{2,1,0:T(8,128)(2,1)} %bitcast.119), calls=%async_computation.1 | async-start | bytes 19660800 | tf_op jit(solution)/shard_map/all_to_all | solution.py:215
  420.3 19.5 %copy-start.45 = (s32[3584]{0:T(1024)S(1)}, s32[3584]{0:T(1024)}, u32[]{:S(2)}) copy-start(s32[3584]{0:T(1024)} %copy-done.44) | copy-start | bytes 43012
  420.3 19.5 %copy-start.48 = (s32[3584]{0:T(1024)S(1)}, s32[3584]{0:T(1024)}, u32[]{:S(2)}) copy-start(s32[3584]{0:T(1024)} %copy-done.47) | copy-start | bytes 43012
  420.3 19.5 %copy-start.62 = (pred[3584]{0:T(1024)(128)(4,1)S(1)}, pred[3584]{0:T(1024)(128)(4,1)}, u32[]{:S(2)}) copy-start(pred[3584]{0:T(1024)(128)(4,1)} %and.62) | copy-start | bytes 10756
  420.3 19.5 %copy-start.50 = (s32[3840]{0:T(1024)S(1)}, s32[3840]{0:T(1024)}, u32[]{:S(2)}) copy-start(s32[3840]{0:T(1024)} %copy-done.49) | copy-start | bytes 46084
  420.3 20.2 %copy-start.40 = (bf16[1280,16]{0,1:T(8,128)(2,1)S(1)}, bf16[1280,16]{0,1:T(8,128)(2,1)}, u32[]{:S(2)}) copy-start(bf16[1280,16]{0,1:T(8,128)(2,1)} %param.22) | copy-start | bytes 122884
  439.8 209.7 %copy-start.60 = (pred[3584]{0:T(1024)(128)(4,1)}, pred[3584]{0:T(1024)(128)(4,1)S(1)}, u32[]{:S(2)}) copy-start(pred[3584]{0:T(1024)(128)(4,1)S(1)} %get-tuple-element.74) | copy-start | bytes 10756
  439.8 209.7 %copy-start.51 = (s32[4096]{0:T(1024)}, s32[4096]{0:T(1024)S(1)}, u32[]{:S(2)}) copy-start(s32[4096]{0:T(1024)S(1)} %pad_clamp_fusion.1) | copy-start | bytes 49156
  442.9 206.6 %copy-start.65 = (f32[512]{0:T(512)}, f32[512]{0:T(512)S(1)}, u32[]{:S(2)}) copy-start(f32[512]{0:T(512)S(1)} %fusion.74) | copy-start | bytes 6148
  649.5 12.5 copy-start.46
  664.3 11.8 copy-start.27
  676.1 25.4 %copy-start.70 = (pred[16,240]{1,0:T(8,128)(4,1)S(1)}, pred[16,240]{1,0:T(8,128)(4,1)}, u32[]{:S(2)}) copy-start(pred[16,240]{1,0:T(8,128)(4,1)} %broadcast_in_dim.150) | copy-start | bytes 11524
  711.0 5.3 copy-start.36
  711.0 5.3 copy-start.39
  711.0 5.3 copy-start.59
  711.0 5.3 copy-start.66
  711.0 222.6 %all-to-all-start.2 = ((bf16[16,240,1280]{2,1,0:T(8,128)(2,1)}), bf16[16,240,1280]{2,1,0:T(8,128)(2,1)}, u32[]{:S(2)}, u32[]{:S(2)}) async-start(bf16[16,240,1280]{2,1,0:T(8,128)(2,1)} %broadcast_select_fusion), calls=%async_computation.2 | async-start | bytes 19660800 | tf_op jit(solution)/shard_map/all_to_all | solution.py:246
  716.3 790.7 %all-reduce.7.cloned.1.call-start = ((), (), s32[]{:S(2)}) async-start(), calls=%async_computation.15 | async-start | bytes 163840
  719.3 789.1 %reduce-scatter.19.cloned.1.call-start = ((), (), s32[]{:S(2)}) async-start(), calls=%async_computation.14 | async-start | bytes 5734400 | tf_op jit(solution)/shard_map/reduce_scatter | solution.py:128
  948.7 671.8 %reduce-scatter.17.cloned.1.call-start = ((), (), s32[]{:S(2)}) async-start(), calls=%async_computation.13 | async-start | bytes 11468800 | tf_op jit(solution)/shard_map/reduce_scatter | solution.py:125
  1000.1 5.9 copy-start.64
  1000.1 624.7 %reduce-scatter.21.cloned.1.call-start = ((), (), s32[]{:S(2)}) async-start(), calls=%async_computation.16 | async-start | bytes 4730880
  1000.7 5.4 copy-start.8
  1000.7 5.4 copy-start.75
  1048.0 274.0 %all-to-all-start.3 = ((bf16[16,240,1280]{2,1,0:T(8,128)(2,1)}), bf16[16,240,1280]{2,1,0:T(8,128)(2,1)}, u32[]{:S(2)}, u32[]{:S(2)}) async-start(bf16[16,240,1280]{2,1,0:T(8,128)(2,1)} %bitcast.120), calls=%async_computation.3 | async-start | bytes 19660800 | tf_op jit(solution)/shard_map/all_to_all | solution.py:269
  1053.2 571.6 %reduce-scatter.15.cloned.1.call-start = ((), (), s32[]{:S(2)}) async-start(), calls=%async_computation.12 | async-start | bytes 9461760 | tf_op jit(solution)/shard_map/reduce_scatter | solution.py:317
  1061.6 260.4 %copy-start.52 = (s32[4096]{0:T(1024)S(1)}, s32[4096]{0:T(1024)}, u32[]{:S(2)}) copy-start(s32[4096]{0:T(1024)} %copy-done.51) | copy-start | bytes 49156
  1061.6 563.2 %reduce-scatter.13.cloned.1.call-start = ((), (), s32[]{:S(2)}) async-start(), calls=%async_computation.11 | async-start | bytes 6758400 | tf_op jit(solution)/shard_map/reduce_scatter | solution.py:314
  1322.0 24.3 %copy-start.61 = (pred[3584]{0:T(1024)(128)(4,1)S(1)}, pred[3584]{0:T(1024)(128)(4,1)}, u32[]{:S(2)}) copy-start(pred[3584]{0:T(1024)(128)(4,1)} %copy-done.60) | copy-start | bytes 10756
  1396.7 6.4 copy-start.3
  1396.7 6.4 copy-start.41
  1396.7 6.4 copy-start.43
  1396.7 6.4 copy-start.56
  1396.7 6.4 copy-start.68
  1411.5 410.4 %reduce-scatter.11.cloned.1.call-start = ((), (), s32[]{:S(2)}) async-start(), calls=%async_computation.10 | async-start | bytes 20275200 | tf_op jit(solution)/shard_map/reduce_scatter | solution.py:313
  1419.6 11.3 slice-start
  1419.6 11.3 slice-start.1
  1419.6 11.3 slice-start.2
  1430.9 6.3 copy-start.15
  1430.9 6.3 copy-start.17
  1448.7 6.3 copy-start.72
  1448.7 6.3 copy-start.73
  1566.3 20.0 %copy-start.28 = (f32[512,7]{1,0:T(8,128)S(1)}, f32[512,7]{1,0:T(8,128)}, u32[]{:S(2)}) copy-start(f32[512,7]{1,0:T(8,128)} %copy-done.27) | copy-start | bytes 43012
  1586.2 28.3 %copy-start.4 = (f32[512,1280]{1,0:T(8,128)S(1)}, f32[512,1280]{1,0:T(8,128)}, u32[]{:S(2)}) copy-start(f32[512,1280]{1,0:T(8,128)} %copy-done.2) | copy-start | bytes 7864324
  1586.2 28.3 %copy-start.32 = (bf16[512,896]{1,0:T(8,128)(2,1)S(1)}, bf16[512,896]{1,0:T(8,128)(2,1)}, u32[]{:S(2)}) copy-start(bf16[512,896]{1,0:T(8,128)(2,1)} %copy-done.31) | copy-start | bytes 2752516
  1586.2 28.3 %copy-start.76 = (bf16[896,1280]{1,0:T(8,128)(2,1)S(1)}, bf16[896,1280]{1,0:T(8,128)(2,1)}, u32[]{:S(2)}) copy-start(bf16[896,1280]{1,0:T(8,128)(2,1)} %param.24) | copy-start | bytes 6881284
  1614.6 3.6 copy-start.24
  (29 other events, 54.3 us)
Sparse Core Ops, SparseCore 0:
  722.7 169.1 all-reduce.6
Sparse Core Ops, SparseCore 1:
  948.8 54.8 reduce-scatter.18
  1006.7 92.7 reduce-scatter.16
  1102.1 199.6 reduce-scatter.20
  1304.7 153.1 reduce-scatter.14
  1460.7 145.6 reduce-scatter.12
  1613.4 208.4 reduce-scatter.10
where the time goes:
time: 1840 us; the launch traced here: 1830 us
  waiting for transfers between devices  853 us (46%)
  blocking collectives  302 us (16%)
  local copies, waits for them, and re-layouts  240 us (13%)
  matrix products  233 us (13%)
  other arithmetic  167 us (9%)
    all_to_all x1, waiting for transfers between devices, per_device(): lax.all_to_all(grad_rows.reshape(-1, capacity, width), 'expert', split_ax...  260 us
    all_to_all x1, blocking collectives, per_device(): lax.all_to_all(send_rows, 'expert', split_axis=0, concat_axis=0, tiled=True)  221 us
    all_to_all x1, waiting for transfers between devices, per_device(): lax.all_to_all(grad_send, 'expert', split_axis=0, concat_axis=0, tiled=True)  214 us
    reduce_scatter x1, waiting for transfers between devices, per_device(): lax.psum_scatter(grad_qkv_weight, ('dp', 'expert'), scatter_dimension=0,...  197 us
    all_to_all x1, waiting for transfers between devices, per_device(): lax.all_to_all(result_rows.reshape(-1, slot_count, width), 'expert', spli...  182 us
    unnamed x1, blocking collectives  41.8 us
    psum x1, blocking collectives, per_device(): counts = lax.psum(jnp.sum(pick_table, axis=0), ('dp', 'expert'))  38.8 us
  transfers between devices with their start and end apart: 10, of which 4 were waited for; matrix products, arithmetic and copies ran while one was open for 20% of the time, Pallas kernels for 0%

commit v1 on v0

--- a/solution.py
+++ b/solution.py
@@ -129,6 +129,12 @@
             grad_down_part.astype(jnp.bfloat16), "dp", scatter_dimension=1, tiled=True
         ).astype(jnp.float32),
     )
+
+
+def reduce_low(part, dimension):
+    return lax.psum_scatter(
+        part.astype(jnp.bfloat16), ("dp", "expert"), scatter_dimension=dimension, tiled=True
+    ).astype(jnp.float32)
 
 
 def per_device(
@@ -156,6 +162,9 @@
     seq_length = lengths[0]
     live_rows = jnp.arange(seq_slots, dtype=jnp.int32) < seq_length
     live_col = live_rows.astype(jnp.float32)[:, None]
+    grad_top = dout.astype(jnp.float32)
+    grad_branch = live_col * grad_top
+    grad_branch_low = grad_branch.astype(jnp.bfloat16)
     cosine, sine_t = rope_tables(seq_slots, HEAD_DIM)
     x_full = layer_input.astype(jnp.float32)
     h1_full, inverse_one = normalize(x_full, norm1)
@@ -178,57 +187,77 @@
     highest = jnp.max(logits, axis=-1, keepdims=True)
     weights_exp = jnp.exp(logits - highest)
     router_probs = weights_exp / jnp.sum(weights_exp, axis=-1, keepdims=True)
-    choose_table = (
-        expert_ids[:, :, None] == jnp.arange(experts, dtype=jnp.int32)[None, None, :]
-    ).astype(jnp.float32)
-    gates = jnp.sum(choose_table * router_probs[:, None, :], axis=-1)
     shared_gu = jnp.dot(h2_low, w_shared_in, preferred_element_type=jnp.float32)
     shared_act, shared_slope = silu_parts(shared_gu[:, :hidden_units])
     shared_up = shared_gu[:, hidden_units:]
     shared_hidden = (shared_act * shared_up).astype(jnp.bfloat16)
     shared_out = jnp.dot(shared_hidden, w_shared_down, preferred_element_type=jnp.float32)
-    flat_ids = expert_ids.reshape(-1)
-    live_flat = jnp.repeat(live_rows, top_k)
-    pick_table = (
-        (flat_ids[:, None] == jnp.arange(experts, dtype=jnp.int32)[None, :]) & live_flat[:, None]
+    slots = jnp.arange(experts, dtype=jnp.int32)
+    picked = (
+        jnp.any(expert_ids[:, :, None] == slots[None, None, :], axis=1) & live_rows[:, None]
     ).astype(jnp.int32)
-    slot_rank = jnp.sum((jnp.cumsum(pick_table, axis=0) - pick_table) * pick_table, axis=-1)
-    slot_index = jnp.where(live_flat, flat_ids * capacity + slot_rank, experts * capacity)
-    slot_source = (
-        jnp.full((experts * capacity,), seq_slots * top_k, jnp.int32)
-        .at[slot_index]
-        .set(jnp.arange(seq_slots * top_k, dtype=jnp.int32), mode="drop")
-    )
-    send_rows = jnp.take(h2_low, slot_source // top_k, axis=0, mode="fill", fill_value=0).reshape(
-        experts, capacity, width
-    )
-    counts = lax.psum(jnp.sum(pick_table, axis=0), ("dp", "expert"))
-    slot_rows = lax.all_to_all(send_rows, "expert", split_axis=0, concat_axis=0, tiled=True)
-    slot_count = slot_rows.shape[1]
-    grouped = slot_rows.reshape(-1, local_experts, slot_count, width)
-    gate_up = jnp.einsum("nscd,sdf->nscf", grouped, w_expert_in, preferred_element_type=jnp.float32)
-    activation, unused_slope = silu_parts(gate_up[..., :hidden_units])
-    hidden_low = (activation * gate_up[..., hidden_units:]).astype(jnp.bfloat16)
-    result_rows = jnp.einsum(
-        "nscf,sfd->nscd", hidden_low, w_expert_down, preferred_element_type=jnp.float32
-    ).astype(jnp.bfloat16)
-    returned_rows = lax.all_to_all(
-        result_rows.reshape(-1, slot_count, width),
-        "expert",
-        split_axis=0,
-        concat_axis=0,
-        tiled=True,
-    )
-    kept_gate_up = gate_up.reshape(-1, slot_count, 2 * hidden_units)
-    picked = jnp.take(
-        returned_rows.reshape(-1, width), slot_index, axis=0, mode="fill", fill_value=0
-    ).reshape(seq_slots, top_k, width)
-    picked_full = picked.astype(jnp.float32)
-    routed_out = jnp.sum(gates[:, :, None] * picked_full, axis=1)
+    counts = lax.psum(jnp.sum(picked, axis=0), ("dp", "expert"))
+    rank = jnp.where(picked > 0, jnp.cumsum(picked, axis=0) - 1, -1)
+    rank_all = lax.all_gather(rank.T, "expert", axis=0)
+    first_expert = lax.axis_index("expert") * local_experts
+    rank_mine = lax.dynamic_slice_in_dim(rank_all, first_expert, local_experts, axis=1)
+    grad_all = lax.all_gather(grad_branch_low, "expert", axis=0)
+    h2_all = lax.all_gather(h2_low, "expert", axis=0)
+    probs_all = lax.all_gather(router_probs.T, "expert", axis=0)
+    probs_mine = lax.dynamic_slice_in_dim(probs_all, first_expert, local_experts, axis=1)
+    hit = rank_mine[:, :, None, :] == jnp.arange(capacity, dtype=jnp.int32)[None, None, :, None]
+    place = hit.astype(jnp.bfloat16)
+    slot_gate = jnp.sum(jnp.where(hit, probs_mine[:, :, None, :], 0.0), axis=-1)
+    rows_held = jnp.einsum(
+        "nsct,ntd->nscd", place, h2_all, preferred_element_type=jnp.float32
+    ).astype(jnp.bfloat16)
+    grad_rows_in = jnp.einsum("nsct,ntd->nscd", place, grad_all, preferred_element_type=jnp.float32)
+    grad_result = (slot_gate[..., None] * grad_rows_in).astype(jnp.bfloat16)
+    gate_up = jnp.einsum(
+        "nscd,sdf->nscf", rows_held, w_expert_in, preferred_element_type=jnp.float32
+    )
+    expert_act, expert_slope = silu_parts(gate_up[..., :hidden_units])
+    expert_up = gate_up[..., hidden_units:]
+    expert_hidden = (expert_act * expert_up).astype(jnp.bfloat16)
+    result_rows = (
+        jnp.einsum("nscf,sfd->nscd", expert_hidden, w_expert_down, preferred_element_type=jnp.float32)
+        .astype(jnp.bfloat16)
+        .astype(jnp.float32)
+    )
+    slot_dot = jnp.sum(result_rows * grad_rows_in, axis=-1)
+    routed_part = jnp.einsum(
+        "nsct,nscd->ntd",
+        place,
+        (slot_gate[..., None] * result_rows).astype(jnp.bfloat16),
+        preferred_element_type=jnp.float32,
+    ).astype(jnp.bfloat16)
+    grad_expert_down = jnp.einsum(
+        "nscf,nscd->sfd", expert_hidden, grad_result, preferred_element_type=jnp.float32
+    )
+    grad_expert_hidden = jnp.einsum(
+        "nscd,sfd->nscf", grad_result, w_expert_down, preferred_element_type=jnp.float32
+    )
+    grad_expert_gu = jnp.concatenate(
+        [grad_expert_hidden * expert_up * expert_slope, grad_expert_hidden * expert_act], axis=-1
+    ).astype(jnp.bfloat16)
+    grad_expert_in = jnp.einsum(
+        "nscd,nscf->sdf", rows_held, grad_expert_gu, preferred_element_type=jnp.float32
+    )
+    grad_rows = jnp.einsum(
+        "nscf,sdf->nscd", grad_expert_gu, w_expert_in, preferred_element_type=jnp.float32
+    ).astype(jnp.bfloat16)
+    grad_h2_part = jnp.einsum(
+        "nsct,nscd->ntd", place, grad_rows, preferred_element_type=jnp.float32
+    ).astype(jnp.bfloat16)
+    dot_mine = jnp.sum(jnp.where(hit, slot_dot[..., None], 0.0), axis=2)
+    dot_part = lax.dynamic_update_slice_in_dim(
+        jnp.zeros((rank_all.shape[0], experts, seq_slots), jnp.float32), dot_mine, first_expert, axis=1
+    )
+    grad_probs = lax.psum_scatter(dot_part, "expert", scatter_dimension=0, tiled=False).T
+    grad_h2_sum = lax.psum_scatter(grad_h2_part, "expert", scatter_dimension=0, tiled=False)
+    routed_out = lax.psum_scatter(routed_part, "expert", scatter_dimension=0, tiled=False)
+    routed_out = routed_out.astype(jnp.float32)
     result = (x_mid + live_col * (shared_out + routed_out)).astype(jnp.bfloat16)
-    grad_top = dout.astype(jnp.float32)
-    grad_branch = live_col * grad_top
-    grad_branch_low = grad_branch.astype(jnp.bfloat16)
     grad_shared_down = jnp.dot(shared_hidden.T, grad_branch_low, preferred_element_type=jnp.float32)
     grad_hidden = jnp.dot(grad_branch_low, w_shared_down.T, preferred_element_type=jnp.float32)
     grad_shared_gu = jnp.concatenate(
@@ -236,44 +265,7 @@
     ).astype(jnp.bfloat16)
     grad_shared_in = jnp.dot(h2_low.T, grad_shared_gu, preferred_element_type=jnp.float32)
     grad_h2 = jnp.dot(grad_shared_gu, w_shared_in.T, preferred_element_type=jnp.float32)
-    grad_picked = (
-        (gates[:, :, None] * grad_branch[:, None, :]).astype(jnp.bfloat16).reshape(-1, width)
-    )
-    grad_gates = jnp.sum(picked_full * grad_branch[:, None, :], axis=-1)
-    grad_send = jnp.take(grad_picked, slot_source, axis=0, mode="fill", fill_value=0).reshape(
-        experts, capacity, width
-    )
-    grad_recv = lax.all_to_all(grad_send, "expert", split_axis=0, concat_axis=0, tiled=True)
-    owners = grad_recv.shape[0] // local_experts
-    grad_result = grad_recv.reshape(owners, local_experts, capacity, width)
-    rows_held = slot_rows.reshape(owners, local_experts, capacity, width)
-    gate_up_held = kept_gate_up.reshape(owners, local_experts, capacity, 2 * hidden_units)
-    expert_act, expert_slope = silu_parts(gate_up_held[..., :hidden_units])
-    expert_up = gate_up_held[..., hidden_units:]
-    expert_hidden = (expert_act * expert_up).astype(jnp.bfloat16)
-    grad_expert_down = jnp.einsum(
-        "nscf,nscd->sfd", expert_hidden, grad_result, preferred_element_type=jnp.float32
-    )
-    grad_expert_hidden = jnp.einsum(
-        "nscd,sfd->nscf", grad_result, w_expert_down, preferred_element_type=jnp.float32
-    )
-    grad_expert_gu = jnp.concatenate(
-        [grad_expert_hidden * expert_up * expert_slope, grad_expert_hidden * expert_act], axis=-1
-    ).astype(jnp.bfloat16)
-    grad_expert_in = jnp.einsum(
-        "nscd,nscf->sdf", rows_held, grad_expert_gu, preferred_element_type=jnp.float32
-    )
-    grad_rows = jnp.einsum(
-        "nscf,sdf->nscd", grad_expert_gu, w_expert_in, preferred_element_type=jnp.float32
-    ).astype(jnp.bfloat16)
-    grad_back = lax.all_to_all(
-        grad_rows.reshape(-1, capacity, width), "expert", split_axis=0, concat_axis=0, tiled=True
-    )
-    grad_slots = jnp.take(
-        grad_back.reshape(-1, width), slot_index, axis=0, mode="fill", fill_value=0
-    ).reshape(seq_slots, top_k, width)
-    grad_h2 = grad_h2 + jnp.sum(grad_slots.astype(jnp.float32), axis=1)
-    grad_probs = jnp.sum(choose_table * grad_gates[:, :, None], axis=1)
+    grad_h2 = grad_h2 + grad_h2_sum.astype(jnp.float32)
     grad_logits = (
         router_probs * (grad_probs - jnp.sum(grad_probs * router_probs, axis=-1, keepdims=True))
     ).astype(jnp.bfloat16)
@@ -310,12 +302,12 @@
     expert_in_sum, expert_down_sum = reduce_experts(grad_expert_in, grad_expert_down)
     norm1_sum, qkv_sum, out_sum, norm2_sum, router_sum, shared_in_sum, shared_down_sum = (
         lax.psum_scatter(grad_norm1, ("dp", "expert"), scatter_dimension=0, tiled=True),
-        lax.psum_scatter(grad_qkv_weight, ("dp", "expert"), scatter_dimension=0, tiled=True),
-        lax.psum_scatter(grad_out_weight, ("dp", "expert"), scatter_dimension=0, tiled=True),
+        reduce_low(grad_qkv_weight, 0),
+        reduce_low(grad_out_weight, 0),
         lax.psum_scatter(grad_norm2, ("dp", "expert"), scatter_dimension=0, tiled=True),
         lax.psum_scatter(grad_router, ("dp", "expert"), scatter_dimension=0, tiled=True),
-        lax.psum_scatter(grad_shared_in, ("dp", "expert"), scatter_dimension=0, tiled=True),
-        lax.psum_scatter(grad_shared_down, ("dp", "expert"), scatter_dimension=1, tiled=True),
+        reduce_low(grad_shared_in, 0),
+        reduce_low(grad_shared_down, 1),
     )
     return (
         result,

time: 1840 us -> 1440 us (0.78)
  local copies, waits for them, and re-layouts: 240 us -> 35.7 us
  blocking collectives: 302 us -> 116 us
  other arithmetic: 167 us -> 68.4 us
  waiting for transfers between devices: 853 us -> 908 us
  matrix products: 233 us -> 284 us
    all_to_all x3 -> x0, waiting for transfers between devices: 656 us -> none  [the longest x1 260 us: per_device(): lax.all_to_all(grad_rows.reshape(-1, capacity, width), 'expert', split_ax...]
    reduce_scatter x3 -> x6, waiting for transfers between devices: 197 us -> 498 us  [the longest x3 414 us: reduce_low(): lax.psum_scatter(part.astype(jnp.bfloat16), ('dp', 'expert'), scatter_dim...]
    all_to_all x1 -> x0, blocking collectives: 221 us -> none  [per_device(): lax.all_to_all(send_rows, 'expert', split_axis=0, concat_axis=0, tiled=True)]
    unnamed x9 -> x14, waiting for transfers between devices: 0.12 us -> 158 us
    all_gather x0 -> x2, waiting for transfers between devices: none -> 99.3 us  [the longest x1 62.4 us: per_device(): h2_all = lax.all_gather(h2_low, 'expert', axis=0)]
    gather x4 -> x0, local copies, waits for them, and re-layouts: 95.7 us -> none  [the longest x1 25.4 us: per_device(): jnp.take(grad_picked, slot_source, axis=0, mode='fill', fill_value=0)]
    reduce_scatter x1, waiting for transfers between devices: 0.01 us -> 93.3 us  [reduce_experts(): lax.psum_scatter(grad_in_part.astype(jnp.bfloat16), 'dp', scatter_dimensi...]
    reduce_scatter x1, waiting for transfers between devices: 0.01 us -> 59.6 us  [reduce_experts(): lax.psum_scatter(grad_down_part.astype(jnp.bfloat16), 'dp', scatter_dimen...]
  transfers between devices with their start and end apart: 10 -> 12, of which waited for: 4 -> 11; matrix products, arithmetic and copies ran while one was open for 20% -> 21% of each run, Pallas kernels for 0% -> 0%
where the time goes in v1:
time: 1440 us; the launch traced here: 1430 us
  waiting for transfers between devices  908 us (63%)
  matrix products  284 us (20%)
  blocking collectives  116 us (8%)
  other arithmetic  68.4 us (5%)
  local copies, waits for them, and re-layouts  35.7 us (2%)
  between operations  16.2 us (1%)
    reduce_scatter x3, waiting for transfers between devices, reduce_low(): lax.psum_scatter(part.astype(jnp.bfloat16), ('dp', 'expert'), scatter_dim...  414 us
    unnamed x14, waiting for transfers between devices  158 us
    reduce_scatter x1, waiting for transfers between devices, reduce_experts(): lax.psum_scatter(grad_in_part.astype(jnp.bfloat16), 'dp', scatter_dimensi...  93.3 us
    all_gather x1, waiting for transfers between devices, per_device(): h2_all = lax.all_gather(h2_low, 'expert', axis=0)  62.4 us
    reduce_scatter x1, waiting for transfers between devices, reduce_experts(): lax.psum_scatter(grad_down_part.astype(jnp.bfloat16), 'dp', scatter_dimen...  59.6 us
    reduce_scatter x1, waiting for transfers between devices, per_device(): lax.psum_scatter(routed_part, 'expert', scatter_dimension=0, tiled=False)  54.5 us
    unnamed x1, blocking collectives  41.5 us
    psum x1, blocking collectives, per_device(): counts = lax.psum(jnp.sum(picked, axis=0), ('dp', 'expert'))  38 us
  transfers between devices with their start and end apart: 12, of which 11 were waited for; matrix products, arithmetic and copies ran while one was open for 21% of the time, Pallas kernels for 0%

profile of v1, /device:TPU:0, one launch (start us, length us, event | category | flops | bytes accessed | tf_op | source)
XLA Modules:
  0.0 1429.1 jit_solution(4179184265757614407)
XLA Ops:
  7.3 1.8 fusion.43
  9.1 8.7 fusion.58
  17.8 3.3 fusion.77
  22.5 3.2 copy.145
  25.7 3.2 copy.146
  28.9 1.7 fusion.63
  31.4 5.5 subtract_convert_fusion.3
  37.0 3.3 fusion.78
  41.9 2.3 copy-done.1
  44.2 4.3 fusion.45
  48.6 2.3 multiply_reduce_fusion.3
  53.8 2.7 fusion.36
  58.1 1.8 fusion.79
  60.5 18.9 %all-gather.1 = f32[128,512]{1,0:T(8,128)S(1)} all-gather(f32[16,512]{1,0:T(8,128)S(1)} %fusion.76), channel_id=3, replica_groups=mesh['dp'=4,'expert'=8] {'expert'}, dimensions={0}, use_global_device_ids=true | all-gather | bytes 294912 | tf_op jit(solution)/shard_map/all_gather | solution.py:206
  79.5 17.4 %all-gather = s32[128,512]{1,0:T(8,128)S(1)} all-gather(s32[16,512]{1,0:T(8,128)S(1)} %bitcast_select_fusion), channel_id=2, replica_groups=mesh['dp'=4,'expert'=8] {'expert'}, dimensions={0}, use_global_device_ids=true | all-gather | bytes 294912 | tf_op jit(solution)/shard_map/all_gather | solution.py:201
  96.9 62.4 %all-gather.7.cloned.1.call-done = bf16[4096,1280]{1,0:T(8,128)(2,1)} async-done(((bf16[512,1280]{1,0:T(8,128)(2,1)}), bf16[4096,1280]{1,0:T(8,128)(2,1)}) %all-gather.7.cloned.1.call-update) | async-done | bytes 10485776 | tf_op jit(solution)/shard_map/all_gather | solution.py:205
  159.3 12.2 convolution_convert_fusion.2
  171.5 25.8 %convolution_bitcast_fusion = f32[8,2,240,1792]{3,2,0,1:T(8,128)} fusion(bf16[8,2,240,1280]{3,2,1,0:T(8,128)(2,1)} %convolution_convert_fusion.2, bf16[2,1280,1792]{2,1,0:T(8,128)(2,1)} %param.23), kind=kOutput, calls=%fused_computation.20 | convolution fusion | flops 17616076800 | bytes 46530560 | tf_op jit(solution)/shard_map/nscd,sdf->nscf/dot_general | solution.py:216
  197.2 10.4 multiply_convert_fusion.1
  207.6 2.8 copy-done.16
  210.5 12.4 convolution_convert_fusion.3
  222.9 37.0 %all-gather.9.cloned.1.call-done = bf16[4096,1280]{1,0:T(8,128)(2,1)} async-done(((bf16[512,1280]{1,0:T(8,128)(2,1)}), bf16[4096,1280]{1,0:T(8,128)(2,1)}) %all-gather.9.cloned.1.call-update) | async-done | bytes 10485776 | tf_op jit(solution)/shard_map/all_gather | solution.py:204
  259.9 15.0 %fusion.1 = (f32[8,2,240]{2,0,1:T(8,128)S(1)}, f32[8,2,240,1280]{3,2,0,1:T(8,128)}) fusion(bf16[2,8,240,1280]{3,2,1,0:T(8,128)(2,1)} %convolution_convert_fusion.3, bf16[8,512,1280,1]{2,1,0,3:T(8,128)(2,1)} %bitcast.165, s32[8,2,512]{2,1,0:T(2,128)S(1)} %constant_dynamic-slice_fusion.1), kind=kOutput, calls=%fused_computation.5 | convolution fusion | flops 5049872384 | bytes 40025088 | tf_op jit(solution)/shard_map/nsct,ntd->nscd/dot_general | solution.py:214
  274.9 11.8 select_reduce_fusion
  287.5 27.4 %fusion.3 = (bf16[8,2,240,896]{3,2,0,1:T(8,128)(2,1)}, bf16[8,2,240,896]{3,2,0,1:T(8,128)(2,1)}) fusion(f32[8,2,240,1792]{3,2,0,1:T(8,128)} %convolution_bitcast_fusion, bf16[2,896,1280]{2,1,0:T(8,128)(2,1)} %param.24, f32[8,2,240,1280]{3,2,0,1:T(8,128)} %get-tuple-element.98, f32[8,2,240]{2,0,1:T(8,128)S(1)} %copy.103), kind=kOutput, calls=%fused_computation.13 | convolution fusion | flops 8862597120 | bytes 65551360 | tf_op jit(solution)/shard_map/nscd,sfd->nscf/dot_general | solution.py:237
  314.9 25.1 %fusion.8 = bf16[8,2,240,1280]{3,2,1,0:T(8,128)(2,1)} fusion(bf16[2,1280,1792]{2,1,0:T(8,128)(2,1)} %param.23, bf16[8,2,240,896]{3,2,0,1:T(8,128)(2,1)} %get-tuple-element.72, bf16[8,2,240,896]{3,2,0,1:T(8,128)(2,1)} %get-tuple-element.71), kind=kOutput, calls=%fused_computation.29 | convolution fusion | flops 17648517120 | bytes 32768000 | tf_op jit(solution)/shard_map/nscf,sdf->nscd/dot_general | solution.py:246
  340.0 12.0 bitcast_convert_fusion
  352.3 5.4 fusion.80
  357.7 3.3 multiply_convert_fusion.8
  361.9 2.9 convolution_convert_fusion.6
  365.0 6.6 convolution_convert_fusion.4
  373.9 2.2 fusion.81
  376.6 17.2 %bitcast_convert_fusion.3 = bf16[2,896,1280]{2,1,0:T(8,128)(2,1)} fusion(bf16[8,2,240,896]{3,2,0,1:T(8,128)(2,1)} %copy-done.16, f32[8,2,240,1280]{3,2,0,1:T(8,128)} %get-tuple-element.98, f32[8,2,240]{2,0,1:T(8,128)S(1)} %copy.103), kind=kOutput, calls=%fused_computation.35 | convolution fusion | flops 8820162560 | bytes 31144960 | tf_op jit(solution)/shard_map/nscf,nscd->sfd/dot_general | solution.py:234
  393.9 25.2 %bitcast_convert_fusion.2 = bf16[2,1280,1792]{2,1,0:T(8,128)(2,1)} fusion(bf16[8,2,240,1280]{3,2,1,0:T(8,128)(2,1)} %convolution_convert_fusion.2, bf16[8,2,240,896]{3,2,0,1:T(8,128)(2,1)} %get-tuple-element.72, bf16[8,2,240,896]{3,2,0,1:T(8,128)(2,1)} %get-tuple-element.71), kind=kOutput, calls=%fused_computation.7 | convolution fusion | flops 17648189440 | bytes 32768000 | tf_op jit(solution)/shard_map/nscd,nscf->sdf/dot_general | solution.py:243
  419.4 11.0 bitcast_convert_fusion.1
  430.5 29.4 %reduce-scatter.16.cloned.1.call-done = bf16[1,512,1280]{2,1,0:T(8,128)(2,1)} async-done(((bf16[8,512,1280]{2,1,0:T(8,128)(2,1)}), bf16[1,512,1280]{2,1,0:T(8,128)(2,1)}) %reduce-scatter.16.cloned.1.call-update) | async-done | bytes 1310736 | tf_op jit(solution)/shard_map/reduce_scatter | solution.py:257
  459.9 5.9 convolution_add_fusion.2
  469.4 3.6 convolution_convert_fusion.5
  473.9 4.7 convolution_convert_fusion.7
  478.6 2.6 copy.110
  481.2 11.1 multiply_reduce_fusion
  492.3 6.3 multiply_convert_fusion.2
  498.7 2.3 multiply_bitcast_fusion.1
  502.6 2.0 subtract_convert_fusion.1
  506.1 1.8 fusion.49
  507.9 2.2 pad_maximum_fusion.1
  510.1 6.3 copy.121
  516.4 10.7 convolution_convert_fusion
  527.9 38.0 %psum.7 = s32[16]{0:T(128)} all-reduce(s32[16]{0:T(128)S(1)} %convert_reduce_fusion), channel_id=1, replica_groups=mesh['dp'=4,'expert'=8] {'dp','expert'}, use_global_device_ids=true, to_apply=%region_31.32 | all-reduce | flops 16 | bytes 128 | tf_op jit(solution)/shard_map/psum | solution.py:199
  565.9 36.5 %reduce-scatter.30.cloned.1.call-done = bf16[896,40]{0,1:T(8,128)(2,1)} async-done(((bf16[896,1280]{0,1:T(8,128)(2,1)}), bf16[896,40]{0,1:T(8,128)(2,1)}) %reduce-scatter.30.cloned.1.call-update) | async-done | bytes 71696
  604.0 141.2 %reduce-scatter.24.cloned.1.call-done = bf16[40,1792]{1,0:T(8,128)(2,1)} async-done(((bf16[1280,1792]{1,0:T(8,128)(2,1)}), bf16[40,1792]{1,0:T(8,128)(2,1)}) %reduce-scatter.24.cloned.1.call-update) | async-done | bytes 143376 | tf_op jit(solution)/shard_map/reduce_scatter | solution.py:135
  746.8 121.2 %all-reduce.7.cloned.1.call-done = f32[1280,16]{0,1:T(8,128)} async-done(((f32[1280,16]{0,1:T(8,128)}), f32[1280,16]{0,1:T(8,128)}) %all-reduce.7.cloned.1.call-update) | async-done | bytes 81936
  869.4 59.6 %reduce-scatter.28.cloned.1.call-done = bf16[2,224,1280]{2,1,0:T(8,128)(2,1)} async-done(((bf16[2,896,1280]{2,1,0:T(8,128)(2,1)}), bf16[2,224,1280]{2,1,0:T(8,128)(2,1)}) %reduce-scatter.28.cloned.1.call-update) | async-done | bytes 1146896 | tf_op jit(solution)/shard_map/reduce_scatter | solution.py:128
  929.0 2.8 convert_element_type.211
  931.8 93.3 %reduce-scatter.26.cloned.1.call-done = bf16[2,320,1792]{2,1,0:T(8,128)(2,1)} async-done(((bf16[2,1280,1792]{2,1,0:T(8,128)(2,1)}), bf16[2,320,1792]{2,1,0:T(8,128)(2,1)}) %reduce-scatter.26.cloned.1.call-update) | async-done | bytes 2293776 | tf_op jit(solution)/shard_map/reduce_scatter | solution.py:125
  1025.1 4.3 convert_element_type.209
  1029.4 11.2 fusion.42
  1040.6 41.5 %all-reduce.4 = (f32[1280]{0:T(1024)S(1)}, f32[1280]{0:T(1024)S(1)}) all-reduce(f32[1280]{0:T(1024)S(1)} %get-tuple-element.55, f32[1280]{0:T(1024)S(1)} %get-tuple-element.53), channel_id=9, replica_groups=mesh['dp'=4,'expert'=8] {'dp','expert'}, use_global_device_ids=true, to_apply=%region_20.21.clone | all-reduce | flops 2560 | bytes 20480
  1083.2 54.5 %reduce-scatter.14.cloned.1.call-done = bf16[1,512,1280]{2,1,0:T(8,128)(2,1)} async-done(((bf16[8,512,1280]{2,1,0:T(8,128)(2,1)}), bf16[1,512,1280]{2,1,0:T(8,128)(2,1)}) %reduce-scatter.14.cloned.1.call-update) | async-done | bytes 1310736 | tf_op jit(solution)/shard_map/reduce_scatter | solution.py:258
  1137.7 5.8 fusion.35
  1143.6 2.2 fusion.41
  1145.7 132.7 %reduce-scatter.22.cloned.1.call-done = bf16[40,1280]{1,0:T(8,128)(2,1)} async-done(((bf16[1280,1280]{1,0:T(8,128)(2,1)}), bf16[40,1280]{1,0:T(8,128)(2,1)}) %reduce-scatter.22.cloned.1.call-update) | async-done | bytes 102416 | tf_op jit(solution)/shard_map/reduce_scatter | solution.py:135
  1280.0 139.9 %reduce-scatter.20.cloned.1.call-done = bf16[40,3840]{1,0:T(8,128)(2,1)} async-done(((bf16[1280,3840]{1,0:T(8,128)(2,1)}), bf16[40,3840]{1,0:T(8,128)(2,1)}) %reduce-scatter.20.cloned.1.call-update) | async-done | bytes 307216 | tf_op jit(solution)/shard_map/reduce_scatter | solution.py:135
  1419.9 1.8 convert_element_type.201
  (195 shorter events, 29.1 us)
Async XLA Ops:
  7.2 41.4 %copy-start = (bf16[1280,1280]{1,0:T(8,128)(2,1)S(1)}, bf16[1280,1280]{1,0:T(8,128)(2,1)}, u32[]{:S(2)}) copy-start(bf16[1280,1280]{1,0:T(8,128)(2,1)} %param.18) | copy-start | bytes 9830404
  7.2 152.1 %all-gather.7.cloned.1.call-start = ((), (), s32[]{:S(2)}) async-start(), calls=%async_computation.17 | async-start | bytes 11796480 | tf_op jit(solution)/shard_map/all_gather | solution.py:205
  9.1 8.7 copy-start.50
  17.8 4.7 copy-start.15
  30.6 6.4 copy-start.24
  31.3 48.2 %copy-start.52 = (pred[512]{0:T(512)(128)(4,1)}, pred[512]{0:T(512)(128)(4,1)S(1)}, u32[]{:S(2)}) copy-start(pred[512]{0:T(512)(128)(4,1)S(1)} %iota_compare_fusion.6) | copy-start | bytes 1540
  37.0 3.4 copy-start.5
  37.0 3.4 copy-start.7
  37.0 3.4 copy-start.9
  37.0 3.4 copy-start.11
  40.4 3.8 copy-start.1
  40.4 3.9 copy-start.32
  44.2 4.3 copy-start.36
  44.2 4.4 copy-start.17
  48.6 2.3 copy-start.57
  48.6 5.2 copy-start.54
  48.6 3.8 copy-start.40
  50.9 1.5 copy-start.2
  53.8 2.8 copy-start.48
  53.8 4.3 copy-start.34
  53.8 206.1 %all-gather.9.cloned.1.call-start = ((), (), s32[]{:S(2)}) async-start(), calls=%async_computation.18 | async-start | bytes 11796480 | tf_op jit(solution)/shard_map/all_gather | solution.py:204
  56.5 315.1 %reduce-scatter.18.cloned.1.call-start = ((), (), s32[]{:S(2)}) async-start(), calls=%async_computation.11 | async-start | bytes 294912 | tf_op jit(solution)/shard_map/reduce_scatter | solution.py:256
  56.6 114.8 %copy-start.38 = (pred[512,16]{0,1:T(8,128)(4,1)}, pred[512,16]{0,1:T(8,128)(4,1)S(1)}, u32[]{:S(2)}) copy-start(pred[512,16]{0,1:T(8,128)(4,1)S(1)} %fusion.62) | copy-start | bytes 24580
  59.9 37.0 %copy-start.42 = (f32[512]{0:T(512)}, f32[512]{0:T(512)S(1)}, u32[]{:S(2)}) copy-start(f32[512]{0:T(512)S(1)} %get-tuple-element.99) | copy-start | bytes 6148
  60.5 18.9 %copy-start.44 = (f32[512]{0:T(512)}, f32[512]{0:T(512)S(1)}, u32[]{:S(2)}) copy-start(f32[512]{0:T(512)S(1)} %fusion.69) | copy-start | bytes 6148
  96.9 177.9 %copy-start.30 = (s32[8,2,512]{2,1,0:T(2,128)}, s32[8,2,512]{2,1,0:T(2,128)S(1)}, u32[]{:S(2)}) copy-start(s32[8,2,512]{2,1,0:T(2,128)S(1)} %constant_dynamic-slice_fusion.1) | copy-start | bytes 98308
  159.3 51.1 %slice-start.3 = ((s8[4587520]{0:T(1024)(128)(4,1)}), s8[4194304]{0:T(1024)(128)(4,1)S(1)}, s32[]{:S(2)}) async-start(s8[4587520]{0:T(1024)(128)(4,1)} %bitcast.174), calls=%async_computation.24 | async-start | bytes 8388608
  171.5 39.0 %slice-start.4 = ((s8[4587520]{0:T(1024)(128)(4,1)}), s8[393216]{0:T(1024)(128)(4,1)S(1)}, s32[]{:S(2)}) async-start(s8[4587520]{0:T(1024)(128)(4,1)} %bitcast.174), calls=%async_computation.25 | async-start | bytes 786432
  207.6 2.8 copy-start.16
  287.4 172.5 %reduce-scatter.16.cloned.1.call-start = ((), (), s32[]{:S(2)}) async-start(), calls=%async_computation.10 | async-start | bytes 11796480 | tf_op jit(solution)/shard_map/reduce_scatter | solution.py:257
  314.9 25.1 %copy-start.31 = (s32[8,2,512]{2,1,0:T(2,128)S(1)}, s32[8,2,512]{2,1,0:T(2,128)}, u32[]{:S(2)}) copy-start(s32[8,2,512]{2,1,0:T(2,128)} %copy-done.30) | copy-start | bytes 98308
  352.0 250.4 %reduce-scatter.30.cloned.1.call-start = ((), (), s32[]{:S(2)}) async-start(), calls=%async_computation.20 | async-start | bytes 2365440
  352.3 5.4 copy-start.21
  352.3 5.4 copy-start.56
  364.9 380.3 %reduce-scatter.24.cloned.1.call-start = ((), (), s32[]{:S(2)}) async-start(), calls=%async_computation.14 | async-start | bytes 4730880 | tf_op jit(solution)/shard_map/reduce_scatter | solution.py:135
  371.6 496.4 %all-reduce.7.cloned.1.call-start = ((), (), s32[]{:S(2)}) async-start(), calls=%async_computation.19 | async-start | bytes 163840
  376.2 552.9 %reduce-scatter.28.cloned.1.call-start = ((), (), s32[]{:S(2)}) async-start(), calls=%async_computation.16 | async-start | bytes 5734400 | tf_op jit(solution)/shard_map/reduce_scatter | solution.py:128
  393.8 631.2 %reduce-scatter.26.cloned.1.call-start = ((), (), s32[]{:S(2)}) async-start(), calls=%async_computation.15 | async-start | bytes 11468800 | tf_op jit(solution)/shard_map/reduce_scatter | solution.py:125
  419.1 718.6 %reduce-scatter.14.cloned.1.call-start = ((), (), s32[]{:S(2)}) async-start(), calls=%async_computation.9 | async-start | bytes 11796480 | tf_op jit(solution)/shard_map/reduce_scatter | solution.py:258
  430.4 35.4 %copy-start.35 = (bf16[1280,16]{0,1:T(8,128)(2,1)S(1)}, bf16[1280,16]{0,1:T(8,128)(2,1)}, u32[]{:S(2)}) copy-start(bf16[1280,16]{0,1:T(8,128)(2,1)} %param.20) | copy-start | bytes 122884
  430.4 35.4 %copy-start.41 = (f32[1280]{0:T(1024)S(1)}, f32[1280]{0:T(1024)}, u32[]{:S(2)}) copy-start(f32[1280]{0:T(1024)} %param.19) | copy-start | bytes 15364
  430.4 35.4 %copy-start.47 = (f32[512]{0:T(512)S(1)}, f32[512]{0:T(512)}, u32[]{:S(2)}) copy-start(f32[512]{0:T(512)} %copy-done.46) | copy-start | bytes 6148
  430.4 848.0 %reduce-scatter.22.cloned.1.call-start = ((), (), s32[]{:S(2)}) async-start(), calls=%async_computation.13 | async-start | bytes 3379200 | tf_op jit(solution)/shard_map/reduce_scatter | solution.py:135
  459.9 6.0 copy-start.3
  467.2 2.2 copy-start.55
  467.2 2.2 copy-start.58
  467.9 1.5 copy-start.13
  473.1 946.8 %reduce-scatter.20.cloned.1.call-start = ((), (), s32[]{:S(2)}) async-start(), calls=%async_computation.12 | async-start | bytes 10137600 | tf_op jit(solution)/shard_map/reduce_scatter | solution.py:135
  481.2 11.1 slice-start
  481.2 11.1 slice-start.1
  481.2 11.1 slice-start.2
  492.3 6.3 copy-start.10
  492.3 6.3 copy-start.12
  498.6 2.3 copy-start.6
  498.6 2.3 copy-start.8
  501.0 1.7 copy-start.25
  501.0 1.7 copy-start.26
  510.1 6.3 copy-start.49
  510.1 6.3 copy-start.51
  1025.1 4.3 copy-start.18
  1025.1 4.3 copy-start.22
  1137.7 5.8 copy-start.14
  1137.7 5.8 copy-start.19
  1137.7 5.8 copy-start.23
  (13 other events, 11.7 us)
Sparse Core Ops, SparseCore 0:
  53.9 105.3 all-gather.6
  161.5 98.2 all-gather.8
  287.6 28.7 reduce-scatter.17
  352.1 107.7 reduce-scatter.15
  462.7 139.6 reduce-scatter.29
  605.2 140.0 reduce-scatter.23
  751.4 116.6 all-reduce.6
  871.1 57.8 reduce-scatter.27
  932.2 92.8 reduce-scatter.25
  1027.2 110.4 reduce-scatter.13
  1140.0 138.3 reduce-scatter.21
  1285.3 134.6 reduce-scatter.19

commit v2 on v1

--- a/solution.py
+++ b/solution.py
@@ -131,10 +131,58 @@
     )
 
 
-def reduce_low(part, dimension):
-    return lax.psum_scatter(
-        part.astype(jnp.bfloat16), ("dp", "expert"), scatter_dimension=dimension, tiled=True
-    ).astype(jnp.float32)
+def swap_cores(values_in):
+    owners = lax.axis_size("expert")
+    return lax.ppermute(values_in, "expert", [(i, i ^ 1) for i in range(owners)])
+
+
+def next_chip(values_in):
+    owners = lax.axis_size("expert")
+    return lax.ppermute(values_in, "expert", [(i, (i + 2) % owners) for i in range(owners)])
+
+
+def axis_bits(name):
+    return [(name, bit) for bit in range(lax.axis_size(name).bit_length() - 1)]
+
+
+def scatter_sum(part, order):
+    positions = axis_bits("dp")[::-1] + axis_bits("expert")[::-1]
+    rows = part.shape[0] >> len(positions)
+    terms = [part.reshape((2,) * len(positions) + (rows, part.shape[1]))]
+    open_bits = list(positions)
+
+    def total(parts):
+        summed = parts[0].astype(jnp.float32)
+        for term in parts[1:]:
+            summed = summed + term.astype(jnp.float32)
+        return summed
+
+    for name, bit in order:
+        dim = open_bits.index((name, bit))
+        mine = (lax.axis_index(name) >> bit) & 1
+        pick = lambda term, index: lax.dynamic_index_in_dim(term, index, dim, keepdims=False)
+        away = total([pick(term, 1 - mine) for term in terms]).astype(part.dtype)
+        came = lax.ppermute(
+            away, name, [(i, i ^ (1 << bit)) for i in range(lax.axis_size(name))]
+        )
+        terms = [pick(term, mine) for term in terms] + [came]
+        open_bits.pop(dim)
+    return total(terms)
+
+
+def scatter_orders():
+    core, *line = axis_bits("expert")
+    plane = axis_bits("dp")
+    return ([core] + plane + line, [core] + plane[::-1] + line)
+
+
+def scatter_columns(part):
+    low_part = part.astype(jnp.bfloat16)
+    first, second = scatter_orders()
+    half = part.shape[1] // 256 * 128
+    return jnp.concatenate(
+        [scatter_sum(low_part[:, :half], first), scatter_sum(low_part[:, half:], second)], axis=1
+    )
 
 
 def per_device(
@@ -196,76 +244,118 @@
     picked = (
         jnp.any(expert_ids[:, :, None] == slots[None, None, :], axis=1) & live_rows[:, None]
     ).astype(jnp.int32)
-    counts = lax.psum(jnp.sum(picked, axis=0), ("dp", "expert"))
-    rank = jnp.where(picked > 0, jnp.cumsum(picked, axis=0) - 1, -1)
-    rank_all = lax.all_gather(rank.T, "expert", axis=0)
+    counts_here = jnp.sum(picked, axis=0).astype(jnp.float32)
+    rank = jnp.where(picked > 0, jnp.cumsum(picked, axis=0) - 1, -1).T
     first_expert = lax.axis_index("expert") * local_experts
-    rank_mine = lax.dynamic_slice_in_dim(rank_all, first_expert, local_experts, axis=1)
-    grad_all = lax.all_gather(grad_branch_low, "expert", axis=0)
-    h2_all = lax.all_gather(h2_low, "expert", axis=0)
-    probs_all = lax.all_gather(router_probs.T, "expert", axis=0)
-    probs_mine = lax.dynamic_slice_in_dim(probs_all, first_expert, local_experts, axis=1)
-    hit = rank_mine[:, :, None, :] == jnp.arange(capacity, dtype=jnp.int32)[None, None, :, None]
-    place = hit.astype(jnp.bfloat16)
-    slot_gate = jnp.sum(jnp.where(hit, probs_mine[:, :, None, :], 0.0), axis=-1)
-    rows_held = jnp.einsum(
-        "nsct,ntd->nscd", place, h2_all, preferred_element_type=jnp.float32
-    ).astype(jnp.bfloat16)
-    grad_rows_in = jnp.einsum("nsct,ntd->nscd", place, grad_all, preferred_element_type=jnp.float32)
-    grad_result = (slot_gate[..., None] * grad_rows_in).astype(jnp.bfloat16)
-    gate_up = jnp.einsum(
-        "nscd,sdf->nscf", rows_held, w_expert_in, preferred_element_type=jnp.float32
-    )
-    expert_act, expert_slope = silu_parts(gate_up[..., :hidden_units])
-    expert_up = gate_up[..., hidden_units:]
-    expert_hidden = (expert_act * expert_up).astype(jnp.bfloat16)
-    result_rows = (
-        jnp.einsum("nscf,sfd->nscd", expert_hidden, w_expert_down, preferred_element_type=jnp.float32)
-        .astype(jnp.bfloat16)
-        .astype(jnp.float32)
-    )
-    slot_dot = jnp.sum(result_rows * grad_rows_in, axis=-1)
-    routed_part = jnp.einsum(
-        "nsct,nscd->ntd",
-        place,
-        (slot_gate[..., None] * result_rows).astype(jnp.bfloat16),
-        preferred_element_type=jnp.float32,
-    ).astype(jnp.bfloat16)
+    chips = experts // local_experts // 2
+    probs_t = router_probs.T
+
+    def both(block):
+        return jnp.stack([block, swap_cores(block)])
+
+    def own_rows(table):
+        return lax.dynamic_slice_in_dim(table, first_expert, local_experts, axis=1)
+
+    kept = []
+    dot_sum = routed_sum = grad_h2_sum = None
+    line_grad, line_rank, line_h2, line_probs = grad_branch_low, rank, h2_low, probs_t
+    held = []
+    for step in range(chips):
+        if step:
+            line_grad, line_rank, line_h2, line_probs = (
+                next_chip(line_grad),
+                next_chip(line_rank),
+                next_chip(line_h2),
+                next_chip(line_probs),
+            )
+        hit = (
+            own_rows(both(line_rank))[:, :, None, :]
+            == jnp.arange(capacity, dtype=jnp.int32)[None, None, :, None]
+        )
+        place = hit.astype(jnp.bfloat16)
+        slot_gate = jnp.sum(
+            jnp.where(hit, own_rows(both(line_probs))[:, :, None, :], 0.0), axis=-1
+        )
+        rows_held = jnp.einsum(
+            "nsct,ntd->nscd", place, both(line_h2), preferred_element_type=jnp.float32
+        ).astype(jnp.bfloat16)
+        grad_rows_in = jnp.einsum(
+            "nsct,ntd->nscd", place, both(line_grad), preferred_element_type=jnp.float32
+        )
+        grad_result = (slot_gate[..., None] * grad_rows_in).astype(jnp.bfloat16)
+        gate_up = jnp.einsum(
+            "nscd,sdf->nscf", rows_held, w_expert_in, preferred_element_type=jnp.float32
+        )
+        expert_act, expert_slope = silu_parts(gate_up[..., :hidden_units])
+        expert_up = gate_up[..., hidden_units:]
+        expert_hidden = (expert_act * expert_up).astype(jnp.bfloat16)
+        result_rows = (
+            jnp.einsum(
+                "nscf,sfd->nscd", expert_hidden, w_expert_down, preferred_element_type=jnp.float32
+            )
+            .astype(jnp.bfloat16)
+            .astype(jnp.float32)
+        )
+        slot_dot = jnp.sum(result_rows * grad_rows_in, axis=-1)
+        routed_part = jnp.einsum(
+            "nsct,nscd->ntd",
+            place,
+            (slot_gate[..., None] * result_rows).astype(jnp.bfloat16),
+            preferred_element_type=jnp.float32,
+        )
+        grad_expert_hidden = jnp.einsum(
+            "nscd,sfd->nscf", grad_result, w_expert_down, preferred_element_type=jnp.float32
+        )
+        grad_expert_gu = jnp.concatenate(
+            [grad_expert_hidden * expert_up * expert_slope, grad_expert_hidden * expert_act],
+            axis=-1,
+        ).astype(jnp.bfloat16)
+        grad_rows = jnp.einsum(
+            "nscf,sdf->nscd", grad_expert_gu, w_expert_in, preferred_element_type=jnp.float32
+        ).astype(jnp.bfloat16)
+        grad_h2_part = jnp.einsum(
+            "nsct,nscd->ntd", place, grad_rows, preferred_element_type=jnp.float32
+        )
+        dot_part = lax.dynamic_update_slice_in_dim(
+            jnp.zeros((2, experts, seq_slots), jnp.float32),
+            jnp.sum(jnp.where(hit, slot_dot[..., None], 0.0), axis=2),
+            first_expert,
+            axis=1,
+        )
+        kept.append((rows_held, grad_result, expert_hidden, grad_expert_gu))
+        held.append((dot_part, routed_part, grad_h2_part))
+
+    def bring_home(index, dtype):
+        travelling = None
+        for step in list(range(1, chips)) + [0]:
+            part = held[step][index]
+            total = part[0] + swap_cores(part[1].astype(dtype)).astype(jnp.float32)
+            if travelling is not None:
+                total = total + next_chip(travelling).astype(jnp.float32)
+            travelling = total.astype(dtype)
+        return total
+
+    grad_probs = bring_home(0, jnp.float32).T
+    grad_h2_sum = bring_home(2, jnp.bfloat16)
+    routed_out = bring_home(1, jnp.bfloat16)
+    rows_held, grad_result, expert_hidden, grad_expert_gu = (
+        jnp.concatenate(pieces, axis=0) for pieces in zip(*kept)
+    )
     grad_expert_down = jnp.einsum(
         "nscf,nscd->sfd", expert_hidden, grad_result, preferred_element_type=jnp.float32
     )
-    grad_expert_hidden = jnp.einsum(
-        "nscd,sfd->nscf", grad_result, w_expert_down, preferred_element_type=jnp.float32
-    )
-    grad_expert_gu = jnp.concatenate(
-        [grad_expert_hidden * expert_up * expert_slope, grad_expert_hidden * expert_act], axis=-1
-    ).astype(jnp.bfloat16)
     grad_expert_in = jnp.einsum(
         "nscd,nscf->sdf", rows_held, grad_expert_gu, preferred_element_type=jnp.float32
     )
-    grad_rows = jnp.einsum(
-        "nscf,sdf->nscd", grad_expert_gu, w_expert_in, preferred_element_type=jnp.float32
-    ).astype(jnp.bfloat16)
-    grad_h2_part = jnp.einsum(
-        "nsct,nscd->ntd", place, grad_rows, preferred_element_type=jnp.float32
-    ).astype(jnp.bfloat16)
-    dot_mine = jnp.sum(jnp.where(hit, slot_dot[..., None], 0.0), axis=2)
-    dot_part = lax.dynamic_update_slice_in_dim(
-        jnp.zeros((rank_all.shape[0], experts, seq_slots), jnp.float32), dot_mine, first_expert, axis=1
-    )
-    grad_probs = lax.psum_scatter(dot_part, "expert", scatter_dimension=0, tiled=False).T
-    grad_h2_sum = lax.psum_scatter(grad_h2_part, "expert", scatter_dimension=0, tiled=False)
-    routed_out = lax.psum_scatter(routed_part, "expert", scatter_dimension=0, tiled=False)
-    routed_out = routed_out.astype(jnp.float32)
     result = (x_mid + live_col * (shared_out + routed_out)).astype(jnp.bfloat16)
-    grad_shared_down = jnp.dot(shared_hidden.T, grad_branch_low, preferred_element_type=jnp.float32)
+    grad_shared_down = jnp.dot(grad_branch_low.T, shared_hidden, preferred_element_type=jnp.float32)
     grad_hidden = jnp.dot(grad_branch_low, w_shared_down.T, preferred_element_type=jnp.float32)
     grad_shared_gu = jnp.concatenate(
         [grad_hidden * shared_up * shared_slope, grad_hidden * shared_act], axis=-1
     ).astype(jnp.bfloat16)
     grad_shared_in = jnp.dot(h2_low.T, grad_shared_gu, preferred_element_type=jnp.float32)
     grad_h2 = jnp.dot(grad_shared_gu, w_shared_in.T, preferred_element_type=jnp.float32)
-    grad_h2 = grad_h2 + grad_h2_sum.astype(jnp.float32)
+    grad_h2 = grad_h2 + grad_h2_sum
     grad_logits = (
         router_probs * (grad_probs - jnp.sum(grad_probs * router_probs, axis=-1, keepdims=True))
     ).astype(jnp.bfloat16)
@@ -300,15 +390,27 @@
     grad_in_norm, grad_norm1 = norm_back(grad_h1, x_full, inverse_one, norm1)
     grad_input = grad_mid + grad_in_norm
     expert_in_sum, expert_down_sum = reduce_experts(grad_expert_in, grad_expert_down)
-    norm1_sum, qkv_sum, out_sum, norm2_sum, router_sum, shared_in_sum, shared_down_sum = (
-        lax.psum_scatter(grad_norm1, ("dp", "expert"), scatter_dimension=0, tiled=True),
-        reduce_low(grad_qkv_weight, 0),
-        reduce_low(grad_out_weight, 0),
-        lax.psum_scatter(grad_norm2, ("dp", "expert"), scatter_dimension=0, tiled=True),
-        lax.psum_scatter(grad_router, ("dp", "expert"), scatter_dimension=0, tiled=True),
-        reduce_low(grad_shared_in, 0),
-        reduce_low(grad_shared_down, 1),
-    )
+    shared_sum = scatter_columns(jnp.concatenate([grad_shared_in, grad_shared_down], axis=1))
+    shared_in_sum = shared_sum[:, : 2 * hidden_units]
+    shared_down_sum = shared_sum[:, 2 * hidden_units :].T
+    out_sum = scatter_columns(grad_out_weight)
+    qkv_sum = scatter_columns(grad_qkv_weight)
+    small_sum = scatter_sum(
+        jnp.concatenate(
+            [
+                grad_router,
+                jnp.broadcast_to(counts_here[None, :], (width, experts)),
+                grad_norm1[:, None],
+                grad_norm2[:, None],
+            ],
+            axis=1,
+        ),
+        scatter_orders()[0],
+    )
+    router_sum = small_sum[:, :experts]
+    counts = small_sum[0, experts : 2 * experts].astype(jnp.int32)
+    norm1_sum = small_sum[:, 2 * experts]
+    norm2_sum = small_sum[:, 2 * experts + 1]
     return (
         result,
         grad_input,

time: 1440 us -> 801 us (0.56)
  waiting for transfers between devices: 908 us -> 180 us
  blocking collectives: 116 us -> 0 us
  other arithmetic: 68.4 us -> 138 us
  starting transfers between devices: 1.29 us -> 68.1 us
  local copies, waits for them, and re-layouts: 35.7 us -> 89.8 us
    reduce_scatter x6 -> x0, waiting for transfers between devices: 498 us -> none  [the longest x3 414 us: reduce_low(): lax.psum_scatter(part.astype(jnp.bfloat16), ('dp', 'expert'), scatter_dim...]
    ppermute x0 -> x84, waiting for transfers between devices: none -> 180 us  [the longest x35 117 us: scatter_sum(): lax.ppermute(away, name, [(i, i ^ 1 << bit) for i in range(lax.axis_size(...]
    unnamed x14 -> x2, waiting for transfers between devices: 158 us -> 0.03 us
    all_gather x2 -> x0, waiting for transfers between devices: 99.3 us -> none  [the longest x1 62.4 us: per_device(): h2_all = lax.all_gather(h2_low, 'expert', axis=0)]
    reduce_scatter x1, waiting for transfers between devices: 93.3 us -> 0.01 us  [reduce_experts(): lax.psum_scatter(grad_in_part.astype(jnp.bfloat16), 'dp', scatter_dimensi...]
    ppermute x0 -> x84, starting transfers between devices: none -> 68 us  [the longest x35 40.6 us: scatter_sum(): lax.ppermute(away, name, [(i, i ^ 1 << bit) for i in range(lax.axis_size(...]
    reduce_scatter x1, waiting for transfers between devices: 59.6 us -> 0.01 us  [reduce_experts(): lax.psum_scatter(grad_down_part.astype(jnp.bfloat16), 'dp', scatter_dimen...]
    convert_element_type x4 -> x36, other arithmetic: 6.61 us -> 61.5 us  [the longest x24 30.5 us: scatter_sum(): away = total([pick(term, 1 - mine) for term in terms]).astype(part.dtype)]
  transfers between devices with their start and end apart: 12 -> 86, of which waited for: 11 -> 30; matrix products, arithmetic and copies ran while one was open for 21% -> 59% of each run, Pallas kernels for 0% -> 0%
where the time goes in v2:
time: 801 us; the launch traced here: 791 us
  matrix products  298 us (37%)
  waiting for transfers between devices  180 us (22%)
  other arithmetic  138 us (17%)
  local copies, waits for them, and re-layouts  89.8 us (11%)
  starting transfers between devices  68.1 us (9%)
  between operations  17.3 us (2%)
    ppermute x35, waiting for transfers between devices, scatter_sum(): lax.ppermute(away, name, [(i, i ^ 1 << bit) for i in range(lax.axis_size(...  117 us
    ppermute x21, waiting for transfers between devices, next_chip(): lax.ppermute(values_in, 'expert', [(i, (i + 2) % owners) for i in range(o...  59.9 us
    dot_general x4, matrix products, per_device(): jnp.einsum('nsct,nscd->ntd', place, grad_rows, preferred_element_type=jnp...  52.2 us
    ppermute x35, starting transfers between devices, scatter_sum(): lax.ppermute(away, name, [(i, i ^ 1 << bit) for i in range(lax.axis_size(...  40.6 us
    convert_element_type x24, other arithmetic, scatter_sum(): away = total([pick(term, 1 - mine) for term in terms]).astype(part.dtype)  30.5 us
    dot_general x4, matrix products, per_device(): jnp.einsum('nscd,sdf->nscf', rows_held, w_expert_in, preferred_element_ty...  28.9 us
    dot_general x1, matrix products, per_device(): jnp.einsum('nscd,nscf->sdf', rows_held, grad_expert_gu, preferred_element...  28.8 us
    dot_general x4, matrix products, per_device(): jnp.einsum('nscd,sfd->nscf', grad_result, w_expert_down, preferred_elemen...  27.3 us
  transfers between devices with their start and end apart: 86, of which 30 were waited for; matrix products, arithmetic and copies ran while one was open for 59% of the time, Pallas kernels for 0%

profile of v2, /device:TPU:0, one launch (start us, length us, event | category | flops | bytes accessed | tf_op | source)
XLA Modules:
  0.0 790.7 jit_solution(8963041631601063147)
XLA Ops:
  9.1 8.7 %fusion.289 = f32[512,3840]{0,1:T(8,128)S(1)} fusion(bf16[1280,3840]{1,0:T(8,128)(2,1)} %param.17, bf16[512,1280]{1,0:T(8,128)(2,1)} %param.13, f32[1280]{0:T(1024)} %param.16, f32[512]{0:T(512)S(1)} %add_rsqrt_fusion.1), kind=kOutput, calls=%fused_computation.389 | convolution fusion | flops 5035786240 | bytes 19012608 | tf_op jit(solution)/shard_map/dot_general | solution.py:220
  17.8 3.4 fusion.354
  31.4 5.4 subtract_convert_fusion.3
  36.9 3.3 fusion.356
  44.2 4.3 fusion.243
  64.8 4.0 fusion.358
  68.8 3.4 multiply_convert_fusion.12
  72.2 6.0 convolution_convert_fusion.1
  78.2 4.1 fusion.261
  82.3 4.3 convolution_convert_fusion.7
  90.3 10.2 %reduce-window.6 = s32[16,4,128]{2,0,1:T(8,128)S(1)} reduce-window(s32[16,4,128]{2,0,1:T(8,128)S(1)} %copy_bitcast_fusion.5, s32[]{:T(128)} %constant.4713.clone.1), window={size=1x1x128 pad=0_0x0_0x127_0}, to_apply=%region_5.6 | reduce-window | flops 1040384 | bytes 65540 | tf_op jit(solution)/shard_map/reduce-window
  100.7 3.9 slice.299
  104.6 4.1 pad_maximum_fusion.1
  118.2 4.1 collective-permute-done.4
  123.5 4.5 collective-permute-done.9
  131.3 3.7 collective-permute-done.10
  137.9 3.3 convolution_convert_fusion.6
  141.3 8.1 %fusion.76 = f32[2,2,240,1792]{3,2,0,1:T(8,128)S(1)} fusion(bf16[2,1280,1792]{2,1,0:T(8,128)(2,1)} %param.23, bf16[2,2,240,1280]{3,2,1,0:T(8,128)(2,1)S(1)} %convolution_convert_fusion.6), kind=kOutput, calls=%fused_computation.101 | convolution fusion | flops 4404019200 | bytes 18513920 | tf_op jit(solution)/shard_map/nscd,sdf->nscf/dot_general | solution.py:286
  159.3 5.4 fusion.126
  164.7 13.0 %convolution_bitcast_fusion.3 = f32[2,512,1280]{2,1,0:T(8,128)} fusion(bf16[2,1280,1792]{2,1,0:T(8,128)(2,1)} %param.23, s32[2,2,512]{2,1,0:T(2,128)S(1)} %fusion.332, bf16[2,2,240,896]{3,2,0,1:T(8,128)(2,1)} %get-tuple-element.77, bf16[2,2,240,896]{3,2,0,1:T(8,128)(2,1)} %get-tuple-element.76), kind=kOutput, calls=%fused_computation.96 | convolution fusion | flops 5670912000 | bytes 17866752 | tf_op jit(solution)/shard_map/nsct,nscd->ntd/dot_general | solution.py:316
  179.9 3.5 convolution_bitcast_fusion.7
  183.4 4.9 fusion.255
  197.3 13.2 %collective-permute-done.75 = bf16[2,2,2,40,1280]{4,3,2,1,0:T(8,128)(2,1)S(1)} collective-permute-done((bf16[2,2,2,40,1280]{4,3,2,1,0:T(8,128)(2,1)S(1)}, bf16[2,2,2,40,1280]{4,3,2,1,0:T(8,128)(2,1)S(1)}, u32[]{:S(2)}, u32[]{:S(2)}) %collective-permute-start.75) | collective-permute-done | bytes 819232 | tf_op jit(solution)/shard_map/ppermute | solution.py:165
  217.6 4.6 fusion.85
  230.7 8.2 %fusion.117 = (bf16[2,2,240,896]{3,2,0,1:T(8,128)(2,1)}, bf16[2,2,240,896]{3,2,0,1:T(8,128)(2,1)}) fusion(f32[2,2,240,1792]{3,2,0,1:T(8,128)S(1)} %fusion.85, bf16[2,2,240,1280]{3,2,0,1:T(8,128)(2,1)S(1)} %get-tuple-element.123, bf16[2,896,1280]{2,1,0:T(8,128)(2,1)} %param.24), kind=kOutput, calls=%fused_computation.135 | convolution fusion | flops 2213191680 | bytes 17367040 | tf_op jit(solution)/shard_map/nscd,sfd->nscf/dot_general | solution.py:306
  244.0 12.9 %convolution_bitcast_fusion = f32[2,512,1280]{2,1,0:T(8,128)} fusion(bf16[2,1280,1792]{2,1,0:T(8,128)(2,1)} %param.23, s32[2,2,512]{2,1,0:T(2,128)S(1)} %fusion.326, bf16[2,2,240,896]{3,2,0,1:T(8,128)(2,1)} %get-tuple-element.79, bf16[2,2,240,896]{3,2,0,1:T(8,128)(2,1)} %get-tuple-element.78), kind=kOutput, calls=%fused_computation.93 | convolution fusion | flops 5670912000 | bytes 17866752 | tf_op jit(solution)/shard_map/nsct,nscd->ntd/dot_general | solution.py:316
  265.4 8.9 %collective-permute-done.81 = bf16[2,2,40,1408]{3,2,0,1:T(8,128)(2,1)S(1)} collective-permute-done((bf16[2,2,40,1408]{3,2,0,1:T(8,128)(2,1)S(1)}, bf16[2,2,40,1408]{3,2,0,1:T(8,128)(2,1)S(1)}, u32[]{:S(2)}, u32[]{:S(2)}) %collective-permute-start.81) | collective-permute-done | bytes 450592 | tf_op jit(solution)/shard_map/ppermute | solution.py:165
  286.5 3.6 collective-permute-start.78
  291.1 4.6 collective-permute-done.78
  297.9 29.1 %collective-permute-done.83 = bf16[40,1408]{1,0:T(8,128)(2,1)S(1)} collective-permute-done((bf16[40,1408]{1,0:T(8,128)(2,1)S(1)}, bf16[40,1408]{1,0:T(8,128)(2,1)S(1)}, u32[]{:S(2)}, u32[]{:S(2)}) %collective-permute-start.83) | collective-permute-done | bytes 112672 | tf_op jit(solution)/shard_map/ppermute | solution.py:165
  332.5 8.1 %fusion.82 = f32[2,2,240,1792]{3,2,0,1:T(8,128)S(1)} fusion(bf16[2,1280,1792]{2,1,0:T(8,128)(2,1)} %param.23, bf16[2,2,240,1280]{3,2,1,0:T(8,128)(2,1)S(1)} %convolution_convert_fusion.4), kind=kOutput, calls=%fused_computation.103 | convolution fusion | flops 4404019200 | bytes 18513920 | tf_op jit(solution)/shard_map/nscd,sdf->nscf/dot_general | solution.py:286
  350.8 8.6 %fusion.120 = (bf16[2,2,240,896]{3,2,0,1:T(8,128)(2,1)}, bf16[2,2,240,896]{3,2,0,1:T(8,128)(2,1)}) fusion(f32[2,2,240,1792]{3,2,0,1:T(8,128)S(1)} %fusion.82, bf16[2,2,240,1280]{3,2,0,1:T(8,128)(2,1)} %get-tuple-element.125, bf16[2,896,1280]{2,1,0:T(8,128)(2,1)} %param.24), kind=kOutput, calls=%fused_computation.140 | convolution fusion | flops 2213191680 | bytes 17367040 | tf_op jit(solution)/shard_map/nscd,sfd->nscf/dot_general | solution.py:306
  362.6 4.0 convolution_bitcast_fusion.5
  366.6 12.9 %convolution_bitcast_fusion.1 = f32[2,512,1280]{2,1,0:T(8,128)} fusion(bf16[2,1280,1792]{2,1,0:T(8,128)(2,1)} %param.23, s32[2,2,512]{2,1,0:T(2,128)S(1)} %fusion.328, bf16[2,2,240,896]{3,2,0,1:T(8,128)(2,1)} %get-tuple-element.81, bf16[2,2,240,896]{3,2,0,1:T(8,128)(2,1)} %get-tuple-element.80), kind=kOutput, calls=%fused_computation.94 | convolution fusion | flops 5670912000 | bytes 17866752 | tf_op jit(solution)/shard_map/nsct,nscd->ntd/dot_general | solution.py:316
  380.1 3.4 fusion.165
  389.9 4.5 collective-permute-start.39
  397.9 8.1 %fusion.79 = f32[2,2,240,1792]{3,2,0,1:T(8,128)S(1)} fusion(bf16[2,1280,1792]{2,1,0:T(8,128)(2,1)} %param.23, bf16[2,2,240,1280]{3,2,1,0:T(8,128)(2,1)S(1)} %convolution_convert_fusion.5), kind=kOutput, calls=%fused_computation.102 | convolution fusion | flops 4404019200 | bytes 18513920 | tf_op jit(solution)/shard_map/nscd,sdf->nscf/dot_general | solution.py:286
  418.5 15.0 %bitcast_convert_fusion.1 = bf16[2,896,1280]{2,1,0:T(8,128)(2,1)} fusion(bf16[2,2,240,1280]{3,2,0,1:T(8,128)(2,1)} %get-tuple-element.127, bf16[2,2,240,1280]{3,2,0,1:T(8,128)(2,1)} %get-tuple-element.125, bf16[2,2,240,1280]{3,2,0,1:T(8,128)(2,1)} %copy-done.38, bf16[2,2,240,1280]{3,2,0,1:T(8,128)(2,1)} %copy-done.37, ...), kind=kOutput, calls=%fused_computation.27 | convolution fusion | flops 8835399680 | bytes 21299200 | tf_op jit(solution)/shard_map/nscf,nscd->sfd/dot_general | solution.py:344
  433.7 4.1 fusion.180
  443.7 4.2 fusion.168
  449.2 5.1 fusion.123
  454.3 13.4 %convolution_bitcast_fusion.2 = f32[2,512,1280]{2,1,0:T(8,128)} fusion(bf16[2,1280,1792]{2,1,0:T(8,128)(2,1)} %param.23, s32[2,2,512]{2,1,0:T(2,128)S(1)} %fusion.330, bf16[2,2,240,896]{3,2,0,1:T(8,128)(2,1)} %get-tuple-element.83, bf16[2,2,240,896]{3,2,0,1:T(8,128)(2,1)} %get-tuple-element.82), kind=kOutput, calls=%fused_computation.95 | convolution fusion | flops 5670912000 | bytes 17866752 | tf_op jit(solution)/shard_map/nsct,nscd->ntd/dot_general | solution.py:316
  470.6 28.8 %bitcast_convert_fusion = bf16[2,1280,1792]{2,1,0:T(8,128)(2,1)} fusion(bf16[2,2,240,1280]{3,2,1,0:T(8,128)(2,1)} %copy-done.25, bf16[2,2,240,1280]{3,2,1,0:T(8,128)(2,1)} %copy-done.24, bf16[2,2,240,1280]{3,2,1,0:T(8,128)(2,1)} %copy-done.23, bf16[2,2,240,1280]{3,2,1,0:T(8,128)(2,1)} %copy-done.22, bf16[2,2,240,896]{3,2,0,1:T(8,128)(2,1)} %get-tuple-element.83, ...), kind=kOutput, calls=%fused_computation | convolution fusion | flops 17745510400 | bytes 32768000 | tf_op jit(solution)/shard_map/nscd,nscf->sdf/dot_general | solution.py:347
  501.2 3.9 fusion.171
  505.2 4.0 collective-permute-start.48
  509.2 3.9 fusion.183
  518.3 24.6 %collective-permute-done.41 = bf16[512,1280]{1,0:T(8,128)(2,1)} collective-permute-done((bf16[512,1280]{1,0:T(8,128)(2,1)}, bf16[512,1280]{1,0:T(8,128)(2,1)}, u32[]{:S(2)}, u32[]{:S(2)}) %collective-permute-start.41) | collective-permute-done | bytes 1310752 | tf_op jit(solution)/shard_map/ppermute | solution.py:141
  542.9 6.2 multiply_reduce_fusion.1
  549.2 20.7 %collective-permute-done.27 = bf16[512,1280]{1,0:T(8,128)(2,1)} collective-permute-done((bf16[512,1280]{1,0:T(8,128)(2,1)}, bf16[512,1280]{1,0:T(8,128)(2,1)}, u32[]{:S(2)}, u32[]{:S(2)}) %collective-permute-start.27) | collective-permute-done | bytes 1310752 | tf_op jit(solution)/shard_map/ppermute | solution.py:141
  569.9 3.9 convert_add_fusion.1
  584.5 11.1 %multiply_reduce_fusion = (f32[10,512]{1,0:T(8,128)S(1)}, f32[10,512,512]{1,2,0:T(8,128)}) fusion(f32[10,512,512]{1,2,0:T(8,128)} %copy-done.1, f32[10,512]{1,0:T(8,128)S(1)} %copy-done.53, bf16[512,10,128]{0,2,1:T(8,128)(2,1)} %bitcast.1014, f32[512,3,10,128]{0,3,2,1:T(8,128)} %bitcast.1018), kind=kOutput, calls=%fused_computation.6 | convolution fusion | flops 678947840 | bytes 23633920 | tf_op jit(solution)/shard_map/while/body/eval_jaxpr/qhd,khd->hqk/dot_general | solution.py:94
  595.7 6.3 multiply_convert_fusion
  613.7 6.3 copy.376
  620.0 10.7 %convolution_convert_fusion = bf16[1280,3840]{1,0:T(8,128)(2,1)} fusion(bf16[512,3840]{0,1:T(8,128)(2,1)} %bitcast.1031, bf16[512,1280]{1,0:T(8,128)(2,1)} %param.13, f32[1280]{0:T(1024)S(1)} %copy-done.71, f32[512]{0:T(512)S(1)} %copy-done.74), kind=kOutput, calls=%fused_computation.1 | convolution fusion | flops 5040701440 | bytes 15080448 | tf_op jit(solution)/shard_map/dot_general | solution.py:388
  630.6 6.7 fusion.353
  637.4 5.1 dynamic-slice_bitcast_fusion.1
  646.4 11.7 %fusion.162 = (f32[1280]{0:T(1024)}, f32[512]{0:T(512)}, f32[512,1280]{1,0:T(8,128)}) fusion(bf16[512,1280]{1,0:T(8,128)(2,1)S(1)} %copy-done.33, f32[512]{0:T(512)S(1)} %copy-done.74, f32[1280]{0:T(1024)S(1)} %copy-done.71, bf16[512,3840]{0,1:T(8,128)(2,1)S(1)} %bitcast.1032, bf16[1280,3840]{1,0:T(8,128)(2,1)} %param.17), kind=kOutput, calls=%fused_computation.181 | convolution fusion | flops 5037750784 | bytes 17709056 | tf_op jit(solution)/shard_map/dot_general | solution.py:389
  667.2 4.2 collective-permute-done.50
  676.1 3.9 collective-permute-done.52
  680.2 4.1 fusion.161
  704.8 23.1 %collective-permute-done.66 = bf16[2,2,40,640]{3,2,0,1:T(8,128)(2,1)S(1)} collective-permute-done((bf16[2,2,40,640]{3,2,0,1:T(8,128)(2,1)S(1)}, bf16[2,2,40,640]{3,2,0,1:T(8,128)(2,1)S(1)}, u32[]{:S(2)}, u32[]{:S(2)}) %collective-permute-start.66) | collective-permute-done | bytes 204832 | tf_op jit(solution)/shard_map/ppermute | solution.py:165
  745.9 5.0 collective-permute-done.56
  757.0 4.9 collective-permute-done.57
  779.2 4.1 convert_element_type.1458
  (563 shorter events, 278.3 us)
Async XLA Ops:
  7.2 769.2 %reduce-scatter.5.cloned.1.call-start = ((), (), s32[]{:S(2)}) async-start(), calls=%async_computation.3 | async-start | bytes 5734400 | tf_op jit(solution)/shard_map/reduce_scatter | solution.py:128
  52.3 85.2 %collective-permute-start.2 = (bf16[512,1280]{1,0:T(8,128)(2,1)}, bf16[512,1280]{1,0:T(8,128)(2,1)}, u32[]{:S(2)}, u32[]{:S(2)}) collective-permute-start(bf16[512,1280]{1,0:T(8,128)(2,1)} %multiply_convert_fusion.10), channel_id=1, source_target_pairs={{0,1},{1,0},{2,3},{3,2},{4,5},{5,4},{6,7},{7,6},{8,9},{9,8},{10,11... | collective-permute-start | bytes 3932168 | tf_op jit(solution)/shard_map/ppermute | solution.py:136
  56.0 59.2 %collective-permute-start.1 = (f32[16,512]{1,0:T(8,128)S(1)}, f32[16,512]{1,0:T(8,128)S(1)}, u32[]{:S(2)}, u32[]{:S(2)}) collective-permute-start(f32[16,512]{1,0:T(8,128)S(1)} %get-tuple-element.115), channel_id=1, source_target_pairs={{0,1},{1,0},{2,3},{3,2},{4,5},{5,4},{6,7},{7,6},{8,9},{9,8},{10,11... | collective-permute-start | bytes 98312 | tf_op jit(solution)/shard_map/ppermute | solution.py:136
  56.5 61.7 %collective-permute-start.8 = (f32[16,512]{1,0:T(8,128)S(1)}, f32[16,512]{1,0:T(8,128)S(1)}, u32[]{:S(2)}, u32[]{:S(2)}) collective-permute-start(f32[16,512]{1,0:T(8,128)S(1)} %get-tuple-element.115), channel_id=1, source_target_pairs={{0,2},{1,3},{2,4},{3,5},{4,6},{5,7},{6,0},{7,1},{8,10},{9,11},{10,... | collective-permute-start | bytes 98312 | tf_op jit(solution)/shard_map/ppermute | solution.py:141
  59.1 118.5 %collective-permute-start.12 = (bf16[512,1280]{1,0:T(8,128)(2,1)}, bf16[512,1280]{1,0:T(8,128)(2,1)}, u32[]{:S(2)}, u32[]{:S(2)}) collective-permute-start(bf16[512,1280]{1,0:T(8,128)(2,1)} %multiply_convert_fusion.10), channel_id=1, source_target_pairs={{0,2},{1,3},{2,4},{3,5},{4,6},{5,7},{6,0},{7,1},{8,10},{9,11},{10,... | collective-permute-start | bytes 3932168 | tf_op jit(solution)/shard_map/ppermute | solution.py:141
  62.0 91.3 %collective-permute-start.28 = (bf16[512,1280]{1,0:T(8,128)(2,1)}, bf16[512,1280]{1,0:T(8,128)(2,1)}, u32[]{:S(2)}, u32[]{:S(2)}) collective-permute-start(bf16[512,1280]{1,0:T(8,128)(2,1)} %fusion.156), channel_id=1, source_target_pairs={{0,1},{1,0},{2,3},{3,2},{4,5},{5,4},{6,7},{7,6},{8,9},{9,8},{10,11... | collective-permute-start | bytes 3932168 | tf_op jit(solution)/shard_map/ppermute | solution.py:136
  136.1 43.0 %collective-permute-start.30 = (bf16[512,1280]{1,0:T(8,128)(2,1)}, bf16[512,1280]{1,0:T(8,128)(2,1)}, u32[]{:S(2)}, u32[]{:S(2)}) collective-permute-start(bf16[512,1280]{1,0:T(8,128)(2,1)} %fusion.156), channel_id=1, source_target_pairs={{0,2},{1,3},{2,4},{3,5},{4,6},{5,7},{6,0},{7,1},{8,10},{9,11},{10,... | collective-permute-start | bytes 3932168 | tf_op jit(solution)/shard_map/ppermute | solution.py:141
  137.4 50.9 %collective-permute-start.74 = (bf16[2,2,2,2,40,1280]{5,4,3,2,1,0:T(8,128)(2,1)}, bf16[2,2,2,2,40,1280]{5,4,3,2,1,0:T(8,128)(2,1)}, u32[]{:S(2)}, u32[]{:S(2)}) collective-permute-start(bf16[2,2,2,2,40,1280]{5,4,3,2,1,0:T(8,128)(2,1)} %dynamic-slice_bitcast_fusion.3), channel_id=1, source_target_pairs={{0,1},{1,0},{2,3},{3,2},{4,5},{5,4},{6,7},{7,6},{8,9},{9,8},{10,11... | collective-permute-start | bytes 4915208 | tf_op jit(solution)/shard_map/ppermute | solution.py:165
  137.5 55.0 %collective-permute-start.79 = (bf16[2,2,2,2,40,1408]{5,4,3,2,1,0:T(8,128)(2,1)}, bf16[2,2,2,2,40,1408]{5,4,3,2,1,0:T(8,128)(2,1)}, u32[]{:S(2)}, u32[]{:S(2)}) collective-permute-start(bf16[2,2,2,2,40,1408]{5,4,3,2,1,0:T(8,128)(2,1)} %dynamic-slice_bitcast_fusion.2), channel_id=1, source_target_pairs={{0,1},{1,0},{2,3},{3,2},{4,5},{5,4},{6,7},{7,6},{8,9},{9,8},{10,11... | collective-permute-start | bytes 5406728 | tf_op jit(solution)/shard_map/ppermute | solution.py:165
  177.6 36.4 %collective-permute-start.23 = (bf16[512,1280]{1,0:T(8,128)(2,1)}, bf16[512,1280]{1,0:T(8,128)(2,1)S(1)}, u32[]{:S(2)}, u32[]{:S(2)}) collective-permute-start(bf16[512,1280]{1,0:T(8,128)(2,1)} %collective-permute-done.12), channel_id=1, source_target_pairs={{0,1},{1,0},{2,3},{3,2},{4,5},{5,4},{6,7},{7,6},{8,9},{9,8},{10,11... | collective-permute-start | bytes 3932168 | tf_op jit(solution)/shard_map/ppermute | solution.py:136
  177.8 85.7 %collective-permute-start.13 = (bf16[512,1280]{1,0:T(8,128)(2,1)}, bf16[512,1280]{1,0:T(8,128)(2,1)}, u32[]{:S(2)}, u32[]{:S(2)}) collective-permute-start(bf16[512,1280]{1,0:T(8,128)(2,1)} %collective-permute-done.12), channel_id=1, source_target_pairs={{0,2},{1,3},{2,4},{3,5},{4,6},{5,7},{6,0},{7,1},{8,10},{9,11},{10,... | collective-permute-start | bytes 3932168 | tf_op jit(solution)/shard_map/ppermute | solution.py:141
  179.2 47.0 %collective-permute-start.37 = (bf16[512,1280]{1,0:T(8,128)(2,1)}, bf16[512,1280]{1,0:T(8,128)(2,1)S(1)}, u32[]{:S(2)}, u32[]{:S(2)}) collective-permute-start(bf16[512,1280]{1,0:T(8,128)(2,1)} %collective-permute-done.30), channel_id=1, source_target_pairs={{0,1},{1,0},{2,3},{3,2},{4,5},{5,4},{6,7},{7,6},{8,9},{9,8},{10,11... | collective-permute-start | bytes 3932168 | tf_op jit(solution)/shard_map/ppermute | solution.py:136
  189.8 20.7 %collective-permute-start.75 = (bf16[2,2,2,40,1280]{4,3,2,1,0:T(8,128)(2,1)S(1)}, bf16[2,2,2,40,1280]{4,3,2,1,0:T(8,128)(2,1)S(1)}, u32[]{:S(2)}, u32[]{:S(2)}) collective-permute-start(bf16[2,2,2,40,1280]{4,3,2,1,0:T(8,128)(2,1)S(1)} %fusion.242), channel_id=1, source_target_pairs={{0,8},{8,0},{16,24},{24,16},{1,9},{9,1},{17,25},{25,17},{2,10},{10... | collective-permute-start | bytes 2457608 | tf_op jit(solution)/shard_map/ppermute | solution.py:165
  192.5 105.3 %collective-permute-start.31 = (bf16[512,1280]{1,0:T(8,128)(2,1)}, bf16[512,1280]{1,0:T(8,128)(2,1)}, u32[]{:S(2)}, u32[]{:S(2)}) collective-permute-start(bf16[512,1280]{1,0:T(8,128)(2,1)} %collective-permute-done.30), channel_id=1, source_target_pairs={{0,2},{1,3},{2,4},{3,5},{4,6},{5,7},{6,0},{7,1},{8,10},{9,11},{10,... | collective-permute-start | bytes 3932168 | tf_op jit(solution)/shard_map/ppermute | solution.py:141
  210.5 49.5 %collective-permute-start.80 = (bf16[2,2,2,40,1408]{4,3,2,1,0:T(8,128)(2,1)}, bf16[2,2,2,40,1408]{4,3,2,1,0:T(8,128)(2,1)}, u32[]{:S(2)}, u32[]{:S(2)}) collective-permute-start(bf16[2,2,2,40,1408]{4,3,2,1,0:T(8,128)(2,1)} %fusion.241), channel_id=1, source_target_pairs={{0,16},{8,24},{16,0},{24,8},{1,17},{9,25},{17,1},{25,9},{2,18},{10... | collective-permute-start | bytes 2703368 | tf_op jit(solution)/shard_map/ppermute | solution.py:165
  214.1 49.6 %collective-permute-start.76 = (bf16[2,2,40,1280]{3,2,0,1:T(8,128)(2,1)}, bf16[2,2,40,1280]{3,2,0,1:T(8,128)(2,1)}, u32[]{:S(2)}, u32[]{:S(2)}) collective-permute-start(bf16[2,2,40,1280]{3,2,0,1:T(8,128)(2,1)} %copy.411), channel_id=1, source_target_pairs={{0,16},{8,24},{16,0},{24,8},{1,17},{9,25},{17,1},{25,9},{2,18},{10... | collective-permute-start | bytes 1228808 | tf_op jit(solution)/shard_map/ppermute | solution.py:165
  244.0 115.4 %collective-permute-start.24 = (bf16[512,1280]{1,0:T(8,128)(2,1)}, bf16[512,1280]{1,0:T(8,128)(2,1)}, u32[]{:S(2)}, u32[]{:S(2)}) collective-permute-start(bf16[512,1280]{1,0:T(8,128)(2,1)} %fusion.254), channel_id=1, source_target_pairs={{0,1},{1,0},{2,3},{3,2},{4,5},{5,4},{6,7},{7,6},{8,9},{9,8},{10,11... | collective-permute-start | bytes 3932168 | tf_op jit(solution)/shard_map/ppermute | solution.py:136
  262.0 12.3 %collective-permute-start.81 = (bf16[2,2,40,1408]{3,2,0,1:T(8,128)(2,1)S(1)}, bf16[2,2,40,1408]{3,2,0,1:T(8,128)(2,1)S(1)}, u32[]{:S(2)}, u32[]{:S(2)}) collective-permute-start(bf16[2,2,40,1408]{3,2,0,1:T(8,128)(2,1)S(1)} %copy.417), channel_id=1, source_target_pairs={{0,8},{8,0},{16,24},{24,16},{1,9},{9,1},{17,25},{25,17},{2,10},{10... | collective-permute-start | bytes 1351688 | tf_op jit(solution)/shard_map/ppermute | solution.py:165
  263.6 116.4 %collective-permute-start.38 = (bf16[512,1280]{1,0:T(8,128)(2,1)}, bf16[512,1280]{1,0:T(8,128)(2,1)}, u32[]{:S(2)}, u32[]{:S(2)}) collective-permute-start(bf16[512,1280]{1,0:T(8,128)(2,1)} %fusion.258), channel_id=1, source_target_pairs={{0,1},{1,0},{2,3},{3,2},{4,5},{5,4},{6,7},{7,6},{8,9},{9,8},{10,11... | collective-permute-start | bytes 3932168 | tf_op jit(solution)/shard_map/ppermute | solution.py:136
  263.7 65.9 %collective-permute-start.19 = (bf16[512,1280]{1,0:T(8,128)(2,1)}, bf16[512,1280]{1,0:T(8,128)(2,1)S(1)}, u32[]{:S(2)}, u32[]{:S(2)}) collective-permute-start(bf16[512,1280]{1,0:T(8,128)(2,1)} %collective-permute-done.13), channel_id=1, source_target_pairs={{0,1},{1,0},{2,3},{3,2},{4,5},{5,4},{6,7},{7,6},{8,9},{9,8},{10,11... | collective-permute-start | bytes 3932168 | tf_op jit(solution)/shard_map/ppermute | solution.py:136
  286.5 9.3 %collective-permute-start.78 = (bf16[40,1280]{1,0:T(8,128)(2,1)S(1)}, bf16[40,1280]{1,0:T(8,128)(2,1)S(1)}, u32[]{:S(2)}, u32[]{:S(2)}) collective-permute-start(bf16[40,1280]{1,0:T(8,128)(2,1)S(1)} %fusion.300), channel_id=1, source_target_pairs={{0,4},{1,5},{2,6},{3,7},{4,0},{5,1},{6,2},{7,3},{8,12},{9,13},{10,... | collective-permute-start | bytes 307208 | tf_op jit(solution)/shard_map/ppermute | solution.py:165
  295.8 31.2 %collective-permute-start.83 = (bf16[40,1408]{1,0:T(8,128)(2,1)S(1)}, bf16[40,1408]{1,0:T(8,128)(2,1)S(1)}, u32[]{:S(2)}, u32[]{:S(2)}) collective-permute-start(bf16[40,1408]{1,0:T(8,128)(2,1)S(1)} %fusion.298), channel_id=1, source_target_pairs={{0,4},{1,5},{2,6},{3,7},{4,0},{5,1},{6,2},{7,3},{8,12},{9,13},{10,... | collective-permute-start | bytes 337928 | tf_op jit(solution)/shard_map/ppermute | solution.py:165
  297.9 81.7 %collective-permute-start.14 = (bf16[512,1280]{1,0:T(8,128)(2,1)}, bf16[512,1280]{1,0:T(8,128)(2,1)}, u32[]{:S(2)}, u32[]{:S(2)}) collective-permute-start(bf16[512,1280]{1,0:T(8,128)(2,1)} %collective-permute-done.13), channel_id=1, source_target_pairs={{0,2},{1,3},{2,4},{3,5},{4,6},{5,7},{6,0},{7,1},{8,10},{9,11},{10,... | collective-permute-start | bytes 3932168 | tf_op jit(solution)/shard_map/ppermute | solution.py:141
  327.0 17.6 %collective-permute-start.35 = (bf16[512,1280]{1,0:T(8,128)(2,1)}, bf16[512,1280]{1,0:T(8,128)(2,1)S(1)}, u32[]{:S(2)}, u32[]{:S(2)}) collective-permute-start(bf16[512,1280]{1,0:T(8,128)(2,1)} %collective-permute-done.31), channel_id=1, source_target_pairs={{0,1},{1,0},{2,3},{3,2},{4,5},{5,4},{6,7},{7,6},{8,9},{9,8},{10,11... | collective-permute-start | bytes 3932168 | tf_op jit(solution)/shard_map/ppermute | solution.py:136
  329.5 64.8 %collective-permute-start.32 = (bf16[512,1280]{1,0:T(8,128)(2,1)}, bf16[512,1280]{1,0:T(8,128)(2,1)}, u32[]{:S(2)}, u32[]{:S(2)}) collective-permute-start(bf16[512,1280]{1,0:T(8,128)(2,1)} %collective-permute-done.31), channel_id=1, source_target_pairs={{0,2},{1,3},{2,4},{3,5},{4,6},{5,7},{6,0},{7,1},{8,10},{9,11},{10,... | collective-permute-start | bytes 3932168 | tf_op jit(solution)/shard_map/ppermute | solution.py:141
  344.7 44.7 %collective-permute-start.46 = (f32[16,512]{1,0:T(8,128)S(1)}, f32[16,512]{1,0:T(8,128)S(1)}, u32[]{:S(2)}, u32[]{:S(2)}) collective-permute-start(f32[16,512]{1,0:T(8,128)S(1)} %fusion.314), channel_id=1, source_target_pairs={{0,2},{1,3},{2,4},{3,5},{4,6},{5,7},{6,0},{7,1},{8,10},{9,11},{10,... | collective-permute-start | bytes 98312 | tf_op jit(solution)/shard_map/ppermute | solution.py:141
  362.2 71.5 %collective-permute-start.25 = (bf16[512,1280]{1,0:T(8,128)(2,1)}, bf16[512,1280]{1,0:T(8,128)(2,1)}, u32[]{:S(2)}, u32[]{:S(2)}) collective-permute-start(bf16[512,1280]{1,0:T(8,128)(2,1)} %fusion.177), channel_id=1, source_target_pairs={{0,2},{1,3},{2,4},{3,5},{4,6},{5,7},{6,0},{7,1},{8,10},{9,11},{10,... | collective-permute-start | bytes 3932168 | tf_op jit(solution)/shard_map/ppermute | solution.py:141
  379.6 10.3 %collective-permute-start.44 = (f32[16,512]{1,0:T(8,128)S(1)}, f32[16,512]{1,0:T(8,128)S(1)}, u32[]{:S(2)}, u32[]{:S(2)}) collective-permute-start(f32[16,512]{1,0:T(8,128)S(1)} %slice_bitcast_fusion.11), channel_id=1, source_target_pairs={{0,1},{1,0},{2,3},{3,2},{4,5},{5,4},{6,7},{7,6},{8,9},{9,8},{10,11... | collective-permute-start | bytes 98312 | tf_op jit(solution)/shard_map/ppermute | solution.py:136
  380.0 14.6 %collective-permute-start.15 = (bf16[512,1280]{1,0:T(8,128)(2,1)}, bf16[512,1280]{1,0:T(8,128)(2,1)S(1)}, u32[]{:S(2)}, u32[]{:S(2)}) collective-permute-start(bf16[512,1280]{1,0:T(8,128)(2,1)} %collective-permute-done.14), channel_id=1, source_target_pairs={{0,1},{1,0},{2,3},{3,2},{4,5},{5,4},{6,7},{7,6},{8,9},{9,8},{10,11... | collective-permute-start | bytes 3932168 | tf_op jit(solution)/shard_map/ppermute | solution.py:136
  389.4 44.3 %collective-permute-start.20 = (bf16[512,1280]{1,0:T(8,128)(2,1)}, bf16[512,1280]{1,0:T(8,128)(2,1)}, u32[]{:S(2)}, u32[]{:S(2)}) collective-permute-start(bf16[512,1280]{1,0:T(8,128)(2,1)} %fusion.253), channel_id=1, source_target_pairs={{0,1},{1,0},{2,3},{3,2},{4,5},{5,4},{6,7},{7,6},{8,9},{9,8},{10,11... | collective-permute-start | bytes 3932168 | tf_op jit(solution)/shard_map/ppermute | solution.py:136
  389.9 53.3 %collective-permute-start.39 = (bf16[512,1280]{1,0:T(8,128)(2,1)}, bf16[512,1280]{1,0:T(8,128)(2,1)}, u32[]{:S(2)}, u32[]{:S(2)}) collective-permute-start(bf16[512,1280]{1,0:T(8,128)(2,1)} %fusion.165), channel_id=1, source_target_pairs={{0,2},{1,3},{2,4},{3,5},{4,6},{5,7},{6,0},{7,1},{8,10},{9,11},{10,... | collective-permute-start | bytes 3932168 | tf_op jit(solution)/shard_map/ppermute | solution.py:141
  394.4 49.4 %collective-permute-start.36 = (bf16[512,1280]{1,0:T(8,128)(2,1)}, bf16[512,1280]{1,0:T(8,128)(2,1)}, u32[]{:S(2)}, u32[]{:S(2)}) collective-permute-start(bf16[512,1280]{1,0:T(8,128)(2,1)} %fusion.257), channel_id=1, source_target_pairs={{0,1},{1,0},{2,3},{3,2},{4,5},{5,4},{6,7},{7,6},{8,9},{9,8},{10,11... | collective-permute-start | bytes 3932168 | tf_op jit(solution)/shard_map/ppermute | solution.py:136
  394.6 17.1 %collective-permute-start.33 = (bf16[512,1280]{1,0:T(8,128)(2,1)}, bf16[512,1280]{1,0:T(8,128)(2,1)S(1)}, u32[]{:S(2)}, u32[]{:S(2)}) collective-permute-start(bf16[512,1280]{1,0:T(8,128)(2,1)} %collective-permute-done.32), channel_id=1, source_target_pairs={{0,1},{1,0},{2,3},{3,2},{4,5},{5,4},{6,7},{7,6},{8,9},{9,8},{10,11... | collective-permute-start | bytes 3932168 | tf_op jit(solution)/shard_map/ppermute | solution.py:136
  411.7 58.9 %collective-permute-start.47 = (f32[16,512]{1,0:T(8,128)S(1)}, f32[16,512]{1,0:T(8,128)S(1)}, u32[]{:S(2)}, u32[]{:S(2)}) collective-permute-start(f32[16,512]{1,0:T(8,128)S(1)} %fusion.316), channel_id=1, source_target_pairs={{0,2},{1,3},{2,4},{3,5},{4,6},{5,7},{6,0},{7,1},{8,10},{9,11},{10,... | collective-permute-start | bytes 98312 | tf_op jit(solution)/shard_map/ppermute | solution.py:141
  433.6 345.6 %reduce-scatter.3.cloned.1.call-start = ((), (), s32[]{:S(2)}) async-start(), calls=%async_computation.2 | async-start | bytes 11468800 | tf_op jit(solution)/shard_map/reduce_scatter | solution.py:125
  437.8 67.4 %collective-permute-start.26 = (bf16[512,1280]{1,0:T(8,128)(2,1)}, bf16[512,1280]{1,0:T(8,128)(2,1)}, u32[]{:S(2)}, u32[]{:S(2)}) collective-permute-start(bf16[512,1280]{1,0:T(8,128)(2,1)} %fusion.180), channel_id=1, source_target_pairs={{0,2},{1,3},{2,4},{3,5},{4,6},{5,7},{6,0},{7,1},{8,10},{9,11},{10,... | collective-permute-start | bytes 3932168 | tf_op jit(solution)/shard_map/ppermute | solution.py:141
  443.1 66.0 %collective-permute-start.16 = (bf16[512,1280]{1,0:T(8,128)(2,1)}, bf16[512,1280]{1,0:T(8,128)(2,1)}, u32[]{:S(2)}, u32[]{:S(2)}) collective-permute-start(bf16[512,1280]{1,0:T(8,128)(2,1)} %fusion.252), channel_id=1, source_target_pairs={{0,1},{1,0},{2,3},{3,2},{4,5},{5,4},{6,7},{7,6},{8,9},{9,8},{10,11... | collective-permute-start | bytes 3932168 | tf_op jit(solution)/shard_map/ppermute | solution.py:136
  443.2 56.2 %collective-permute-start.43 = (f32[16,512]{1,0:T(8,128)S(1)}, f32[16,512]{1,0:T(8,128)S(1)}, u32[]{:S(2)}, u32[]{:S(2)}) collective-permute-start(f32[16,512]{1,0:T(8,128)S(1)} %slice_bitcast_fusion.13), channel_id=1, source_target_pairs={{0,1},{1,0},{2,3},{3,2},{4,5},{5,4},{6,7},{7,6},{8,9},{9,8},{10,11... | collective-permute-start | bytes 98312 | tf_op jit(solution)/shard_map/ppermute | solution.py:136
  447.9 52.7 %collective-permute-start.40 = (bf16[512,1280]{1,0:T(8,128)(2,1)}, bf16[512,1280]{1,0:T(8,128)(2,1)}, u32[]{:S(2)}, u32[]{:S(2)}) collective-permute-start(bf16[512,1280]{1,0:T(8,128)(2,1)} %fusion.168), channel_id=1, source_target_pairs={{0,2},{1,3},{2,4},{3,5},{4,6},{5,7},{6,0},{7,1},{8,10},{9,11},{10,... | collective-permute-start | bytes 3932168 | tf_op jit(solution)/shard_map/ppermute | solution.py:141
  470.6 30.1 %collective-permute-start.34 = (bf16[512,1280]{1,0:T(8,128)(2,1)}, bf16[512,1280]{1,0:T(8,128)(2,1)}, u32[]{:S(2)}, u32[]{:S(2)}) collective-permute-start(bf16[512,1280]{1,0:T(8,128)(2,1)} %fusion.256), channel_id=1, source_target_pairs={{0,1},{1,0},{2,3},{3,2},{4,5},{5,4},{6,7},{7,6},{8,9},{9,8},{10,11... | collective-permute-start | bytes 3932168 | tf_op jit(solution)/shard_map/ppermute | solution.py:136
  500.1 13.0 %collective-permute-start.42 = (f32[16,512]{1,0:T(8,128)S(1)}, f32[16,512]{1,0:T(8,128)S(1)}, u32[]{:S(2)}, u32[]{:S(2)}) collective-permute-start(f32[16,512]{1,0:T(8,128)S(1)} %copy-done.65), channel_id=1, source_target_pairs={{0,1},{1,0},{2,3},{3,2},{4,5},{5,4},{6,7},{7,6},{8,9},{9,8},{10,11... | collective-permute-start | bytes 98312 | tf_op jit(solution)/shard_map/ppermute | solution.py:136
  500.6 17.7 %collective-permute-start.29 = (bf16[512,1280]{1,0:T(8,128)(2,1)}, bf16[512,1280]{1,0:T(8,128)(2,1)}, u32[]{:S(2)}, u32[]{:S(2)}) collective-permute-start(bf16[512,1280]{1,0:T(8,128)(2,1)} %fusion.255), channel_id=1, source_target_pairs={{0,1},{1,0},{2,3},{3,2},{4,5},{5,4},{6,7},{7,6},{8,9},{9,8},{10,11... | collective-permute-start | bytes 3932168 | tf_op jit(solution)/shard_map/ppermute | solution.py:136
  500.7 48.4 %collective-permute-start.3 = (bf16[512,1280]{1,0:T(8,128)(2,1)}, bf16[512,1280]{1,0:T(8,128)(2,1)}, u32[]{:S(2)}, u32[]{:S(2)}) collective-permute-start(bf16[512,1280]{1,0:T(8,128)(2,1)} %fusion.251), channel_id=1, source_target_pairs={{0,1},{1,0},{2,3},{3,2},{4,5},{5,4},{6,7},{7,6},{8,9},{9,8},{10,11... | collective-permute-start | bytes 3932168 | tf_op jit(solution)/shard_map/ppermute | solution.py:136
  505.2 8.4 %collective-permute-start.48 = (f32[16,512]{1,0:T(8,128)S(1)}, f32[16,512]{1,0:T(8,128)S(1)}, u32[]{:S(2)}, u32[]{:S(2)}) collective-permute-start(f32[16,512]{1,0:T(8,128)S(1)} %fusion.318), channel_id=1, source_target_pairs={{0,2},{1,3},{2,4},{3,5},{4,6},{5,7},{6,0},{7,1},{8,10},{9,11},{10,... | collective-permute-start | bytes 98312 | tf_op jit(solution)/shard_map/ppermute | solution.py:141
  509.1 33.8 %collective-permute-start.41 = (bf16[512,1280]{1,0:T(8,128)(2,1)}, bf16[512,1280]{1,0:T(8,128)(2,1)}, u32[]{:S(2)}, u32[]{:S(2)}) collective-permute-start(bf16[512,1280]{1,0:T(8,128)(2,1)} %fusion.171), channel_id=1, source_target_pairs={{0,2},{1,3},{2,4},{3,5},{4,6},{5,7},{6,0},{7,1},{8,10},{9,11},{10,... | collective-permute-start | bytes 3932168 | tf_op jit(solution)/shard_map/ppermute | solution.py:141
  513.2 56.7 %collective-permute-start.27 = (bf16[512,1280]{1,0:T(8,128)(2,1)}, bf16[512,1280]{1,0:T(8,128)(2,1)}, u32[]{:S(2)}, u32[]{:S(2)}) collective-permute-start(bf16[512,1280]{1,0:T(8,128)(2,1)} %fusion.183), channel_id=1, source_target_pairs={{0,2},{1,3},{2,4},{3,5},{4,6},{5,7},{6,0},{7,1},{8,10},{9,11},{10,... | collective-permute-start | bytes 3932168 | tf_op jit(solution)/shard_map/ppermute | solution.py:141
  580.2 105.1 %collective-permute-start.64 = (bf16[2,2,2,2,40,640]{5,4,3,2,1,0:T(8,128)(2,1)}, bf16[2,2,2,2,40,640]{5,4,3,2,1,0:T(8,128)(2,1)}, u32[]{:S(2)}, u32[]{:S(2)}) collective-permute-start(bf16[2,2,2,2,40,640]{5,4,3,2,1,0:T(8,128)(2,1)} %dynamic-slice_bitcast_fusion.5), channel_id=1, source_target_pairs={{0,1},{1,0},{2,3},{3,2},{4,5},{5,4},{6,7},{7,6},{8,9},{9,8},{10,11... | collective-permute-start | bytes 2457608 | tf_op jit(solution)/shard_map/ppermute | solution.py:165
  582.0 106.0 %collective-permute-start.69 = (bf16[2,2,2,2,40,640]{5,4,2,3,1,0:T(8,128)(2,1)}, bf16[2,2,2,2,40,640]{5,4,2,3,1,0:T(8,128)(2,1)}, u32[]{:S(2)}, u32[]{:S(2)}) collective-permute-start(bf16[2,2,2,2,40,640]{5,4,2,3,1,0:T(8,128)(2,1)} %copy.403), channel_id=1, source_target_pairs={{0,1},{1,0},{2,3},{3,2},{4,5},{5,4},{6,7},{7,6},{8,9},{9,8},{10,11... | collective-permute-start | bytes 2457608 | tf_op jit(solution)/shard_map/ppermute | solution.py:165
  642.5 48.3 %collective-permute-start.54 = (bf16[2,2,2,2,40,1920]{5,4,3,2,1,0:T(8,128)(2,1)}, bf16[2,2,2,2,40,1920]{5,4,3,2,1,0:T(8,128)(2,1)}, u32[]{:S(2)}, u32[]{:S(2)}) collective-permute-start(bf16[2,2,2,2,40,1920]{5,4,3,2,1,0:T(8,128)(2,1)} %dynamic-slice_bitcast_fusion.1), channel_id=1, source_target_pairs={{0,1},{1,0},{2,3},{3,2},{4,5},{5,4},{6,7},{7,6},{8,9},{9,8},{10,11... | collective-permute-start | bytes 7372808 | tf_op jit(solution)/shard_map/ppermute | solution.py:165
  644.7 48.5 %collective-permute-start.59 = (bf16[2,2,2,2,40,1920]{5,4,2,3,1,0:T(8,128)(2,1)}, bf16[2,2,2,2,40,1920]{5,4,2,3,1,0:T(8,128)(2,1)}, u32[]{:S(2)}, u32[]{:S(2)}) collective-permute-start(bf16[2,2,2,2,40,1920]{5,4,2,3,1,0:T(8,128)(2,1)} %copy.392), channel_id=1, source_target_pairs={{0,1},{1,0},{2,3},{3,2},{4,5},{5,4},{6,7},{7,6},{8,9},{9,8},{10,11... | collective-permute-start | bytes 7372808 | tf_op jit(solution)/shard_map/ppermute | solution.py:165
  686.5 11.2 %collective-permute-start.65 = (bf16[2,2,2,40,640]{4,3,2,1,0:T(8,128)(2,1)S(1)}, bf16[2,2,2,40,640]{4,3,2,1,0:T(8,128)(2,1)S(1)}, u32[]{:S(2)}, u32[]{:S(2)}) collective-permute-start(bf16[2,2,2,40,640]{4,3,2,1,0:T(8,128)(2,1)S(1)} %fusion.278), channel_id=1, source_target_pairs={{0,8},{8,0},{16,24},{24,16},{1,9},{9,1},{17,25},{25,17},{2,10},{10... | collective-permute-start | bytes 1228808 | tf_op jit(solution)/shard_map/ppermute | solution.py:165
  689.1 12.2 %collective-permute-start.70 = (bf16[2,2,2,40,640]{4,3,2,1,0:T(8,128)(2,1)S(1)}, bf16[2,2,2,40,640]{4,3,2,1,0:T(8,128)(2,1)S(1)}, u32[]{:S(2)}, u32[]{:S(2)}) collective-permute-start(bf16[2,2,2,40,640]{4,3,2,1,0:T(8,128)(2,1)S(1)} %fusion.277), channel_id=1, source_target_pairs={{0,16},{8,24},{16,0},{24,8},{1,17},{9,25},{17,1},{25,9},{2,18},{10... | collective-permute-start | bytes 1228808 | tf_op jit(solution)/shard_map/ppermute | solution.py:165
  692.7 46.2 %collective-permute-start.55 = (bf16[2,2,2,40,1920]{4,3,2,1,0:T(8,128)(2,1)S(1)}, bf16[2,2,2,40,1920]{4,3,2,1,0:T(8,128)(2,1)S(1)}, u32[]{:S(2)}, u32[]{:S(2)}) collective-permute-start(bf16[2,2,2,40,1920]{4,3,2,1,0:T(8,128)(2,1)S(1)} %fusion.211), channel_id=1, source_target_pairs={{0,8},{8,0},{16,24},{24,16},{1,9},{9,1},{17,25},{25,17},{2,10},{10... | collective-permute-start | bytes 3686408 | tf_op jit(solution)/shard_map/ppermute | solution.py:165
  694.8 47.1 %collective-permute-start.60 = (bf16[2,2,2,40,1920]{4,3,2,1,0:T(8,128)(2,1)S(1)}, bf16[2,2,2,40,1920]{4,3,2,1,0:T(8,128)(2,1)S(1)}, u32[]{:S(2)}, u32[]{:S(2)}) collective-permute-start(bf16[2,2,2,40,1920]{4,3,2,1,0:T(8,128)(2,1)S(1)} %fusion.210), channel_id=1, source_target_pairs={{0,16},{8,24},{16,0},{24,8},{1,17},{9,25},{17,1},{25,9},{2,18},{10... | collective-permute-start | bytes 3686408 | tf_op jit(solution)/shard_map/ppermute | solution.py:165
  698.7 29.1 %collective-permute-start.66 = (bf16[2,2,40,640]{3,2,0,1:T(8,128)(2,1)S(1)}, bf16[2,2,40,640]{3,2,0,1:T(8,128)(2,1)S(1)}, u32[]{:S(2)}, u32[]{:S(2)}) collective-permute-start(bf16[2,2,40,640]{3,2,0,1:T(8,128)(2,1)S(1)} %copy.400), channel_id=1, source_target_pairs={{0,16},{8,24},{16,0},{24,8},{1,17},{9,25},{17,1},{25,9},{2,18},{10... | collective-permute-start | bytes 614408 | tf_op jit(solution)/shard_map/ppermute | solution.py:165
  702.3 26.6 %collective-permute-start.71 = (bf16[2,2,40,640]{3,2,1,0:T(8,128)(2,1)S(1)}, bf16[2,2,40,640]{3,2,1,0:T(8,128)(2,1)S(1)}, u32[]{:S(2)}, u32[]{:S(2)}) collective-permute-start(bf16[2,2,40,640]{3,2,1,0:T(8,128)(2,1)S(1)} %fusion.286), channel_id=1, source_target_pairs={{0,8},{8,0},{16,24},{24,16},{1,9},{9,1},{17,25},{25,17},{2,10},{10... | collective-permute-start | bytes 614408 | tf_op jit(solution)/shard_map/ppermute | solution.py:165
  734.9 9.2 %collective-permute-start.68 = (bf16[40,640]{1,0:T(8,128)(2,1)S(1)}, bf16[40,640]{1,0:T(8,128)(2,1)S(1)}, u32[]{:S(2)}, u32[]{:S(2)}) collective-permute-start(bf16[40,640]{1,0:T(8,128)(2,1)S(1)} %fusion.306), channel_id=1, source_target_pairs={{0,4},{1,5},{2,6},{3,7},{4,0},{5,1},{6,2},{7,3},{8,12},{9,13},{10,... | collective-permute-start | bytes 153608 | tf_op jit(solution)/shard_map/ppermute | solution.py:165
  737.6 7.4 collective-permute-start.73
  740.7 10.2 %collective-permute-start.56 = (bf16[2,2,40,1920]{3,2,0,1:T(8,128)(2,1)S(1)}, bf16[2,2,40,1920]{3,2,0,1:T(8,128)(2,1)S(1)}, u32[]{:S(2)}, u32[]{:S(2)}) collective-permute-start(bf16[2,2,40,1920]{3,2,0,1:T(8,128)(2,1)S(1)} %copy.389), channel_id=1, source_target_pairs={{0,16},{8,24},{16,0},{24,8},{1,17},{9,25},{17,1},{25,9},{2,18},{10... | collective-permute-start | bytes 1843208 | tf_op jit(solution)/shard_map/ppermute | solution.py:165
  743.2 10.5 %collective-permute-start.61 = (bf16[2,2,40,1920]{3,2,1,0:T(8,128)(2,1)S(1)}, bf16[2,2,40,1920]{3,2,1,0:T(8,128)(2,1)S(1)}, u32[]{:S(2)}, u32[]{:S(2)}) collective-permute-start(bf16[2,2,40,1920]{3,2,1,0:T(8,128)(2,1)S(1)} %fusion.259), channel_id=1, source_target_pairs={{0,8},{8,0},{16,24},{24,16},{1,9},{9,1},{17,25},{25,17},{2,10},{10... | collective-permute-start | bytes 1843208 | tf_op jit(solution)/shard_map/ppermute | solution.py:165
  752.1 9.8 %collective-permute-start.57 = (bf16[2,40,1920]{2,1,0:T(8,128)(2,1)S(1)}, bf16[2,40,1920]{2,1,0:T(8,128)(2,1)S(1)}, u32[]{:S(2)}, u32[]{:S(2)}) collective-permute-start(bf16[2,40,1920]{2,1,0:T(8,128)(2,1)S(1)} %fusion.280), channel_id=1, source_target_pairs={{0,2},{1,3},{2,0},{3,1},{4,6},{5,7},{6,4},{7,5},{8,10},{9,11},{10,... | collective-permute-start | bytes 921608 | tf_op jit(solution)/shard_map/ppermute | solution.py:165
  754.9 10.8 %collective-permute-start.62 = (bf16[2,40,1920]{2,1,0:T(8,128)(2,1)S(1)}, bf16[2,40,1920]{2,1,0:T(8,128)(2,1)S(1)}, u32[]{:S(2)}, u32[]{:S(2)}) collective-permute-start(bf16[2,40,1920]{2,1,0:T(8,128)(2,1)S(1)} %fusion.279), channel_id=1, source_target_pairs={{0,2},{1,3},{2,0},{3,1},{4,6},{5,7},{6,4},{7,5},{8,10},{9,11},{10,... | collective-permute-start | bytes 921608 | tf_op jit(solution)/shard_map/ppermute | solution.py:165
  763.0 7.8 collective-permute-start.58
  766.7 7.8 collective-permute-start.63
  (128 other events, 1286.0 us)
Sparse Core Ops, SparseCore 0:
  433.7 57.4 reduce-scatter.4
  499.5 94.4 reduce-scatter.2

commit v3 on v1

v3 whole, which is shorter than its diff:
```python
import jax
import jax.numpy as jnp
from jax import lax
from jax.experimental import pallas as pl
from jax.experimental.pallas import tpu as pltpu
from jax.sharding import PartitionSpec as P

HEAD_DIM = 128
NORM_EPS = 1e-06
MASK_VALUE = -1e30
NT = (((1,), (1,)), ((), ()))
TN = (((0,), (0,)), ((), ()))

def turn(values_in, cosine, signed_sine):
    return values_in * cosine + pltpu.roll(values_in, HEAD_DIM // 2, 1) * signed_sine

def block_scores(q, k, start, seq_length):
    s = lax.dot_general(q, k, NT, preferred_element_type=jnp.float32) * HEAD_DIM ** (-0.5)
    query_pos = start + lax.broadcasted_iota(jnp.int32, s.shape, 0)
    key_pos = lax.broadcasted_iota(jnp.int32, s.shape, 1)
    return jnp.where((key_pos <= query_pos) & (key_pos < seq_length), s, MASK_VALUE)

def attention_kernel(length_ref, x, norm1, wq, wk, wv, cosine, sine, w_out, norm2, h1, q_o, k_o, v_o, att, lse, x_mid, h2):
    f32, bf16 = jnp.float32, jnp.bfloat16
    p = pl.program_id(0)
    tokens = x.shape[0]
    seq_length = length_ref[0]
    span = min(256, tokens)

    @pl.when(p == 0)
    def _():
        xf = x[...].astype(f32)
        inverse = lax.rsqrt(jnp.mean(xf * xf, axis=-1, keepdims=True) + NORM_EPS)
        h1[...] = (xf * inverse * norm1[...]).astype(bf16)
        lse[...] = jnp.zeros_like(lse)

    for w, o in ((wq, q_o), (wk, k_o), (wv, v_o)):
        full = jnp.dot(h1[...], w[...], preferred_element_type=f32)
        for j in (0, 1):
            part = full[:, j * HEAD_DIM:(j + 1) * HEAD_DIM]
            if w is not wv:
                part = turn(part, cosine[...], sine[...])
            o[:, pl.ds(j * HEAD_DIM, HEAD_DIM)] = part.astype(bf16)
    lane = lax.broadcasted_iota(jnp.int32, (span, lse.shape[1]), 1)
    for j in (0, 1):
        cols = pl.ds(j * HEAD_DIM, HEAD_DIM)
        for start in range(0, tokens, span):
            rows = pl.ds(start, span)
            seen = pl.ds(0, start + span)
            s = block_scores(q_o[rows, cols], k_o[seen, cols], start, seq_length)
            high = jnp.max(s, axis=-1, keepdims=True)
            ex = jnp.exp(s - high)
            total = jnp.sum(ex, axis=-1, keepdims=True)
            low = (ex / total).astype(bf16)
            out = jnp.dot(low, v_o[seen, cols], preferred_element_type=f32)
            att[rows, pl.ds(pl.multiple_of(p * 2 * HEAD_DIM + j * HEAD_DIM, HEAD_DIM), HEAD_DIM)] = out.astype(bf16)
            lse[rows, :] = jnp.where(lane == 2 * p + j, high + jnp.log(total), lse[rows, :])

    @pl.when(p == pl.num_programs(0) - 1)
    def _():
        branch = jnp.dot(att[...], w_out[...], preferred_element_type=f32)
        live = lax.broadcasted_iota(jnp.int32, (tokens, 1), 0) < seq_length
        mid = x[...].astype(f32) + jnp.where(live, branch, 0.0)
        x_mid[...] = mid
        inverse = lax.rsqrt(jnp.mean(mid * mid, axis=-1, keepdims=True) + NORM_EPS)
        h2[...] = (mid * inverse * norm2[...]).astype(bf16)

def whole(a):
    return pl.BlockSpec(a.shape, lambda p: (0,) * len(a.shape), pipeline_mode=pl.Buffered(1))

def attention_forward(lengths, x, norm1, w_qkv, cosine, sine, w_out, norm2):
    tokens, width = x.shape
    pairs = width // (2 * HEAD_DIM)
    f32, bf16 = jnp.float32, jnp.bfloat16
    wide = 2 * HEAD_DIM
    col = lambda k: pl.BlockSpec((width, wide), lambda p, k=k: (0, k * pairs + p))
    head = pl.BlockSpec((tokens, wide), lambda p: (0, p))
    full = pl.BlockSpec((tokens, width), lambda p: (0, 0))
    sd = jax.ShapeDtypeStruct
    return pl.pallas_call(
        attention_kernel, grid=(pairs,),
        in_specs=[pl.BlockSpec(memory_space=pltpu.SMEM), whole(x), whole(norm1), col(0), col(1), col(2), whole(cosine), whole(sine), whole(w_out), whole(norm2)],
        out_specs=[full, head, head, head, full, pl.BlockSpec((tokens, 128), lambda p: (0, 0)), full, full],
        out_shape=[sd((tokens, width), bf16)] * 5 + [sd((tokens, 128), f32), sd((tokens, width), f32), sd((tokens, width), bf16)],
        compiler_params=pltpu.CompilerParams(vmem_limit_bytes=48 * 2**20),
        cost_estimate=pl.CostEstimate(flops=0, bytes_accessed=0, transcendentals=0),
        name="attention_forward",
    )(lengths, x, norm1, w_qkv, w_qkv, w_qkv, cosine, sine, w_out, norm2)

def attention_back_kernel(rows, extra, carried, length_ref, core_ref, da, w_out, q, k, v, lse, cosine, sine, h1, att, wq, wk, wv, *rest):
    f32, bf16 = jnp.float32, jnp.bfloat16
    dh1_in = None
    if carried:
        dh1_in, *rest = rest
    if extra:
        x, gain, grad_mid, small, *rest = rest
    *grads, dh1, dk_s, dv_s, dproj = rest
    p = pl.program_id(0)
    pair = length_ref[1] + p
    tokens, width = da.shape
    seq_length = length_ref[0]
    span = min(256, tokens)
    scale = HEAD_DIM ** (-0.5)
    mine = core_ref[0] == 0
    wide = 2 * HEAD_DIM
    do_full = lax.dot_general(da[...], w_out[...], NT, preferred_element_type=f32).astype(bf16)
    lane = lax.broadcasted_iota(jnp.int32, (span, lse.shape[1]), 1)
    back_sine = -sine[...]
    for j in (0, 1):
        cols = pl.ds(j * HEAD_DIM, HEAD_DIM)
        do_head = do_full[:, j * HEAD_DIM : (j + 1) * HEAD_DIM]
        for start in range(tokens - span, -1, -span):
            r = pl.ds(start, span)
            seen = pl.ds(0, start + span)
            s = block_scores(q[r, cols], k[seen, cols], start, seq_length)
            norm = jnp.sum(jnp.where(lane == 2 * pair + j, lse[r, :], 0.0), axis=1, keepdims=True)
            probs = jnp.exp(s - norm)
            do = do_head[start : start + span]
            dp = lax.dot_general(do, v[seen, cols], NT, preferred_element_type=f32)
            row = jnp.sum(dp * probs, axis=1, keepdims=True)
            ds = (probs * (dp - row)).astype(bf16)
            dq = jnp.dot(ds, k[seen, cols], preferred_element_type=f32) * scale
            dproj[r, pl.ds(j * HEAD_DIM, HEAD_DIM)] = turn(
                dq, cosine[r, :], back_sine[start : start + span]
            ).astype(bf16)
            dk = lax.dot_general(ds, q[r, cols], TN, preferred_element_type=f32) * scale
            dv = lax.dot_general(probs.astype(bf16), do, TN, preferred_element_type=f32)
            if start == tokens - span:
                dk_s[seen, :] = dk
                dv_s[seen, :] = dv
            else:
                dk_s[seen, :] += dk
                dv_s[seen, :] += dv
        dproj[:, pl.ds(wide + j * HEAD_DIM, HEAD_DIM)] = turn(dk_s[...], cosine[...], back_sine).astype(bf16)
        dproj[:, pl.ds(2 * wide + j * HEAD_DIM, HEAD_DIM)] = dv_s[...].astype(bf16)
    total = jnp.where(p == 0, dh1_in[...] if carried else 0.0, dh1[...])
    for i, w in enumerate((wq, wk, wv)):
        part = dproj[:, pl.ds(i * wide, wide)]
        grad = lax.dot_general(h1[...], part, TN, preferred_element_type=f32)
        store_grad(grad, pl.ds(i * wide, wide), rows, mine, grads)
        total += lax.dot_general(part, w[...], NT, preferred_element_type=f32)
    part = da[:, pl.ds(pl.multiple_of(pair * wide, wide), wide)]
    grad = lax.dot_general(att[...], part, TN, preferred_element_type=f32)
    store_grad(grad, pl.ds(3 * wide, wide), rows, mine, grads)
    dh1[...] = total
    if not extra:
        return

    @pl.when(p < pl.num_programs(0) - 1)
    def _():
        store_grad(jnp.zeros(small.shape, f32), pl.ds(4 * wide, small.shape[1]), rows, mine, grads)

    @pl.when(p == pl.num_programs(0) - 1)
    def _():
        full = x[...].astype(f32)
        inverse = lax.rsqrt(jnp.mean(full * full, axis=-1, keepdims=True) + NORM_EPS)
        scaled = full * inverse
        inner = total * gain[...]
        dh1[...] = grad_mid[...] + inverse * (
            inner - scaled * jnp.mean(inner * scaled, axis=-1, keepdims=True)
        )
        column = lax.broadcasted_iota(jnp.int32, (tokens, small.shape[1]), 1)
        grad = small[...] + lax.dot_general(
            total * scaled, jnp.where(column == extra + 1, 1.0, 0.0), TN,
            precision=lax.Precision.HIGHEST, preferred_element_type=f32,
        )
        store_grad(grad, pl.ds(4 * wide, small.shape[1]), rows, mine, grads)


def attention_backward(lengths, core, da, w_out, q, k, v, lse, cosine, sine, h1, att, w_qkv, dh1_in, first, count, rows, tail):
    tokens, width = da.shape
    pairs = width // (2 * HEAD_DIM)
    wide = 2 * HEAD_DIM
    f32, bf16 = jnp.float32, jnp.bfloat16
    col = lambda k: pl.BlockSpec((width, wide), lambda p, k=k: (0, k * pairs + first + p))
    head = pl.BlockSpec((tokens, wide), lambda p: (0, first + p))
    sd = jax.ShapeDtypeStruct
    smem = pl.BlockSpec(memory_space=pltpu.SMEM)
    n = width // 2 if rows else width
    extra, tail_args = tail if tail else (0, ())
    columns = 4 * wide + (tail_args[-1].shape[1] if extra else 0)
    grads = [sd((n, count * columns), bf16)] * (2 if rows else 1)
    carried = dh1_in is not None
    tail_args = ((dh1_in,) if carried else ()) + tuple(tail_args)
    whole_args = (da, lse, cosine, sine, h1, att) + tail_args
    spec = {id(a): whole(a) for a in whole_args}
    return pl.pallas_call(
        lambda *r: attention_back_kernel(rows, extra, carried, *r),
        grid=(count,),
        in_specs=[smem, smem, spec[id(da)], pl.BlockSpec((wide, width), lambda p: (first + p, 0)), head, head, head]
        + [spec[id(a)] for a in (lse, cosine, sine, h1, att)]
        + [col(0), col(1), col(2)]
        + [spec[id(a)] for a in tail_args],
        out_specs=[pl.BlockSpec((n, columns), lambda p: (0, p))] * len(grads)
        + [pl.BlockSpec((tokens, width), lambda p: (0, 0))],
        out_shape=grads + [sd((tokens, width), f32)],
        scratch_shapes=[pltpu.VMEM((tokens, HEAD_DIM), f32), pltpu.VMEM((tokens, HEAD_DIM), f32), pltpu.VMEM((tokens, 3 * wide), bf16)],
        compiler_params=pltpu.CompilerParams(vmem_limit_bytes=48 * 2**20),
        cost_estimate=pl.CostEstimate(flops=0, bytes_accessed=0, transcendentals=0),
        name="attention_backward",
    )(
        jnp.concatenate([lengths, jnp.full((1,), first, jnp.int32)]), core, da, w_out, q, k, v,
        lse, cosine, sine, h1, att, w_qkv, w_qkv, w_qkv, *tail_args,
    )


def expert_kernel(cap, tokens, hidden, last_slot, *refs):
    (first_ref, h2a, h2b, cba, cbb, wr, w_in, w_down) = refs[:8]
    (dra, drb, outa, outb, rows_o, dy_o, act_o, dgu_o, gu, cbrow, oh, gy, drs, probs, dots) = refs[-15:]
    f32, bf16 = jnp.float32, jnp.bfloat16
    e = pl.program_id(0)
    experts = wr.shape[0]
    width = wr.shape[1]
    mine = first_ref[0] + e
    table_rows = probs.shape[1]

    @pl.when(e == 0)
    def _():
        for src, h2 in ((0, h2a), (1, h2b)):
            logits = lax.dot_general(wr[...], h2[...], (((1,), (1,)), ((), ())), preferred_element_type=f32)
            row = lax.broadcasted_iota(jnp.int32, logits.shape, 0)
            logits = jnp.where(row < experts - 1, logits, MASK_VALUE)
            ex = jnp.exp(logits - jnp.max(logits, axis=0, keepdims=True))
            probs[src] = ex / jnp.sum(ex, axis=0, keepdims=True)
            dots[src] = jnp.zeros_like(probs[src])

    gates = []
    masks = []
    for src, h2, cb in ((0, h2a, cba), (1, h2b, cbb)):
        row_id = lax.broadcasted_iota(jnp.int32, (table_rows, tokens), 0)
        table = cb[pl.ds(tokens, table_rows), pl.ds(0, tokens)].astype(f32)
        rank = jnp.sum(jnp.where(row_id == mine, table, 0.0), axis=0, keepdims=True)
        prob = jnp.sum(jnp.where(row_id == mine, probs[src], 0.0), axis=0, keepdims=True)
        hit = lax.broadcasted_iota(jnp.int32, (cap, tokens), 0).astype(f32) == rank
        masks.append(hit)
        gates.append(jnp.sum(jnp.where(hit, prob, 0.0), axis=1, keepdims=True))
        onehot = jnp.where(hit, 1.0, 0.0).astype(bf16)
        oh[src, pl.ds(e * cap, cap), :] = onehot
        half = pl.ds(src * cap, cap)
        @pl.loop(0, width // 256, unroll=True)
        def _(i):
            t = pl.ds(pl.multiple_of(i * 256, 256), 256)
            rows_o[0, half, t] = jnp.dot(onehot, h2[:, t], preferred_element_type=f32).astype(bf16)
            cbrow[half, t] = jnp.dot(onehot, cb[pl.ds(0, tokens), t], preferred_element_type=f32).astype(bf16)
    gate = jnp.concatenate(gates, axis=0)

    @pl.loop(0, 2 * hidden // 256, unroll=True)
    def _(i):
        t = pl.ds(pl.multiple_of(i * 256, 256), 256)
        gu[:, t] = jnp.dot(rows_o[0], w_in[0, :, t], preferred_element_type=f32)

    @pl.loop(0, hidden // 128, unroll=True)
    def _(i):
        ta = pl.ds(pl.multiple_of(i * 128, 128), 128)
        tb = pl.ds(pl.multiple_of(hidden + i * 128, 128), 128)
        a = gu[:, ta]
        b = gu[:, tb]
        sig = jax.nn.sigmoid(a)
        silu = a * sig
        act_o[0, :, ta] = (silu * b).astype(bf16)
        gu[:, ta] = b * (sig * (1.0 + a * (1.0 - sig)))
        gu[:, tb] = silu

    def down(i, dot):
        t = pl.ds(pl.multiple_of(i * 256, 256), 256)
        y = jnp.dot(act_o[0], w_down[0, :, t], preferred_element_type=f32).astype(bf16).astype(f32)
        c = cbrow[:, t].astype(f32)
        gyt = (gate * y).astype(bf16)
        for src in (0, 1):
            gy[src, pl.ds(e * cap, cap), t] = gyt[src * cap:(src + 1) * cap]
        dy_o[0, :, t] = (gate * c).astype(bf16)
        return dot + jnp.sum(y * c, axis=1, keepdims=True)
    dot = lax.fori_loop(0, width // 256, down, jnp.zeros((2 * cap, 1), f32), unroll=True)
    for src in (0, 1):
        back = jnp.sum(jnp.where(masks[src], dot[src * cap:(src + 1) * cap], 0.0), axis=0, keepdims=True)
        row_id = lax.broadcasted_iota(jnp.int32, (table_rows, tokens), 0)
        dots[src] += jnp.where(row_id == mine, back, 0.0)

    for start in range(0, hidden, 256):
        n = min(256, hidden - start)
        dact = lax.dot_general(dy_o[0], w_down[0, pl.ds(start, n), :], (((1,), (1,)), ((), ())), preferred_element_type=f32)
        dgu_o[0, :, pl.ds(start, n)] = (dact * gu[:, pl.ds(start, n)]).astype(bf16)
        dgu_o[0, :, pl.ds(hidden + start, n)] = (dact * gu[:, pl.ds(hidden + start, n)]).astype(bf16)

    @pl.loop(0, width // 256, unroll=True)
    def _(i):
        t = pl.ds(pl.multiple_of(i * 256, 256), 256)
        dr = lax.dot_general(dgu_o[0], w_in[0, t, :], (((1,), (1,)), ((), ())), preferred_element_type=f32).astype(bf16)
        for src in (0, 1):
            drs[src, pl.ds(e * cap, cap), t] = dr[src * cap:(src + 1) * cap]

    @pl.when(e == pl.num_programs(0) - 1)
    def _():
        for src, dro, outo in ((0, dra, outa), (1, drb, outb)):
            @pl.loop(0, width // 256, unroll=True)
            def _(i):
                t = pl.ds(pl.multiple_of(i * 256, 256), 256)
                dims = (((0,), (0,)), ((), ()))
                outo[:, t] = lax.dot_general(oh[src], gy[src, :, t], dims, preferred_element_type=f32).astype(bf16)
                dro[pl.ds(0, tokens), t] = lax.dot_general(oh[src], drs[src, :, t], dims, preferred_element_type=f32).astype(bf16)
            hi = dots[src].astype(bf16)
            lo = (dots[src] - hi.astype(f32)).astype(bf16)
            pad = jnp.zeros((2 * table_rows, width - tokens), bf16)
            dro[pl.ds(tokens, table_rows), pl.ds(0, tokens)] = hi
            dro[pl.ds(tokens + table_rows, table_rows), pl.ds(0, tokens)] = lo
            dro[pl.ds(tokens, 2 * table_rows), pl.ds(tokens, width - tokens)] = pad

def expert_step(first, h2a, h2b, cba, cbb, wr, w_in, w_down, step, steps, cap, kept):
    tokens, width = h2a.shape
    local, _, hidden2 = w_in.shape
    hidden = hidden2 // 2
    table_rows = cba.shape[0] - tokens
    bf16, f32 = jnp.bfloat16, jnp.float32
    whole = lambda a: pl.BlockSpec(a.shape, lambda e: (0,) * a.ndim, pipeline_mode=pl.Buffered(1))
    ins = [pl.BlockSpec(memory_space=pltpu.SMEM)] + [whole(a) for a in (h2a, h2b, cba, cbb, wr)]
    ins += [pl.BlockSpec((1,) + w_in.shape[1:], lambda e: (e, 0, 0)), pl.BlockSpec((1,) + w_down.shape[1:], lambda e: (e, 0, 0))]
    kept_shapes = [jax.ShapeDtypeStruct((local, steps * 2 * cap, n), bf16) for n in (width, width, hidden, 2 * hidden)]
    sums = [jax.ShapeDtypeStruct((tokens + 2 * table_rows, width), bf16)] * 2 + [jax.ShapeDtypeStruct((tokens, width), bf16)] * 2
    args = [first, h2a, h2b, cba, cbb, wr, w_in, w_down]
    alias = {}
    if kept is not None:
        ins += [pl.BlockSpec(memory_space=pl.ANY)] * 4
        alias = {len(args) + i: 4 + i for i in range(4)}
        args += list(kept)
    outs = [pl.BlockSpec(s.shape, lambda e: (0, 0)) for s in sums]
    outs += [pl.BlockSpec((1, 2 * cap, s.shape[2]), lambda e: (e, step, 0)) for s in kept_shapes]
    rows = 2 * cap
    flops = 2 * local * rows * (2 * (3 * width * hidden) + 4 * tokens * width)
    res = pl.pallas_call(
        lambda *r: expert_kernel(cap, tokens, hidden, None, *r),
        grid=(local,),
        in_specs=ins, out_specs=outs, out_shape=sums + kept_shapes,
        scratch_shapes=[pltpu.VMEM((rows, 2 * hidden), f32), pltpu.VMEM((rows, width), bf16), pltpu.VMEM((2, local * cap, tokens), bf16),
                        pltpu.VMEM((2, local * cap, width), bf16), pltpu.VMEM((2, local * cap, width), bf16),
                        pltpu.VMEM((2, table_rows, tokens), f32), pltpu.VMEM((2, table_rows, tokens), f32)],
        input_output_aliases=alias,
        compiler_params=pltpu.CompilerParams(vmem_limit_bytes=60 * 2**20),
        cost_estimate=pl.CostEstimate(flops=0, bytes_accessed=0, transcendentals=0),
        name="expert_step",
    )(*args)
    return res[:4], res[4:]


def token_kernel(length_ref, ids, dout, rows_o):
    f32, bf16 = jnp.float32, jnp.bfloat16
    tokens = dout.shape[0]
    table_rows = rows_o.shape[0] - tokens
    live = lax.broadcasted_iota(jnp.int32, (tokens, 1), 0) < length_ref[0]
    rows_o[pl.ds(0, tokens), :] = jnp.where(live, dout[...].astype(f32), 0.0).astype(bf16)
    lane = lax.broadcasted_iota(jnp.int32, (tokens, 128), 1)
    picked = jnp.zeros((tokens, 128), f32)
    for k in range(ids.shape[1]):
        picked = jnp.where(lane == ids[:, k:k + 1], 1.0, picked)
    picked = jnp.where(live, picked, 0.0).astype(bf16)
    earlier = lax.broadcasted_iota(jnp.int32, (tokens, tokens), 0)
    later = lax.broadcasted_iota(jnp.int32, (tokens, tokens), 1)
    before = jnp.where(earlier < later, 1.0, 0.0).astype(bf16)
    same = jnp.where(earlier == later, 1.0, 0.0).astype(bf16)
    rank = lax.dot_general(picked, before, TN, preferred_element_type=f32)
    hit = lax.dot_general(picked, same, TN, preferred_element_type=f32)
    table = jnp.where(hit > 0.5, rank, -1.0)[:table_rows].astype(bf16)
    rows_o[pl.ds(tokens, table_rows), pl.ds(0, tokens)] = table
    rows_o[pl.ds(tokens, table_rows), pl.ds(tokens, dout.shape[1] - tokens)] = jnp.zeros(
        (table_rows, dout.shape[1] - tokens), bf16
    )


def token_rows(lengths, expert_ids, dout, experts):
    return pl.pallas_call(
        token_kernel,
        in_specs=[
            pl.BlockSpec(memory_space=pltpu.SMEM),
            pl.BlockSpec(memory_space=pltpu.VMEM),
            pl.BlockSpec(memory_space=pltpu.VMEM),
        ],
        out_specs=pl.BlockSpec(memory_space=pltpu.VMEM),
        out_shape=jax.ShapeDtypeStruct((dout.shape[0] + experts, dout.shape[1]), jnp.bfloat16),
        cost_estimate=pl.CostEstimate(flops=0, bytes_accessed=0, transcendentals=0),
        name="token_rows",
    )(lengths, expert_ids, dout)


def store_grad(grad, cols, rows, mine, outs):
    low = jnp.bfloat16
    if not rows:
        outs[0][:, cols] = grad.astype(low)
        return
    for c in range(grad.shape[0] // (2 * rows)):
        first = grad[2 * c * rows : (2 * c + 1) * rows]
        second = grad[(2 * c + 1) * rows : (2 * c + 2) * rows]
        outs[0][pl.ds(c * rows, rows), cols] = jnp.where(mine, first, second).astype(low)
        outs[1][pl.ds(c * rows, rows), cols] = jnp.where(mine, second, first).astype(low)


def shared_kernel(rows, experts, core_ref, h2, cb, w_in, w_down, w_router, shared_out, grad_h2, probs, *rest):
    f32, bf16 = jnp.float32, jnp.bfloat16
    *grads, gu, hs, dgu = rest
    tokens, width = h2.shape
    hidden = w_down.shape[0]
    mine = core_ref[0] == 0
    own = pl.ds(0, tokens)

    logits = jnp.dot(h2[...], w_router[...], preferred_element_type=f32)
    column = lax.broadcasted_iota(jnp.int32, logits.shape, 1)
    logits = jnp.where(column < experts - 1, logits, MASK_VALUE)
    ex = jnp.exp(logits - jnp.max(logits, axis=1, keepdims=True))
    probs[...] = ex / jnp.sum(ex, axis=1, keepdims=True)
    for start in range(0, 2 * hidden, 256):
        t = pl.ds(start, 256)
        gu[:, t] = jnp.dot(h2[...], w_in[:, t], preferred_element_type=f32)
    for start in range(0, hidden, 128):
        ta, tb = pl.ds(start, 128), pl.ds(hidden + start, 128)
        a, b = gu[:, ta], gu[:, tb]
        sig = jax.nn.sigmoid(a)
        silu = a * sig
        hs[:, ta] = (silu * b).astype(bf16)
        gu[:, ta] = b * (sig * (1.0 + a * (1.0 - sig)))
        gu[:, tb] = silu
    for start in range(0, hidden, 256):
        n = min(256, hidden - start)
        dhs = lax.dot_general(cb[own, :], w_down[pl.ds(start, n), :], NT, preferred_element_type=f32)
        for t in (pl.ds(start, n), pl.ds(hidden + start, n)):
            dgu[:, t] = (dhs * gu[:, t]).astype(bf16)
    for start in range(0, width, 256):
        t = pl.ds(start, 256)
        shared_out[:, t] = jnp.dot(hs[...], w_down[:, t], preferred_element_type=f32)
        grad_h2[:, t] = lax.dot_general(dgu[...], w_in[t, :], NT, preferred_element_type=f32)
    for start in range(0, 2 * hidden, 256):
        t = pl.ds(start, 256)
        grad = lax.dot_general(h2[...], dgu[:, t], TN, preferred_element_type=f32)
        store_grad(grad, t, rows, mine, grads)
    for start in range(0, hidden, 256):
        n = min(256, hidden - start)
        grad = lax.dot_general(cb[own, :], hs[:, pl.ds(start, n)], TN, preferred_element_type=f32)
        store_grad(grad, pl.ds(2 * hidden + start, n), rows, mine, grads)


def shared_expert(core, h2, cb, w_in, w_down, w_router, rows, experts):
    tokens, width = h2.shape
    hidden = w_down.shape[0]
    f32, bf16 = jnp.float32, jnp.bfloat16
    sd = jax.ShapeDtypeStruct
    vmem = pl.BlockSpec(memory_space=pltpu.VMEM)
    grads = [sd((width // 2, 3 * hidden), bf16)] * 2 if rows else [sd((width, 3 * hidden), bf16)]
    outs = [sd((tokens, width), f32), sd((tokens, width), f32), sd((tokens, w_router.shape[1]), f32)] + grads
    return pl.pallas_call(
        lambda *r: shared_kernel(rows, experts, *r),
        in_specs=[pl.BlockSpec(memory_space=pltpu.SMEM)] + [vmem] * 5,
        out_specs=[vmem] * len(outs),
        out_shape=outs,
        scratch_shapes=[pltpu.VMEM((tokens, 2 * hidden), f32), pltpu.VMEM((tokens, hidden), bf16), pltpu.VMEM((tokens, 2 * hidden), bf16)],
        compiler_params=pltpu.CompilerParams(vmem_limit_bytes=48 * 2**20),
        cost_estimate=pl.CostEstimate(flops=0, bytes_accessed=0, transcendentals=0),
        name="shared_expert",
    )(core, h2, cb, w_in, w_down, w_router)


def middle_kernel(experts, length_ref, home_a, home_b, home_c, grad_shared, probs, h2, w_router, x_mid, dout, gain, grad_mid, da, small):
    f32, bf16 = jnp.float32, jnp.bfloat16
    tokens = x_mid.shape[0]
    own, table = pl.ds(0, tokens), pl.ds(tokens, 2 * experts)
    total = lambda r, c: home_a[r, c].astype(f32) + home_b[r, c].astype(f32) + home_c[r, c].astype(f32)
    dots = total(table, own)
    dots = dots[:experts] + dots[experts:]
    grad_probs = jnp.concatenate([dots, jnp.zeros((128 - experts, tokens), f32)], axis=0).T
    p = probs[...]
    low = (p * (grad_probs - jnp.sum(grad_probs * p, axis=1, keepdims=True))).astype(bf16)
    incoming = total(own, slice(None)) + grad_shared[...]
    incoming += lax.dot_general(low, w_router[...], NT, preferred_element_type=f32)
    mid = x_mid[...]
    inverse = lax.rsqrt(jnp.mean(mid * mid, axis=-1, keepdims=True) + NORM_EPS)
    scaled = mid * inverse
    column = lax.broadcasted_iota(jnp.int32, (tokens, 128), 1)
    small[...] = lax.dot_general(h2[...], low, TN, preferred_element_type=f32) + lax.dot_general(
        incoming * scaled, jnp.where(column == experts, 1.0, 0.0), TN,
        precision=lax.Precision.HIGHEST, preferred_element_type=f32,
    )
    inner = incoming * gain[...]
    back = inverse * (inner - scaled * jnp.mean(inner * scaled, axis=-1, keepdims=True))
    grad = dout[...].astype(f32) + back
    grad_mid[...] = grad
    live = lax.broadcasted_iota(jnp.int32, (tokens, 1), 0) < length_ref[0]
    da[...] = jnp.where(live, grad, 0.0).astype(bf16)


def middle_back(lengths, home, grad_shared, probs, h2, w_router, x_mid, dout, gain, experts):
    tokens, width = x_mid.shape
    f32 = jnp.float32
    sd = jax.ShapeDtypeStruct
    vmem = pl.BlockSpec(memory_space=pltpu.VMEM)
    return pl.pallas_call(
        lambda *r: middle_kernel(experts, *r),
        in_specs=[pl.BlockSpec(memory_space=pltpu.SMEM)] + [vmem] * 10,
        out_specs=[vmem] * 3,
        out_shape=[sd((tokens, width), f32), sd((tokens, width), jnp.bfloat16), sd((width, 128), f32)],
        compiler_params=pltpu.CompilerParams(vmem_limit_bytes=48 * 2**20),
        cost_estimate=pl.CostEstimate(flops=0, bytes_accessed=0, transcendentals=0),
        name="middle_back",
    )(lengths, *home, grad_shared, probs, h2, w_router, x_mid, dout, gain)


def weight_grad_kernel(parts, bit, index_ref, lhs, rhs, keep, away):
    f32, bf16 = jnp.float32, jnp.bfloat16
    grad = lax.dot_general(lhs[0], rhs[0], TN, preferred_element_type=f32)
    mine = ((index_ref[0] >> bit) & 1) == 0
    rows = grad.shape[0] // parts
    at = 0
    for c in range(parts):
        if (c >> bit) & 1:
            continue
        other = c | (1 << bit)
        first = grad[c * rows : (c + 1) * rows]
        second = grad[other * rows : (other + 1) * rows]
        keep[pl.ds(at, rows), :] = jnp.where(mine, first, second).astype(bf16)
        away[pl.ds(at, rows), :] = jnp.where(mine, second, first).astype(bf16)
        at += rows


def weight_grad(index, lhs, rhs, expert, parts, bit):
    _, rows, m = lhs.shape
    n = rhs.shape[2]
    return pl.pallas_call(
        lambda *r: weight_grad_kernel(parts, bit, *r),
        grid=(n // 256,),
        in_specs=[
            pl.BlockSpec(memory_space=pltpu.SMEM),
            pl.BlockSpec((1, rows, m), lambda i: (expert, 0, 0)),
            pl.BlockSpec((1, rows, 256), lambda i: (expert, 0, i)),
        ],
        out_specs=[pl.BlockSpec((m // 2, 256), lambda i: (0, i))] * 2,
        out_shape=[jax.ShapeDtypeStruct((m // 2, n), jnp.bfloat16)] * 2,
        compiler_params=pltpu.CompilerParams(vmem_limit_bytes=48 * 2**20),
        cost_estimate=pl.CostEstimate(flops=0, bytes_accessed=0, transcendentals=0),
        name="weight_grad",
    )(index, lhs, rhs)


def rope_tables(seq_slots):
    half_dim = HEAD_DIM // 2
    inv_freq = 1.0 / 10000.0 ** (jnp.arange(half_dim, dtype=jnp.float32) * 2.0 / HEAD_DIM)
    angles = jnp.arange(seq_slots, dtype=jnp.float32)[:, None] * inv_freq[None, :]
    cosine, sine = jnp.cos(angles), jnp.sin(angles)
    return jnp.concatenate([cosine, cosine], axis=1), jnp.concatenate([-sine, sine], axis=1)


def swap_cores(values_in):
    owners = lax.axis_size("expert")
    return lax.ppermute(values_in, "expert", [(i, i ^ 1) for i in range(owners)])


def next_chip(values_in):
    owners = lax.axis_size("expert")
    return lax.ppermute(values_in, "expert", [(i, (i + 2) % owners) for i in range(owners)])


def axis_bits(name):
    return [(name, bit) for bit in range(lax.axis_size(name).bit_length() - 1)]


def row_bits():
    return axis_bits("dp")[::-1] + axis_bits("expert")[::-1]


def sum_terms(parts):
    summed = parts[0].astype(jnp.float32)
    for term in parts[1:]:
        summed = summed + term.astype(jnp.float32)
    return summed


def after(values_in, *earlier):
    return lax.optimization_barrier((values_in, earlier))[0]


class Scatter:
    def __init__(self, terms, open_bits, order):
        self.terms, self.open_bits, self.order = list(terms), list(open_bits), list(order)

    def advance(self, *earlier):
        name, bit = self.order.pop(0)
        dim = self.open_bits.index((name, bit))
        mine = (lax.axis_index(name) >> bit) & 1
        terms = after(self.terms, *earlier) if earlier else self.terms
        pick = lambda term, index: lax.dynamic_index_in_dim(term, index, dim, keepdims=False)
        away = sum_terms([pick(term, 1 - mine) for term in terms]).astype(terms[0].dtype)
        came = lax.ppermute(
            away, name, [(i, i ^ (1 << bit)) for i in range(lax.axis_size(name))]
        )
        self.terms = [pick(term, mine) for term in terms] + [came]
        self.open_bits.pop(dim)
        return away

    def finish(self):
        while self.order:
            self.advance()
        return sum_terms(self.terms)


def split_rows(part, bits):
    rows = part.shape[0] >> len(bits)
    return part.reshape((2,) * len(bits) + (rows, part.shape[1]))


def scatter_orders():
    core, *line = axis_bits("expert")
    plane = axis_bits("dp")
    return ([core] + plane + line, [core] + plane[::-1] + line, [core] + plane + line)


def per_device(
    layer_input,
    lengths,
    expert_ids,
    norm1,
    w_qkv,
    w_out,
    norm2,
    w_router,
    w_shared_in,
    w_shared_down,
    w_expert_in,
    w_expert_down,
    dout,
):
    seq_slots, width = layer_input.shape
    top_k = expert_ids.shape[1]
    experts = w_router.shape[1]
    local_experts = w_expert_in.shape[0]
    hidden_units = w_shared_down.shape[0]
    capacity = (seq_slots * top_k // (experts - 1) // 8 + 1) * 8
    live_col = (jnp.arange(seq_slots, dtype=jnp.int32) < lengths[0]).astype(jnp.float32)[:, None]
    cosine, sine = rope_tables(seq_slots)

    bits = row_bits()
    rows = width >> len(bits)
    rows = rows if rows % 8 == 0 else 0
    core = (lax.axis_index("expert") & 1).astype(jnp.int32)[None]
    orders = scatter_orders()
    chips = experts // local_experts // 2
    first_expert = (lax.axis_index("expert") * local_experts).astype(jnp.int32)[None]
    router_t = w_router.T

    def start_scatter(grads, order):
        if rows:
            terms = [split_rows(grads[0], bits[:-1]), split_rows(swap_cores(grads[1]), bits[:-1])]
            return Scatter(terms, bits[:-1], order[1:])
        return Scatter([split_rows(grads[0], bits)], bits, order)

    def run_step(step, h2_pair, grad_pair, kept, *earlier):
        sums, kept = expert_step(
            first_expert, after(h2_pair[0], *earlier), h2_pair[1], grad_pair[0], grad_pair[1],
            router_t, w_expert_in, w_expert_down, step, chips, capacity, kept,
        )
        parts.append(sums)
        return kept, sums[0]

    parts = []
    router_wide = jnp.pad(w_router, ((0, 0), (0, 128 - experts)))
    grad_table = token_rows(lengths, expert_ids, dout, experts)
    grad_here = (grad_table, swap_cores(grad_table))
    grad_next = next_chip(grad_table)
    counts_here = jnp.sum((grad_table[seq_slots:, :seq_slots] >= 0).astype(jnp.int32), axis=1)
    places = jnp.minimum(jnp.arange(width >> len(bits), dtype=jnp.int32), 30)
    digits = ((counts_here[None, :] >> places[:, None]) & 1).astype(jnp.float32)
    small_columns = -(-(2 * experts + 2) // 128) * 128
    digits = jnp.pad(
        jnp.tile(digits, (1 << len(bits), 1)),
        ((0, 0), (experts + 2, small_columns - 2 * experts - 2)),
    )
    h1_low, queries, keys_in, values_in, attended_low, log_norm, x_mid, h2_low = attention_forward(
        lengths, after(layer_input, grad_table), norm1[None, :], w_qkv, cosine, sine, w_out,
        norm2[None, :],
    )
    h2_here = (h2_low, swap_cores(h2_low))
    h2_next = next_chip(h2_low)
    grad_next = after(grad_next, h2_low)
    grad_other = swap_cores(grad_next)
    grad_ahead = next_chip(grad_next)
    kept, done = run_step(0, h2_here, grad_here, None, grad_next)
    shared_out, grad_shared, router_probs, *shared_grads = shared_expert(
        core, after(h2_low, done), grad_table, w_shared_in, w_shared_down, router_wide, rows, experts
    )
    shared_scatter = start_scatter(after(shared_grads, h2_next, grad_ahead), orders[0])
    fence = shared_out
    shared_away = []
    swapped = [swap_cores(after(parts[0][3], fence, h2_next, grad_ahead))]
    travelling = None
    for step in range(1, chips):
        h2_next, grad_next = after(h2_next, fence), after(grad_next, fence)
        pair_h2 = (h2_next, swap_cores(h2_next))
        pair_grad = (grad_next, grad_other)
        earlier = [] if travelling is None else [travelling]
        earlier += shared_away
        if step + 1 < chips:
            h2_next = next_chip(h2_next)
            grad_next = after(grad_ahead, fence)
            grad_other = swap_cores(grad_next)
            if step + 2 < chips:
                grad_ahead = next_chip(grad_next)
        kept, fence = run_step(step, pair_h2, pair_grad, kept, *earlier)
        mine, theirs = parts[step][:2]
        if step + 1 < chips:
            theirs = after(theirs, h2_next, grad_ahead)
        theirs = after(theirs, *swapped)
        swapped.append(swap_cores(after(parts[step][3], theirs)))
        if shared_away:
            theirs = after(theirs, shared_scatter.terms[-1])
        if travelling is None:
            total = mine.astype(jnp.float32) + swap_cores(theirs).astype(jnp.float32)
        else:
            came = next_chip(travelling)
            total = (
                mine.astype(jnp.float32)
                + swap_cores(after(theirs, came)).astype(jnp.float32)
                + came.astype(jnp.float32)
            )
        travelling = total.astype(mine.dtype)
        if shared_scatter.order[0][0] == "dp":
            shared_away = [shared_scatter.advance(fence)]

    home_hop = next_chip(travelling)
    rows_held, grad_result, expert_hidden, grad_expert_gu = kept

    plane = axis_bits("dp")
    plane_index = lax.axis_index("dp").astype(jnp.int32)[None]

    def expert_grads(lhs, rhs, expert):
        order = plane if expert % 2 == 0 else plane[::-1]
        return order, weight_grad(
            plane_index, lhs, rhs, expert, 1 << len(plane), order[0][1]
        )

    def plane_scatter(order, grads, *earlier):
        name, bit = order[0]
        keep, away = after(grads, *earlier)
        came = lax.ppermute(
            away, name, [(i, i ^ (1 << bit)) for i in range(lax.axis_size(name))]
        )
        open_bits = [place for place in plane[::-1] if place != order[0]]
        terms = [split_rows(piece, open_bits) for piece in (keep, came)]
        return Scatter(terms, open_bits, order[1:])

    fence = [travelling, shared_scatter.terms[-1]]
    down_parts, in_parts = [], []
    for i in range(local_experts):
        down_parts.append(
            expert_grads(after(expert_hidden, *fence), grad_result, i)
        )
        fence = down_parts[-1][1]
    down_scatters = [plane_scatter(*part, *fence) for part in down_parts]
    fence = list(fence) + [shared_scatter.advance(*fence)]
    for i in range(local_experts):
        in_parts.append(expert_grads(after(rows_held, *fence), grad_expert_gu, i))
        fence = in_parts[-1][1]
    there = [home_hop, swapped[-1], shared_scatter.terms[-1]] + [scatter.terms[-1] for scatter in down_scatters]
    in_scatters = [plane_scatter(*part, *there, *fence) for part in in_parts]
    fence = list(fence) + there + [shared_scatter.advance(*there)]

    mine, theirs = parts[0][:2]
    home = after((mine, swap_cores(theirs), home_hop), *fence)
    grad_mid, grad_attn_branch, small = middle_back(
        lengths, home, grad_shared, router_probs, h2_low, router_wide, x_mid, dout, norm2[None, :],
        experts,
    )
    small = digits + jnp.pad(small, ((0, 0), (0, small_columns - 128)))
    out_order = list(range(1, chips)) + [0]

    def add_routed(index, came, *earlier):
        mine, theirs = after((parts[out_order[index]][2], swapped[out_order[index]]), *earlier)
        total = mine.astype(jnp.float32) + theirs.astype(jnp.float32)
        return total if came is None else total + came.astype(jnp.float32)

    out_hop = next_chip(add_routed(0, None, *fence).astype(jnp.bfloat16))

    pairs = width // (2 * HEAD_DIM)
    half = (pairs - 1) // 2
    cuts = (0, pairs - 2 * half, pairs - half, pairs)
    running = None
    scatters, pending = [], []
    fence = (grad_attn_branch,)
    column_orders = (orders[0], orders[0], orders[1])
    for index, (first, last) in enumerate(zip(cuts[:-1], cuts[1:])):
        tail = None
        if last == pairs:
            tail = (experts, (layer_input, norm1[None, :], grad_mid, small))
        *grads, running = attention_backward(
            lengths, core, after(grad_attn_branch, *fence), w_out, queries, keys_in, values_in,
            log_norm, cosine, sine, h1_low, attended_low, w_qkv, running, first, last - first, rows,
            tail,
        )
        fence = [running]
        if index == 0:
            scatters.append(start_scatter(grads, column_orders[0]))
        elif index == 1:
            landed = [scatter.terms[-1] for scatter in in_scatters]
            landed += [running, out_hop, shared_scatter.terms[-1]]
            scatters.append(start_scatter(after(grads, *landed), column_orders[1]))
            fence = [scatters[0].advance(*landed)]
            routed = add_routed(1, out_hop, *fence).astype(jnp.bfloat16)
            out_hop = next_chip(routed)
            fence.append(routed)
        else:
            landed = [running, out_hop, scatters[0].terms[-1]]
            scatters.append(start_scatter(after(grads, *landed), column_orders[2]))
    grad_input = running
    first_cols, second_cols, third_cols = scatters
    fence = second_cols.advance(*landed)
    hops = 2
    rest = [third_cols, first_cols, None, second_cols, third_cols, first_cols] + in_scatters
    rest += down_scatters + [second_cols, third_cols, first_cols, second_cols, third_cols]
    for scatter in rest:
        if scatter is not None:
            if scatter.order:
                fence = scatter.advance(fence)
        elif hops < chips:
            routed = add_routed(hops, out_hop, fence)
            hops, fence = hops + 1, routed
            if hops < chips:
                out_hop = next_chip(routed.astype(jnp.bfloat16))
    while hops < chips:
        routed = add_routed(hops, out_hop, fence)
        out_hop = next_chip(routed.astype(jnp.bfloat16))
        hops += 1
    result = (x_mid + live_col * (shared_out + routed)).astype(jnp.bfloat16)
    shared_sum = shared_scatter.finish()
    expert_in_sum = jnp.stack([scatter.finish() for scatter in in_scatters])
    expert_down_sum = jnp.stack([scatter.finish() for scatter in down_scatters])
    pieces = []
    for scatter, first, last in zip(scatters, cuts[:-1], cuts[1:]):
        piece = scatter.finish().reshape(width >> len(bits), last - first, -1)
        small_sum = piece[:, -1, 8 * HEAD_DIM :]
        piece = piece[:, :, : 8 * HEAD_DIM].reshape(-1, last - first, 4, 2 * HEAD_DIM)
        pieces.append(piece.transpose(0, 2, 1, 3).reshape(piece.shape[0], 4, -1))
    pieces = jnp.concatenate(pieces, axis=2)
    counts = jnp.sum(
        small_sum[:, experts + 2 : 2 * experts + 2] * (1 << places).astype(jnp.float32)[:, None],
        axis=0,
    )
    return (
        result,
        grad_input,
        small_sum[:, experts + 1],
        pieces[:, :3].reshape(-1, 3 * width),
        pieces[:, 3],
        small_sum[:, experts],
        small_sum[:, :experts],
        shared_sum[:, : 2 * hidden_units],
        shared_sum[:, 2 * hidden_units :].T,
        expert_in_sum,
        expert_down_sum,
        counts.astype(jnp.int32),
    )


def solution(mesh):
    return jax.shard_map(
        per_device,
        mesh=mesh,
        in_specs=(
            P(("dp", "expert"), None),
            P(("dp", "expert")),
            P(("dp", "expert"), None),
            P(),
            P(),
            P(),
            P(),
            P(),
            P(),
            P(),
            P("expert", None, None),
            P("expert", None, None),
            P(("dp", "expert"), None),
        ),
        out_specs=(
            P(("dp", "expert"), None),
            P(("dp", "expert"), None),
            P(("dp", "expert")),
            P(("dp", "expert"), None),
            P(("dp", "expert"), None),
            P(("dp", "expert")),
            P(("dp", "expert"), None),
            P(("dp", "expert"), None),
            P(None, ("dp", "expert")),
            P("expert", "dp", None),
            P("expert", "dp", None),
            P(),
        ),
        check_vma=False,
    )
```

time: 1440 us -> 584 us (0.41)
  waiting for transfers between devices: 908 us -> 147 us
  matrix products: 284 us -> 0 us
  Pallas kernels: 0 us -> 276 us
  blocking collectives: 116 us -> 0 us
  starting transfers between devices: 1.29 us -> 35.1 us
    reduce_scatter x8 -> x0, waiting for transfers between devices: 651 us -> none  [the longest x3 414 us: reduce_low(): lax.psum_scatter(part.astype(jnp.bfloat16), ('dp', 'expert'), scatter_dim...]
    dot_general x31 -> x0, matrix products: 284 us -> none  [the longest x1 27.4 us: per_device(): jnp.einsum('nscd,sfd->nscf', grad_result, w_expert_down, preferred_elemen...]
    pallas_call x0 -> x15, Pallas kernels: none -> 276 us  [the longest x4 129 us: expert_step(): pl.pallas_call(lambda *r: expert_kernel(cap, tokens, hidden, None, *r), g...]
    unnamed x14 -> x0, waiting for transfers between devices: 158 us -> none
    ppermute x0 -> x56, waiting for transfers between devices: none -> 147 us  [the longest x20 76.9 us: advance(): lax.ppermute(away, name, [(i, i ^ 1 << bit) for i in range(lax.axis_size(...]
    all_gather x2 -> x0, waiting for transfers between devices: 99.3 us -> none  [the longest x1 62.4 us: per_device(): h2_all = lax.all_gather(h2_low, 'expert', axis=0)]
    unnamed x1 -> x0, blocking collectives: 41.5 us -> none
    psum x1 -> x0, blocking collectives: 38 us -> none  [per_device(): counts = lax.psum(jnp.sum(picked, axis=0), ('dp', 'expert'))]
  transfers between devices with their start and end apart: 12 -> 56, of which waited for: 11 -> 18; matrix products, arithmetic and copies ran while one was open for 21% -> 15% of each run, Pallas kernels for 0% -> 47%
where the time goes in v3:
time: 584 us; the launch traced here: 576 us
  Pallas kernels  276 us (47%)
  waiting for transfers between devices  147 us (25%)
  other arithmetic  70.1 us (12%)
  local copies, waits for them, and re-layouts  45.5 us (8%)
  starting transfers between devices  35.1 us (6%)
    pallas_call x4, Pallas kernels, expert_step(): pl.pallas_call(lambda *r: expert_kernel(cap, tokens, hidden, None, *r), g...  129 us
    ppermute x20, waiting for transfers between devices, advance(): lax.ppermute(away, name, [(i, i ^ 1 << bit) for i in range(lax.axis_size(...  76.9 us
    ppermute x12, waiting for transfers between devices, next_chip(): lax.ppermute(values_in, 'expert', [(i, (i + 2) % owners) for i in range(o...  57.7 us
    pallas_call x3, Pallas kernels, attention_backward(): pl.pallas_call(lambda *r: attention_back_kernel(rows, extra, carried, *r)...  48.5 us
    pallas_call x4, Pallas kernels, weight_grad(): pl.pallas_call(lambda *r: weight_grad_kernel(parts, bit, *r), grid=(n //...  45.2 us
    pallas_call x1, Pallas kernels, attention_forward(): pl.pallas_call(attention_kernel, grid=(pairs,), in_specs=[pl.BlockSpec(me...  24.6 us
    convert_element_type x16, other arithmetic, advance(): sum_terms([pick(term, 1 - mine) for term in terms]).astype(terms[0].dtype)  24.3 us
    unnamed x129, local copies, waits for them, and re-layouts  21.8 us
  transfers between devices with their start and end apart: 56, of which 18 were waited for; matrix products, arithmetic and copies ran while one was open for 15% of the time, Pallas kernels for 47%

profile of v3, /device:TPU:0, one launch (start us, length us, event | category | flops | bytes accessed | tf_op | source)
XLA Modules:
  0.0 576.5 jit_solution(7778548315349783164)
XLA Ops:
  1.3 1.6 copy.61.ids
  2.9 3.4 token_rows.1.r_3_.r_2_
  6.2 3.0 collective-permute-start
  10.5 24.6 %attention_forward.1 = (bf16[512,1280]{1,0:T(8,128)(2,1)S(1)}, bf16[512,1280]{1,0:T(8,128)(2,1)S(1)}, bf16[512,1280]{1,0:T(8,128)(2,1)S(1)}, bf16[512,1280]{1,0:...) custom-call(s32[1]{0:T(128)} %copy.108.length_ref.r_0_, ...), custom_call_target="tpu_custom_call" | custom-call | tf_op jit(solution)/shard_map/attention_forward/pallas_call | solution.py:80
  39.0 2.2 collective-permute-done.r_3_
  41.3 1.7 collective-permute-start.3
  46.0 32.2 %expert_step.4 = (bf16[544,1280]{1,0:T(8,128)(2,1)}, bf16[544,1280]{1,0:T(8,128)(2,1)}, bf16[512,1280]{1,0:T(8,128)(2,1)}, bf16[512,1280]{1,0:T(8,128)(2,1)}, bf...) custom-call(s32[1]{0:T(128)} %bitcast.2.r_0_, ...), custom_call_target="tpu_custom_call" | custom-call | tf_op jit(solution)/shard_map/expert_step/pallas_call | solution.py:329
  79.6 1.6 copy-done.19
  81.2 17.4 %shared_expert.1 = (f32[512,1280]{1,0:T(8,128)}, f32[512,1280]{1,0:T(8,128)}, f32[512,128]{1,0:T(8,128)S(1)}, bf16[640,2688]{1,0:T(8,128)(2,1)}, bf16[640,2688]{1,0:T(8,128)(2,1)}) custom-call(s32[1]{0:T(128)} %bitcast.1.r_0_.r_1_, bf16[512,1280]{1,0:T(8,128)(2,1)S(1)} %copy-done.9, bf16[528,1280]{1,0:T(8,128)(2,1)S(1)} %copy-done, bf16[1280,1792]{1,0:T(8,128)(2,1)} %r_3_.4, ...), custom_call_target="tpu_custom_call" | custom-call | tf_op jit(solution)/shard_map/shared_expert/pallas_call | solution.py:446
  99.3 3.0 collective-permute-done.3.r_1_
  103.7 6.9 %collective-permute-done.8.r_2_ = bf16[512,1280]{1,0:T(8,128)(2,1)} collective-permute-done((bf16[512,1280]{1,0:T(8,128)(2,1)}, bf16[512,1280]{1,0:T(8,128)(2,1)}, u32[]{:S(2)}, u32[]{:S(2)}) %collective-permute-start.8) | collective-permute-done | bytes 1310752 | tf_op jit(solution)/shard_map/ppermute | solution.py:548
  110.8 1.8 collective-permute-done.9.r_4_
  112.5 32.4 %expert_step.5 = (bf16[544,1280]{1,0:T(8,128)(2,1)}, bf16[544,1280]{1,0:T(8,128)(2,1)}, bf16[512,1280]{1,0:T(8,128)(2,1)}, bf16[512,1280]{1,0:T(8,128)(2,1)}, bf...) custom-call(s32[1]{0:T(128)} %bitcast.2.r_0_, ...), custom_call_target="tpu_custom_call", output_to_operand_aliasing={{4}: (8, {}), {5}: (9, {}), {6}: (10, {}), {7}: (11, {})} | custom-call | tf_op jit(solution)/shard_map/expert_step/pallas_call | solution.py:329
  144.9 20.2 %collective-permute-done.7.r_1_ = bf16[512,1280]{1,0:T(8,128)(2,1)} collective-permute-done((bf16[512,1280]{1,0:T(8,128)(2,1)}, bf16[512,1280]{1,0:T(8,128)(2,1)}, u32[]{:S(2)}, u32[]{:S(2)}) %collective-permute-start.7) | collective-permute-done | bytes 1310752 | tf_op jit(solution)/shard_map/ppermute | solution.py:553
  165.6 3.7 fusion.2
  170.5 2.8 add_convert_fusion.4
  174.4 2.4 collective-permute-done.15.r_4_
  176.8 32.1 %expert_step.6 = (bf16[544,1280]{1,0:T(8,128)(2,1)}, bf16[544,1280]{1,0:T(8,128)(2,1)}, bf16[512,1280]{1,0:T(8,128)(2,1)}, bf16[512,1280]{1,0:T(8,128)(2,1)}, bf...) custom-call(s32[1]{0:T(128)} %bitcast.2.r_0_, ...), custom_call_target="tpu_custom_call", output_to_operand_aliasing={{4}: (8, {}), {5}: (9, {}), {6}: (10, {}), {7}: (11, {})} | custom-call | tf_op jit(solution)/shard_map/expert_step/pallas_call | solution.py:329
  209.0 26.9 %collective-permute-done.10.r_1_ = bf16[512,1280]{1,0:T(8,128)(2,1)} collective-permute-done((bf16[512,1280]{1,0:T(8,128)(2,1)}, bf16[512,1280]{1,0:T(8,128)(2,1)}, u32[]{:S(2)}, u32[]{:S(2)}) %collective-permute-start.10) | collective-permute-done | bytes 1310752 | tf_op jit(solution)/shard_map/ppermute | solution.py:553
  236.9 1.6 copy_bitcast_fusion
  239.4 4.2 add_convert_fusion.3
  243.9 3.0 fusion.9
  247.0 1.5 collective-permute-start.23
  248.5 32.1 %expert_step.7 = (bf16[544,1280]{1,0:T(8,128)(2,1)}, bf16[544,1280]{1,0:T(8,128)(2,1)}, bf16[512,1280]{1,0:T(8,128)(2,1)}, bf16[512,1280]{1,0:T(8,128)(2,1)}, bf...) custom-call(s32[1]{0:T(128)} %bitcast.2.r_0_, ...), custom_call_target="tpu_custom_call", output_to_operand_aliasing={{4}: (8, {}), {5}: (9, {}), {6}: (10, {}), {7}: (11, {})} | custom-call | tf_op jit(solution)/shard_map/expert_step/pallas_call | solution.py:329
  284.6 3.4 add_convert_fusion.2
  288.0 8.5 %weight_grad.4 = (bf16[448,1280]{1,0:T(8,128)(2,1)S(1)}, bf16[448,1280]{1,0:T(8,128)(2,1)S(1)}) custom-call(s32[1]{0:T(128)} %bitcast.10.r_0_, bf16[2,1920,896]{2,1,0:T(8,128)(2,1)} %get-tuple-element.268.r_1_, bf16[2,1920,1280]{2,1,0:T(8,128)(2,1)} %get-tuple-element.265.r_2_), custom_call_target="tpu_custom_call" | custom-call | tf_op jit(solution)/shard_map/weight_grad/pallas_call | solution.py:522
  297.5 8.3 %weight_grad.5 = (bf16[448,1280]{1,0:T(8,128)(2,1)S(1)}, bf16[448,1280]{1,0:T(8,128)(2,1)S(1)}) custom-call(s32[1]{0:T(128)} %bitcast.10.r_0_, bf16[2,1920,896]{2,1,0:T(8,128)(2,1)} %get-tuple-element.268.r_1_, bf16[2,1920,1280]{2,1,0:T(8,128)(2,1)} %get-tuple-element.265.r_2_), custom_call_target="tpu_custom_call" | custom-call | tf_op jit(solution)/shard_map/weight_grad/pallas_call | solution.py:522
  307.3 2.2 fusion.15
  310.5 14.2 %weight_grad.6 = (bf16[640,1792]{1,0:T(8,128)(2,1)S(1)}, bf16[640,1792]{1,0:T(8,128)(2,1)S(1)}) custom-call(s32[1]{0:T(128)} %bitcast.10.r_0_, bf16[2,1920,1280]{2,1,0:T(8,128)(2,1)} %get-tuple-element.279.r_1_, bf16[2,1920,1792]{2,1,0:T(8,128)(2,1)} %get-tuple-element.276.r_2_), custom_call_target="tpu_custom_call" | custom-call | tf_op jit(solution)/shard_map/weight_grad/pallas_call | solution.py:522
  326.0 14.2 %weight_grad.7 = (bf16[640,1792]{1,0:T(8,128)(2,1)S(1)}, bf16[640,1792]{1,0:T(8,128)(2,1)S(1)}) custom-call(s32[1]{0:T(128)} %bitcast.10.r_0_, bf16[2,1920,1280]{2,1,0:T(8,128)(2,1)} %get-tuple-element.279.r_1_, bf16[2,1920,1792]{2,1,0:T(8,128)(2,1)} %get-tuple-element.276.r_2_), custom_call_target="tpu_custom_call" | custom-call | tf_op jit(solution)/shard_map/weight_grad/pallas_call | solution.py:522
  343.0 1.6 collective-permute-start.33
  346.9 8.7 %middle_back.1 = (f32[512,1280]{1,0:T(8,128)}, bf16[512,1280]{1,0:T(8,128)(2,1)S(1)}, f32[1280,128]{1,0:T(8,128)S(1)}) custom-call(s32[1]{0:T(128)} %copy.108.length_ref.r_0_, bf16[544,1280]{1,0:T(8,128)(2,1)} %get-tuple-element.291.r_1_, bf16[544,1280]{1,0:T(8,128)(2,1)} %collective-permute-done.6.r_2_, bf16[544,1280]{1,0:T(8,128)(2,1)} %collective-permute-done.26.r_3_, ...), custom_call_target="tpu_custom_call" | custom-call | tf_op jit(solution)/shard_map/middle_back/pallas_call | solution.py:491
  355.6 3.8 add_convert_fusion.8
  359.4 1.6 collective-permute-start.34
  361.0 9.7 %attention_backward.3 = (bf16[640,1024]{1,0:T(8,128)(2,1)S(1)}, bf16[640,1024]{1,0:T(8,128)(2,1)S(1)}, f32[512,1280]{1,0:T(8,128)}) custom-call(s32[2]{0:T(128)S(1)} %pad_add_fusion.2.r_0_, s32[1]{0:T(128)} %bitcast.1.r_0_.r_1_, bf16[512,1280]{1,0:T(8,128)(2,1)S(1)} %get-tuple-element.319.r_2_, bf16[1280,1280]{1,0:T(8,128)(2,1)} %r_3_.7, ...), custom_call_target="tpu_custom_call" | custom-call | tf_op jit(solution)/shard_map/attention_backward/pallas_call | solution.py:187
  370.7 4.4 collective-permute-start.35
  375.2 16.9 %attention_backward.4 = (bf16[640,2048]{1,0:T(8,128)(2,1)}, bf16[640,2048]{1,0:T(8,128)(2,1)}, f32[512,1280]{1,0:T(8,128)}) custom-call(s32[2]{0:T(128)S(1)} %get-tuple-element.396.r_0_, s32[1]{0:T(128)} %bitcast.1.r_0_.r_1_, bf16[512,1280]{1,0:T(8,128)(2,1)S(1)} %get-tuple-element.319.r_2_, bf16[1280,1280]{1,0:T(8,128)(2,1)} %r_3_.7, ...), custom_call_target="tpu_custom_call" | custom-call | tf_op jit(solution)/shard_map/attention_backward/pallas_call | solution.py:187
  392.1 9.8 %collective-permute-done.35 = bf16[40,2688]{1,0:T(8,128)(2,1)S(1)} collective-permute-done((bf16[40,2688]{1,0:T(8,128)(2,1)S(1)}, bf16[40,2688]{1,0:T(8,128)(2,1)S(1)}, u32[]{:S(2)}, u32[]{:S(2)}) %collective-permute-start.35) | collective-permute-done | bytes 215072 | tf_op jit(solution)/shard_map/ppermute | solution.py:586
  401.9 2.2 fusion.11
  404.2 2.9 add_convert_fusion.7
  412.8 21.9 %attention_backward.5 = (bf16[640,2304]{1,0:T(8,128)(2,1)}, bf16[640,2304]{1,0:T(8,128)(2,1)}, f32[512,1280]{1,0:T(8,128)}) custom-call(s32[2]{0:T(128)S(1)} %get-tuple-element.395.r_0_, s32[1]{0:T(128)} %bitcast.1.r_0_.r_1_, bf16[512,1280]{1,0:T(8,128)(2,1)S(1)} %copy-done.8, bf16[1280,1280]{1,0:T(8,128)(2,1)} %r_3_.7, ...), custom_call_target="tpu_custom_call" | custom-call | tf_op jit(solution)/shard_map/attention_backward/pallas_call | solution.py:187
  434.8 5.4 collective-permute-done.36
  444.2 2.3 fusion.4
  447.9 1.6 dynamic-slice_bitcast_fusion.2
  450.1 1.9 fusion.3
  453.8 1.4 collective-permute-start.44
  455.2 2.9 convert_add_fusion
  459.4 18.4 %collective-permute-done.41 = bf16[2,2,2,40,2048]{4,3,2,1,0:T(8,128)(2,1)S(1)} collective-permute-done((bf16[2,2,2,40,2048]{4,3,2,1,0:T(8,128)(2,1)S(1)}, bf16[2,2,2,40,2048]{4,3,2,1,0:T(8,128)(2,1)S(1)}, u32[]{:S(2)}, u32[]{:S(2)}) %collective-permute-start.41) | collective-permute-done | bytes 1310752 | tf_op jit(solution)/shard_map/ppermute | solution.py:586
  479.0 1.5 dynamic-slice_bitcast_fusion
  480.5 6.6 %collective-permute-done.40 = bf16[2,2,2,40,2304]{4,3,2,1,0:T(8,128)(2,1)S(1)} collective-permute-done((bf16[2,2,2,40,2304]{4,3,2,1,0:T(8,128)(2,1)S(1)}, bf16[2,2,2,40,2304]{4,3,2,1,0:T(8,128)(2,1)S(1)}, u32[]{:S(2)}, u32[]{:S(2)}) %collective-permute-start.40) | collective-permute-done | bytes 1474592 | tf_op jit(solution)/shard_map/ppermute | solution.py:586
  488.4 5.8 collective-permute-done.44
  494.4 2.7 fusion.5
  497.1 2.7 fusion.6
  502.3 5.2 collective-permute-done.43
  509.3 12.9 %collective-permute-done.55 = bf16[224,1280]{1,0:T(8,128)(2,1)S(1)} collective-permute-done((bf16[224,1280]{1,0:T(8,128)(2,1)S(1)}, bf16[224,1280]{1,0:T(8,128)(2,1)S(1)}, u32[]{:S(2)}, u32[]{:S(2)}) %collective-permute-start.55) | collective-permute-done | bytes 573472 | tf_op jit(solution)/shard_map/ppermute | solution.py:586
  525.0 1.5 pad_maximum_fusion.1
  529.8 2.0 collective-permute-start.45
  532.7 5.4 collective-permute-done.46
  538.2 7.4 %collective-permute-done.50 = bf16[40,1024]{1,0:T(8,128)(2,1)S(1)} collective-permute-done((bf16[40,1024]{1,0:T(8,128)(2,1)S(1)}, bf16[40,1024]{1,0:T(8,128)(2,1)S(1)}, u32[]{:S(2)}, u32[]{:S(2)}) %collective-permute-start.50) | collective-permute-done | bytes 81952 | tf_op jit(solution)/shard_map/ppermute | solution.py:586
  546.4 5.4 collective-permute-done.51
  558.2 5.4 add_convert_fusion.5
  563.6 2.1 fusion
  565.7 2.0 fusion.1
  567.7 2.4 pad_maximum_fusion
  (297 shorter events, 72.3 us)
Async XLA Ops:
  6.2 35.0 %collective-permute-start = (bf16[528,1280]{1,0:T(8,128)(2,1)}, bf16[528,1280]{1,0:T(8,128)(2,1)}, u32[]{:S(2)}, u32[]{:S(2)}) collective-permute-start(bf16[528,1280]{1,0:T(8,128)(2,1)} %token_rows.1.r_3_.r_2_), channel_id=1, source_target_pairs={{0,2},{1,3},{2,4},{3,5},{4,6},{5,7},{6,0},{7,1},{8,10},{9,11},{10,... | collective-permute-start | bytes 4055048 | tf_op jit(solution)/shard_map/ppermute | solution.py:553
  9.3 35.7 %collective-permute-start.2 = (bf16[528,1280]{1,0:T(8,128)(2,1)}, bf16[528,1280]{1,0:T(8,128)(2,1)}, u32[]{:S(2)}, u32[]{:S(2)}) collective-permute-start(bf16[528,1280]{1,0:T(8,128)(2,1)} %token_rows.1.r_3_.r_2_), channel_id=1, source_target_pairs={{0,1},{1,0},{2,3},{3,2},{4,5},{5,4},{6,7},{7,6},{8,9},{9,8},{10,11... | collective-permute-start | bytes 4055048 | tf_op jit(solution)/shard_map/ppermute | solution.py:548
  10.5 32.5 %copy-start.56 = (bf16[1280,16]{0,1:T(8,128)(2,1)S(1)}, bf16[1280,16]{0,1:T(8,128)(2,1)}, u32[]{:S(2)}) copy-start(bf16[1280,16]{0,1:T(8,128)(2,1)} %param.20) | copy-start | bytes 122884
  41.3 61.0 %collective-permute-start.4 = (bf16[528,1280]{1,0:T(8,128)(2,1)}, bf16[528,1280]{1,0:T(8,128)(2,1)}, u32[]{:S(2)}, u32[]{:S(2)}) collective-permute-start(bf16[528,1280]{1,0:T(8,128)(2,1)} %collective-permute-done.r_3_), channel_id=1, source_target_pairs={{0,2},{1,3},{2,4},{3,5},{4,6},{5,7},{6,0},{7,1},{8,10},{9,11},{10,... | collective-permute-start | bytes 4055048 | tf_op jit(solution)/shard_map/ppermute | solution.py:553
  41.3 3.7 collective-permute-start.1
  41.3 61.0 %collective-permute-start.3 = (bf16[512,1280]{1,0:T(8,128)(2,1)}, bf16[512,1280]{1,0:T(8,128)(2,1)}, u32[]{:S(2)}, u32[]{:S(2)}) collective-permute-start(bf16[512,1280]{1,0:T(8,128)(2,1)} %get-tuple-element.206.r_1_.r_6_), channel_id=1, source_target_pairs={{0,2},{1,3},{2,4},{3,5},{4,6},{5,7},{6,0},{7,1},{8,10},{9,11},{10,... | collective-permute-start | bytes 3932168 | tf_op jit(solution)/shard_map/ppermute | solution.py:553
  46.0 32.2 %copy-start = (bf16[528,1280]{1,0:T(8,128)(2,1)S(1)}, bf16[528,1280]{1,0:T(8,128)(2,1)}, u32[]{:S(2)}) copy-start(bf16[528,1280]{1,0:T(8,128)(2,1)} %token_rows.1.r_3_.r_2_) | copy-start | bytes 4055044
  102.3 63.3 %collective-permute-start.13 = (bf16[640,2688]{1,0:T(8,128)(2,1)}, bf16[640,2688]{1,0:T(8,128)(2,1)}, u32[]{:S(2)}, u32[]{:S(2)}) collective-permute-start(bf16[640,2688]{1,0:T(8,128)(2,1)} %get-tuple-element.227), channel_id=1, source_target_pairs={{0,1},{1,0},{2,3},{3,2},{4,5},{5,4},{6,7},{7,6},{8,9},{9,8},{10,11... | collective-permute-start | bytes 10321928 | tf_op jit(solution)/shard_map/ppermute | solution.py:548
  102.3 8.3 %collective-permute-start.8 = (bf16[512,1280]{1,0:T(8,128)(2,1)}, bf16[512,1280]{1,0:T(8,128)(2,1)}, u32[]{:S(2)}, u32[]{:S(2)}) collective-permute-start(bf16[512,1280]{1,0:T(8,128)(2,1)} %collective-permute-done.3.r_1_), channel_id=1, source_target_pairs={{0,1},{1,0},{2,3},{3,2},{4,5},{5,4},{6,7},{7,6},{8,9},{9,8},{10,11... | collective-permute-start | bytes 3932168 | tf_op jit(solution)/shard_map/ppermute | solution.py:548
  102.8 9.7 %collective-permute-start.9 = (bf16[528,1280]{1,0:T(8,128)(2,1)}, bf16[528,1280]{1,0:T(8,128)(2,1)}, u32[]{:S(2)}, u32[]{:S(2)}) collective-permute-start(bf16[528,1280]{1,0:T(8,128)(2,1)} %collective-permute-done.r_3_), channel_id=1, source_target_pairs={{0,1},{1,0},{2,3},{3,2},{4,5},{5,4},{6,7},{7,6},{8,9},{9,8},{10,11... | collective-permute-start | bytes 4055048 | tf_op jit(solution)/shard_map/ppermute | solution.py:548
  102.8 62.3 %collective-permute-start.11 = (bf16[528,1280]{1,0:T(8,128)(2,1)}, bf16[528,1280]{1,0:T(8,128)(2,1)}, u32[]{:S(2)}, u32[]{:S(2)}) collective-permute-start(bf16[528,1280]{1,0:T(8,128)(2,1)} %collective-permute-done.4.r_3_), channel_id=1, source_target_pairs={{0,2},{1,3},{2,4},{3,5},{4,6},{5,7},{6,0},{7,1},{8,10},{9,11},{10,... | collective-permute-start | bytes 4055048 | tf_op jit(solution)/shard_map/ppermute | solution.py:553
  102.8 62.3 %collective-permute-start.7 = (bf16[512,1280]{1,0:T(8,128)(2,1)}, bf16[512,1280]{1,0:T(8,128)(2,1)}, u32[]{:S(2)}, u32[]{:S(2)}) collective-permute-start(bf16[512,1280]{1,0:T(8,128)(2,1)} %collective-permute-done.3.r_1_), channel_id=1, source_target_pairs={{0,2},{1,3},{2,4},{3,5},{4,6},{5,7},{6,0},{7,1},{8,10},{9,11},{10,... | collective-permute-start | bytes 3932168 | tf_op jit(solution)/shard_map/ppermute | solution.py:553
  110.6 54.5 %collective-permute-start.5 = (bf16[512,1280]{1,0:T(8,128)(2,1)}, bf16[512,1280]{1,0:T(8,128)(2,1)}, u32[]{:S(2)}, u32[]{:S(2)}) collective-permute-start(bf16[512,1280]{1,0:T(8,128)(2,1)} %get-tuple-element.210), channel_id=1, source_target_pairs={{0,1},{1,0},{2,3},{3,2},{4,5},{5,4},{6,7},{7,6},{8,9},{9,8},{10,11... | collective-permute-start | bytes 3932168 | tf_op jit(solution)/shard_map/ppermute | solution.py:548
  165.1 5.4 collective-permute-start.12
  165.1 8.7 %collective-permute-start.14 = (bf16[512,1280]{1,0:T(8,128)(2,1)}, bf16[512,1280]{1,0:T(8,128)(2,1)}, u32[]{:S(2)}, u32[]{:S(2)}) collective-permute-start(bf16[512,1280]{1,0:T(8,128)(2,1)} %collective-permute-done.7.r_1_), channel_id=1, source_target_pairs={{0,1},{1,0},{2,3},{3,2},{4,5},{5,4},{6,7},{7,6},{8,9},{9,8},{10,11... | collective-permute-start | bytes 3932168 | tf_op jit(solution)/shard_map/ppermute | solution.py:548
  169.3 66.5 %collective-permute-start.17 = (bf16[2,2,2,40,2688]{4,3,1,2,0:T(8,128)(2,1)}, bf16[2,2,2,40,2688]{4,3,1,2,0:T(8,128)(2,1)}, u32[]{:S(2)}, u32[]{:S(2)}) collective-permute-start(bf16[2,2,2,40,2688]{4,3,1,2,0:T(8,128)(2,1)} %fusion.2), channel_id=1, source_target_pairs={{0,8},{8,0},{16,24},{24,16},{1,9},{9,1},{17,25},{25,17},{2,10},{10... | collective-permute-start | bytes 5160968 | tf_op jit(solution)/shard_map/ppermute | solution.py:586
  173.4 62.5 %collective-permute-start.18 = (bf16[544,1280]{1,0:T(8,128)(2,1)}, bf16[544,1280]{1,0:T(8,128)(2,1)}, u32[]{:S(2)}, u32[]{:S(2)}) collective-permute-start(bf16[544,1280]{1,0:T(8,128)(2,1)} %add_convert_fusion.4), channel_id=1, source_target_pairs={{0,2},{1,3},{2,4},{3,5},{4,6},{5,7},{6,0},{7,1},{8,10},{9,11},{10,... | collective-permute-start | bytes 4177928 | tf_op jit(solution)/shard_map/ppermute | solution.py:553
  173.4 3.4 collective-permute-start.15
  173.4 62.4 %collective-permute-start.10 = (bf16[512,1280]{1,0:T(8,128)(2,1)}, bf16[512,1280]{1,0:T(8,128)(2,1)}, u32[]{:S(2)}, u32[]{:S(2)}) collective-permute-start(bf16[512,1280]{1,0:T(8,128)(2,1)} %collective-permute-done.7.r_1_), channel_id=1, source_target_pairs={{0,2},{1,3},{2,4},{3,5},{4,6},{5,7},{6,0},{7,1},{8,10},{9,11},{10,... | collective-permute-start | bytes 3932168 | tf_op jit(solution)/shard_map/ppermute | solution.py:553
  173.9 62.0 %collective-permute-start.16 = (bf16[512,1280]{1,0:T(8,128)(2,1)}, bf16[512,1280]{1,0:T(8,128)(2,1)}, u32[]{:S(2)}, u32[]{:S(2)}) collective-permute-start(bf16[512,1280]{1,0:T(8,128)(2,1)} %get-tuple-element.241), channel_id=1, source_target_pairs={{0,1},{1,0},{2,3},{3,2},{4,5},{5,4},{6,7},{7,6},{8,9},{9,8},{10,11... | collective-permute-start | bytes 3932168 | tf_op jit(solution)/shard_map/ppermute | solution.py:548
  235.8 3.6 collective-permute-start.19
  235.9 12.6 %collective-permute-start.21 = (bf16[528,1280]{1,0:T(8,128)(2,1)}, bf16[528,1280]{1,0:T(8,128)(2,1)}, u32[]{:S(2)}, u32[]{:S(2)}) collective-permute-start(bf16[528,1280]{1,0:T(8,128)(2,1)} %collective-permute-done.11.r_3_), channel_id=1, source_target_pairs={{0,1},{1,0},{2,3},{3,2},{4,5},{5,4},{6,7},{7,6},{8,9},{9,8},{10,11... | collective-permute-start | bytes 4055048 | tf_op jit(solution)/shard_map/ppermute | solution.py:548
  236.4 12.1 %collective-permute-start.20 = (bf16[512,1280]{1,0:T(8,128)(2,1)}, bf16[512,1280]{1,0:T(8,128)(2,1)}, u32[]{:S(2)}, u32[]{:S(2)}) collective-permute-start(bf16[512,1280]{1,0:T(8,128)(2,1)} %collective-permute-done.10.r_1_), channel_id=1, source_target_pairs={{0,1},{1,0},{2,3},{3,2},{4,5},{5,4},{6,7},{7,6},{8,9},{9,8},{10,11... | collective-permute-start | bytes 3932168 | tf_op jit(solution)/shard_map/ppermute | solution.py:548
  236.5 44.2 %collective-permute-start.22 = (bf16[512,1280]{1,0:T(8,128)(2,1)}, bf16[512,1280]{1,0:T(8,128)(2,1)}, u32[]{:S(2)}, u32[]{:S(2)}) collective-permute-start(bf16[512,1280]{1,0:T(8,128)(2,1)} %get-tuple-element.258), channel_id=1, source_target_pairs={{0,1},{1,0},{2,3},{3,2},{4,5},{5,4},{6,7},{7,6},{8,9},{9,8},{10,11... | collective-permute-start | bytes 3932168 | tf_op jit(solution)/shard_map/ppermute | solution.py:548
  243.6 37.1 %collective-permute-start.24 = (bf16[544,1280]{1,0:T(8,128)(2,1)}, bf16[544,1280]{1,0:T(8,128)(2,1)}, u32[]{:S(2)}, u32[]{:S(2)}) collective-permute-start(bf16[544,1280]{1,0:T(8,128)(2,1)} %add_convert_fusion.3), channel_id=1, source_target_pairs={{0,2},{1,3},{2,4},{3,5},{4,6},{5,7},{6,0},{7,1},{8,10},{9,11},{10,... | collective-permute-start | bytes 4177928 | tf_op jit(solution)/shard_map/ppermute | solution.py:553
  247.0 33.7 %collective-permute-start.23 = (bf16[2,2,40,2688]{3,2,0,1:T(8,128)(2,1)}, bf16[2,2,40,2688]{3,2,0,1:T(8,128)(2,1)}, u32[]{:S(2)}, u32[]{:S(2)}) collective-permute-start(bf16[2,2,40,2688]{3,2,0,1:T(8,128)(2,1)} %fusion.9), channel_id=1, source_target_pairs={{0,16},{8,24},{16,0},{24,8},{1,17},{9,25},{17,1},{25,9},{2,18},{10... | collective-permute-start | bytes 2580488 | tf_op jit(solution)/shard_map/ppermute | solution.py:586
  280.7 3.9 collective-permute-start.25
  280.9 66.0 %collective-permute-start.6 = (bf16[544,1280]{1,0:T(8,128)(2,1)}, bf16[544,1280]{1,0:T(8,128)(2,1)}, u32[]{:S(2)}, u32[]{:S(2)}) collective-permute-start(bf16[544,1280]{1,0:T(8,128)(2,1)} %get-tuple-element.211), channel_id=1, source_target_pairs={{0,1},{1,0},{2,3},{3,2},{4,5},{5,4},{6,7},{7,6},{8,9},{9,8},{10,11... | collective-permute-start | bytes 4177928 | tf_op jit(solution)/shard_map/ppermute | solution.py:548
  284.1 25.3 %collective-permute-start.27 = (bf16[512,1280]{1,0:T(8,128)(2,1)S(1)}, bf16[512,1280]{1,0:T(8,128)(2,1)S(1)}, u32[]{:S(2)}, u32[]{:S(2)}) collective-permute-start(bf16[512,1280]{1,0:T(8,128)(2,1)S(1)} %copy-done.61), channel_id=1, source_target_pairs={{0,1},{1,0},{2,3},{3,2},{4,5},{5,4},{6,7},{7,6},{8,9},{9,8},{10,11... | collective-permute-start | bytes 3932168 | tf_op jit(solution)/shard_map/ppermute | solution.py:548
  288.0 53.7 %collective-permute-start.26 = (bf16[544,1280]{1,0:T(8,128)(2,1)}, bf16[544,1280]{1,0:T(8,128)(2,1)}, u32[]{:S(2)}, u32[]{:S(2)}) collective-permute-start(bf16[544,1280]{1,0:T(8,128)(2,1)} %add_convert_fusion.2), channel_id=1, source_target_pairs={{0,2},{1,3},{2,4},{3,5},{4,6},{5,7},{6,0},{7,1},{8,10},{9,11},{10,... | collective-permute-start | bytes 4177928 | tf_op jit(solution)/shard_map/ppermute | solution.py:553
  305.9 35.8 %collective-permute-start.29 = (bf16[448,1280]{1,0:T(8,128)(2,1)S(1)}, bf16[448,1280]{1,0:T(8,128)(2,1)S(1)}, u32[]{:S(2)}, u32[]{:S(2)}) collective-permute-start(bf16[448,1280]{1,0:T(8,128)(2,1)S(1)} %get-tuple-element.284), channel_id=1, source_target_pairs={{0,8},{8,0},{16,24},{24,16},{1,9},{9,1},{17,25},{25,17},{2,10},{10... | collective-permute-start | bytes 3440648 | tf_op jit(solution)/shard_map/ppermute | solution.py:736
  306.5 35.2 %collective-permute-start.30 = (bf16[448,1280]{1,0:T(8,128)(2,1)S(1)}, bf16[448,1280]{1,0:T(8,128)(2,1)}, u32[]{:S(2)}, u32[]{:S(2)}) collective-permute-start(bf16[448,1280]{1,0:T(8,128)(2,1)S(1)} %get-tuple-element.285), channel_id=1, source_target_pairs={{0,16},{8,24},{16,0},{24,8},{1,17},{9,25},{17,1},{25,9},{2,18},{10... | collective-permute-start | bytes 3440648 | tf_op jit(solution)/shard_map/ppermute | solution.py:736
  307.2 38.3 %copy-start.35 = (bf16[2,40,2688]{2,1,0:T(8,128)(2,1)}, bf16[2,40,2688]{2,1,0:T(8,128)(2,1)S(1)}, u32[]{:S(2)}) copy-start(bf16[2,40,2688]{2,1,0:T(8,128)(2,1)S(1)} %dynamic-slice_bitcast_fusion.16) | copy-start | bytes 1290244
  309.4 32.2 %collective-permute-start.28 = (bf16[2,40,2688]{2,1,0:T(8,128)(2,1)}, bf16[2,40,2688]{2,1,0:T(8,128)(2,1)}, u32[]{:S(2)}, u32[]{:S(2)}) collective-permute-start(bf16[2,40,2688]{2,1,0:T(8,128)(2,1)} %fusion.15), channel_id=1, source_target_pairs={{0,2},{1,3},{2,0},{3,1},{4,6},{5,7},{6,4},{7,5},{8,10},{9,11},{10,... | collective-permute-start | bytes 1290248 | tf_op jit(solution)/shard_map/ppermute | solution.py:586
  310.2 35.4 %copy-start.37 = (bf16[2,40,2688]{2,1,0:T(8,128)(2,1)}, bf16[2,40,2688]{2,1,0:T(8,128)(2,1)S(1)}, u32[]{:S(2)}) copy-start(bf16[2,40,2688]{2,1,0:T(8,128)(2,1)S(1)} %dynamic-slice_bitcast_fusion.15) | copy-start | bytes 1290244
  341.7 60.2 %collective-permute-start.32 = (bf16[640,1792]{1,0:T(8,128)(2,1)S(1)}, bf16[640,1792]{1,0:T(8,128)(2,1)}, u32[]{:S(2)}, u32[]{:S(2)}) collective-permute-start(bf16[640,1792]{1,0:T(8,128)(2,1)S(1)} %get-tuple-element.306), channel_id=1, source_target_pairs={{0,8},{8,0},{16,24},{24,16},{1,9},{9,1},{17,25},{25,17},{2,10},{10... | collective-permute-start | bytes 6881288 | tf_op jit(solution)/shard_map/ppermute | solution.py:736
  343.0 58.9 %collective-permute-start.33 = (bf16[640,1792]{1,0:T(8,128)(2,1)S(1)}, bf16[640,1792]{1,0:T(8,128)(2,1)}, u32[]{:S(2)}, u32[]{:S(2)}) collective-permute-start(bf16[640,1792]{1,0:T(8,128)(2,1)S(1)} %get-tuple-element.307), channel_id=1, source_target_pairs={{0,16},{8,24},{16,0},{24,8},{1,17},{9,25},{17,1},{25,9},{2,18},{10... | collective-permute-start | bytes 6881288 | tf_op jit(solution)/shard_map/ppermute | solution.py:736
  355.6 19.6 %copy-start.7 = (bf16[512,1280]{1,0:T(8,128)(2,1)}, bf16[512,1280]{1,0:T(8,128)(2,1)S(1)}, u32[]{:S(2)}) copy-start(bf16[512,1280]{1,0:T(8,128)(2,1)S(1)} %get-tuple-element.319.r_2_) | copy-start | bytes 3932164
  359.4 42.5 %collective-permute-start.34 = (bf16[512,1280]{1,0:T(8,128)(2,1)}, bf16[512,1280]{1,0:T(8,128)(2,1)S(1)}, u32[]{:S(2)}, u32[]{:S(2)}) collective-permute-start(bf16[512,1280]{1,0:T(8,128)(2,1)} %add_convert_fusion.8), channel_id=1, source_target_pairs={{0,2},{1,3},{2,4},{3,5},{4,6},{5,7},{6,0},{7,1},{8,10},{9,11},{10,... | collective-permute-start | bytes 3932168 | tf_op jit(solution)/shard_map/ppermute | solution.py:553
  370.7 31.3 %copy-start.20 = (bf16[640,1024]{1,0:T(8,128)(2,1)}, bf16[640,1024]{1,0:T(8,128)(2,1)S(1)}, u32[]{:S(2)}) copy-start(bf16[640,1024]{1,0:T(8,128)(2,1)S(1)} %get-tuple-element.304) | copy-start | bytes 3932164
  370.7 31.2 %collective-permute-start.31 = (bf16[640,1024]{1,0:T(8,128)(2,1)S(1)}, bf16[640,1024]{1,0:T(8,128)(2,1)}, u32[]{:S(2)}, u32[]{:S(2)}) collective-permute-start(bf16[640,1024]{1,0:T(8,128)(2,1)S(1)} %get-tuple-element.305), channel_id=1, source_target_pairs={{0,1},{1,0},{2,3},{3,2},{4,5},{5,4},{6,7},{7,6},{8,9},{9,8},{10,11... | collective-permute-start | bytes 3932168 | tf_op jit(solution)/shard_map/ppermute | solution.py:548
  370.7 31.2 %collective-permute-start.35 = (bf16[40,2688]{1,0:T(8,128)(2,1)S(1)}, bf16[40,2688]{1,0:T(8,128)(2,1)S(1)}, u32[]{:S(2)}, u32[]{:S(2)}) collective-permute-start(bf16[40,2688]{1,0:T(8,128)(2,1)S(1)} %fusion.21), channel_id=1, source_target_pairs={{0,4},{1,5},{2,6},{3,7},{4,0},{5,1},{6,2},{7,3},{8,12},{9,13},{10,... | collective-permute-start | bytes 645128 | tf_op jit(solution)/shard_map/ppermute | solution.py:586
  407.1 33.0 %collective-permute-start.36 = (bf16[512,1280]{1,0:T(8,128)(2,1)}, bf16[512,1280]{1,0:T(8,128)(2,1)}, u32[]{:S(2)}, u32[]{:S(2)}) collective-permute-start(bf16[512,1280]{1,0:T(8,128)(2,1)} %add_convert_fusion.7), channel_id=1, source_target_pairs={{0,2},{1,3},{2,4},{3,5},{4,6},{5,7},{6,0},{7,1},{8,10},{9,11},{10,... | collective-permute-start | bytes 3932168 | tf_op jit(solution)/shard_map/ppermute | solution.py:553
  407.4 27.4 %collective-permute-start.37 = (bf16[2,2,2,40,1024]{4,3,1,2,0:T(8,128)(2,1)}, bf16[2,2,2,40,1024]{4,3,1,2,0:T(8,128)(2,1)}, u32[]{:S(2)}, u32[]{:S(2)}) collective-permute-start(bf16[2,2,2,40,1024]{4,3,1,2,0:T(8,128)(2,1)} %fusion.11), channel_id=1, source_target_pairs={{0,8},{8,0},{16,24},{24,16},{1,9},{9,1},{17,25},{25,17},{2,10},{10... | collective-permute-start | bytes 1966088 | tf_op jit(solution)/shard_map/ppermute | solution.py:586
  408.8 35.4 %collective-permute-start.39 = (bf16[640,2048]{1,0:T(8,128)(2,1)}, bf16[640,2048]{1,0:T(8,128)(2,1)}, u32[]{:S(2)}, u32[]{:S(2)}) collective-permute-start(bf16[640,2048]{1,0:T(8,128)(2,1)} %get-tuple-element.330), channel_id=1, source_target_pairs={{0,1},{1,0},{2,3},{3,2},{4,5},{5,4},{6,7},{7,6},{8,9},{9,8},{10,11... | collective-permute-start | bytes 7864328 | tf_op jit(solution)/shard_map/ppermute | solution.py:548
  412.8 27.3 %copy-start.36 = (bf16[2,40,2688]{2,1,0:T(8,128)(2,1)S(1)}, bf16[2,40,2688]{2,1,0:T(8,128)(2,1)}, u32[]{:S(2)}) copy-start(bf16[2,40,2688]{2,1,0:T(8,128)(2,1)} %copy-done.35) | copy-start | bytes 1290244
  412.8 27.3 %copy-start.58 = (bf16[40,2688]{1,0:T(8,128)(2,1)S(1)}, bf16[40,2688]{1,0:T(8,128)(2,1)}, u32[]{:S(2)}) copy-start(bf16[40,2688]{1,0:T(8,128)(2,1)} %copy-done.57) | copy-start | bytes 645124
  440.1 9.4 %collective-permute-start.38 = (bf16[640,2304]{1,0:T(8,128)(2,1)}, bf16[640,2304]{1,0:T(8,128)(2,1)}, u32[]{:S(2)}, u32[]{:S(2)}) collective-permute-start(bf16[640,2304]{1,0:T(8,128)(2,1)} %get-tuple-element.326), channel_id=1, source_target_pairs={{0,1},{1,0},{2,3},{3,2},{4,5},{5,4},{6,7},{7,6},{8,9},{9,8},{10,11... | collective-permute-start | bytes 8847368 | tf_op jit(solution)/shard_map/ppermute | solution.py:548
  446.6 31.2 %collective-permute-start.41 = (bf16[2,2,2,40,2048]{4,3,2,1,0:T(8,128)(2,1)S(1)}, bf16[2,2,2,40,2048]{4,3,2,1,0:T(8,128)(2,1)S(1)}, u32[]{:S(2)}, u32[]{:S(2)}) collective-permute-start(bf16[2,2,2,40,2048]{4,3,2,1,0:T(8,128)(2,1)S(1)} %fusion.4), channel_id=1, source_target_pairs={{0,8},{8,0},{16,24},{24,16},{1,9},{9,1},{17,25},{25,17},{2,10},{10... | collective-permute-start | bytes 3932168 | tf_op jit(solution)/shard_map/ppermute | solution.py:586
  451.9 35.2 %collective-permute-start.40 = (bf16[2,2,2,40,2304]{4,3,2,1,0:T(8,128)(2,1)S(1)}, bf16[2,2,2,40,2304]{4,3,2,1,0:T(8,128)(2,1)S(1)}, u32[]{:S(2)}, u32[]{:S(2)}) collective-permute-start(bf16[2,2,2,40,2304]{4,3,2,1,0:T(8,128)(2,1)S(1)} %fusion.3), channel_id=1, source_target_pairs={{0,16},{8,24},{16,0},{24,8},{1,17},{9,25},{17,1},{25,9},{2,18},{10... | collective-permute-start | bytes 4423688 | tf_op jit(solution)/shard_map/ppermute | solution.py:586
  453.8 40.4 %collective-permute-start.44 = (bf16[2,2,40,1024]{3,2,0,1:T(8,128)(2,1)S(1)}, bf16[2,2,40,1024]{3,2,0,1:T(8,128)(2,1)S(1)}, u32[]{:S(2)}, u32[]{:S(2)}) collective-permute-start(bf16[2,2,40,1024]{3,2,0,1:T(8,128)(2,1)S(1)} %fusion.17), channel_id=1, source_target_pairs={{0,16},{8,24},{16,0},{24,8},{1,17},{9,25},{17,1},{25,9},{2,18},{10... | collective-permute-start | bytes 983048 | tf_op jit(solution)/shard_map/ppermute | solution.py:586
  458.2 100.0 %collective-permute-start.48 = (bf16[512,1280]{1,0:T(8,128)(2,1)}, bf16[512,1280]{1,0:T(8,128)(2,1)}, u32[]{:S(2)}, u32[]{:S(2)}) collective-permute-start(bf16[512,1280]{1,0:T(8,128)(2,1)} %convert_add_fusion), channel_id=1, source_target_pairs={{0,2},{1,3},{2,4},{3,5},{4,6},{5,7},{6,0},{7,1},{8,10},{9,11},{10,... | collective-permute-start | bytes 3932168 | tf_op jit(solution)/shard_map/ppermute | solution.py:553
  478.2 29.3 %collective-permute-start.43 = (bf16[2,2,40,2048]{3,2,1,0:T(8,128)(2,1)S(1)}, bf16[2,2,40,2048]{3,2,1,0:T(8,128)(2,1)S(1)}, u32[]{:S(2)}, u32[]{:S(2)}) collective-permute-start(bf16[2,2,40,2048]{3,2,1,0:T(8,128)(2,1)S(1)} %fusion.12), channel_id=1, source_target_pairs={{0,16},{8,24},{16,0},{24,8},{1,17},{9,25},{17,1},{25,9},{2,18},{10... | collective-permute-start | bytes 1966088 | tf_op jit(solution)/shard_map/ppermute | solution.py:586
  487.4 39.1 %collective-permute-start.42 = (bf16[2,2,40,2304]{3,2,1,0:T(8,128)(2,1)S(1)}, bf16[2,2,40,2304]{3,2,1,0:T(8,128)(2,1)S(1)}, u32[]{:S(2)}, u32[]{:S(2)}) collective-permute-start(bf16[2,2,40,2304]{3,2,1,0:T(8,128)(2,1)S(1)} %fusion.10), channel_id=1, source_target_pairs={{0,8},{8,0},{16,24},{24,16},{1,9},{9,1},{17,25},{25,17},{2,10},{10... | collective-permute-start | bytes 2211848 | tf_op jit(solution)/shard_map/ppermute | solution.py:586
  494.3 35.5 %collective-permute-start.47 = (bf16[2,40,1024]{2,1,0:T(8,128)(2,1)S(1)}, bf16[2,40,1024]{2,1,0:T(8,128)(2,1)S(1)}, u32[]{:S(2)}, u32[]{:S(2)}) collective-permute-start(bf16[2,40,1024]{2,1,0:T(8,128)(2,1)S(1)} %fusion.23), channel_id=1, source_target_pairs={{0,2},{1,3},{2,0},{3,1},{4,6},{5,7},{6,4},{7,5},{8,10},{9,11},{10,... | collective-permute-start | bytes 491528 | tf_op jit(solution)/shard_map/ppermute | solution.py:586
  507.8 14.3 %collective-permute-start.55 = (bf16[224,1280]{1,0:T(8,128)(2,1)S(1)}, bf16[224,1280]{1,0:T(8,128)(2,1)S(1)}, u32[]{:S(2)}, u32[]{:S(2)}) collective-permute-start(bf16[224,1280]{1,0:T(8,128)(2,1)S(1)} %fusion.14), channel_id=1, source_target_pairs={{0,8},{8,0},{16,24},{24,16},{1,9},{9,1},{17,25},{25,17},{2,10},{10... | collective-permute-start | bytes 1720328 | tf_op jit(solution)/shard_map/ppermute | solution.py:586
  508.7 15.5 %collective-permute-start.54 = (bf16[224,1280]{1,0:T(8,128)(2,1)S(1)}, bf16[224,1280]{1,0:T(8,128)(2,1)S(1)}, u32[]{:S(2)}, u32[]{:S(2)}) collective-permute-start(bf16[224,1280]{1,0:T(8,128)(2,1)S(1)} %fusion.13), channel_id=1, source_target_pairs={{0,16},{8,24},{16,0},{24,8},{1,17},{9,25},{17,1},{25,9},{2,18},{10... | collective-permute-start | bytes 1720328 | tf_op jit(solution)/shard_map/ppermute | solution.py:586
  522.2 41.4 %collective-permute-start.53 = (bf16[320,1792]{1,0:T(8,128)(2,1)}, bf16[320,1792]{1,0:T(8,128)(2,1)}, u32[]{:S(2)}, u32[]{:S(2)}) collective-permute-start(bf16[320,1792]{1,0:T(8,128)(2,1)} %fusion.6), channel_id=1, source_target_pairs={{0,8},{8,0},{16,24},{24,16},{1,9},{9,1},{17,25},{25,17},{2,10},{10... | collective-permute-start | bytes 3440648 | tf_op jit(solution)/shard_map/ppermute | solution.py:586
  524.3 41.4 %collective-permute-start.52 = (bf16[320,1792]{1,0:T(8,128)(2,1)}, bf16[320,1792]{1,0:T(8,128)(2,1)}, u32[]{:S(2)}, u32[]{:S(2)}) collective-permute-start(bf16[320,1792]{1,0:T(8,128)(2,1)} %fusion.5), channel_id=1, source_target_pairs={{0,16},{8,24},{16,0},{24,8},{1,17},{9,25},{17,1},{25,9},{2,18},{10... | collective-permute-start | bytes 3440648 | tf_op jit(solution)/shard_map/ppermute | solution.py:586
  526.5 11.5 %collective-permute-start.46 = (bf16[2,40,2048]{2,1,0:T(8,128)(2,1)S(1)}, bf16[2,40,2048]{2,1,0:T(8,128)(2,1)S(1)}, u32[]{:S(2)}, u32[]{:S(2)}) collective-permute-start(bf16[2,40,2048]{2,1,0:T(8,128)(2,1)S(1)} %fusion.18), channel_id=1, source_target_pairs={{0,2},{1,3},{2,0},{3,1},{4,6},{5,7},{6,4},{7,5},{8,10},{9,11},{10,... | collective-permute-start | bytes 983048 | tf_op jit(solution)/shard_map/ppermute | solution.py:586
  529.8 27.0 %collective-permute-start.45 = (bf16[2,40,2304]{2,1,0:T(8,128)(2,1)}, bf16[2,40,2304]{2,1,0:T(8,128)(2,1)}, u32[]{:S(2)}, u32[]{:S(2)}) collective-permute-start(bf16[2,40,2304]{2,1,0:T(8,128)(2,1)} %fusion.16), channel_id=1, source_target_pairs={{0,2},{1,3},{2,0},{3,1},{4,6},{5,7},{6,4},{7,5},{8,10},{9,11},{10,... | collective-permute-start | bytes 1105928 | tf_op jit(solution)/shard_map/ppermute | solution.py:586
  538.0 7.5 %collective-permute-start.50 = (bf16[40,1024]{1,0:T(8,128)(2,1)S(1)}, bf16[40,1024]{1,0:T(8,128)(2,1)S(1)}, u32[]{:S(2)}, u32[]{:S(2)}) collective-permute-start(bf16[40,1024]{1,0:T(8,128)(2,1)S(1)} %fusion.26), channel_id=1, source_target_pairs={{0,4},{1,5},{2,6},{3,7},{4,0},{5,1},{6,2},{7,3},{8,12},{9,13},{10,... | collective-permute-start | bytes 245768 | tf_op jit(solution)/shard_map/ppermute | solution.py:586
  545.6 6.2 %collective-permute-start.51 = (bf16[40,2048]{1,0:T(8,128)(2,1)S(1)}, bf16[40,2048]{1,0:T(8,128)(2,1)S(1)}, u32[]{:S(2)}, u32[]{:S(2)}) collective-permute-start(bf16[40,2048]{1,0:T(8,128)(2,1)S(1)} %fusion.24), channel_id=1, source_target_pairs={{0,4},{1,5},{2,6},{3,7},{4,0},{5,1},{6,2},{7,3},{8,12},{9,13},{10,... | collective-permute-start | bytes 491528 | tf_op jit(solution)/shard_map/ppermute | solution.py:586
  558.1 12.1 %collective-permute-start.49 = (bf16[40,2304]{1,0:T(8,128)(2,1)S(1)}, bf16[40,2304]{1,0:T(8,128)(2,1)S(1)}, u32[]{:S(2)}, u32[]{:S(2)}) collective-permute-start(bf16[40,2304]{1,0:T(8,128)(2,1)S(1)} %fusion.22), channel_id=1, source_target_pairs={{0,4},{1,5},{2,6},{3,7},{4,0},{5,1},{6,2},{7,3},{8,12},{9,13},{10,... | collective-permute-start | bytes 552968 | tf_op jit(solution)/shard_map/ppermute | solution.py:586
  (54 other events, 208.5 us)

commit v4 on v3

--- a/solution.py
+++ b/solution.py
@@ -81,7 +81,7 @@
         attention_kernel, grid=(pairs,),
         in_specs=[pl.BlockSpec(memory_space=pltpu.SMEM), whole(x), whole(norm1), col(0), col(1), col(2), whole(cosine), whole(sine), whole(w_out), whole(norm2)],
         out_specs=[full, head, head, head, full, pl.BlockSpec((tokens, 128), lambda p: (0, 0)), full, full],
-        out_shape=[sd((tokens, width), bf16)] * 5 + [sd((tokens, 128), f32), sd((tokens, width), f32), sd((tokens, width), bf16)],
+        out_shape=[pltpu.HBM((tokens, width), bf16)] * 5 + [pltpu.HBM((tokens, 128), f32), pltpu.HBM((tokens, width), f32), pltpu.HBM((tokens, width), bf16)],
         compiler_params=pltpu.CompilerParams(vmem_limit_bytes=48 * 2**20),
         cost_estimate=pl.CostEstimate(flops=0, bytes_accessed=0, transcendentals=0),
         name="attention_forward",
@@ -322,19 +322,19 @@
         ins += [pl.BlockSpec(memory_space=pl.ANY)] * 4
         alias = {len(args) + i: 4 + i for i in range(4)}
         args += list(kept)
-    outs = [pl.BlockSpec(s.shape, lambda e: (0, 0)) for s in sums]
+    outs = [pl.BlockSpec(s.shape, lambda e: (0, 0), pipeline_mode=pl.Buffered(1)) for s in sums]
     outs += [pl.BlockSpec((1, 2 * cap, s.shape[2]), lambda e: (e, step, 0)) for s in kept_shapes]
     rows = 2 * cap
     flops = 2 * local * rows * (2 * (3 * width * hidden) + 4 * tokens * width)
     res = pl.pallas_call(
         lambda *r: expert_kernel(cap, tokens, hidden, None, *r),
         grid=(local,),
-        in_specs=ins, out_specs=outs, out_shape=sums + kept_shapes,
+        in_specs=ins, out_specs=outs, out_shape=[pltpu.HBM(x.shape, x.dtype) for x in sums + kept_shapes],
         scratch_shapes=[pltpu.VMEM((rows, 2 * hidden), f32), pltpu.VMEM((rows, width), bf16), pltpu.VMEM((2, local * cap, tokens), bf16),
                         pltpu.VMEM((2, local * cap, width), bf16), pltpu.VMEM((2, local * cap, width), bf16),
                         pltpu.VMEM((2, table_rows, tokens), f32), pltpu.VMEM((2, table_rows, tokens), f32)],
         input_output_aliases=alias,
-        compiler_params=pltpu.CompilerParams(vmem_limit_bytes=60 * 2**20),
+        compiler_params=pltpu.CompilerParams(vmem_limit_bytes=50 * 2**20),
         cost_estimate=pl.CostEstimate(flops=0, bytes_accessed=0, transcendentals=0),
         name="expert_step",
     )(*args)
@@ -519,15 +519,16 @@
 def weight_grad(index, lhs, rhs, expert, parts, bit):
     _, rows, m = lhs.shape
     n = rhs.shape[2]
+    tile = 256
     return pl.pallas_call(
         lambda *r: weight_grad_kernel(parts, bit, *r),
-        grid=(n // 256,),
+        grid=(n // tile,),
         in_specs=[
             pl.BlockSpec(memory_space=pltpu.SMEM),
             pl.BlockSpec((1, rows, m), lambda i: (expert, 0, 0)),
-            pl.BlockSpec((1, rows, 256), lambda i: (expert, 0, i)),
+            pl.BlockSpec((1, rows, tile), lambda i: (expert, 0, i)),
         ],
-        out_specs=[pl.BlockSpec((m // 2, 256), lambda i: (0, i))] * 2,
+        out_specs=[pl.BlockSpec((m // 2, tile), lambda i: (0, i))] * 2,
         out_shape=[jax.ShapeDtypeStruct((m // 2, n), jnp.bfloat16)] * 2,
         compiler_params=pltpu.CompilerParams(vmem_limit_bytes=48 * 2**20),
         cost_estimate=pl.CostEstimate(flops=0, bytes_accessed=0, transcendentals=0),
@@ -572,28 +573,37 @@
     return lax.optimization_barrier((values_in, earlier))[0]
 
 
+def picked(term, choices):
+    for dim, index in choices:
+        term = lax.dynamic_index_in_dim(term, index, dim, keepdims=False)
+    return term
+
+
 class Scatter:
     def __init__(self, terms, open_bits, order):
-        self.terms, self.open_bits, self.order = list(terms), list(open_bits), list(order)
+        self.terms, self.choices = list(terms), [[] for _ in terms]
+        self.open_bits, self.order = list(open_bits), list(order)
 
     def advance(self, *earlier):
         name, bit = self.order.pop(0)
         dim = self.open_bits.index((name, bit))
         mine = (lax.axis_index(name) >> bit) & 1
         terms = after(self.terms, *earlier) if earlier else self.terms
-        pick = lambda term, index: lax.dynamic_index_in_dim(term, index, dim, keepdims=False)
-        away = sum_terms([pick(term, 1 - mine) for term in terms]).astype(terms[0].dtype)
+        away = sum_terms(
+            [picked(term, made + [(dim, 1 - mine)]) for term, made in zip(terms, self.choices)]
+        ).astype(terms[0].dtype)
         came = lax.ppermute(
             away, name, [(i, i ^ (1 << bit)) for i in range(lax.axis_size(name))]
         )
-        self.terms = [pick(term, mine) for term in terms] + [came]
+        self.choices = [made + [(dim, mine)] for made in self.choices] + [[]]
+        self.terms.append(came)
         self.open_bits.pop(dim)
         return away
 
     def finish(self):
         while self.order:
             self.advance()
-        return sum_terms(self.terms)
+        return sum_terms([picked(term, made) for term, made in zip(self.terms, self.choices)])
 
 
 def split_rows(part, bits):
@@ -680,15 +690,19 @@
     shared_out, grad_shared, router_probs, *shared_grads = shared_expert(
         core, after(h2_low, done), grad_table, w_shared_in, w_shared_down, router_wide, rows, experts
     )
-    shared_scatter = start_scatter(after(shared_grads, h2_next, grad_ahead), orders[0])
     fence = shared_out
     shared_away = []
-    swapped = [swap_cores(after(parts[0][3], fence, h2_next, grad_ahead))]
+    swapped = []
+    shared_scatter = None
     travelling = None
     for step in range(1, chips):
         h2_next, grad_next = after(h2_next, fence), after(grad_next, fence)
         pair_h2 = (h2_next, swap_cores(h2_next))
         pair_grad = (grad_next, grad_other)
+        if shared_scatter is None:
+            ready = (fence, grad_ahead, pair_h2[1], grad_other)
+            shared_scatter = start_scatter(after(shared_grads, *ready), orders[0])
+            swapped.append(swap_cores(after(parts[0][3], *ready)))
         earlier = [] if travelling is None else [travelling]
         earlier += shared_away
         if step + 1 < chips:
@@ -702,9 +716,16 @@
         if step + 1 < chips:
             theirs = after(theirs, h2_next, grad_ahead)
         theirs = after(theirs, *swapped)
+        if step == 2:
+            first_routed = parts[1][2].astype(jnp.float32) + swapped[1].astype(jnp.float32)
+            first_routed = first_routed.astype(jnp.bfloat16)
+            theirs = after(theirs, first_routed)
         swapped.append(swap_cores(after(parts[step][3], theirs)))
         if shared_away:
             theirs = after(theirs, shared_scatter.terms[-1])
+        if shared_scatter.order[0][0] == "dp":
+            shared_away = [shared_scatter.advance(fence)]
+            theirs = after(theirs, *shared_away)
         if travelling is None:
             total = mine.astype(jnp.float32) + swap_cores(theirs).astype(jnp.float32)
         else:
@@ -715,8 +736,6 @@
                 + came.astype(jnp.float32)
             )
         travelling = total.astype(mine.dtype)
-        if shared_scatter.order[0][0] == "dp":
-            shared_away = [shared_scatter.advance(fence)]
 
     home_hop = next_chip(travelling)
     rows_held, grad_result, expert_hidden, grad_expert_gu = kept
@@ -732,7 +751,7 @@
 
     def plane_scatter(order, grads, *earlier):
         name, bit = order[0]
-        keep, away = after(grads, *earlier)
+        keep, away = after(grads, *earlier) if earlier else grads
         came = lax.ppermute(
             away, name, [(i, i ^ (1 << bit)) for i in range(lax.axis_size(name))]
         )
@@ -743,26 +762,15 @@
     fence = [travelling, shared_scatter.terms[-1]]
     down_parts, in_parts = [], []
     for i in range(local_experts):
-        down_parts.append(
-            expert_grads(after(expert_hidden, *fence), grad_result, i)
-        )
+        down_parts.append(expert_grads(after(expert_hidden, *fence), grad_result, i))
         fence = down_parts[-1][1]
-    down_scatters = [plane_scatter(*part, *fence) for part in down_parts]
-    fence = list(fence) + [shared_scatter.advance(*fence)]
+    down_scatters = [plane_scatter(*part) for part in down_parts]
     for i in range(local_experts):
         in_parts.append(expert_grads(after(rows_held, *fence), grad_expert_gu, i))
         fence = in_parts[-1][1]
-    there = [home_hop, swapped[-1], shared_scatter.terms[-1]] + [scatter.terms[-1] for scatter in down_scatters]
-    in_scatters = [plane_scatter(*part, *there, *fence) for part in in_parts]
-    fence = list(fence) + there + [shared_scatter.advance(*there)]
 
     mine, theirs = parts[0][:2]
-    home = after((mine, swap_cores(theirs), home_hop), *fence)
-    grad_mid, grad_attn_branch, small = middle_back(
-        lengths, home, grad_shared, router_probs, h2_low, router_wide, x_mid, dout, norm2[None, :],
-        experts,
-    )
-    small = digits + jnp.pad(small, ((0, 0), (0, small_columns - 128)))
+    own_home = (mine, swap_cores(after(theirs, travelling)))
     out_order = list(range(1, chips)) + [0]
 
     def add_routed(index, came, *earlier):
@@ -770,15 +778,27 @@
         total = mine.astype(jnp.float32) + theirs.astype(jnp.float32)
         return total if came is None else total + came.astype(jnp.float32)
 
-    out_hop = next_chip(add_routed(0, None, *fence).astype(jnp.bfloat16))
+    routed = first_routed if chips > 2 else add_routed(0, None, travelling).astype(jnp.bfloat16)
+    landed = list(fence) + [home_hop, own_home[1], swapped[-1], routed]
+    landed += [scatter.terms[-1] for scatter in down_scatters]
+    in_scatters = [plane_scatter(*part, *landed) for part in in_parts]
+    out_hop = next_chip(after(routed, *landed))
+    fence = landed
+    for scatter in down_scatters:
+        fence = [scatter.advance(*fence)]
+    home = after((*own_home, home_hop), *fence)
+    grad_mid, grad_attn_branch, small = middle_back(
+        lengths, home, grad_shared, router_probs, h2_low, router_wide, x_mid, dout, norm2[None, :],
+        experts,
+    )
+    small = digits + jnp.pad(small, ((0, 0), (0, small_columns - 128)))
 
     pairs = width // (2 * HEAD_DIM)
     half = (pairs - 1) // 2
-    cuts = (0, pairs - 2 * half, pairs - half, pairs)
+    cuts = (0, half, 2 * half, pairs)
     running = None
-    scatters, pending = [], []
-    fence = (grad_attn_branch,)
-    column_orders = (orders[0], orders[0], orders[1])
+    columns = []
+    fence = [grad_attn_branch]
     for index, (first, last) in enumerate(zip(cuts[:-1], cuts[1:])):
         tail = None
         if last == pairs:
@@ -789,49 +809,56 @@
             tail,
         )
         fence = [running]
+        columns.append(grads)
         if index == 0:
-            scatters.append(start_scatter(grads, column_orders[0]))
-        elif index == 1:
-            landed = [scatter.terms[-1] for scatter in in_scatters]
-            landed += [running, out_hop, shared_scatter.terms[-1]]
-            scatters.append(start_scatter(after(grads, *landed), column_orders[1]))
-            fence = [scatters[0].advance(*landed)]
-            routed = add_routed(1, out_hop, *fence).astype(jnp.bfloat16)
+            routed = add_routed(1, out_hop, running).astype(jnp.bfloat16)
             out_hop = next_chip(routed)
             fence.append(routed)
-        else:
-            landed = [running, out_hop, scatters[0].terms[-1]]
-            scatters.append(start_scatter(after(grads, *landed), column_orders[2]))
     grad_input = running
+    landed = [running, out_hop]
+    landed += [scatter.terms[-1] for scatter in in_scatters + down_scatters]
+    scatters = []
+    for grads, order in zip(columns, orders):
+        scatters.append(start_scatter(after(grads, *landed), order))
+    fence = landed
+    hops = 2
     first_cols, second_cols, third_cols = scatters
-    fence = second_cols.advance(*landed)
-    hops = 2
-    rest = [third_cols, first_cols, None, second_cols, third_cols, first_cols] + in_scatters
-    rest += down_scatters + [second_cols, third_cols, first_cols, second_cols, third_cols]
-    for scatter in rest:
+    plan = [first_cols, second_cols, None, third_cols, shared_scatter]
+    plan += [first_cols, second_cols, third_cols, shared_scatter, None]
+    plan += [first_cols, second_cols, third_cols] + in_scatters
+    plan += [first_cols, second_cols, third_cols]
+    for scatter in plan:
         if scatter is not None:
             if scatter.order:
-                fence = scatter.advance(fence)
+                fence = [scatter.advance(*fence)]
         elif hops < chips:
-            routed = add_routed(hops, out_hop, fence)
-            hops, fence = hops + 1, routed
+            routed = add_routed(hops, out_hop, *fence)
+            hops += 1
             if hops < chips:
                 out_hop = next_chip(routed.astype(jnp.bfloat16))
-    while hops < chips:
-        routed = add_routed(hops, out_hop, fence)
+            fence = [routed]
+    for hops in range(hops, chips):
+        routed = add_routed(hops, out_hop, *fence)
         out_hop = next_chip(routed.astype(jnp.bfloat16))
-        hops += 1
+    for scatter in down_scatters + in_scatters:
+        scatter.terms = after(scatter.terms, *fence)
     result = (x_mid + live_col * (shared_out + routed)).astype(jnp.bfloat16)
     shared_sum = shared_scatter.finish()
     expert_in_sum = jnp.stack([scatter.finish() for scatter in in_scatters])
     expert_down_sum = jnp.stack([scatter.finish() for scatter in down_scatters])
-    pieces = []
+    wide = 2 * HEAD_DIM
+    blocks = []
     for scatter, first, last in zip(scatters, cuts[:-1], cuts[1:]):
-        piece = scatter.finish().reshape(width >> len(bits), last - first, -1)
-        small_sum = piece[:, -1, 8 * HEAD_DIM :]
-        piece = piece[:, :, : 8 * HEAD_DIM].reshape(-1, last - first, 4, 2 * HEAD_DIM)
-        pieces.append(piece.transpose(0, 2, 1, 3).reshape(piece.shape[0], 4, -1))
-    pieces = jnp.concatenate(pieces, axis=2)
+        piece = scatter.finish()
+        step = piece.shape[1] // (last - first)
+        blocks += [piece[:, at * step : (at + 1) * step] for at in range(last - first)]
+    small_sum = blocks[-1][:, 4 * wide :]
+    qkv_sum, out_sum = (
+        jnp.concatenate(
+            [block[:, k * wide : (k + 1) * wide] for k in kinds for block in blocks], axis=1
+        )
+        for kinds in ((0, 1, 2), (3,))
+    )
     counts = jnp.sum(
         small_sum[:, experts + 2 : 2 * experts + 2] * (1 << places).astype(jnp.float32)[:, None],
         axis=0,
@@ -840,8 +867,8 @@
         result,
         grad_input,
         small_sum[:, experts + 1],
-        pieces[:, :3].reshape(-1, 3 * width),
-        pieces[:, 3],
+        qkv_sum,
+        out_sum,
         small_sum[:, experts],
         small_sum[:, :experts],
         shared_sum[:, : 2 * hidden_units],

time: 584 us -> 541 us (0.926)
  local copies, waits for them, and re-layouts: 45.5 us -> 23 us
  waiting for transfers between devices: 147 us -> 127 us
    ppermute x20, waiting for transfers between devices: 76.9 us -> 51.8 us  [advance(): lax.ppermute(away, name, [(i, i ^ 1 << bit) for i in range(lax.axis_size(...]
    squeeze x39 -> x0, local copies, waits for them, and re-layouts: 15.8 us -> none  [the longest x36 14.6 us: advance(): lax.dynamic_index_in_dim(term, index, dim, keepdims=False)]
    ppermute x20, waiting for transfers between devices: 12 us -> 20.2 us  [swap_cores(): lax.ppermute(values_in, 'expert', [(i, i ^ 1) for i in range(owners)])]
    convert_element_type x18 -> x22, other arithmetic: 31 us -> 36.6 us  [the longest x20 31.9 us: advance(): away = sum_terms([picked(term, made + [(dim, 1 - mine)]) for term, made i...]
    unnamed x129 -> x167, local copies, waits for them, and re-layouts: 21.8 us -> 19.9 us
  transfers between devices with their start and end apart: 56 -> 56, of which waited for: 18 -> 20; matrix products, arithmetic and copies ran while one was open for 15% -> 11% of each run, Pallas kernels for 47% -> 51%
where the time goes in v4:
time: 541 us; the launch traced here: 534 us
  Pallas kernels  275 us (51%)
  waiting for transfers between devices  127 us (23%)
  other arithmetic  65.8 us (12%)
  starting transfers between devices  40.2 us (7%)
  local copies, waits for them, and re-layouts  23 us (4%)
    pallas_call x4, Pallas kernels, expert_step(): pl.pallas_call(lambda *r: expert_kernel(cap, tokens, hidden, None, *r), g...  127 us
    ppermute x12, waiting for transfers between devices, next_chip(): lax.ppermute(values_in, 'expert', [(i, (i + 2) % owners) for i in range(o...  54.9 us
    ppermute x20, waiting for transfers between devices, advance(): lax.ppermute(away, name, [(i, i ^ 1 << bit) for i in range(lax.axis_size(...  51.8 us
    pallas_call x3, Pallas kernels, attention_backward(): pl.pallas_call(lambda *r: attention_back_kernel(rows, extra, carried, *r)...  49.1 us
    pallas_call x4, Pallas kernels, weight_grad(): pl.pallas_call(lambda *r: weight_grad_kernel(parts, bit, *r), grid=(n //...  46.6 us
    convert_element_type x20, other arithmetic, advance(): away = sum_terms([picked(term, made + [(dim, 1 - mine)]) for term, made i...  31.9 us
    pallas_call x1, Pallas kernels, attention_forward(): pl.pallas_call(attention_kernel, grid=(pairs,), in_specs=[pl.BlockSpec(me...  23.1 us
    ppermute x20, waiting for transfers between devices, swap_cores(): lax.ppermute(values_in, 'expert', [(i, i ^ 1) for i in range(owners)])  20.2 us
  transfers between devices with their start and end apart: 56, of which 20 were waited for; matrix products, arithmetic and copies ran while one was open for 11% of the time, Pallas kernels for 51%

profile of v4, /device:TPU:0, one launch (start us, length us, event | category | flops | bytes accessed | tf_op | source)
XLA Modules:
  0.0 534.1 jit_solution(15322652142629489536)
XLA Ops:
  1.3 1.6 copy.109.ids
  2.9 3.5 token_rows.1.r_3_.r_2_
  6.8 2.6 collective-permute-start
  10.8 23.1 %attention_forward.1 = (bf16[512,1280]{1,0:T(8,128)(2,1)}, bf16[512,1280]{1,0:T(8,128)(2,1)}, bf16[512,1280]{1,0:T(8,128)(2,1)}, bf16[512,1280]{1,0:T(8,128)(2,1...) custom-call(s32[1]{0:T(128)} %copy.182.length_ref.r_0_, ...), custom_call_target="tpu_custom_call" | custom-call | tf_op jit(solution)/shard_map/attention_forward/pallas_call | solution.py:80
  34.2 1.6 collective-permute-start.4
  35.7 6.6 %collective-permute-done.r_3_ = bf16[528,1280]{1,0:T(8,128)(2,1)} collective-permute-done((bf16[528,1280]{1,0:T(8,128)(2,1)}, bf16[528,1280]{1,0:T(8,128)(2,1)}, u32[]{:S(2)}, u32[]{:S(2)}) %collective-permute-start) | collective-permute-done | bytes 1351712 | tf_op jit(solution)/shard_map/ppermute | solution.py:554
  47.3 31.2 %expert_step.4 = (bf16[544,1280]{1,0:T(8,128)(2,1)}, bf16[544,1280]{1,0:T(8,128)(2,1)}, bf16[512,1280]{1,0:T(8,128)(2,1)}, bf16[512,1280]{1,0:T(8,128)(2,1)}, bf...) custom-call(s32[1]{0:T(128)} %bitcast.2.r_0_, ...), custom_call_target="tpu_custom_call" | custom-call | tf_op jit(solution)/shard_map/expert_step/pallas_call | solution.py:329
  78.6 17.3 %shared_expert.1 = (f32[512,1280]{1,0:T(8,128)}, f32[512,1280]{1,0:T(8,128)}, f32[512,128]{1,0:T(8,128)S(1)}, bf16[640,2688]{1,0:T(8,128)(2,1)}, bf16[640,2688]{1,0:T(8,128)(2,1)}) custom-call(s32[1]{0:T(128)} %bitcast.1.r_0_.r_1_, bf16[512,1280]{1,0:T(8,128)(2,1)S(1)} %copy-done.10, bf16[528,1280]{1,0:T(8,128)(2,1)S(1)} %copy-done.2, ...), custom_call_target="tpu_custom_call" | custom-call | tf_op jit(solution)/shard_map/shared_expert/pallas_call | solution.py:446
  97.1 2.9 collective-permute-done.5.r_2_
  102.5 1.6 collective-permute-start.10
  105.5 32.0 %expert_step.5 = (bf16[544,1280]{1,0:T(8,128)(2,1)}, bf16[544,1280]{1,0:T(8,128)(2,1)}, bf16[512,1280]{1,0:T(8,128)(2,1)}, bf16[512,1280]{1,0:T(8,128)(2,1)}, bf...) custom-call(s32[1]{0:T(128)} %bitcast.2.r_0_, ...), custom_call_target="tpu_custom_call", output_to_operand_aliasing={{4}: (8, {}), {5}: (9, {}), {6}: (10, {}), {7}: (11, {})} | custom-call | tf_op jit(solution)/shard_map/expert_step/pallas_call | solution.py:329
  137.5 25.9 %collective-permute-done.10.r_1_ = bf16[512,1280]{1,0:T(8,128)(2,1)} collective-permute-done((bf16[512,1280]{1,0:T(8,128)(2,1)}, bf16[512,1280]{1,0:T(8,128)(2,1)}, u32[]{:S(2)}, u32[]{:S(2)}) %collective-permute-start.10) | collective-permute-done | bytes 1310752 | tf_op jit(solution)/shard_map/ppermute | solution.py:554
  163.4 3.3 fusion.2
  167.2 1.6 collective-permute-start.9
  168.8 2.3 collective-permute-done.12
  172.8 3.1 add_convert_fusion.8
  175.9 32.5 %expert_step.6 = (bf16[544,1280]{1,0:T(8,128)(2,1)}, bf16[544,1280]{1,0:T(8,128)(2,1)}, bf16[512,1280]{1,0:T(8,128)(2,1)}, bf16[512,1280]{1,0:T(8,128)(2,1)}, bf...) custom-call(s32[1]{0:T(128)} %bitcast.2.r_0_, ...), custom_call_target="tpu_custom_call", output_to_operand_aliasing={{4}: (8, {}), {5}: (9, {}), {6}: (10, {}), {7}: (11, {})} | custom-call | tf_op jit(solution)/shard_map/expert_step/pallas_call | solution.py:329
  208.5 2.1 fusion.3
  210.6 21.3 %collective-permute-done.18 = bf16[544,1280]{1,0:T(8,128)(2,1)} collective-permute-done((bf16[544,1280]{1,0:T(8,128)(2,1)}, bf16[544,1280]{1,0:T(8,128)(2,1)}, u32[]{:S(2)}, u32[]{:S(2)}) %collective-permute-start.18) | collective-permute-done | bytes 1392672 | tf_op jit(solution)/shard_map/ppermute | solution.py:554
  231.9 3.1 collective-permute-done.19
  235.1 1.9 add_convert_fusion.2
  238.0 1.5 collective-permute-start.15
  241.0 1.5 collective-permute-done.20.r_2_
  242.5 31.4 %expert_step.7 = (bf16[544,1280]{1,0:T(8,128)(2,1)}, bf16[544,1280]{1,0:T(8,128)(2,1)}, bf16[512,1280]{1,0:T(8,128)(2,1)}, bf16[512,1280]{1,0:T(8,128)(2,1)}, bf...) custom-call(s32[1]{0:T(128)} %bitcast.2.r_0_, ...), custom_call_target="tpu_custom_call", output_to_operand_aliasing={{4}: (8, {}), {5}: (9, {}), {6}: (10, {}), {7}: (11, {})} | custom-call | tf_op jit(solution)/shard_map/expert_step/pallas_call | solution.py:329
  274.1 3.2 collective-permute-done.24
  277.3 1.9 add_convert_fusion.1
  280.3 8.3 %weight_grad.4 = (bf16[448,1280]{1,0:T(8,128)(2,1)S(1)}, bf16[448,1280]{1,0:T(8,128)(2,1)S(1)}) custom-call(s32[1]{0:T(128)} %bitcast.9.r_0_, bf16[2,1920,896]{2,1,0:T(8,128)(2,1)} %get-tuple-element.285.r_1_, bf16[2,1920,1280]{2,1,0:T(8,128)(2,1)} %get-tuple-element.282.r_2_), custom_call_target="tpu_custom_call" | custom-call | tf_op jit(solution)/shard_map/weight_grad/pallas_call | solution.py:523
  288.7 8.7 %weight_grad.5 = (bf16[448,1280]{1,0:T(8,128)(2,1)S(1)}, bf16[448,1280]{1,0:T(8,128)(2,1)S(1)}) custom-call(s32[1]{0:T(128)} %bitcast.9.r_0_, bf16[2,1920,896]{2,1,0:T(8,128)(2,1)} %get-tuple-element.285.r_1_, bf16[2,1920,1280]{2,1,0:T(8,128)(2,1)} %get-tuple-element.282.r_2_), custom_call_target="tpu_custom_call" | custom-call | tf_op jit(solution)/shard_map/weight_grad/pallas_call | solution.py:523
  297.4 1.6 collective-permute-start.27
  299.6 14.8 %weight_grad.6 = (bf16[640,1792]{1,0:T(8,128)(2,1)S(1)}, bf16[640,1792]{1,0:T(8,128)(2,1)}) custom-call(s32[1]{0:T(128)} %bitcast.9.r_0_, bf16[2,1920,1280]{2,1,0:T(8,128)(2,1)} %get-tuple-element.293.r_1_, bf16[2,1920,1792]{2,1,0:T(8,128)(2,1)} %get-tuple-element.290.r_2_), custom_call_target="tpu_custom_call" | custom-call | tf_op jit(solution)/shard_map/weight_grad/pallas_call | solution.py:523
  315.8 14.7 %weight_grad.7 = (bf16[640,1792]{1,0:T(8,128)(2,1)S(1)}, bf16[640,1792]{1,0:T(8,128)(2,1)}) custom-call(s32[1]{0:T(128)} %bitcast.9.r_0_, bf16[2,1920,1280]{2,1,0:T(8,128)(2,1)} %get-tuple-element.293.r_1_, bf16[2,1920,1792]{2,1,0:T(8,128)(2,1)} %get-tuple-element.290.r_2_), custom_call_target="tpu_custom_call" | custom-call | tf_op jit(solution)/shard_map/weight_grad/pallas_call | solution.py:523
  331.9 1.6 collective-permute-start.30
  335.6 2.0 fusion.17
  338.7 8.8 %middle_back.1 = (f32[512,1280]{1,0:T(8,128)}, bf16[512,1280]{1,0:T(8,128)(2,1)S(1)}, f32[1280,128]{1,0:T(8,128)S(1)}) custom-call(s32[1]{0:T(128)} %copy.182.length_ref.r_0_, bf16[544,1280]{1,0:T(8,128)(2,1)} %get-tuple-element.302.r_1_, bf16[544,1280]{1,0:T(8,128)(2,1)} %copy-done.41, bf16[544,1280]{1,0:T(8,128)(2,1)} %copy-done.42, ...), custom_call_target="tpu_custom_call" | custom-call | tf_op jit(solution)/shard_map/middle_back/pallas_call | solution.py:491
  347.6 16.7 %attention_backward.3 = (bf16[640,2048]{1,0:T(8,128)(2,1)}, bf16[640,2048]{1,0:T(8,128)(2,1)}, f32[512,1280]{1,0:T(8,128)}) custom-call(s32[2]{0:T(128)S(1)} %pad_add_fusion.3.r_0_, s32[1]{0:T(128)} %bitcast.1.r_0_.r_1_, bf16[512,1280]{1,0:T(8,128)(2,1)S(1)} %get-tuple-element.322.r_2_, bf16[1280,1280]{1,0:T(8,128)(2,1)} %r_3_.7, ...), custom_call_target="tpu_custom_call" | custom-call | tf_op jit(solution)/shard_map/attention_backward/pallas_call | solution.py:187
  365.4 1.6 add_convert_fusion.7
  367.0 3.0 collective-permute-start.31
  370.7 1.7 collective-permute-start.34
  377.8 16.8 %attention_backward.4 = (bf16[640,2048]{1,0:T(8,128)(2,1)}, bf16[640,2048]{1,0:T(8,128)(2,1)}, f32[512,1280]{1,0:T(8,128)}) custom-call(s32[2]{0:T(128)S(1)} %get-tuple-element.482.r_0_, s32[1]{0:T(128)} %bitcast.1.r_0_.r_1_, bf16[512,1280]{1,0:T(8,128)(2,1)S(1)} %copy-done.9, bf16[1280,1280]{1,0:T(8,128)(2,1)} %r_3_.7, bf16[512,1280]{1,0:T(8,128)(2,1)S(1)} %copy-done.3, ...), custom_call_target="tpu_custom_call" | custom-call | tf_op jit(solution)/shard_map/attention_backward/pallas_call | solution.py:187
  394.6 15.5 %attention_backward.5 = (bf16[640,1152]{1,0:T(8,128)(2,1)}, bf16[640,1152]{1,0:T(8,128)(2,1)}, f32[512,1280]{1,0:T(8,128)}) custom-call(s32[2]{0:T(128)S(1)} %get-tuple-element.481.r_0_, s32[1]{0:T(128)} %bitcast.1.r_0_.r_1_, bf16[512,1280]{1,0:T(8,128)(2,1)S(1)} %copy-done.9, bf16[1280,1280]{1,0:T(8,128)(2,1)} %r_3_.7, bf16[512,1280]{1,0:T(8,128)(2,1)S(1)} %copy-done.3, ...), custom_call_target="tpu_custom_call" | custom-call | tf_op jit(solution)/shard_map/attention_backward/pallas_call | solution.py:187
  411.6 3.8 collective-permute-done.38
  415.5 2.4 fusion.4
  419.4 1.8 collective-permute-done.37
  423.5 2.4 convert_add_fusion.1
  430.9 18.7 %collective-permute-done.42 = bf16[2,2,2,40,2048]{4,3,2,1,0:T(8,128)(2,1)S(1)} collective-permute-done((bf16[2,2,2,40,2048]{4,3,2,1,0:T(8,128)(2,1)S(1)}, bf16[2,2,2,40,2048]{4,3,2,1,0:T(8,128)(2,1)S(1)}, u32[]{:S(2)}, u32[]{:S(2)}) %collective-permute-start.42) | collective-permute-done | bytes 1310752 | tf_op jit(solution)/shard_map/ppermute | solution.py:595
  449.6 2.1 fusion.7
  454.4 11.0 %collective-permute-done.40 = bf16[2,2,2,40,1152]{4,3,2,1,0:T(8,128)(2,1)S(1)} collective-permute-done((bf16[2,2,2,40,1152]{4,3,2,1,0:T(8,128)(2,1)S(1)}, bf16[2,2,2,40,1152]{4,3,2,1,0:T(8,128)(2,1)S(1)}, u32[]{:S(2)}, u32[]{:S(2)}) %collective-permute-start.40) | collective-permute-done | bytes 737312 | tf_op jit(solution)/shard_map/ppermute | solution.py:595
  469.9 3.3 add_convert_fusion.4
  473.2 7.8 %collective-permute-done.53 = bf16[40,2688]{1,0:T(8,128)(2,1)S(1)} collective-permute-done((bf16[40,2688]{1,0:T(8,128)(2,1)S(1)}, bf16[40,2688]{1,0:T(8,128)(2,1)S(1)}, u32[]{:S(2)}, u32[]{:S(2)}) %collective-permute-start.53) | collective-permute-done | bytes 215072 | tf_op jit(solution)/shard_map/ppermute | solution.py:595
  486.8 2.0 collective-permute-start.48
  490.0 1.7 fusion.8
  492.1 2.6 fusion.9
  494.7 1.6 collective-permute-start.55
  496.3 1.9 fusion.25
  498.9 7.5 %collective-permute-done.48 = bf16[2,40,2048]{2,1,0:T(8,128)(2,1)S(1)} collective-permute-done((bf16[2,40,2048]{2,1,0:T(8,128)(2,1)S(1)}, bf16[2,40,2048]{2,1,0:T(8,128)(2,1)S(1)}, u32[]{:S(2)}, u32[]{:S(2)}) %collective-permute-start.48) | collective-permute-done | bytes 327712 | tf_op jit(solution)/shard_map/ppermute | solution.py:595
  506.4 1.8 fusion.24
  510.5 1.7 collective-permute-start.50
  513.8 1.5 pad_maximum_fusion.1
  515.3 4.1 collective-permute-done.50
  522.3 1.5 slice_reduce_fusion
  525.3 1.5 fusion.22
  527.3 2.2 fusion
  529.5 2.0 fusion.1
  531.4 2.4 pad_maximum_fusion
  (289 shorter events, 65.5 us)
Async XLA Ops:
  6.4 37.5 %collective-permute-start.2 = (bf16[528,1280]{1,0:T(8,128)(2,1)}, bf16[528,1280]{1,0:T(8,128)(2,1)}, u32[]{:S(2)}, u32[]{:S(2)}) collective-permute-start(bf16[528,1280]{1,0:T(8,128)(2,1)} %token_rows.1.r_3_.r_2_), channel_id=1, source_target_pairs={{0,1},{1,0},{2,3},{3,2},{4,5},{5,4},{6,7},{7,6},{8,9},{9,8},{10,11... | collective-permute-start | bytes 4055048 | tf_op jit(solution)/shard_map/ppermute | solution.py:549
  6.8 35.5 %collective-permute-start = (bf16[528,1280]{1,0:T(8,128)(2,1)}, bf16[528,1280]{1,0:T(8,128)(2,1)}, u32[]{:S(2)}, u32[]{:S(2)}) collective-permute-start(bf16[528,1280]{1,0:T(8,128)(2,1)} %token_rows.1.r_3_.r_2_), channel_id=1, source_target_pairs={{0,2},{1,3},{2,4},{3,5},{4,6},{5,7},{6,0},{7,1},{8,10},{9,11},{10,... | collective-permute-start | bytes 4055048 | tf_op jit(solution)/shard_map/ppermute | solution.py:554
  33.9 9.9 %collective-permute-start.1 = (bf16[512,1280]{1,0:T(8,128)(2,1)}, bf16[512,1280]{1,0:T(8,128)(2,1)S(1)}, u32[]{:S(2)}, u32[]{:S(2)}) collective-permute-start(bf16[512,1280]{1,0:T(8,128)(2,1)} %get-tuple-element.219.r_1_.r_6_), channel_id=1, source_target_pairs={{0,1},{1,0},{2,3},{3,2},{4,5},{5,4},{6,7},{7,6},{8,9},{9,8},{10,11... | collective-permute-start | bytes 3932168 | tf_op jit(solution)/shard_map/ppermute | solution.py:549
  34.2 62.4 %collective-permute-start.4 = (bf16[512,1280]{1,0:T(8,128)(2,1)}, bf16[512,1280]{1,0:T(8,128)(2,1)}, u32[]{:S(2)}, u32[]{:S(2)}) collective-permute-start(bf16[512,1280]{1,0:T(8,128)(2,1)} %get-tuple-element.219.r_1_.r_6_), channel_id=1, source_target_pairs={{0,2},{1,3},{2,4},{3,5},{4,6},{5,7},{6,0},{7,1},{8,10},{9,11},{10,... | collective-permute-start | bytes 3932168 | tf_op jit(solution)/shard_map/ppermute | solution.py:554
  42.3 58.7 %collective-permute-start.6 = (bf16[528,1280]{1,0:T(8,128)(2,1)}, bf16[528,1280]{1,0:T(8,128)(2,1)}, u32[]{:S(2)}, u32[]{:S(2)}) collective-permute-start(bf16[528,1280]{1,0:T(8,128)(2,1)} %collective-permute-done.r_3_), channel_id=1, source_target_pairs={{0,1},{1,0},{2,3},{3,2},{4,5},{5,4},{6,7},{7,6},{8,9},{9,8},{10,11... | collective-permute-start | bytes 4055048 | tf_op jit(solution)/shard_map/ppermute | solution.py:549
  42.3 58.7 %collective-permute-start.3 = (bf16[528,1280]{1,0:T(8,128)(2,1)}, bf16[528,1280]{1,0:T(8,128)(2,1)}, u32[]{:S(2)}, u32[]{:S(2)}) collective-permute-start(bf16[528,1280]{1,0:T(8,128)(2,1)} %collective-permute-done.r_3_), channel_id=1, source_target_pairs={{0,2},{1,3},{2,4},{3,5},{4,6},{5,7},{6,0},{7,1},{8,10},{9,11},{10,... | collective-permute-start | bytes 4055048 | tf_op jit(solution)/shard_map/ppermute | solution.py:554
  47.3 31.2 %copy-start.2 = (bf16[528,1280]{1,0:T(8,128)(2,1)S(1)}, bf16[528,1280]{1,0:T(8,128)(2,1)}, u32[]{:S(2)}) copy-start(bf16[528,1280]{1,0:T(8,128)(2,1)} %token_rows.1.r_3_.r_2_) | copy-start | bytes 4055044
  47.3 31.2 %copy-start.23 = (bf16[896,1280]{1,0:T(8,128)(2,1)S(1)}, bf16[896,1280]{1,0:T(8,128)(2,1)}, u32[]{:S(2)}) copy-start(bf16[896,1280]{1,0:T(8,128)(2,1)} %r_4_.1) | copy-start | bytes 6881284
  96.5 3.4 collective-permute-start.5
  101.0 62.4 %collective-permute-start.8 = (bf16[640,2688]{1,0:T(8,128)(2,1)}, bf16[640,2688]{1,0:T(8,128)(2,1)}, u32[]{:S(2)}, u32[]{:S(2)}) collective-permute-start(bf16[640,2688]{1,0:T(8,128)(2,1)} %get-tuple-element.228), channel_id=1, source_target_pairs={{0,1},{1,0},{2,3},{3,2},{4,5},{5,4},{6,7},{7,6},{8,9},{9,8},{10,11... | collective-permute-start | bytes 10321928 | tf_op jit(solution)/shard_map/ppermute | solution.py:549
  101.4 62.0 %collective-permute-start.11 = (bf16[528,1280]{1,0:T(8,128)(2,1)}, bf16[528,1280]{1,0:T(8,128)(2,1)S(1)}, u32[]{:S(2)}, u32[]{:S(2)}) collective-permute-start(bf16[528,1280]{1,0:T(8,128)(2,1)} %collective-permute-done.3.r_3_), channel_id=1, source_target_pairs={{0,2},{1,3},{2,4},{3,5},{4,6},{5,7},{6,0},{7,1},{8,10},{9,11},{10,... | collective-permute-start | bytes 4055048 | tf_op jit(solution)/shard_map/ppermute | solution.py:554
  102.5 60.8 %collective-permute-start.10 = (bf16[512,1280]{1,0:T(8,128)(2,1)}, bf16[512,1280]{1,0:T(8,128)(2,1)}, u32[]{:S(2)}, u32[]{:S(2)}) collective-permute-start(bf16[512,1280]{1,0:T(8,128)(2,1)} %collective-permute-done.4.r_1_), channel_id=1, source_target_pairs={{0,2},{1,3},{2,4},{3,5},{4,6},{5,7},{6,0},{7,1},{8,10},{9,11},{10,... | collective-permute-start | bytes 3932168 | tf_op jit(solution)/shard_map/ppermute | solution.py:554
  104.1 59.2 %collective-permute-start.7 = (bf16[512,1280]{1,0:T(8,128)(2,1)}, bf16[512,1280]{1,0:T(8,128)(2,1)}, u32[]{:S(2)}, u32[]{:S(2)}) collective-permute-start(bf16[512,1280]{1,0:T(8,128)(2,1)} %get-tuple-element.224), channel_id=1, source_target_pairs={{0,1},{1,0},{2,3},{3,2},{4,5},{5,4},{6,7},{7,6},{8,9},{9,8},{10,11... | collective-permute-start | bytes 3932168 | tf_op jit(solution)/shard_map/ppermute | solution.py:549
  105.5 57.9 %copy-start.36 = (bf16[640,2688]{1,0:T(8,128)(2,1)S(1)}, bf16[640,2688]{1,0:T(8,128)(2,1)}, u32[]{:S(2)}) copy-start(bf16[640,2688]{1,0:T(8,128)(2,1)} %get-tuple-element.227) | copy-start | bytes 10321924
  166.7 4.4 collective-permute-start.12
  166.7 5.9 %collective-permute-start.17 = (bf16[512,1280]{1,0:T(8,128)(2,1)S(1)}, bf16[512,1280]{1,0:T(8,128)(2,1)}, u32[]{:S(2)}, u32[]{:S(2)}) collective-permute-start(bf16[512,1280]{1,0:T(8,128)(2,1)S(1)} %copy-done.74), channel_id=1, source_target_pairs={{0,1},{1,0},{2,3},{3,2},{4,5},{5,4},{6,7},{7,6},{8,9},{9,8},{10,11... | collective-permute-start | bytes 3932168 | tf_op jit(solution)/shard_map/ppermute | solution.py:549
  167.2 41.2 %collective-permute-start.9 = (bf16[2,2,2,40,2688]{4,3,2,1,0:T(8,128)(2,1)}, bf16[2,2,2,40,2688]{4,3,2,1,0:T(8,128)(2,1)}, u32[]{:S(2)}, u32[]{:S(2)}) collective-permute-start(bf16[2,2,2,40,2688]{4,3,2,1,0:T(8,128)(2,1)} %fusion.2), channel_id=1, source_target_pairs={{0,8},{8,0},{16,24},{24,16},{1,9},{9,1},{17,25},{25,17},{2,10},{10... | collective-permute-start | bytes 5160968 | tf_op jit(solution)/shard_map/ppermute | solution.py:595
  168.8 7.1 %collective-permute-start.14 = (bf16[528,1280]{1,0:T(8,128)(2,1)}, bf16[528,1280]{1,0:T(8,128)(2,1)}, u32[]{:S(2)}, u32[]{:S(2)}) collective-permute-start(bf16[528,1280]{1,0:T(8,128)(2,1)} %collective-permute-done.3.r_3_), channel_id=1, source_target_pairs={{0,1},{1,0},{2,3},{3,2},{4,5},{5,4},{6,7},{7,6},{8,9},{9,8},{10,11... | collective-permute-start | bytes 4055048 | tf_op jit(solution)/shard_map/ppermute | solution.py:549
  168.8 39.7 %collective-permute-start.16 = (bf16[512,1280]{1,0:T(8,128)(2,1)}, bf16[512,1280]{1,0:T(8,128)(2,1)}, u32[]{:S(2)}, u32[]{:S(2)}) collective-permute-start(bf16[512,1280]{1,0:T(8,128)(2,1)} %collective-permute-done.10.r_1_), channel_id=1, source_target_pairs={{0,2},{1,3},{2,4},{3,5},{4,6},{5,7},{6,0},{7,1},{8,10},{9,11},{10,... | collective-permute-start | bytes 3932168 | tf_op jit(solution)/shard_map/ppermute | solution.py:554
  171.1 4.8 collective-permute-start.13
  172.7 59.3 %collective-permute-start.18 = (bf16[544,1280]{1,0:T(8,128)(2,1)}, bf16[544,1280]{1,0:T(8,128)(2,1)}, u32[]{:S(2)}, u32[]{:S(2)}) collective-permute-start(bf16[544,1280]{1,0:T(8,128)(2,1)} %add_convert_fusion.3), channel_id=1, source_target_pairs={{0,2},{1,3},{2,4},{3,5},{4,6},{5,7},{6,0},{7,1},{8,10},{9,11},{10,... | collective-permute-start | bytes 4177928 | tf_op jit(solution)/shard_map/ppermute | solution.py:554
  231.9 3.2 collective-permute-start.19
  237.0 36.9 %collective-permute-start.23 = (bf16[544,1280]{1,0:T(8,128)(2,1)S(1)}, bf16[544,1280]{1,0:T(8,128)(2,1)S(1)}, u32[]{:S(2)}, u32[]{:S(2)}) collective-permute-start(bf16[544,1280]{1,0:T(8,128)(2,1)S(1)} %add_convert_fusion.2), channel_id=1, source_target_pairs={{0,2},{1,3},{2,4},{3,5},{4,6},{5,7},{6,0},{7,1},{8,10},{9,11},{10,... | collective-permute-start | bytes 4177928 | tf_op jit(solution)/shard_map/ppermute | solution.py:554
  237.3 3.7 collective-permute-start.21
  237.5 5.0 collective-permute-start.20
  237.8 36.0 %collective-permute-start.22 = (bf16[512,1280]{1,0:T(8,128)(2,1)}, bf16[512,1280]{1,0:T(8,128)(2,1)S(1)}, u32[]{:S(2)}, u32[]{:S(2)}) collective-permute-start(bf16[512,1280]{1,0:T(8,128)(2,1)} %get-tuple-element.275), channel_id=1, source_target_pairs={{0,1},{1,0},{2,3},{3,2},{4,5},{5,4},{6,7},{7,6},{8,9},{9,8},{10,11... | collective-permute-start | bytes 3932168 | tf_op jit(solution)/shard_map/ppermute | solution.py:549
  238.0 35.9 %collective-permute-start.15 = (bf16[2,2,40,2688]{3,2,1,0:T(8,128)(2,1)S(1)}, bf16[2,2,40,2688]{3,2,1,0:T(8,128)(2,1)S(1)}, u32[]{:S(2)}, u32[]{:S(2)}) collective-permute-start(bf16[2,2,40,2688]{3,2,1,0:T(8,128)(2,1)S(1)} %fusion.3), channel_id=1, source_target_pairs={{0,16},{8,24},{16,0},{24,8},{1,17},{9,25},{17,1},{25,9},{2,18},{10... | collective-permute-start | bytes 2580488 | tf_op jit(solution)/shard_map/ppermute | solution.py:595
  273.9 3.4 collective-permute-start.24
  279.3 52.6 %collective-permute-start.25 = (bf16[544,1280]{1,0:T(8,128)(2,1)}, bf16[544,1280]{1,0:T(8,128)(2,1)S(1)}, u32[]{:S(2)}, u32[]{:S(2)}) collective-permute-start(bf16[544,1280]{1,0:T(8,128)(2,1)} %get-tuple-element.279), channel_id=1, source_target_pairs={{0,1},{1,0},{2,3},{3,2},{4,5},{5,4},{6,7},{7,6},{8,9},{9,8},{10,11... | collective-permute-start | bytes 4177928 | tf_op jit(solution)/shard_map/ppermute | solution.py:549
  279.5 52.4 %collective-permute-start.26 = (bf16[544,1280]{1,0:T(8,128)(2,1)S(1)}, bf16[544,1280]{1,0:T(8,128)(2,1)S(1)}, u32[]{:S(2)}, u32[]{:S(2)}) collective-permute-start(bf16[544,1280]{1,0:T(8,128)(2,1)S(1)} %add_convert_fusion.1), channel_id=1, source_target_pairs={{0,2},{1,3},{2,4},{3,5},{4,6},{5,7},{6,0},{7,1},{8,10},{9,11},{10,... | collective-permute-start | bytes 4177928 | tf_op jit(solution)/shard_map/ppermute | solution.py:554
  279.9 52.0 %collective-permute-start.29 = (bf16[512,1280]{1,0:T(8,128)(2,1)}, bf16[512,1280]{1,0:T(8,128)(2,1)}, u32[]{:S(2)}, u32[]{:S(2)}) collective-permute-start(bf16[512,1280]{1,0:T(8,128)(2,1)} %get-tuple-element.297), channel_id=1, source_target_pairs={{0,1},{1,0},{2,3},{3,2},{4,5},{5,4},{6,7},{7,6},{8,9},{9,8},{10,11... | collective-permute-start | bytes 3932168 | tf_op jit(solution)/shard_map/ppermute | solution.py:549
  288.7 46.9 %copy-start.26 = (bf16[448,1280]{1,0:T(8,128)(2,1)}, bf16[448,1280]{1,0:T(8,128)(2,1)S(1)}, u32[]{:S(2)}) copy-start(bf16[448,1280]{1,0:T(8,128)(2,1)S(1)} %get-tuple-element.283) | copy-start | bytes 3440644
  297.4 40.2 %copy-start.28 = (bf16[448,1280]{1,0:T(8,128)(2,1)}, bf16[448,1280]{1,0:T(8,128)(2,1)S(1)}, u32[]{:S(2)}) copy-start(bf16[448,1280]{1,0:T(8,128)(2,1)S(1)} %get-tuple-element.286) | copy-start | bytes 3440644
  297.4 34.5 %collective-permute-start.27 = (bf16[448,1280]{1,0:T(8,128)(2,1)S(1)}, bf16[448,1280]{1,0:T(8,128)(2,1)S(1)}, u32[]{:S(2)}, u32[]{:S(2)}) collective-permute-start(bf16[448,1280]{1,0:T(8,128)(2,1)S(1)} %get-tuple-element.287), channel_id=1, source_target_pairs={{0,16},{8,24},{16,0},{24,8},{1,17},{9,25},{17,1},{25,9},{2,18},{10... | collective-permute-start | bytes 3440648 | tf_op jit(solution)/shard_map/ppermute | solution.py:755
  299.0 32.9 %collective-permute-start.28 = (bf16[448,1280]{1,0:T(8,128)(2,1)S(1)}, bf16[448,1280]{1,0:T(8,128)(2,1)}, u32[]{:S(2)}, u32[]{:S(2)}) collective-permute-start(bf16[448,1280]{1,0:T(8,128)(2,1)S(1)} %get-tuple-element.284), channel_id=1, source_target_pairs={{0,8},{8,0},{16,24},{24,16},{1,9},{9,1},{17,25},{25,17},{2,10},{10... | collective-permute-start | bytes 3440648 | tf_op jit(solution)/shard_map/ppermute | solution.py:755
  331.9 33.5 %collective-permute-start.30 = (bf16[512,1280]{1,0:T(8,128)(2,1)}, bf16[512,1280]{1,0:T(8,128)(2,1)S(1)}, u32[]{:S(2)}, u32[]{:S(2)}) collective-permute-start(bf16[512,1280]{1,0:T(8,128)(2,1)} %add_convert_fusion.8), channel_id=1, source_target_pairs={{0,2},{1,3},{2,4},{3,5},{4,6},{5,7},{6,0},{7,1},{8,10},{9,11},{10,... | collective-permute-start | bytes 3932168 | tf_op jit(solution)/shard_map/ppermute | solution.py:554
  333.6 76.5 %collective-permute-start.32 = (bf16[640,1792]{1,0:T(8,128)(2,1)}, bf16[640,1792]{1,0:T(8,128)(2,1)}, u32[]{:S(2)}, u32[]{:S(2)}) collective-permute-start(bf16[640,1792]{1,0:T(8,128)(2,1)} %get-tuple-element.328), channel_id=1, source_target_pairs={{0,8},{8,0},{16,24},{24,16},{1,9},{9,1},{17,25},{25,17},{2,10},{10... | collective-permute-start | bytes 6881288 | tf_op jit(solution)/shard_map/ppermute | solution.py:755
  335.1 75.1 %collective-permute-start.33 = (bf16[640,1792]{1,0:T(8,128)(2,1)}, bf16[640,1792]{1,0:T(8,128)(2,1)}, u32[]{:S(2)}, u32[]{:S(2)}) collective-permute-start(bf16[640,1792]{1,0:T(8,128)(2,1)} %get-tuple-element.329), channel_id=1, source_target_pairs={{0,16},{8,24},{16,0},{24,8},{1,17},{9,25},{17,1},{25,9},{2,18},{10... | collective-permute-start | bytes 6881288 | tf_op jit(solution)/shard_map/ppermute | solution.py:755
  367.0 43.2 %collective-permute-start.31 = (bf16[512,1280]{1,0:T(8,128)(2,1)}, bf16[512,1280]{1,0:T(8,128)(2,1)}, u32[]{:S(2)}, u32[]{:S(2)}) collective-permute-start(bf16[512,1280]{1,0:T(8,128)(2,1)} %add_convert_fusion.7), channel_id=1, source_target_pairs={{0,2},{1,3},{2,4},{3,5},{4,6},{5,7},{6,0},{7,1},{8,10},{9,11},{10,... | collective-permute-start | bytes 3932168 | tf_op jit(solution)/shard_map/ppermute | solution.py:554
  370.2 39.9 %collective-permute-start.35 = (bf16[224,1280]{1,0:T(8,128)(2,1)}, bf16[224,1280]{1,0:T(8,128)(2,1)S(1)}, u32[]{:S(2)}, u32[]{:S(2)}) collective-permute-start(bf16[224,1280]{1,0:T(8,128)(2,1)} %fusion.18), channel_id=1, source_target_pairs={{0,8},{8,0},{16,24},{24,16},{1,9},{9,1},{17,25},{25,17},{2,10},{10... | collective-permute-start | bytes 1720328 | tf_op jit(solution)/shard_map/ppermute | solution.py:595
  370.7 39.4 %collective-permute-start.34 = (bf16[224,1280]{1,0:T(8,128)(2,1)}, bf16[224,1280]{1,0:T(8,128)(2,1)S(1)}, u32[]{:S(2)}, u32[]{:S(2)}) collective-permute-start(bf16[224,1280]{1,0:T(8,128)(2,1)} %fusion.17), channel_id=1, source_target_pairs={{0,16},{8,24},{16,0},{24,8},{1,17},{9,25},{17,1},{25,9},{2,18},{10... | collective-permute-start | bytes 1720328 | tf_op jit(solution)/shard_map/ppermute | solution.py:595
  410.2 5.3 collective-permute-start.38
  411.1 10.1 %collective-permute-start.37 = (bf16[640,2048]{1,0:T(8,128)(2,1)}, bf16[640,2048]{1,0:T(8,128)(2,1)S(1)}, u32[]{:S(2)}, u32[]{:S(2)}) collective-permute-start(bf16[640,2048]{1,0:T(8,128)(2,1)} %get-tuple-element.336), channel_id=1, source_target_pairs={{0,1},{1,0},{2,3},{3,2},{4,5},{5,4},{6,7},{7,6},{8,9},{9,8},{10,11... | collective-permute-start | bytes 7864328 | tf_op jit(solution)/shard_map/ppermute | solution.py:549
  411.1 15.4 %collective-permute-start.36 = (bf16[640,1152]{1,0:T(8,128)(2,1)}, bf16[640,1152]{1,0:T(8,128)(2,1)}, u32[]{:S(2)}, u32[]{:S(2)}) collective-permute-start(bf16[640,1152]{1,0:T(8,128)(2,1)} %get-tuple-element.331), channel_id=1, source_target_pairs={{0,1},{1,0},{2,3},{3,2},{4,5},{5,4},{6,7},{7,6},{8,9},{9,8},{10,11... | collective-permute-start | bytes 4423688 | tf_op jit(solution)/shard_map/ppermute | solution.py:549
  417.9 31.7 %collective-permute-start.42 = (bf16[2,2,2,40,2048]{4,3,2,1,0:T(8,128)(2,1)S(1)}, bf16[2,2,2,40,2048]{4,3,2,1,0:T(8,128)(2,1)S(1)}, u32[]{:S(2)}, u32[]{:S(2)}) collective-permute-start(bf16[2,2,2,40,2048]{4,3,2,1,0:T(8,128)(2,1)S(1)} %fusion.4), channel_id=1, source_target_pairs={{0,8},{8,0},{16,24},{24,16},{1,9},{9,1},{17,25},{25,17},{2,10},{10... | collective-permute-start | bytes 3932168 | tf_op jit(solution)/shard_map/ppermute | solution.py:595
  421.2 31.4 %copy-start.38 = (bf16[640,2048]{1,0:T(8,128)(2,1)}, bf16[640,2048]{1,0:T(8,128)(2,1)S(1)}, u32[]{:S(2)}) copy-start(bf16[640,2048]{1,0:T(8,128)(2,1)S(1)} %collective-permute-done.37) | copy-start | bytes 7864324
  421.7 30.9 %collective-permute-start.41 = (bf16[2,2,2,40,2048]{4,3,2,1,0:T(8,128)(2,1)S(1)}, bf16[2,2,2,40,2048]{4,3,2,1,0:T(8,128)(2,1)S(1)}, u32[]{:S(2)}, u32[]{:S(2)}) collective-permute-start(bf16[2,2,2,40,2048]{4,3,2,1,0:T(8,128)(2,1)S(1)} %fusion.5), channel_id=1, source_target_pairs={{0,16},{8,24},{16,0},{24,8},{1,17},{9,25},{17,1},{25,9},{2,18},{10... | collective-permute-start | bytes 3932168 | tf_op jit(solution)/shard_map/ppermute | solution.py:595
  425.9 44.0 %collective-permute-start.43 = (bf16[512,1280]{1,0:T(8,128)(2,1)S(1)}, bf16[512,1280]{1,0:T(8,128)(2,1)S(1)}, u32[]{:S(2)}, u32[]{:S(2)}) collective-permute-start(bf16[512,1280]{1,0:T(8,128)(2,1)S(1)} %convert_add_fusion.1), channel_id=1, source_target_pairs={{0,2},{1,3},{2,4},{3,5},{4,6},{5,7},{6,0},{7,1},{8,10},{9,11},{10,... | collective-permute-start | bytes 3932168 | tf_op jit(solution)/shard_map/ppermute | solution.py:554
  427.8 37.6 %collective-permute-start.40 = (bf16[2,2,2,40,1152]{4,3,2,1,0:T(8,128)(2,1)S(1)}, bf16[2,2,2,40,1152]{4,3,2,1,0:T(8,128)(2,1)S(1)}, u32[]{:S(2)}, u32[]{:S(2)}) collective-permute-start(bf16[2,2,2,40,1152]{4,3,2,1,0:T(8,128)(2,1)S(1)} %fusion.13), channel_id=1, source_target_pairs={{0,8},{8,0},{16,24},{24,16},{1,9},{9,1},{17,25},{25,17},{2,10},{10... | collective-permute-start | bytes 2211848 | tf_op jit(solution)/shard_map/ppermute | solution.py:595
  430.8 37.2 %collective-permute-start.39 = (bf16[2,40,2688]{2,1,0:T(8,128)(2,1)S(1)}, bf16[2,40,2688]{2,1,0:T(8,128)(2,1)S(1)}, u32[]{:S(2)}, u32[]{:S(2)}) collective-permute-start(bf16[2,40,2688]{2,1,0:T(8,128)(2,1)S(1)} %fusion.12), channel_id=1, source_target_pairs={{0,2},{1,3},{2,0},{3,1},{4,6},{5,7},{6,4},{7,5},{8,10},{9,11},{10,... | collective-permute-start | bytes 1290248 | tf_op jit(solution)/shard_map/ppermute | solution.py:595
  449.6 46.6 %copy-start.51 = (bf16[2,2,2,40,2048]{4,3,2,1,0:T(8,128)(2,1)}, bf16[2,2,2,40,2048]{4,3,2,1,0:T(8,128)(2,1)S(1)}, u32[]{:S(2)}) copy-start(bf16[2,2,2,40,2048]{4,3,2,1,0:T(8,128)(2,1)S(1)} %collective-permute-done.42) | copy-start | bytes 3932164
  451.7 32.0 %collective-permute-start.46 = (bf16[2,2,40,2048]{3,2,1,0:T(8,128)(2,1)S(1)}, bf16[2,2,40,2048]{3,2,1,0:T(8,128)(2,1)S(1)}, u32[]{:S(2)}, u32[]{:S(2)}) collective-permute-start(bf16[2,2,40,2048]{3,2,1,0:T(8,128)(2,1)S(1)} %fusion.7), channel_id=1, source_target_pairs={{0,16},{8,24},{16,0},{24,8},{1,17},{9,25},{17,1},{25,9},{2,18},{10... | collective-permute-start | bytes 1966088 | tf_op jit(solution)/shard_map/ppermute | solution.py:595
  452.6 53.8 %copy-start.50 = (bf16[2,2,2,40,2048]{4,3,2,1,0:T(8,128)(2,1)}, bf16[2,2,2,40,2048]{4,3,2,1,0:T(8,128)(2,1)S(1)}, u32[]{:S(2)}) copy-start(bf16[2,2,2,40,2048]{4,3,2,1,0:T(8,128)(2,1)S(1)} %collective-permute-done.41) | copy-start | bytes 3932164
  452.9 32.4 %collective-permute-start.45 = (bf16[2,2,40,2048]{3,2,1,0:T(8,128)(2,1)S(1)}, bf16[2,2,40,2048]{3,2,1,0:T(8,128)(2,1)S(1)}, u32[]{:S(2)}, u32[]{:S(2)}) collective-permute-start(bf16[2,2,40,2048]{3,2,1,0:T(8,128)(2,1)S(1)} %fusion.6), channel_id=1, source_target_pairs={{0,8},{8,0},{16,24},{24,16},{1,9},{9,1},{17,25},{25,17},{2,10},{10... | collective-permute-start | bytes 1966088 | tf_op jit(solution)/shard_map/ppermute | solution.py:595
  466.6 22.2 %collective-permute-start.44 = (bf16[2,2,40,1152]{3,2,1,0:T(8,128)(2,1)S(1)}, bf16[2,2,40,1152]{3,2,1,0:T(8,128)(2,1)S(1)}, u32[]{:S(2)}, u32[]{:S(2)}) collective-permute-start(bf16[2,2,40,1152]{3,2,1,0:T(8,128)(2,1)S(1)} %fusion.14), channel_id=1, source_target_pairs={{0,16},{8,24},{16,0},{24,8},{1,17},{9,25},{17,1},{25,9},{2,18},{10... | collective-permute-start | bytes 1105928 | tf_op jit(solution)/shard_map/ppermute | solution.py:595
  469.2 11.8 %collective-permute-start.53 = (bf16[40,2688]{1,0:T(8,128)(2,1)S(1)}, bf16[40,2688]{1,0:T(8,128)(2,1)S(1)}, u32[]{:S(2)}, u32[]{:S(2)}) collective-permute-start(bf16[40,2688]{1,0:T(8,128)(2,1)S(1)} %fusion.20), channel_id=1, source_target_pairs={{0,4},{1,5},{2,6},{3,7},{4,0},{5,1},{6,2},{7,3},{8,12},{9,13},{10,... | collective-permute-start | bytes 645128 | tf_op jit(solution)/shard_map/ppermute | solution.py:595
  485.2 11.0 %collective-permute-start.49 = (bf16[2,40,2048]{2,1,0:T(8,128)(2,1)S(1)}, bf16[2,40,2048]{2,1,0:T(8,128)(2,1)S(1)}, u32[]{:S(2)}, u32[]{:S(2)}) collective-permute-start(bf16[2,40,2048]{2,1,0:T(8,128)(2,1)S(1)} %fusion.16), channel_id=1, source_target_pairs={{0,2},{1,3},{2,0},{3,1},{4,6},{5,7},{6,4},{7,5},{8,10},{9,11},{10,... | collective-permute-start | bytes 983048 | tf_op jit(solution)/shard_map/ppermute | solution.py:595
  486.8 19.6 %collective-permute-start.48 = (bf16[2,40,2048]{2,1,0:T(8,128)(2,1)S(1)}, bf16[2,40,2048]{2,1,0:T(8,128)(2,1)S(1)}, u32[]{:S(2)}, u32[]{:S(2)}) collective-permute-start(bf16[2,40,2048]{2,1,0:T(8,128)(2,1)S(1)} %fusion.15), channel_id=1, source_target_pairs={{0,2},{1,3},{2,0},{3,1},{4,6},{5,7},{6,4},{7,5},{8,10},{9,11},{10,... | collective-permute-start | bytes 983048 | tf_op jit(solution)/shard_map/ppermute | solution.py:595
  489.8 19.7 %collective-permute-start.47 = (bf16[2,40,1152]{2,1,0:T(8,128)(2,1)S(1)}, bf16[2,40,1152]{2,1,0:T(8,128)(2,1)S(1)}, u32[]{:S(2)}, u32[]{:S(2)}) collective-permute-start(bf16[2,40,1152]{2,1,0:T(8,128)(2,1)S(1)} %fusion.21), channel_id=1, source_target_pairs={{0,2},{1,3},{2,0},{3,1},{4,6},{5,7},{6,4},{7,5},{8,10},{9,11},{10,... | collective-permute-start | bytes 552968 | tf_op jit(solution)/shard_map/ppermute | solution.py:595
  491.7 35.4 %collective-permute-start.54 = (bf16[320,1792]{1,0:T(8,128)(2,1)S(1)}, bf16[320,1792]{1,0:T(8,128)(2,1)}, u32[]{:S(2)}, u32[]{:S(2)}) collective-permute-start(bf16[320,1792]{1,0:T(8,128)(2,1)S(1)} %fusion.8), channel_id=1, source_target_pairs={{0,16},{8,24},{16,0},{24,8},{1,17},{9,25},{17,1},{25,9},{2,18},{10... | collective-permute-start | bytes 3440648 | tf_op jit(solution)/shard_map/ppermute | solution.py:595
  494.7 32.4 %collective-permute-start.55 = (bf16[320,1792]{1,0:T(8,128)(2,1)}, bf16[320,1792]{1,0:T(8,128)(2,1)}, u32[]{:S(2)}, u32[]{:S(2)}) collective-permute-start(bf16[320,1792]{1,0:T(8,128)(2,1)} %fusion.9), channel_id=1, source_target_pairs={{0,8},{8,0},{16,24},{24,16},{1,9},{9,1},{17,25},{25,17},{2,10},{10... | collective-permute-start | bytes 3440648 | tf_op jit(solution)/shard_map/ppermute | solution.py:595
  498.2 25.6 %collective-permute-start.51 = (bf16[40,2048]{1,0:T(8,128)(2,1)}, bf16[40,2048]{1,0:T(8,128)(2,1)}, u32[]{:S(2)}, u32[]{:S(2)}) collective-permute-start(bf16[40,2048]{1,0:T(8,128)(2,1)} %fusion.25), channel_id=1, source_target_pairs={{0,4},{1,5},{2,6},{3,7},{4,0},{5,1},{6,2},{7,3},{8,12},{9,13},{10,... | collective-permute-start | bytes 491528 | tf_op jit(solution)/shard_map/ppermute | solution.py:595
  508.2 17.1 %collective-permute-start.52 = (bf16[40,2048]{1,0:T(8,128)(2,1)}, bf16[40,2048]{1,0:T(8,128)(2,1)}, u32[]{:S(2)}, u32[]{:S(2)}) collective-permute-start(bf16[40,2048]{1,0:T(8,128)(2,1)} %fusion.24), channel_id=1, source_target_pairs={{0,4},{1,5},{2,6},{3,7},{4,0},{5,1},{6,2},{7,3},{8,12},{9,13},{10,... | collective-permute-start | bytes 491528 | tf_op jit(solution)/shard_map/ppermute | solution.py:595
  510.5 8.9 %collective-permute-start.50 = (bf16[40,1152]{1,0:T(8,128)(2,1)S(1)}, bf16[40,1152]{1,0:T(8,128)(2,1)S(1)}, u32[]{:S(2)}, u32[]{:S(2)}) collective-permute-start(bf16[40,1152]{1,0:T(8,128)(2,1)S(1)} %fusion.28), channel_id=1, source_target_pairs={{0,4},{1,5},{2,6},{3,7},{4,0},{5,1},{6,2},{7,3},{8,12},{9,13},{10,... | collective-permute-start | bytes 276488 | tf_op jit(solution)/shard_map/ppermute | solution.py:595
  (67 other events, 530.3 us)

commit v5 on v4

--- a/solution.py
+++ b/solution.py
@@ -184,6 +184,9 @@
     tail_args = ((dh1_in,) if carried else ()) + tuple(tail_args)
     whole_args = (da, lse, cosine, sine, h1, att) + tail_args
     spec = {id(a): whole(a) for a in whole_args}
+    *held, h1_held, att_held = (
+        pltpu.with_memory_space_constraint(a, pltpu.HBM) for a in (q, k, v, h1, att)
+    )
     return pl.pallas_call(
         lambda *r: attention_back_kernel(rows, extra, carried, *r),
         grid=(count,),
@@ -199,8 +202,8 @@
         cost_estimate=pl.CostEstimate(flops=0, bytes_accessed=0, transcendentals=0),
         name="attention_backward",
     )(
-        jnp.concatenate([lengths, jnp.full((1,), first, jnp.int32)]), core, da, w_out, q, k, v,
-        lse, cosine, sine, h1, att, w_qkv, w_qkv, w_qkv, *tail_args,
+        jnp.concatenate([lengths, jnp.full((1,), first, jnp.int32)]), core, da, w_out, *held,
+        lse, cosine, sine, h1_held, att_held, w_qkv, w_qkv, w_qkv, *tail_args,
     )
 
 
@@ -542,6 +545,34 @@
     angles = jnp.arange(seq_slots, dtype=jnp.float32)[:, None] * inv_freq[None, :]
     cosine, sine = jnp.cos(angles), jnp.sin(angles)
     return jnp.concatenate([cosine, cosine], axis=1), jnp.concatenate([-sine, sine], axis=1)
+
+
+def assemble_kernel(wide, *refs):
+    *pieces, qkv, out = refs
+    pair, pairs = 0, out.shape[1] // wide
+    for piece, count in zip(pieces, (pairs // 2, pairs // 2, pairs - 2 * (pairs // 2))):
+        step = piece.shape[1] // count
+        for at in range(count):
+            for kind in range(4):
+                block = piece[:, at * step + kind * wide : at * step + (kind + 1) * wide]
+                if kind < 3:
+                    qkv[:, pl.ds((kind * pairs + pair) * wide, wide)] = block
+                else:
+                    out[:, pl.ds(pair * wide, wide)] = block
+            pair += 1
+
+
+def assemble(pieces, width):
+    rows = pieces[0].shape[0]
+    vmem = pl.BlockSpec(memory_space=pltpu.VMEM)
+    return pl.pallas_call(
+        lambda *r: assemble_kernel(2 * HEAD_DIM, *r),
+        in_specs=[vmem] * len(pieces),
+        out_specs=[vmem] * 2,
+        out_shape=[jax.ShapeDtypeStruct((rows, n), jnp.float32) for n in (3 * width, width)],
+        cost_estimate=pl.CostEstimate(flops=0, bytes_accessed=0, transcendentals=0),
+        name="assemble",
+    )(*pieces)
 
 
 def swap_cores(values_in):
@@ -823,10 +854,7 @@
     fence = landed
     hops = 2
     first_cols, second_cols, third_cols = scatters
-    plan = [first_cols, second_cols, None, third_cols, shared_scatter]
-    plan += [first_cols, second_cols, third_cols, shared_scatter, None]
-    plan += [first_cols, second_cols, third_cols] + in_scatters
-    plan += [first_cols, second_cols, third_cols]
+    plan = [first_cols, second_cols, None, third_cols, shared_scatter, first_cols, second_cols, third_cols, shared_scatter, None, first_cols, second_cols, third_cols, in_scatters[0], in_scatters[1], first_cols, second_cols, third_cols]
     for scatter in plan:
         if scatter is not None:
             if scatter.order:
@@ -840,25 +868,15 @@
     for hops in range(hops, chips):
         routed = add_routed(hops, out_hop, *fence)
         out_hop = next_chip(routed.astype(jnp.bfloat16))
-    for scatter in down_scatters + in_scatters:
+    for scatter in down_scatters + in_scatters + [shared_scatter]:
         scatter.terms = after(scatter.terms, *fence)
     result = (x_mid + live_col * (shared_out + routed)).astype(jnp.bfloat16)
     shared_sum = shared_scatter.finish()
     expert_in_sum = jnp.stack([scatter.finish() for scatter in in_scatters])
     expert_down_sum = jnp.stack([scatter.finish() for scatter in down_scatters])
-    wide = 2 * HEAD_DIM
-    blocks = []
-    for scatter, first, last in zip(scatters, cuts[:-1], cuts[1:]):
-        piece = scatter.finish()
-        step = piece.shape[1] // (last - first)
-        blocks += [piece[:, at * step : (at + 1) * step] for at in range(last - first)]
-    small_sum = blocks[-1][:, 4 * wide :]
-    qkv_sum, out_sum = (
-        jnp.concatenate(
-            [block[:, k * wide : (k + 1) * wide] for k in kinds for block in blocks], axis=1
-        )
-        for kinds in ((0, 1, 2), (3,))
-    )
+    pieces = [scatter.finish() for scatter in scatters]
+    qkv_sum, out_sum = assemble(pieces, width)
+    small_sum = pieces[-1][:, 8 * HEAD_DIM :]
     counts = jnp.sum(
         small_sum[:, experts + 2 : 2 * experts + 2] * (1 << places).astype(jnp.float32)[:, None],
         axis=0,

time: 541 us -> 540 us (level)
  waiting for transfers between devices: 127 us -> 119 us
  other arithmetic: 65.8 us -> 73.5 us
    ppermute x20, waiting for transfers between devices: 51.8 us -> 41.7 us  [advance(): lax.ppermute(away, name, [(i, i ^ 1 << bit) for i in range(lax.axis_size(...]
    unnamed x167 -> x135, local copies, waits for them, and re-layouts: 19.9 us -> 16.5 us
  transfers between devices with their start and end apart: 56 -> 56, of which waited for: 20 -> 18; matrix products, arithmetic and copies ran while one was open for 11% -> 12% of each run, Pallas kernels for 51% -> 51%
where the time goes in v5:
time: 540 us; the launch traced here: 533 us
  Pallas kernels  277 us (51%)
  waiting for transfers between devices  119 us (22%)
  other arithmetic  73.5 us (14%)
  starting transfers between devices  42.7 us (8%)
  local copies, waits for them, and re-layouts  18.8 us (3%)
    pallas_call x4, Pallas kernels, expert_step(): pl.pallas_call(lambda *r: expert_kernel(cap, tokens, hidden, None, *r), g...  127 us
    ppermute x12, waiting for transfers between devices, next_chip(): lax.ppermute(values_in, 'expert', [(i, (i + 2) % owners) for i in range(o...  54 us
    pallas_call x3, Pallas kernels, attention_backward(): pl.pallas_call(lambda *r: attention_back_kernel(rows, extra, carried, *r)...  48.7 us
    pallas_call x4, Pallas kernels, weight_grad(): pl.pallas_call(lambda *r: weight_grad_kernel(parts, bit, *r), grid=(n //...  46.6 us
    ppermute x20, waiting for transfers between devices, advance(): lax.ppermute(away, name, [(i, i ^ 1 << bit) for i in range(lax.axis_size(...  41.7 us
    convert_element_type x20, other arithmetic, advance(): away = sum_terms([picked(term, made + [(dim, 1 - mine)]) for term, made i...  36.6 us
    pallas_call x1, Pallas kernels, attention_forward(): pl.pallas_call(attention_kernel, grid=(pairs,), in_specs=[pl.BlockSpec(me...  23.1 us
    ppermute x20, waiting for transfers between devices, swap_cores(): lax.ppermute(values_in, 'expert', [(i, i ^ 1) for i in range(owners)])  22.9 us
  transfers between devices with their start and end apart: 56, of which 18 were waited for; matrix products, arithmetic and copies ran while one was open for 12% of the time, Pallas kernels for 51%

profile of v5, /device:TPU:0, one launch (start us, length us, event | category | flops | bytes accessed | tf_op | source)
XLA Modules:
  0.0 533.0 jit_solution(17015627674733052304)
XLA Ops:
  1.3 1.6 copy.72.ids
  2.9 3.5 token_rows.1.r_3_.r_2_
  6.8 2.6 collective-permute-start
  10.8 23.1 %attention_forward.1 = (bf16[512,1280]{1,0:T(8,128)(2,1)}, bf16[512,1280]{1,0:T(8,128)(2,1)}, bf16[512,1280]{1,0:T(8,128)(2,1)}, bf16[512,1280]{1,0:T(8,128)(2,1...) custom-call(s32[1]{0:T(128)} %copy.133.length_ref.r_0_, ...), custom_call_target="tpu_custom_call" | custom-call | tf_op jit(solution)/shard_map/attention_forward/pallas_call | solution.py:80
  34.1 1.6 collective-permute-start.4
  35.7 6.6 %collective-permute-done.r_3_ = bf16[528,1280]{1,0:T(8,128)(2,1)} collective-permute-done((bf16[528,1280]{1,0:T(8,128)(2,1)}, bf16[528,1280]{1,0:T(8,128)(2,1)}, u32[]{:S(2)}, u32[]{:S(2)}) %collective-permute-start) | collective-permute-done | bytes 1351712 | tf_op jit(solution)/shard_map/ppermute | solution.py:585
  47.3 31.3 %expert_step.4 = (bf16[544,1280]{1,0:T(8,128)(2,1)}, bf16[544,1280]{1,0:T(8,128)(2,1)}, bf16[512,1280]{1,0:T(8,128)(2,1)}, bf16[512,1280]{1,0:T(8,128)(2,1)}, bf...) custom-call(s32[1]{0:T(128)} %bitcast.2.r_0_, ...), custom_call_target="tpu_custom_call" | custom-call | tf_op jit(solution)/shard_map/expert_step/pallas_call | solution.py:332
  78.6 17.3 %shared_expert.1 = (f32[512,1280]{1,0:T(8,128)}, f32[512,1280]{1,0:T(8,128)}, f32[512,128]{1,0:T(8,128)S(1)}, bf16[640,2688]{1,0:T(8,128)(2,1)}, bf16[640,2688]{1,0:T(8,128)(2,1)}) custom-call(s32[1]{0:T(128)} %bitcast.1.r_0_.r_1_, bf16[512,1280]{1,0:T(8,128)(2,1)S(1)} %copy-done.3, bf16[528,1280]{1,0:T(8,128)(2,1)S(1)} %copy-done.2, ...), custom_call_target="tpu_custom_call" | custom-call | tf_op jit(solution)/shard_map/shared_expert/pallas_call | solution.py:449
  97.2 2.9 collective-permute-done.5.r_2_
  102.7 1.6 collective-permute-start.10
  105.6 32.0 %expert_step.5 = (bf16[544,1280]{1,0:T(8,128)(2,1)}, bf16[544,1280]{1,0:T(8,128)(2,1)}, bf16[512,1280]{1,0:T(8,128)(2,1)}, bf16[512,1280]{1,0:T(8,128)(2,1)}, bf...) custom-call(s32[1]{0:T(128)} %bitcast.2.r_0_, ...), custom_call_target="tpu_custom_call", output_to_operand_aliasing={{4}: (8, {}), {5}: (9, {}), {6}: (10, {}), {7}: (11, {})} | custom-call | tf_op jit(solution)/shard_map/expert_step/pallas_call | solution.py:332
  137.6 25.9 %collective-permute-done.10.r_1_ = bf16[512,1280]{1,0:T(8,128)(2,1)} collective-permute-done((bf16[512,1280]{1,0:T(8,128)(2,1)}, bf16[512,1280]{1,0:T(8,128)(2,1)}, u32[]{:S(2)}, u32[]{:S(2)}) %collective-permute-start.10) | collective-permute-done | bytes 1310752 | tf_op jit(solution)/shard_map/ppermute | solution.py:585
  163.6 3.3 fusion.2
  167.3 1.6 collective-permute-start.9
  169.0 2.3 collective-permute-done.12
  172.8 3.1 add_convert_fusion.8
  176.0 32.5 %expert_step.6 = (bf16[544,1280]{1,0:T(8,128)(2,1)}, bf16[544,1280]{1,0:T(8,128)(2,1)}, bf16[512,1280]{1,0:T(8,128)(2,1)}, bf16[512,1280]{1,0:T(8,128)(2,1)}, bf...) custom-call(s32[1]{0:T(128)} %bitcast.2.r_0_, ...), custom_call_target="tpu_custom_call", output_to_operand_aliasing={{4}: (8, {}), {5}: (9, {}), {6}: (10, {}), {7}: (11, {})} | custom-call | tf_op jit(solution)/shard_map/expert_step/pallas_call | solution.py:332
  208.6 2.1 fusion.3
  210.7 21.4 %collective-permute-done.18 = bf16[544,1280]{1,0:T(8,128)(2,1)} collective-permute-done((bf16[544,1280]{1,0:T(8,128)(2,1)}, bf16[544,1280]{1,0:T(8,128)(2,1)}, u32[]{:S(2)}, u32[]{:S(2)}) %collective-permute-start.18) | collective-permute-done | bytes 1392672 | tf_op jit(solution)/shard_map/ppermute | solution.py:585
  232.1 3.1 collective-permute-done.19
  235.3 1.9 add_convert_fusion.2
  242.7 31.4 %expert_step.7 = (bf16[544,1280]{1,0:T(8,128)(2,1)}, bf16[544,1280]{1,0:T(8,128)(2,1)}, bf16[512,1280]{1,0:T(8,128)(2,1)}, bf16[512,1280]{1,0:T(8,128)(2,1)}, bf...) custom-call(s32[1]{0:T(128)} %bitcast.2.r_0_, ...), custom_call_target="tpu_custom_call", output_to_operand_aliasing={{4}: (8, {}), {5}: (9, {}), {6}: (10, {}), {7}: (11, {})} | custom-call | tf_op jit(solution)/shard_map/expert_step/pallas_call | solution.py:332
  274.3 3.2 collective-permute-done.24
  277.5 1.9 add_convert_fusion.1
  280.5 8.3 %weight_grad.4 = (bf16[448,1280]{1,0:T(8,128)(2,1)S(1)}, bf16[448,1280]{1,0:T(8,128)(2,1)S(1)}) custom-call(s32[1]{0:T(128)} %bitcast.9.r_0_, bf16[2,1920,896]{2,1,0:T(8,128)(2,1)} %get-tuple-element.293.r_1_, bf16[2,1920,1280]{2,1,0:T(8,128)(2,1)} %get-tuple-element.290.r_2_), custom_call_target="tpu_custom_call" | custom-call | tf_op jit(solution)/shard_map/weight_grad/pallas_call | solution.py:526
  288.9 8.7 %weight_grad.5 = (bf16[448,1280]{1,0:T(8,128)(2,1)S(1)}, bf16[448,1280]{1,0:T(8,128)(2,1)S(1)}) custom-call(s32[1]{0:T(128)} %bitcast.9.r_0_, bf16[2,1920,896]{2,1,0:T(8,128)(2,1)} %get-tuple-element.293.r_1_, bf16[2,1920,1280]{2,1,0:T(8,128)(2,1)} %get-tuple-element.290.r_2_), custom_call_target="tpu_custom_call" | custom-call | tf_op jit(solution)/shard_map/weight_grad/pallas_call | solution.py:526
  297.6 1.6 collective-permute-start.27
  299.8 14.8 %weight_grad.6 = (bf16[640,1792]{1,0:T(8,128)(2,1)S(1)}, bf16[640,1792]{1,0:T(8,128)(2,1)}) custom-call(s32[1]{0:T(128)} %bitcast.9.r_0_, bf16[2,1920,1280]{2,1,0:T(8,128)(2,1)} %get-tuple-element.301.r_1_, bf16[2,1920,1792]{2,1,0:T(8,128)(2,1)} %get-tuple-element.298.r_2_), custom_call_target="tpu_custom_call" | custom-call | tf_op jit(solution)/shard_map/weight_grad/pallas_call | solution.py:526
  316.0 14.7 %weight_grad.7 = (bf16[640,1792]{1,0:T(8,128)(2,1)S(1)}, bf16[640,1792]{1,0:T(8,128)(2,1)}) custom-call(s32[1]{0:T(128)} %bitcast.9.r_0_, bf16[2,1920,1280]{2,1,0:T(8,128)(2,1)} %get-tuple-element.301.r_1_, bf16[2,1920,1792]{2,1,0:T(8,128)(2,1)} %get-tuple-element.298.r_2_), custom_call_target="tpu_custom_call" | custom-call | tf_op jit(solution)/shard_map/weight_grad/pallas_call | solution.py:526
  332.1 1.6 collective-permute-start.30
  335.8 2.0 fusion.17
  337.9 2.0 fusion.18
  339.9 8.6 %middle_back.1 = (f32[512,1280]{1,0:T(8,128)}, bf16[512,1280]{1,0:T(8,128)(2,1)S(1)}, f32[1280,128]{1,0:T(8,128)S(1)}) custom-call(s32[1]{0:T(128)} %copy.133.length_ref.r_0_, bf16[544,1280]{1,0:T(8,128)(2,1)} %get-tuple-element.310.r_1_, bf16[544,1280]{1,0:T(8,128)(2,1)} %copy-done.39, bf16[544,1280]{1,0:T(8,128)(2,1)} %copy-done.40, ...), custom_call_target="tpu_custom_call" | custom-call | tf_op jit(solution)/shard_map/middle_back/pallas_call | solution.py:494
  348.5 16.9 %attention_backward.3 = (bf16[640,2048]{1,0:T(8,128)(2,1)S(1)}, bf16[640,2048]{1,0:T(8,128)(2,1)}, f32[512,1280]{1,0:T(8,128)}) custom-call(s32[2]{0:T(128)S(1)} %pad_add_fusion.3.r_0_, s32[1]{0:T(128)} %bitcast.1.r_0_.r_1_, bf16[512,1280]{1,0:T(8,128)(2,1)S(1)} %get-tuple-element.330.r_2_, bf16[1280,1280]{1,0:T(8,128)(2,1)} %r_3_.7, ...), custom_call_target="tpu_custom_call" | custom-call | tf_op jit(solution)/shard_map/attention_backward/pallas_call | solution.py:190
  365.6 1.8 add_convert_fusion.7
  367.4 4.0 collective-permute-start.31
  372.1 1.7 collective-permute-start.34
  375.2 17.7 %attention_backward.4 = (bf16[640,2048]{1,0:T(8,128)(2,1)S(1)}, bf16[640,2048]{1,0:T(8,128)(2,1)}, f32[512,1280]{1,0:T(8,128)}) custom-call(s32[2]{0:T(128)S(1)} %get-tuple-element.476.r_0_, s32[1]{0:T(128)} %bitcast.1.r_0_.r_1_, bf16[512,1280]{1,0:T(8,128)(2,1)S(1)} %get-tuple-element.330.r_2_, bf16[1280,1280]{1,0:T(8,128)(2,1)} %r_3_.7, ...), custom_call_target="tpu_custom_call" | custom-call | tf_op jit(solution)/shard_map/attention_backward/pallas_call | solution.py:190
  394.4 14.0 %attention_backward.5 = (bf16[640,1152]{1,0:T(8,128)(2,1)S(1)}, bf16[640,1152]{1,0:T(8,128)(2,1)}, f32[512,1280]{1,0:T(8,128)}) custom-call(s32[2]{0:T(128)S(1)} %get-tuple-element.475.r_0_, s32[1]{0:T(128)} %bitcast.1.r_0_.r_1_, bf16[512,1280]{1,0:T(8,128)(2,1)S(1)} %get-tuple-element.330.r_2_, bf16[1280,1280]{1,0:T(8,128)(2,1)} %r_3_.7, ...), custom_call_target="tpu_custom_call" | custom-call | tf_op jit(solution)/shard_map/attention_backward/pallas_call | solution.py:190
  411.2 8.3 %collective-permute-done.38 = bf16[640,2048]{1,0:T(8,128)(2,1)S(1)} collective-permute-done((bf16[640,2048]{1,0:T(8,128)(2,1)}, bf16[640,2048]{1,0:T(8,128)(2,1)S(1)}, u32[]{:S(2)}, u32[]{:S(2)}) %collective-permute-start.38) | collective-permute-done | bytes 2621472 | tf_op jit(solution)/shard_map/ppermute | solution.py:580
  419.5 2.8 fusion.4
  423.8 1.9 fusion.5
  426.3 2.4 convert_add_fusion.1
  433.6 20.4 %collective-permute-done.42 = bf16[2,2,2,40,2048]{4,3,2,1,0:T(8,128)(2,1)S(1)} collective-permute-done((bf16[2,2,2,40,2048]{4,3,2,1,0:T(8,128)(2,1)S(1)}, bf16[2,2,2,40,2048]{4,3,2,1,0:T(8,128)(2,1)S(1)}, u32[]{:S(2)}, u32[]{:S(2)}) %collective-permute-start.42) | collective-permute-done | bytes 1310752 | tf_op jit(solution)/shard_map/ppermute | solution.py:626
  454.0 1.9 fusion.7
  456.3 1.9 fusion.6
  458.3 1.7 collective-permute-start.45
  460.0 9.8 %collective-permute-done.40 = bf16[2,2,2,40,1152]{4,3,2,1,0:T(8,128)(2,1)S(1)} collective-permute-done((bf16[2,2,2,40,1152]{4,3,2,1,0:T(8,128)(2,1)S(1)}, bf16[2,2,2,40,1152]{4,3,2,1,0:T(8,128)(2,1)S(1)}, u32[]{:S(2)}, u32[]{:S(2)}) %collective-permute-start.40) | collective-permute-done | bytes 737312 | tf_op jit(solution)/shard_map/ppermute | solution.py:626
  473.3 3.3 add_convert_fusion.4
  478.7 4.4 collective-permute-done.45
  485.8 1.7 collective-permute-start.47
  487.6 2.7 fusion.8
  490.6 2.6 fusion.9
  493.2 1.7 collective-permute-start.55
  494.9 1.7 fusion.25
  498.1 1.8 fusion.24
  502.0 1.7 collective-permute-start.50
  514.7 4.5 collective-permute-done.52
  519.3 2.2 fusion.22.r_1_
  521.5 2.0 fusion.23.r_0_
  523.5 2.1 assemble.1
  525.5 2.5 fusion
  528.2 2.1 fusion.1
  530.3 2.4 pad_maximum_fusion
  (257 shorter events, 63.8 us)
Async XLA Ops:
  6.4 37.5 %collective-permute-start.2 = (bf16[528,1280]{1,0:T(8,128)(2,1)}, bf16[528,1280]{1,0:T(8,128)(2,1)}, u32[]{:S(2)}, u32[]{:S(2)}) collective-permute-start(bf16[528,1280]{1,0:T(8,128)(2,1)} %token_rows.1.r_3_.r_2_), channel_id=1, source_target_pairs={{0,1},{1,0},{2,3},{3,2},{4,5},{5,4},{6,7},{7,6},{8,9},{9,8},{10,11... | collective-permute-start | bytes 4055048 | tf_op jit(solution)/shard_map/ppermute | solution.py:580
  6.8 35.5 %collective-permute-start = (bf16[528,1280]{1,0:T(8,128)(2,1)}, bf16[528,1280]{1,0:T(8,128)(2,1)}, u32[]{:S(2)}, u32[]{:S(2)}) collective-permute-start(bf16[528,1280]{1,0:T(8,128)(2,1)} %token_rows.1.r_3_.r_2_), channel_id=1, source_target_pairs={{0,2},{1,3},{2,4},{3,5},{4,6},{5,7},{6,0},{7,1},{8,10},{9,11},{10,... | collective-permute-start | bytes 4055048 | tf_op jit(solution)/shard_map/ppermute | solution.py:585
  33.9 10.0 %collective-permute-start.1 = (bf16[512,1280]{1,0:T(8,128)(2,1)}, bf16[512,1280]{1,0:T(8,128)(2,1)S(1)}, u32[]{:S(2)}, u32[]{:S(2)}) collective-permute-start(bf16[512,1280]{1,0:T(8,128)(2,1)} %get-tuple-element.227.r_1_.r_6_), channel_id=1, source_target_pairs={{0,1},{1,0},{2,3},{3,2},{4,5},{5,4},{6,7},{7,6},{8,9},{9,8},{10,11... | collective-permute-start | bytes 3932168 | tf_op jit(solution)/shard_map/ppermute | solution.py:580
  34.1 62.5 %collective-permute-start.4 = (bf16[512,1280]{1,0:T(8,128)(2,1)}, bf16[512,1280]{1,0:T(8,128)(2,1)}, u32[]{:S(2)}, u32[]{:S(2)}) collective-permute-start(bf16[512,1280]{1,0:T(8,128)(2,1)} %get-tuple-element.227.r_1_.r_6_), channel_id=1, source_target_pairs={{0,2},{1,3},{2,4},{3,5},{4,6},{5,7},{6,0},{7,1},{8,10},{9,11},{10,... | collective-permute-start | bytes 3932168 | tf_op jit(solution)/shard_map/ppermute | solution.py:585
  42.3 58.8 %collective-permute-start.6 = (bf16[528,1280]{1,0:T(8,128)(2,1)}, bf16[528,1280]{1,0:T(8,128)(2,1)}, u32[]{:S(2)}, u32[]{:S(2)}) collective-permute-start(bf16[528,1280]{1,0:T(8,128)(2,1)} %collective-permute-done.r_3_), channel_id=1, source_target_pairs={{0,1},{1,0},{2,3},{3,2},{4,5},{5,4},{6,7},{7,6},{8,9},{9,8},{10,11... | collective-permute-start | bytes 4055048 | tf_op jit(solution)/shard_map/ppermute | solution.py:580
  42.3 58.8 %collective-permute-start.3 = (bf16[528,1280]{1,0:T(8,128)(2,1)}, bf16[528,1280]{1,0:T(8,128)(2,1)}, u32[]{:S(2)}, u32[]{:S(2)}) collective-permute-start(bf16[528,1280]{1,0:T(8,128)(2,1)} %collective-permute-done.r_3_), channel_id=1, source_target_pairs={{0,2},{1,3},{2,4},{3,5},{4,6},{5,7},{6,0},{7,1},{8,10},{9,11},{10,... | collective-permute-start | bytes 4055048 | tf_op jit(solution)/shard_map/ppermute | solution.py:585
  47.3 31.3 %copy-start.2 = (bf16[528,1280]{1,0:T(8,128)(2,1)S(1)}, bf16[528,1280]{1,0:T(8,128)(2,1)}, u32[]{:S(2)}) copy-start(bf16[528,1280]{1,0:T(8,128)(2,1)} %token_rows.1.r_3_.r_2_) | copy-start | bytes 4055044
  47.3 31.3 %copy-start.21 = (bf16[896,1280]{1,0:T(8,128)(2,1)S(1)}, bf16[896,1280]{1,0:T(8,128)(2,1)}, u32[]{:S(2)}) copy-start(bf16[896,1280]{1,0:T(8,128)(2,1)} %r_4_.1) | copy-start | bytes 6881284
  96.7 3.4 collective-permute-start.5
  101.1 62.4 %collective-permute-start.8 = (bf16[640,2688]{1,0:T(8,128)(2,1)}, bf16[640,2688]{1,0:T(8,128)(2,1)}, u32[]{:S(2)}, u32[]{:S(2)}) collective-permute-start(bf16[640,2688]{1,0:T(8,128)(2,1)} %get-tuple-element.236), channel_id=1, source_target_pairs={{0,1},{1,0},{2,3},{3,2},{4,5},{5,4},{6,7},{7,6},{8,9},{9,8},{10,11... | collective-permute-start | bytes 10321928 | tf_op jit(solution)/shard_map/ppermute | solution.py:580
  101.5 62.0 %collective-permute-start.11 = (bf16[528,1280]{1,0:T(8,128)(2,1)}, bf16[528,1280]{1,0:T(8,128)(2,1)S(1)}, u32[]{:S(2)}, u32[]{:S(2)}) collective-permute-start(bf16[528,1280]{1,0:T(8,128)(2,1)} %collective-permute-done.3.r_3_), channel_id=1, source_target_pairs={{0,2},{1,3},{2,4},{3,5},{4,6},{5,7},{6,0},{7,1},{8,10},{9,11},{10,... | collective-permute-start | bytes 4055048 | tf_op jit(solution)/shard_map/ppermute | solution.py:585
  102.7 60.8 %collective-permute-start.10 = (bf16[512,1280]{1,0:T(8,128)(2,1)}, bf16[512,1280]{1,0:T(8,128)(2,1)}, u32[]{:S(2)}, u32[]{:S(2)}) collective-permute-start(bf16[512,1280]{1,0:T(8,128)(2,1)} %collective-permute-done.4.r_1_), channel_id=1, source_target_pairs={{0,2},{1,3},{2,4},{3,5},{4,6},{5,7},{6,0},{7,1},{8,10},{9,11},{10,... | collective-permute-start | bytes 3932168 | tf_op jit(solution)/shard_map/ppermute | solution.py:585
  104.3 59.2 %collective-permute-start.7 = (bf16[512,1280]{1,0:T(8,128)(2,1)}, bf16[512,1280]{1,0:T(8,128)(2,1)}, u32[]{:S(2)}, u32[]{:S(2)}) collective-permute-start(bf16[512,1280]{1,0:T(8,128)(2,1)} %get-tuple-element.232), channel_id=1, source_target_pairs={{0,1},{1,0},{2,3},{3,2},{4,5},{5,4},{6,7},{7,6},{8,9},{9,8},{10,11... | collective-permute-start | bytes 3932168 | tf_op jit(solution)/shard_map/ppermute | solution.py:580
  105.6 57.9 %copy-start.36 = (bf16[640,2688]{1,0:T(8,128)(2,1)S(1)}, bf16[640,2688]{1,0:T(8,128)(2,1)}, u32[]{:S(2)}) copy-start(bf16[640,2688]{1,0:T(8,128)(2,1)} %get-tuple-element.235) | copy-start | bytes 10321924
  166.8 4.4 collective-permute-start.12
  166.8 6.0 %collective-permute-start.17 = (bf16[512,1280]{1,0:T(8,128)(2,1)S(1)}, bf16[512,1280]{1,0:T(8,128)(2,1)}, u32[]{:S(2)}, u32[]{:S(2)}) collective-permute-start(bf16[512,1280]{1,0:T(8,128)(2,1)S(1)} %copy-done.65), channel_id=1, source_target_pairs={{0,1},{1,0},{2,3},{3,2},{4,5},{5,4},{6,7},{7,6},{8,9},{9,8},{10,11... | collective-permute-start | bytes 3932168 | tf_op jit(solution)/shard_map/ppermute | solution.py:580
  167.3 41.2 %collective-permute-start.9 = (bf16[2,2,2,40,2688]{4,3,2,1,0:T(8,128)(2,1)}, bf16[2,2,2,40,2688]{4,3,2,1,0:T(8,128)(2,1)}, u32[]{:S(2)}, u32[]{:S(2)}) collective-permute-start(bf16[2,2,2,40,2688]{4,3,2,1,0:T(8,128)(2,1)} %fusion.2), channel_id=1, source_target_pairs={{0,8},{8,0},{16,24},{24,16},{1,9},{9,1},{17,25},{25,17},{2,10},{10... | collective-permute-start | bytes 5160968 | tf_op jit(solution)/shard_map/ppermute | solution.py:626
  169.0 7.0 %collective-permute-start.14 = (bf16[528,1280]{1,0:T(8,128)(2,1)}, bf16[528,1280]{1,0:T(8,128)(2,1)}, u32[]{:S(2)}, u32[]{:S(2)}) collective-permute-start(bf16[528,1280]{1,0:T(8,128)(2,1)} %collective-permute-done.3.r_3_), channel_id=1, source_target_pairs={{0,1},{1,0},{2,3},{3,2},{4,5},{5,4},{6,7},{7,6},{8,9},{9,8},{10,11... | collective-permute-start | bytes 4055048 | tf_op jit(solution)/shard_map/ppermute | solution.py:580
  169.0 39.6 %collective-permute-start.16 = (bf16[512,1280]{1,0:T(8,128)(2,1)}, bf16[512,1280]{1,0:T(8,128)(2,1)}, u32[]{:S(2)}, u32[]{:S(2)}) collective-permute-start(bf16[512,1280]{1,0:T(8,128)(2,1)} %collective-permute-done.10.r_1_), channel_id=1, source_target_pairs={{0,2},{1,3},{2,4},{3,5},{4,6},{5,7},{6,0},{7,1},{8,10},{9,11},{10,... | collective-permute-start | bytes 3932168 | tf_op jit(solution)/shard_map/ppermute | solution.py:585
  171.2 4.8 collective-permute-start.13
  172.8 59.3 %collective-permute-start.18 = (bf16[544,1280]{1,0:T(8,128)(2,1)}, bf16[544,1280]{1,0:T(8,128)(2,1)}, u32[]{:S(2)}, u32[]{:S(2)}) collective-permute-start(bf16[544,1280]{1,0:T(8,128)(2,1)} %add_convert_fusion.3), channel_id=1, source_target_pairs={{0,2},{1,3},{2,4},{3,5},{4,6},{5,7},{6,0},{7,1},{8,10},{9,11},{10,... | collective-permute-start | bytes 4177928 | tf_op jit(solution)/shard_map/ppermute | solution.py:585
  208.6 26.7 %copy-start.41 = (bf16[544,1280]{1,0:T(8,128)(2,1)S(1)}, bf16[544,1280]{1,0:T(8,128)(2,1)}, u32[]{:S(2)}) copy-start(bf16[544,1280]{1,0:T(8,128)(2,1)} %get-tuple-element.257) | copy-start | bytes 4177924
  232.1 3.2 collective-permute-start.19
  237.2 36.9 %collective-permute-start.23 = (bf16[544,1280]{1,0:T(8,128)(2,1)S(1)}, bf16[544,1280]{1,0:T(8,128)(2,1)S(1)}, u32[]{:S(2)}, u32[]{:S(2)}) collective-permute-start(bf16[544,1280]{1,0:T(8,128)(2,1)S(1)} %add_convert_fusion.2), channel_id=1, source_target_pairs={{0,2},{1,3},{2,4},{3,5},{4,6},{5,7},{6,0},{7,1},{8,10},{9,11},{10,... | collective-permute-start | bytes 4177928 | tf_op jit(solution)/shard_map/ppermute | solution.py:585
  237.4 3.7 collective-permute-start.21
  237.6 5.0 collective-permute-start.20
  238.0 36.1 %collective-permute-start.22 = (bf16[512,1280]{1,0:T(8,128)(2,1)}, bf16[512,1280]{1,0:T(8,128)(2,1)S(1)}, u32[]{:S(2)}, u32[]{:S(2)}) collective-permute-start(bf16[512,1280]{1,0:T(8,128)(2,1)} %get-tuple-element.283), channel_id=1, source_target_pairs={{0,1},{1,0},{2,3},{3,2},{4,5},{5,4},{6,7},{7,6},{8,9},{9,8},{10,11... | collective-permute-start | bytes 3932168 | tf_op jit(solution)/shard_map/ppermute | solution.py:580
  238.1 35.9 %collective-permute-start.15 = (bf16[2,2,40,2688]{3,2,1,0:T(8,128)(2,1)S(1)}, bf16[2,2,40,2688]{3,2,1,0:T(8,128)(2,1)S(1)}, u32[]{:S(2)}, u32[]{:S(2)}) collective-permute-start(bf16[2,2,40,2688]{3,2,1,0:T(8,128)(2,1)S(1)} %fusion.3), channel_id=1, source_target_pairs={{0,16},{8,24},{16,0},{24,8},{1,17},{9,25},{17,1},{25,9},{2,18},{10... | collective-permute-start | bytes 2580488 | tf_op jit(solution)/shard_map/ppermute | solution.py:626
  274.1 3.4 collective-permute-start.24
  279.5 52.6 %collective-permute-start.25 = (bf16[544,1280]{1,0:T(8,128)(2,1)}, bf16[544,1280]{1,0:T(8,128)(2,1)S(1)}, u32[]{:S(2)}, u32[]{:S(2)}) collective-permute-start(bf16[544,1280]{1,0:T(8,128)(2,1)} %get-tuple-element.287), channel_id=1, source_target_pairs={{0,1},{1,0},{2,3},{3,2},{4,5},{5,4},{6,7},{7,6},{8,9},{9,8},{10,11... | collective-permute-start | bytes 4177928 | tf_op jit(solution)/shard_map/ppermute | solution.py:580
  279.7 52.4 %collective-permute-start.26 = (bf16[544,1280]{1,0:T(8,128)(2,1)S(1)}, bf16[544,1280]{1,0:T(8,128)(2,1)S(1)}, u32[]{:S(2)}, u32[]{:S(2)}) collective-permute-start(bf16[544,1280]{1,0:T(8,128)(2,1)S(1)} %add_convert_fusion.1), channel_id=1, source_target_pairs={{0,2},{1,3},{2,4},{3,5},{4,6},{5,7},{6,0},{7,1},{8,10},{9,11},{10,... | collective-permute-start | bytes 4177928 | tf_op jit(solution)/shard_map/ppermute | solution.py:585
  280.1 52.0 %collective-permute-start.29 = (bf16[512,1280]{1,0:T(8,128)(2,1)}, bf16[512,1280]{1,0:T(8,128)(2,1)}, u32[]{:S(2)}, u32[]{:S(2)}) collective-permute-start(bf16[512,1280]{1,0:T(8,128)(2,1)} %get-tuple-element.305), channel_id=1, source_target_pairs={{0,1},{1,0},{2,3},{3,2},{4,5},{5,4},{6,7},{7,6},{8,9},{9,8},{10,11... | collective-permute-start | bytes 3932168 | tf_op jit(solution)/shard_map/ppermute | solution.py:580
  288.9 47.0 %copy-start.26 = (bf16[448,1280]{1,0:T(8,128)(2,1)}, bf16[448,1280]{1,0:T(8,128)(2,1)S(1)}, u32[]{:S(2)}) copy-start(bf16[448,1280]{1,0:T(8,128)(2,1)S(1)} %get-tuple-element.291) | copy-start | bytes 3440644
  297.6 40.3 %copy-start.28 = (bf16[448,1280]{1,0:T(8,128)(2,1)}, bf16[448,1280]{1,0:T(8,128)(2,1)S(1)}, u32[]{:S(2)}) copy-start(bf16[448,1280]{1,0:T(8,128)(2,1)S(1)} %get-tuple-element.294) | copy-start | bytes 3440644
  297.6 34.4 %collective-permute-start.27 = (bf16[448,1280]{1,0:T(8,128)(2,1)S(1)}, bf16[448,1280]{1,0:T(8,128)(2,1)}, u32[]{:S(2)}, u32[]{:S(2)}) collective-permute-start(bf16[448,1280]{1,0:T(8,128)(2,1)S(1)} %get-tuple-element.295), channel_id=1, source_target_pairs={{0,16},{8,24},{16,0},{24,8},{1,17},{9,25},{17,1},{25,9},{2,18},{10... | collective-permute-start | bytes 3440648 | tf_op jit(solution)/shard_map/ppermute | solution.py:786
  299.2 32.9 %collective-permute-start.28 = (bf16[448,1280]{1,0:T(8,128)(2,1)S(1)}, bf16[448,1280]{1,0:T(8,128)(2,1)}, u32[]{:S(2)}, u32[]{:S(2)}) collective-permute-start(bf16[448,1280]{1,0:T(8,128)(2,1)S(1)} %get-tuple-element.292), channel_id=1, source_target_pairs={{0,8},{8,0},{16,24},{24,16},{1,9},{9,1},{17,25},{25,17},{2,10},{10... | collective-permute-start | bytes 3440648 | tf_op jit(solution)/shard_map/ppermute | solution.py:786
  332.1 33.4 %collective-permute-start.30 = (bf16[512,1280]{1,0:T(8,128)(2,1)}, bf16[512,1280]{1,0:T(8,128)(2,1)S(1)}, u32[]{:S(2)}, u32[]{:S(2)}) collective-permute-start(bf16[512,1280]{1,0:T(8,128)(2,1)} %add_convert_fusion.8), channel_id=1, source_target_pairs={{0,2},{1,3},{2,4},{3,5},{4,6},{5,7},{6,0},{7,1},{8,10},{9,11},{10,... | collective-permute-start | bytes 3932168 | tf_op jit(solution)/shard_map/ppermute | solution.py:585
  333.8 75.8 %collective-permute-start.32 = (bf16[640,1792]{1,0:T(8,128)(2,1)}, bf16[640,1792]{1,0:T(8,128)(2,1)}, u32[]{:S(2)}, u32[]{:S(2)}) collective-permute-start(bf16[640,1792]{1,0:T(8,128)(2,1)} %get-tuple-element.336), channel_id=1, source_target_pairs={{0,8},{8,0},{16,24},{24,16},{1,9},{9,1},{17,25},{25,17},{2,10},{10... | collective-permute-start | bytes 6881288 | tf_op jit(solution)/shard_map/ppermute | solution.py:786
  335.3 74.3 %collective-permute-start.33 = (bf16[640,1792]{1,0:T(8,128)(2,1)}, bf16[640,1792]{1,0:T(8,128)(2,1)}, u32[]{:S(2)}, u32[]{:S(2)}) collective-permute-start(bf16[640,1792]{1,0:T(8,128)(2,1)} %get-tuple-element.337), channel_id=1, source_target_pairs={{0,16},{8,24},{16,0},{24,8},{1,17},{9,25},{17,1},{25,9},{2,18},{10... | collective-permute-start | bytes 6881288 | tf_op jit(solution)/shard_map/ppermute | solution.py:786
  367.4 42.3 %collective-permute-start.31 = (bf16[512,1280]{1,0:T(8,128)(2,1)}, bf16[512,1280]{1,0:T(8,128)(2,1)}, u32[]{:S(2)}, u32[]{:S(2)}) collective-permute-start(bf16[512,1280]{1,0:T(8,128)(2,1)} %add_convert_fusion.7), channel_id=1, source_target_pairs={{0,2},{1,3},{2,4},{3,5},{4,6},{5,7},{6,0},{7,1},{8,10},{9,11},{10,... | collective-permute-start | bytes 3932168 | tf_op jit(solution)/shard_map/ppermute | solution.py:585
  371.7 37.9 %collective-permute-start.35 = (bf16[224,1280]{1,0:T(8,128)(2,1)}, bf16[224,1280]{1,0:T(8,128)(2,1)S(1)}, u32[]{:S(2)}, u32[]{:S(2)}) collective-permute-start(bf16[224,1280]{1,0:T(8,128)(2,1)} %fusion.18), channel_id=1, source_target_pairs={{0,8},{8,0},{16,24},{24,16},{1,9},{9,1},{17,25},{25,17},{2,10},{10... | collective-permute-start | bytes 1720328 | tf_op jit(solution)/shard_map/ppermute | solution.py:626
  372.1 37.5 %collective-permute-start.34 = (bf16[224,1280]{1,0:T(8,128)(2,1)}, bf16[224,1280]{1,0:T(8,128)(2,1)S(1)}, u32[]{:S(2)}, u32[]{:S(2)}) collective-permute-start(bf16[224,1280]{1,0:T(8,128)(2,1)} %fusion.17), channel_id=1, source_target_pairs={{0,16},{8,24},{16,0},{24,8},{1,17},{9,25},{17,1},{25,9},{2,18},{10... | collective-permute-start | bytes 1720328 | tf_op jit(solution)/shard_map/ppermute | solution.py:626
  410.6 8.8 %collective-permute-start.38 = (bf16[640,2048]{1,0:T(8,128)(2,1)}, bf16[640,2048]{1,0:T(8,128)(2,1)S(1)}, u32[]{:S(2)}, u32[]{:S(2)}) collective-permute-start(bf16[640,2048]{1,0:T(8,128)(2,1)} %get-tuple-element.348), channel_id=1, source_target_pairs={{0,1},{1,0},{2,3},{3,2},{4,5},{5,4},{6,7},{7,6},{8,9},{9,8},{10,11... | collective-permute-start | bytes 7864328 | tf_op jit(solution)/shard_map/ppermute | solution.py:580
  410.6 13.2 %collective-permute-start.37 = (bf16[640,2048]{1,0:T(8,128)(2,1)}, bf16[640,2048]{1,0:T(8,128)(2,1)}, u32[]{:S(2)}, u32[]{:S(2)}) collective-permute-start(bf16[640,2048]{1,0:T(8,128)(2,1)} %get-tuple-element.344), channel_id=1, source_target_pairs={{0,1},{1,0},{2,3},{3,2},{4,5},{5,4},{6,7},{7,6},{8,9},{9,8},{10,11... | collective-permute-start | bytes 7864328 | tf_op jit(solution)/shard_map/ppermute | solution.py:580
  411.1 18.1 %collective-permute-start.36 = (bf16[640,1152]{1,0:T(8,128)(2,1)}, bf16[640,1152]{1,0:T(8,128)(2,1)}, u32[]{:S(2)}, u32[]{:S(2)}) collective-permute-start(bf16[640,1152]{1,0:T(8,128)(2,1)} %get-tuple-element.339), channel_id=1, source_target_pairs={{0,1},{1,0},{2,3},{3,2},{4,5},{5,4},{6,7},{7,6},{8,9},{9,8},{10,11... | collective-permute-start | bytes 4423688 | tf_op jit(solution)/shard_map/ppermute | solution.py:580
  422.3 31.7 %collective-permute-start.42 = (bf16[2,2,2,40,2048]{4,3,2,1,0:T(8,128)(2,1)S(1)}, bf16[2,2,2,40,2048]{4,3,2,1,0:T(8,128)(2,1)S(1)}, u32[]{:S(2)}, u32[]{:S(2)}) collective-permute-start(bf16[2,2,2,40,2048]{4,3,2,1,0:T(8,128)(2,1)S(1)} %fusion.4), channel_id=1, source_target_pairs={{0,8},{8,0},{16,24},{24,16},{1,9},{9,1},{17,25},{25,17},{2,10},{10... | collective-permute-start | bytes 3932168 | tf_op jit(solution)/shard_map/ppermute | solution.py:626
  425.7 30.6 %collective-permute-start.41 = (bf16[2,2,2,40,2048]{4,3,2,1,0:T(8,128)(2,1)S(1)}, bf16[2,2,2,40,2048]{4,3,2,1,0:T(8,128)(2,1)S(1)}, u32[]{:S(2)}, u32[]{:S(2)}) collective-permute-start(bf16[2,2,2,40,2048]{4,3,2,1,0:T(8,128)(2,1)S(1)} %fusion.5), channel_id=1, source_target_pairs={{0,16},{8,24},{16,0},{24,8},{1,17},{9,25},{17,1},{25,9},{2,18},{10... | collective-permute-start | bytes 3932168 | tf_op jit(solution)/shard_map/ppermute | solution.py:626
  428.7 44.6 %collective-permute-start.43 = (bf16[512,1280]{1,0:T(8,128)(2,1)S(1)}, bf16[512,1280]{1,0:T(8,128)(2,1)S(1)}, u32[]{:S(2)}, u32[]{:S(2)}) collective-permute-start(bf16[512,1280]{1,0:T(8,128)(2,1)S(1)} %convert_add_fusion.1), channel_id=1, source_target_pairs={{0,2},{1,3},{2,4},{3,5},{4,6},{5,7},{6,0},{7,1},{8,10},{9,11},{10,... | collective-permute-start | bytes 3932168 | tf_op jit(solution)/shard_map/ppermute | solution.py:585
  430.8 39.0 %collective-permute-start.40 = (bf16[2,2,2,40,1152]{4,3,2,1,0:T(8,128)(2,1)S(1)}, bf16[2,2,2,40,1152]{4,3,2,1,0:T(8,128)(2,1)S(1)}, u32[]{:S(2)}, u32[]{:S(2)}) collective-permute-start(bf16[2,2,2,40,1152]{4,3,2,1,0:T(8,128)(2,1)S(1)} %fusion.13), channel_id=1, source_target_pairs={{0,8},{8,0},{16,24},{24,16},{1,9},{9,1},{17,25},{25,17},{2,10},{10... | collective-permute-start | bytes 2211848 | tf_op jit(solution)/shard_map/ppermute | solution.py:626
  433.1 38.2 %collective-permute-start.39 = (bf16[2,40,2688]{2,1,0:T(8,128)(2,1)S(1)}, bf16[2,40,2688]{2,1,0:T(8,128)(2,1)S(1)}, u32[]{:S(2)}, u32[]{:S(2)}) collective-permute-start(bf16[2,40,2688]{2,1,0:T(8,128)(2,1)S(1)} %fusion.12), channel_id=1, source_target_pairs={{0,2},{1,3},{2,0},{3,1},{4,6},{5,7},{6,4},{7,5},{8,10},{9,11},{10,... | collective-permute-start | bytes 1290248 | tf_op jit(solution)/shard_map/ppermute | solution.py:626
  454.0 40.9 %copy-start.48 = (bf16[2,2,2,40,2048]{4,3,2,1,0:T(8,128)(2,1)}, bf16[2,2,2,40,2048]{4,3,2,1,0:T(8,128)(2,1)S(1)}, u32[]{:S(2)}) copy-start(bf16[2,2,2,40,2048]{4,3,2,1,0:T(8,128)(2,1)S(1)} %collective-permute-done.42) | copy-start | bytes 3932164
  455.9 20.7 %collective-permute-start.46 = (bf16[2,2,40,2048]{3,2,1,0:T(8,128)(2,1)S(1)}, bf16[2,2,40,2048]{3,2,1,0:T(8,128)(2,1)S(1)}, u32[]{:S(2)}, u32[]{:S(2)}) collective-permute-start(bf16[2,2,40,2048]{3,2,1,0:T(8,128)(2,1)S(1)} %fusion.7), channel_id=1, source_target_pairs={{0,16},{8,24},{16,0},{24,8},{1,17},{9,25},{17,1},{25,9},{2,18},{10... | collective-permute-start | bytes 1966088 | tf_op jit(solution)/shard_map/ppermute | solution.py:626
  456.3 41.7 %copy-start.49 = (bf16[2,2,2,40,2048]{4,3,2,1,0:T(8,128)(2,1)}, bf16[2,2,2,40,2048]{4,3,2,1,0:T(8,128)(2,1)S(1)}, u32[]{:S(2)}) copy-start(bf16[2,2,2,40,2048]{4,3,2,1,0:T(8,128)(2,1)S(1)} %collective-permute-done.41) | copy-start | bytes 3932164
  458.3 24.7 %collective-permute-start.45 = (bf16[2,2,40,2048]{3,2,1,0:T(8,128)(2,1)S(1)}, bf16[2,2,40,2048]{3,2,1,0:T(8,128)(2,1)S(1)}, u32[]{:S(2)}, u32[]{:S(2)}) collective-permute-start(bf16[2,2,40,2048]{3,2,1,0:T(8,128)(2,1)S(1)} %fusion.6), channel_id=1, source_target_pairs={{0,8},{8,0},{16,24},{24,16},{1,9},{9,1},{17,25},{25,17},{2,10},{10... | collective-permute-start | bytes 1966088 | tf_op jit(solution)/shard_map/ppermute | solution.py:626
  470.9 13.9 %collective-permute-start.44 = (bf16[2,2,40,1152]{3,2,1,0:T(8,128)(2,1)S(1)}, bf16[2,2,40,1152]{3,2,1,0:T(8,128)(2,1)S(1)}, u32[]{:S(2)}, u32[]{:S(2)}) collective-permute-start(bf16[2,2,40,1152]{3,2,1,0:T(8,128)(2,1)S(1)} %fusion.14), channel_id=1, source_target_pairs={{0,16},{8,24},{16,0},{24,8},{1,17},{9,25},{17,1},{25,9},{2,18},{10... | collective-permute-start | bytes 1105928 | tf_op jit(solution)/shard_map/ppermute | solution.py:626
  472.6 31.1 %collective-permute-start.53 = (bf16[40,2688]{1,0:T(8,128)(2,1)S(1)}, bf16[40,2688]{1,0:T(8,128)(2,1)S(1)}, u32[]{:S(2)}, u32[]{:S(2)}) collective-permute-start(bf16[40,2688]{1,0:T(8,128)(2,1)S(1)} %fusion.20), channel_id=1, source_target_pairs={{0,4},{1,5},{2,6},{3,7},{4,0},{5,1},{6,2},{7,3},{8,12},{9,13},{10,... | collective-permute-start | bytes 645128 | tf_op jit(solution)/shard_map/ppermute | solution.py:626
  477.7 15.4 %collective-permute-start.49 = (bf16[2,40,2048]{2,1,0:T(8,128)(2,1)S(1)}, bf16[2,40,2048]{2,1,0:T(8,128)(2,1)S(1)}, u32[]{:S(2)}, u32[]{:S(2)}) collective-permute-start(bf16[2,40,2048]{2,1,0:T(8,128)(2,1)S(1)} %fusion.16), channel_id=1, source_target_pairs={{0,2},{1,3},{2,0},{3,1},{4,6},{5,7},{6,4},{7,5},{8,10},{9,11},{10,... | collective-permute-start | bytes 983048 | tf_op jit(solution)/shard_map/ppermute | solution.py:626
  484.4 13.7 %collective-permute-start.48 = (bf16[2,40,2048]{2,1,0:T(8,128)(2,1)S(1)}, bf16[2,40,2048]{2,1,0:T(8,128)(2,1)S(1)}, u32[]{:S(2)}, u32[]{:S(2)}) collective-permute-start(bf16[2,40,2048]{2,1,0:T(8,128)(2,1)S(1)} %fusion.15), channel_id=1, source_target_pairs={{0,2},{1,3},{2,0},{3,1},{4,6},{5,7},{6,4},{7,5},{8,10},{9,11},{10,... | collective-permute-start | bytes 983048 | tf_op jit(solution)/shard_map/ppermute | solution.py:626
  485.8 15.2 %collective-permute-start.47 = (bf16[2,40,1152]{2,1,0:T(8,128)(2,1)S(1)}, bf16[2,40,1152]{2,1,0:T(8,128)(2,1)S(1)}, u32[]{:S(2)}, u32[]{:S(2)}) collective-permute-start(bf16[2,40,1152]{2,1,0:T(8,128)(2,1)S(1)} %fusion.21), channel_id=1, source_target_pairs={{0,2},{1,3},{2,0},{3,1},{4,6},{5,7},{6,4},{7,5},{8,10},{9,11},{10,... | collective-permute-start | bytes 552968 | tf_op jit(solution)/shard_map/ppermute | solution.py:626
  490.2 35.3 %collective-permute-start.54 = (bf16[320,1792]{1,0:T(8,128)(2,1)}, bf16[320,1792]{1,0:T(8,128)(2,1)}, u32[]{:S(2)}, u32[]{:S(2)}) collective-permute-start(bf16[320,1792]{1,0:T(8,128)(2,1)} %fusion.8), channel_id=1, source_target_pairs={{0,16},{8,24},{16,0},{24,8},{1,17},{9,25},{17,1},{25,9},{2,18},{10... | collective-permute-start | bytes 3440648 | tf_op jit(solution)/shard_map/ppermute | solution.py:626
  493.2 32.3 %collective-permute-start.55 = (bf16[320,1792]{1,0:T(8,128)(2,1)}, bf16[320,1792]{1,0:T(8,128)(2,1)}, u32[]{:S(2)}, u32[]{:S(2)}) collective-permute-start(bf16[320,1792]{1,0:T(8,128)(2,1)} %fusion.9), channel_id=1, source_target_pairs={{0,8},{8,0},{16,24},{24,16},{1,9},{9,1},{17,25},{25,17},{2,10},{10... | collective-permute-start | bytes 3440648 | tf_op jit(solution)/shard_map/ppermute | solution.py:626
  498.0 23.4 %collective-permute-start.51 = (bf16[40,2048]{1,0:T(8,128)(2,1)}, bf16[40,2048]{1,0:T(8,128)(2,1)}, u32[]{:S(2)}, u32[]{:S(2)}) collective-permute-start(bf16[40,2048]{1,0:T(8,128)(2,1)} %fusion.25), channel_id=1, source_target_pairs={{0,4},{1,5},{2,6},{3,7},{4,0},{5,1},{6,2},{7,3},{8,12},{9,13},{10,... | collective-permute-start | bytes 491528 | tf_op jit(solution)/shard_map/ppermute | solution.py:626
  502.0 9.8 %collective-permute-start.50 = (bf16[40,1152]{1,0:T(8,128)(2,1)S(1)}, bf16[40,1152]{1,0:T(8,128)(2,1)S(1)}, u32[]{:S(2)}, u32[]{:S(2)}) collective-permute-start(bf16[40,1152]{1,0:T(8,128)(2,1)S(1)} %fusion.28), channel_id=1, source_target_pairs={{0,4},{1,5},{2,6},{3,7},{4,0},{5,1},{6,2},{7,3},{8,12},{9,13},{10,... | collective-permute-start | bytes 276488 | tf_op jit(solution)/shard_map/ppermute | solution.py:626
  510.5 8.7 %collective-permute-start.52 = (bf16[40,2048]{1,0:T(8,128)(2,1)}, bf16[40,2048]{1,0:T(8,128)(2,1)}, u32[]{:S(2)}, u32[]{:S(2)}) collective-permute-start(bf16[40,2048]{1,0:T(8,128)(2,1)} %fusion.24), channel_id=1, source_target_pairs={{0,4},{1,5},{2,6},{3,7},{4,0},{5,1},{6,2},{7,3},{8,12},{9,13},{10,... | collective-permute-start | bytes 491528 | tf_op jit(solution)/shard_map/ppermute | solution.py:626
  (58 other events, 441.7 us)

commit v6 on v5

--- a/solution.py
+++ b/solution.py
@@ -207,7 +207,7 @@
     )
 
 
-def expert_kernel(cap, tokens, hidden, last_slot, *refs):
+def expert_kernel(cap, tokens, hidden, unrolled, *refs):
     (first_ref, h2a, h2b, cba, cbb, wr, w_in, w_down) = refs[:8]
     (dra, drb, outa, outb, rows_o, dy_o, act_o, dgu_o, gu, cbrow, oh, gy, drs, probs, dots) = refs[-15:]
     f32, bf16 = jnp.float32, jnp.bfloat16
@@ -240,19 +240,19 @@
         onehot = jnp.where(hit, 1.0, 0.0).astype(bf16)
         oh[src, pl.ds(e * cap, cap), :] = onehot
         half = pl.ds(src * cap, cap)
-        @pl.loop(0, width // 256, unroll=True)
+        @pl.loop(0, width // 256, unroll=unrolled)
         def _(i):
             t = pl.ds(pl.multiple_of(i * 256, 256), 256)
             rows_o[0, half, t] = jnp.dot(onehot, h2[:, t], preferred_element_type=f32).astype(bf16)
             cbrow[half, t] = jnp.dot(onehot, cb[pl.ds(0, tokens), t], preferred_element_type=f32).astype(bf16)
     gate = jnp.concatenate(gates, axis=0)
 
-    @pl.loop(0, 2 * hidden // 256, unroll=True)
+    @pl.loop(0, 2 * hidden // 256, unroll=unrolled)
     def _(i):
         t = pl.ds(pl.multiple_of(i * 256, 256), 256)
         gu[:, t] = jnp.dot(rows_o[0], w_in[0, :, t], preferred_element_type=f32)
 
-    @pl.loop(0, hidden // 128, unroll=True)
+    @pl.loop(0, hidden // 128, unroll=unrolled)
     def _(i):
         ta = pl.ds(pl.multiple_of(i * 128, 128), 128)
         tb = pl.ds(pl.multiple_of(hidden + i * 128, 128), 128)
@@ -273,7 +273,7 @@
             gy[src, pl.ds(e * cap, cap), t] = gyt[src * cap:(src + 1) * cap]
         dy_o[0, :, t] = (gate * c).astype(bf16)
         return dot + jnp.sum(y * c, axis=1, keepdims=True)
-    dot = lax.fori_loop(0, width // 256, down, jnp.zeros((2 * cap, 1), f32), unroll=True)
+    dot = lax.fori_loop(0, width // 256, down, jnp.zeros((2 * cap, 1), f32), unroll=unrolled)
     for src in (0, 1):
         back = jnp.sum(jnp.where(masks[src], dot[src * cap:(src + 1) * cap], 0.0), axis=0, keepdims=True)
         row_id = lax.broadcasted_iota(jnp.int32, (table_rows, tokens), 0)
@@ -285,7 +285,7 @@
         dgu_o[0, :, pl.ds(start, n)] = (dact * gu[:, pl.ds(start, n)]).astype(bf16)
         dgu_o[0, :, pl.ds(hidden + start, n)] = (dact * gu[:, pl.ds(hidden + start, n)]).astype(bf16)
 
-    @pl.loop(0, width // 256, unroll=True)
+    @pl.loop(0, width // 256, unroll=unrolled)
     def _(i):
         t = pl.ds(pl.multiple_of(i * 256, 256), 256)
         dr = lax.dot_general(dgu_o[0], w_in[0, t, :], (((1,), (1,)), ((), ())), preferred_element_type=f32).astype(bf16)
@@ -295,7 +295,7 @@
     @pl.when(e == pl.num_programs(0) - 1)
     def _():
         for src, dro, outo in ((0, dra, outa), (1, drb, outb)):
-            @pl.loop(0, width // 256, unroll=True)
+            @pl.loop(0, width // 256, unroll=unrolled)
             def _(i):
                 t = pl.ds(pl.multiple_of(i * 256, 256), 256)
                 dims = (((0,), (0,)), ((), ()))
@@ -330,7 +330,7 @@
     rows = 2 * cap
     flops = 2 * local * rows * (2 * (3 * width * hidden) + 4 * tokens * width)
     res = pl.pallas_call(
-        lambda *r: expert_kernel(cap, tokens, hidden, None, *r),
+        lambda *r: expert_kernel(cap, tokens, hidden, step in (0, steps - 1), *r),
         grid=(local,),
         in_specs=ins, out_specs=outs, out_shape=[pltpu.HBM(x.shape, x.dtype) for x in sums + kept_shapes],
         scratch_shapes=[pltpu.VMEM((rows, 2 * hidden), f32), pltpu.VMEM((rows, width), bf16), pltpu.VMEM((2, local * cap, tokens), bf16),
@@ -458,7 +458,7 @@
     )(core, h2, cb, w_in, w_down, w_router)
 
 
-def middle_kernel(experts, length_ref, home_a, home_b, home_c, grad_shared, probs, h2, w_router, x_mid, dout, gain, grad_mid, da, small):
+def middle_kernel(experts, length_ref, home_a, home_b, home_c, grad_shared, probs, h2, w_router, x_mid, dout, gain, digits, grad_mid, da, small):
     f32, bf16 = jnp.float32, jnp.bfloat16
     tokens = x_mid.shape[0]
     own, table = pl.ds(0, tokens), pl.ds(tokens, 2 * experts)
@@ -474,7 +474,8 @@
     inverse = lax.rsqrt(jnp.mean(mid * mid, axis=-1, keepdims=True) + NORM_EPS)
     scaled = mid * inverse
     column = lax.broadcasted_iota(jnp.int32, (tokens, 128), 1)
-    small[...] = lax.dot_general(h2[...], low, TN, preferred_element_type=f32) + lax.dot_general(
+    small[...] = digits[...]
+    small[:, pl.ds(0, 128)] += lax.dot_general(h2[...], low, TN, preferred_element_type=f32) + lax.dot_general(
         incoming * scaled, jnp.where(column == experts, 1.0, 0.0), TN,
         precision=lax.Precision.HIGHEST, preferred_element_type=f32,
     )
@@ -486,20 +487,20 @@
     da[...] = jnp.where(live, grad, 0.0).astype(bf16)
 
 
-def middle_back(lengths, home, grad_shared, probs, h2, w_router, x_mid, dout, gain, experts):
+def middle_back(lengths, home, grad_shared, probs, h2, w_router, x_mid, dout, gain, digits, experts):
     tokens, width = x_mid.shape
     f32 = jnp.float32
     sd = jax.ShapeDtypeStruct
     vmem = pl.BlockSpec(memory_space=pltpu.VMEM)
     return pl.pallas_call(
         lambda *r: middle_kernel(experts, *r),
-        in_specs=[pl.BlockSpec(memory_space=pltpu.SMEM)] + [vmem] * 10,
+        in_specs=[pl.BlockSpec(memory_space=pltpu.SMEM)] + [vmem] * 11,
         out_specs=[vmem] * 3,
-        out_shape=[sd((tokens, width), f32), sd((tokens, width), jnp.bfloat16), sd((width, 128), f32)],
+        out_shape=[sd((tokens, width), f32), sd((tokens, width), jnp.bfloat16), sd(digits.shape, f32)],
         compiler_params=pltpu.CompilerParams(vmem_limit_bytes=48 * 2**20),
         cost_estimate=pl.CostEstimate(flops=0, bytes_accessed=0, transcendentals=0),
         name="middle_back",
-    )(lengths, *home, grad_shared, probs, h2, w_router, x_mid, dout, gain)
+    )(lengths, *home, grad_shared, probs, h2, w_router, x_mid, dout, gain, digits)
 
 
 def weight_grad_kernel(parts, bit, index_ref, lhs, rhs, keep, away):
@@ -573,6 +574,41 @@
         cost_estimate=pl.CostEstimate(flops=0, bytes_accessed=0, transcendentals=0),
         name="assemble",
     )(*pieces)
+
+
+def final_kernel(chosen_ref, *refs):
+    *terms, out = refs
+    for i in range(len(terms) // 3):
+        keep, came, last = (term[...].astype(jnp.float32) for term in terms[3 * i : 3 * i + 3])
+        out[i] = keep + came + last
+
+
+def final_sums(chosen, groups):
+    rows, n = groups[0][2].shape
+    cut = rows // 4
+    half = lambda i: pl.BlockSpec((cut, n), lambda c, chosen, i=i: (chosen[i] * 4 + c, 0))
+    row = pl.BlockSpec((cut, n), lambda c, chosen: (c, 0))
+    return pl.pallas_call(
+        final_kernel,
+        grid_spec=pltpu.PrefetchScalarGridSpec(
+            num_scalar_prefetch=1,
+            grid=(4,),
+            in_specs=[spec for i in range(len(groups)) for spec in (half(i), half(i), row)],
+            out_specs=pl.BlockSpec((len(groups), cut, n), lambda c, chosen: (0, c, 0)),
+        ),
+        out_shape=jax.ShapeDtypeStruct((len(groups), rows, n), jnp.float32),
+        compiler_params=pltpu.CompilerParams(vmem_limit_bytes=24 * 2**20),
+        cost_estimate=pl.CostEstimate(flops=0, bytes_accessed=0, transcendentals=0),
+        name="final_sums",
+    )(chosen, *[term for group in groups for term in group])
+
+
+def expert_sums(scatters):
+    flat = lambda term: term.reshape(-1, term.shape[-1])
+    if True or any(len(scatter.choices[0]) != 1 for scatter in scatters):
+        return jnp.stack([scatter.finish() for scatter in scatters])
+    chosen = jnp.stack([scatter.choices[0][0][1] for scatter in scatters]).astype(jnp.int32)
+    return final_sums(chosen, [[flat(term) for term in scatter.terms] for scatter in scatters])
 
 
 def swap_cores(values_in):
@@ -820,9 +856,8 @@
     home = after((*own_home, home_hop), *fence)
     grad_mid, grad_attn_branch, small = middle_back(
         lengths, home, grad_shared, router_probs, h2_low, router_wide, x_mid, dout, norm2[None, :],
-        experts,
-    )
-    small = digits + jnp.pad(small, ((0, 0), (0, small_columns - 128)))
+        digits, experts,
+    )
 
     pairs = width // (2 * HEAD_DIM)
     half = (pairs - 1) // 2
@@ -849,13 +884,18 @@
     landed = [running, out_hop]
     landed += [scatter.terms[-1] for scatter in in_scatters + down_scatters]
     scatters = []
+    fence = landed
     for grads, order in zip(columns, orders):
-        scatters.append(start_scatter(after(grads, *landed), order))
-    fence = landed
+        scatters.append(start_scatter(after(grads, *landed, *fence), order))
     hops = 2
     first_cols, second_cols, third_cols = scatters
     plan = [first_cols, second_cols, None, third_cols, shared_scatter, first_cols, second_cols, third_cols, shared_scatter, None, first_cols, second_cols, third_cols, in_scatters[0], in_scatters[1], first_cols, second_cols, third_cols]
-    for scatter in plan:
+    for position, scatter in enumerate(plan):
+        if position == 5:
+            for held in down_scatters:
+                held.terms = after(held.terms, *fence)
+            expert_down_sum = expert_sums(down_scatters)
+            fence = fence + [expert_down_sum]
         if scatter is not None:
             if scatter.order:
                 fence = [scatter.advance(*fence)]
@@ -868,12 +908,11 @@
     for hops in range(hops, chips):
         routed = add_routed(hops, out_hop, *fence)
         out_hop = next_chip(routed.astype(jnp.bfloat16))
-    for scatter in down_scatters + in_scatters + [shared_scatter]:
+    for scatter in in_scatters + [shared_scatter]:
         scatter.terms = after(scatter.terms, *fence)
     result = (x_mid + live_col * (shared_out + routed)).astype(jnp.bfloat16)
     shared_sum = shared_scatter.finish()
-    expert_in_sum = jnp.stack([scatter.finish() for scatter in in_scatters])
-    expert_down_sum = jnp.stack([scatter.finish() for scatter in down_scatters])
+    expert_in_sum = expert_sums(in_scatters)
     pieces = [scatter.finish() for scatter in scatters]
     qkv_sum, out_sum = assemble(pieces, width)
     small_sum = pieces[-1][:, 8 * HEAD_DIM :]

time: 540 us -> 537 us (level)
  waiting for transfers between devices: 119 us -> 90.6 us
  Pallas kernels: 277 us -> 300 us
    pallas_call x4, Pallas kernels: 127 us -> 151 us  [expert_step(): pl.pallas_call(lambda *r: expert_kernel(cap, tokens, hidden, step in (0,...]
    ppermute x12, waiting for transfers between devices: 54 us -> 31.6 us  [next_chip(): lax.ppermute(values_in, 'expert', [(i, (i + 2) % owners) for i in range(o...]
  transfers between devices with their start and end apart: 56 -> 56, of which waited for: 18 -> 21; matrix products, arithmetic and copies ran while one was open for 12% -> 11% of each run, Pallas kernels for 51% -> 56%
where the time goes in v6:
time: 537 us; the launch traced here: 530 us
  Pallas kernels  300 us (56%)
  waiting for transfers between devices  90.6 us (17%)
  other arithmetic  69.5 us (13%)
  starting transfers between devices  44.6 us (8%)
  local copies, waits for them, and re-layouts  23.1 us (4%)
    pallas_call x4, Pallas kernels, expert_step(): pl.pallas_call(lambda *r: expert_kernel(cap, tokens, hidden, step in (0,...  151 us
    pallas_call x3, Pallas kernels, attention_backward(): pl.pallas_call(lambda *r: attention_back_kernel(rows, extra, carried, *r)...  48.8 us
    pallas_call x4, Pallas kernels, weight_grad(): pl.pallas_call(lambda *r: weight_grad_kernel(parts, bit, *r), grid=(n //...  45.8 us
    ppermute x20, waiting for transfers between devices, advance(): lax.ppermute(away, name, [(i, i ^ 1 << bit) for i in range(lax.axis_size(...  39.5 us
    convert_element_type x20, other arithmetic, advance(): away = sum_terms([picked(term, made + [(dim, 1 - mine)]) for term, made i...  34.1 us
    ppermute x12, waiting for transfers between devices, next_chip(): lax.ppermute(values_in, 'expert', [(i, (i + 2) % owners) for i in range(o...  31.6 us
    pallas_call x1, Pallas kernels, attention_forward(): pl.pallas_call(attention_kernel, grid=(pairs,), in_specs=[pl.BlockSpec(me...  23.1 us
    ppermute x20, starting transfers between devices, advance(): lax.ppermute(away, name, [(i, i ^ 1 << bit) for i in range(lax.axis_size(...  22.5 us
  transfers between devices with their start and end apart: 56, of which 21 were waited for; matrix products, arithmetic and copies ran while one was open for 11% of the time, Pallas kernels for 56%

profile of v6, /device:TPU:0, one launch (start us, length us, event | category | flops | bytes accessed | tf_op | source)
XLA Modules:
  0.0 530.3 jit_solution(347971716623959840)
XLA Ops:
  1.3 1.6 copy.72.ids
  2.9 3.5 token_rows.1.r_3_.r_2_
  6.8 2.6 collective-permute-start
  10.8 23.1 %attention_forward.1 = (bf16[512,1280]{1,0:T(8,128)(2,1)}, bf16[512,1280]{1,0:T(8,128)(2,1)}, bf16[512,1280]{1,0:T(8,128)(2,1)}, bf16[512,1280]{1,0:T(8,128)(2,1...) custom-call(s32[1]{0:T(128)} %copy.133.length_ref.r_0_, ...), custom_call_target="tpu_custom_call" | custom-call | tf_op jit(solution)/shard_map/attention_forward/pallas_call | solution.py:80
  34.1 1.6 collective-permute-start.4
  35.7 6.6 %collective-permute-done.r_3_ = bf16[528,1280]{1,0:T(8,128)(2,1)} collective-permute-done((bf16[528,1280]{1,0:T(8,128)(2,1)}, bf16[528,1280]{1,0:T(8,128)(2,1)}, u32[]{:S(2)}, u32[]{:S(2)}) %collective-permute-start) | collective-permute-done | bytes 1351712 | tf_op jit(solution)/shard_map/ppermute | solution.py:621
  47.1 31.5 %expert_step.4 = (bf16[544,1280]{1,0:T(8,128)(2,1)}, bf16[544,1280]{1,0:T(8,128)(2,1)}, bf16[512,1280]{1,0:T(8,128)(2,1)}, bf16[512,1280]{1,0:T(8,128)(2,1)}, bf...) custom-call(s32[1]{0:T(128)} %bitcast.2.r_0_, ...), custom_call_target="tpu_custom_call" | custom-call | tf_op jit(solution)/shard_map/expert_step/pallas_call | solution.py:332
  78.6 17.2 %shared_expert.1 = (f32[512,1280]{1,0:T(8,128)}, f32[512,1280]{1,0:T(8,128)}, f32[512,128]{1,0:T(8,128)S(1)}, bf16[640,2688]{1,0:T(8,128)(2,1)}, bf16[640,2688]{1,0:T(8,128)(2,1)}) custom-call(s32[1]{0:T(128)} %bitcast.1.r_0_.r_1_, bf16[512,1280]{1,0:T(8,128)(2,1)S(1)} %copy-done.3, bf16[528,1280]{1,0:T(8,128)(2,1)S(1)} %copy-done.2, ...), custom_call_target="tpu_custom_call" | custom-call | tf_op jit(solution)/shard_map/shared_expert/pallas_call | solution.py:449
  97.1 2.9 collective-permute-done.5.r_2_
  102.6 1.6 collective-permute-start.10
  105.5 43.8 %expert_step.5 = (bf16[544,1280]{1,0:T(8,128)(2,1)}, bf16[544,1280]{1,0:T(8,128)(2,1)}, bf16[512,1280]{1,0:T(8,128)(2,1)}, bf16[512,1280]{1,0:T(8,128)(2,1)}, bf...) custom-call(s32[1]{0:T(128)} %bitcast.2.r_0_, ...), custom_call_target="tpu_custom_call", output_to_operand_aliasing={{4}: (8, {}), {5}: (9, {}), {6}: (10, {}), {7}: (11, {})} | custom-call | tf_op jit(solution)/shard_map/expert_step/pallas_call | solution.py:332
  149.3 14.1 %collective-permute-done.10.r_1_ = bf16[512,1280]{1,0:T(8,128)(2,1)} collective-permute-done((bf16[512,1280]{1,0:T(8,128)(2,1)}, bf16[512,1280]{1,0:T(8,128)(2,1)}, u32[]{:S(2)}, u32[]{:S(2)}) %collective-permute-start.10) | collective-permute-done | bytes 1310752 | tf_op jit(solution)/shard_map/ppermute | solution.py:621
  163.5 3.3 fusion.2
  167.2 1.6 collective-permute-start.9
  168.9 2.3 collective-permute-done.12
  172.8 3.1 add_convert_fusion.8
  175.9 44.1 %expert_step.6 = (bf16[544,1280]{1,0:T(8,128)(2,1)}, bf16[544,1280]{1,0:T(8,128)(2,1)}, bf16[512,1280]{1,0:T(8,128)(2,1)}, bf16[512,1280]{1,0:T(8,128)(2,1)}, bf...) custom-call(s32[1]{0:T(128)} %bitcast.2.r_0_, ...), custom_call_target="tpu_custom_call", output_to_operand_aliasing={{4}: (8, {}), {5}: (9, {}), {6}: (10, {}), {7}: (11, {})} | custom-call | tf_op jit(solution)/shard_map/expert_step/pallas_call | solution.py:332
  220.0 2.1 fusion.3
  222.1 9.8 %collective-permute-done.18 = bf16[544,1280]{1,0:T(8,128)(2,1)} collective-permute-done((bf16[544,1280]{1,0:T(8,128)(2,1)}, bf16[544,1280]{1,0:T(8,128)(2,1)}, u32[]{:S(2)}, u32[]{:S(2)}) %collective-permute-start.18) | collective-permute-done | bytes 1392672 | tf_op jit(solution)/shard_map/ppermute | solution.py:621
  232.0 3.1 collective-permute-done.19
  235.2 1.9 add_convert_fusion.2
  242.4 31.6 %expert_step.7 = (bf16[544,1280]{1,0:T(8,128)(2,1)}, bf16[544,1280]{1,0:T(8,128)(2,1)}, bf16[512,1280]{1,0:T(8,128)(2,1)}, bf16[512,1280]{1,0:T(8,128)(2,1)}, bf...) custom-call(s32[1]{0:T(128)} %bitcast.2.r_0_, ...), custom_call_target="tpu_custom_call", output_to_operand_aliasing={{4}: (8, {}), {5}: (9, {}), {6}: (10, {}), {7}: (11, {})} | custom-call | tf_op jit(solution)/shard_map/expert_step/pallas_call | solution.py:332
  274.2 3.2 collective-permute-done.24
  277.5 1.9 add_convert_fusion.1
  280.0 8.7 %weight_grad.4 = (bf16[448,1280]{1,0:T(8,128)(2,1)S(1)}, bf16[448,1280]{1,0:T(8,128)(2,1)S(1)}) custom-call(s32[1]{0:T(128)} %bitcast.9.r_0_, bf16[2,1920,896]{2,1,0:T(8,128)(2,1)} %get-tuple-element.293.r_1_, bf16[2,1920,1280]{2,1,0:T(8,128)(2,1)} %get-tuple-element.290.r_2_), custom_call_target="tpu_custom_call" | custom-call | tf_op jit(solution)/shard_map/weight_grad/pallas_call | solution.py:527
  288.7 8.7 %weight_grad.5 = (bf16[448,1280]{1,0:T(8,128)(2,1)S(1)}, bf16[448,1280]{1,0:T(8,128)(2,1)S(1)}) custom-call(s32[1]{0:T(128)} %bitcast.9.r_0_, bf16[2,1920,896]{2,1,0:T(8,128)(2,1)} %get-tuple-element.293.r_1_, bf16[2,1920,1280]{2,1,0:T(8,128)(2,1)} %get-tuple-element.290.r_2_), custom_call_target="tpu_custom_call" | custom-call | tf_op jit(solution)/shard_map/weight_grad/pallas_call | solution.py:527
  300.6 14.2 %weight_grad.6 = (bf16[640,1792]{1,0:T(8,128)(2,1)S(1)}, bf16[640,1792]{1,0:T(8,128)(2,1)S(1)}) custom-call(s32[1]{0:T(128)} %bitcast.9.r_0_, bf16[2,1920,1280]{2,1,0:T(8,128)(2,1)} %get-tuple-element.301.r_1_, bf16[2,1920,1792]{2,1,0:T(8,128)(2,1)} %get-tuple-element.298.r_2_), custom_call_target="tpu_custom_call" | custom-call | tf_op jit(solution)/shard_map/weight_grad/pallas_call | solution.py:527
  317.6 14.2 %weight_grad.7 = (bf16[640,1792]{1,0:T(8,128)(2,1)S(1)}, bf16[640,1792]{1,0:T(8,128)(2,1)S(1)}) custom-call(s32[1]{0:T(128)} %bitcast.9.r_0_, bf16[2,1920,1280]{2,1,0:T(8,128)(2,1)} %get-tuple-element.301.r_1_, bf16[2,1920,1792]{2,1,0:T(8,128)(2,1)} %get-tuple-element.298.r_2_), custom_call_target="tpu_custom_call" | custom-call | tf_op jit(solution)/shard_map/weight_grad/pallas_call | solution.py:527
  334.6 1.7 collective-permute-start.30
  341.6 8.5 %middle_back.1 = (f32[512,1280]{1,0:T(8,128)}, bf16[512,1280]{1,0:T(8,128)(2,1)S(1)}, f32[1280,128]{1,0:T(8,128)S(1)}) custom-call(s32[1]{0:T(128)} %copy.133.length_ref.r_0_, bf16[544,1280]{1,0:T(8,128)(2,1)} %get-tuple-element.310.r_1_, bf16[544,1280]{1,0:T(8,128)(2,1)} %copy-done.37, bf16[544,1280]{1,0:T(8,128)(2,1)} %copy-done.38, ...), custom_call_target="tpu_custom_call" | custom-call | tf_op jit(solution)/shard_map/middle_back/pallas_call | solution.py:495
  350.2 17.0 %attention_backward.3 = (bf16[640,2048]{1,0:T(8,128)(2,1)S(1)}, bf16[640,2048]{1,0:T(8,128)(2,1)}, f32[512,1280]{1,0:T(8,128)}) custom-call(s32[2]{0:T(128)S(1)} %pad_add_fusion.2.r_0_, s32[1]{0:T(128)} %bitcast.1.r_0_.r_1_, bf16[512,1280]{1,0:T(8,128)(2,1)S(1)} %get-tuple-element.330.r_2_, bf16[1280,1280]{1,0:T(8,128)(2,1)} %r_3_.7, ...), custom_call_target="tpu_custom_call" | custom-call | tf_op jit(solution)/shard_map/attention_backward/pallas_call | solution.py:190
  368.2 1.9 add_convert_fusion.7
  370.0 2.8 collective-permute-start.31
  373.3 1.7 collective-permute-start.34
  375.0 17.8 %attention_backward.4 = (bf16[640,2048]{1,0:T(8,128)(2,1)S(1)}, bf16[640,2048]{1,0:T(8,128)(2,1)}, f32[512,1280]{1,0:T(8,128)}) custom-call(s32[2]{0:T(128)S(1)} %get-tuple-element.476.r_0_, s32[1]{0:T(128)} %bitcast.1.r_0_.r_1_, bf16[512,1280]{1,0:T(8,128)(2,1)S(1)} %get-tuple-element.330.r_2_, bf16[1280,1280]{1,0:T(8,128)(2,1)} %r_3_.7, ...), custom_call_target="tpu_custom_call" | custom-call | tf_op jit(solution)/shard_map/attention_backward/pallas_call | solution.py:190
  394.4 14.0 %attention_backward.5 = (bf16[640,1152]{1,0:T(8,128)(2,1)S(1)}, bf16[640,1152]{1,0:T(8,128)(2,1)}, f32[512,1280]{1,0:T(8,128)}) custom-call(s32[2]{0:T(128)S(1)} %get-tuple-element.475.r_0_, s32[1]{0:T(128)} %bitcast.1.r_0_.r_1_, bf16[512,1280]{1,0:T(8,128)(2,1)S(1)} %get-tuple-element.330.r_2_, bf16[1280,1280]{1,0:T(8,128)(2,1)} %r_3_.7, ...), custom_call_target="tpu_custom_call" | custom-call | tf_op jit(solution)/shard_map/attention_backward/pallas_call | solution.py:190
  411.0 4.7 collective-permute-done.38
  415.7 1.9 fusion.4
  417.7 1.5 collective-permute-start.42
  419.5 1.9 fusion.5
  421.9 2.0 convert_add_fusion.1
  423.8 2.0 collective-permute-start.43
  427.2 1.7 collective-permute-start.40
  435.0 14.3 %collective-permute-done.42 = bf16[2,2,2,40,2048]{4,3,2,1,0:T(8,128)(2,1)S(1)} collective-permute-done((bf16[2,2,2,40,2048]{4,3,2,1,0:T(8,128)(2,1)S(1)}, bf16[2,2,2,40,2048]{4,3,2,1,0:T(8,128)(2,1)S(1)}, u32[]{:S(2)}, u32[]{:S(2)}) %collective-permute-start.42) | collective-permute-done | bytes 1310752 | tf_op jit(solution)/shard_map/ppermute | solution.py:662
  449.4 1.9 fusion.7
  452.3 1.9 fusion.6
  455.8 9.4 %collective-permute-done.40 = bf16[2,2,2,40,1152]{4,3,2,1,0:T(8,128)(2,1)S(1)} collective-permute-done((bf16[2,2,2,40,1152]{4,3,2,1,0:T(8,128)(2,1)S(1)}, bf16[2,2,2,40,1152]{4,3,2,1,0:T(8,128)(2,1)S(1)}, u32[]{:S(2)}, u32[]{:S(2)}) %collective-permute-start.40) | collective-permute-done | bytes 737312 | tf_op jit(solution)/shard_map/ppermute | solution.py:662
  469.6 3.3 add_convert_fusion.4
  475.3 3.1 collective-permute-done.45
  479.8 1.8 collective-permute-start.48
  483.0 2.8 fusion.8
  486.1 2.6 fusion.9
  488.7 1.6 collective-permute-start.55
  490.3 1.7 fusion.25
  492.0 2.0 collective-permute-done.48
  494.0 1.8 fusion.24
  501.0 2.0 collective-permute-start.52
  507.1 9.3 %collective-permute-done.52 = bf16[40,2048]{1,0:T(8,128)(2,1)} collective-permute-done((bf16[40,2048]{1,0:T(8,128)(2,1)}, bf16[40,2048]{1,0:T(8,128)(2,1)}, u32[]{:S(2)}, u32[]{:S(2)}) %collective-permute-start.52) | collective-permute-done | bytes 163872 | tf_op jit(solution)/shard_map/ppermute | solution.py:662
  516.4 2.1 fusion.22.r_1_
  518.6 2.0 fusion.23.r_0_
  520.6 2.1 assemble.1
  522.7 2.5 fusion
  525.3 2.1 fusion.1
  527.5 2.4 pad_maximum_fusion
  (257 shorter events, 69.9 us)
Async XLA Ops:
  6.4 37.2 %collective-permute-start.2 = (bf16[528,1280]{1,0:T(8,128)(2,1)}, bf16[528,1280]{1,0:T(8,128)(2,1)}, u32[]{:S(2)}, u32[]{:S(2)}) collective-permute-start(bf16[528,1280]{1,0:T(8,128)(2,1)} %token_rows.1.r_3_.r_2_), channel_id=1, source_target_pairs={{0,1},{1,0},{2,3},{3,2},{4,5},{5,4},{6,7},{7,6},{8,9},{9,8},{10,11... | collective-permute-start | bytes 4055048 | tf_op jit(solution)/shard_map/ppermute | solution.py:616
  6.8 35.5 %collective-permute-start = (bf16[528,1280]{1,0:T(8,128)(2,1)}, bf16[528,1280]{1,0:T(8,128)(2,1)}, u32[]{:S(2)}, u32[]{:S(2)}) collective-permute-start(bf16[528,1280]{1,0:T(8,128)(2,1)} %token_rows.1.r_3_.r_2_), channel_id=1, source_target_pairs={{0,2},{1,3},{2,4},{3,5},{4,6},{5,7},{6,0},{7,1},{8,10},{9,11},{10,... | collective-permute-start | bytes 4055048 | tf_op jit(solution)/shard_map/ppermute | solution.py:621
  10.7 23.2 %copy-start.5 = (f32[512,128]{1,0:T(8,128)}, f32[512,128]{1,0:T(8,128)S(1)}, u32[]{:S(2)}) copy-start(f32[512,128]{1,0:T(8,128)S(1)} %get-tuple-element.478.sine.r_9_) | copy-start | bytes 786436
  33.9 9.7 %collective-permute-start.1 = (bf16[512,1280]{1,0:T(8,128)(2,1)}, bf16[512,1280]{1,0:T(8,128)(2,1)S(1)}, u32[]{:S(2)}, u32[]{:S(2)}) collective-permute-start(bf16[512,1280]{1,0:T(8,128)(2,1)} %get-tuple-element.227.r_1_.r_6_), channel_id=1, source_target_pairs={{0,1},{1,0},{2,3},{3,2},{4,5},{5,4},{6,7},{7,6},{8,9},{9,8},{10,11... | collective-permute-start | bytes 3932168 | tf_op jit(solution)/shard_map/ppermute | solution.py:616
  34.1 62.4 %collective-permute-start.4 = (bf16[512,1280]{1,0:T(8,128)(2,1)}, bf16[512,1280]{1,0:T(8,128)(2,1)}, u32[]{:S(2)}, u32[]{:S(2)}) collective-permute-start(bf16[512,1280]{1,0:T(8,128)(2,1)} %get-tuple-element.227.r_1_.r_6_), channel_id=1, source_target_pairs={{0,2},{1,3},{2,4},{3,5},{4,6},{5,7},{6,0},{7,1},{8,10},{9,11},{10,... | collective-permute-start | bytes 3932168 | tf_op jit(solution)/shard_map/ppermute | solution.py:621
  42.3 58.7 %collective-permute-start.6 = (bf16[528,1280]{1,0:T(8,128)(2,1)}, bf16[528,1280]{1,0:T(8,128)(2,1)}, u32[]{:S(2)}, u32[]{:S(2)}) collective-permute-start(bf16[528,1280]{1,0:T(8,128)(2,1)} %collective-permute-done.r_3_), channel_id=1, source_target_pairs={{0,1},{1,0},{2,3},{3,2},{4,5},{5,4},{6,7},{7,6},{8,9},{9,8},{10,11... | collective-permute-start | bytes 4055048 | tf_op jit(solution)/shard_map/ppermute | solution.py:616
  42.3 58.7 %collective-permute-start.3 = (bf16[528,1280]{1,0:T(8,128)(2,1)}, bf16[528,1280]{1,0:T(8,128)(2,1)}, u32[]{:S(2)}, u32[]{:S(2)}) collective-permute-start(bf16[528,1280]{1,0:T(8,128)(2,1)} %collective-permute-done.r_3_), channel_id=1, source_target_pairs={{0,2},{1,3},{2,4},{3,5},{4,6},{5,7},{6,0},{7,1},{8,10},{9,11},{10,... | collective-permute-start | bytes 4055048 | tf_op jit(solution)/shard_map/ppermute | solution.py:621
  47.1 31.5 %copy-start.2 = (bf16[528,1280]{1,0:T(8,128)(2,1)S(1)}, bf16[528,1280]{1,0:T(8,128)(2,1)}, u32[]{:S(2)}) copy-start(bf16[528,1280]{1,0:T(8,128)(2,1)} %token_rows.1.r_3_.r_2_) | copy-start | bytes 4055044
  47.1 31.5 %copy-start.18 = (bf16[896,1280]{1,0:T(8,128)(2,1)S(1)}, bf16[896,1280]{1,0:T(8,128)(2,1)}, u32[]{:S(2)}) copy-start(bf16[896,1280]{1,0:T(8,128)(2,1)} %r_4_.1) | copy-start | bytes 6881284
  78.6 25.6 %copy-start.29 = (bf16[1280,16]{0,1:T(8,128)(2,1)S(1)}, bf16[1280,16]{0,1:T(8,128)(2,1)}, u32[]{:S(2)}) copy-start(bf16[1280,16]{0,1:T(8,128)(2,1)} %param.20) | copy-start | bytes 122884
  96.6 3.4 collective-permute-start.5
  101.0 62.4 %collective-permute-start.8 = (bf16[640,2688]{1,0:T(8,128)(2,1)}, bf16[640,2688]{1,0:T(8,128)(2,1)}, u32[]{:S(2)}, u32[]{:S(2)}) collective-permute-start(bf16[640,2688]{1,0:T(8,128)(2,1)} %get-tuple-element.236), channel_id=1, source_target_pairs={{0,1},{1,0},{2,3},{3,2},{4,5},{5,4},{6,7},{7,6},{8,9},{9,8},{10,11... | collective-permute-start | bytes 10321928 | tf_op jit(solution)/shard_map/ppermute | solution.py:616
  101.4 62.0 %collective-permute-start.11 = (bf16[528,1280]{1,0:T(8,128)(2,1)}, bf16[528,1280]{1,0:T(8,128)(2,1)S(1)}, u32[]{:S(2)}, u32[]{:S(2)}) collective-permute-start(bf16[528,1280]{1,0:T(8,128)(2,1)} %collective-permute-done.3.r_3_), channel_id=1, source_target_pairs={{0,2},{1,3},{2,4},{3,5},{4,6},{5,7},{6,0},{7,1},{8,10},{9,11},{10,... | collective-permute-start | bytes 4055048 | tf_op jit(solution)/shard_map/ppermute | solution.py:621
  102.6 60.8 %collective-permute-start.10 = (bf16[512,1280]{1,0:T(8,128)(2,1)}, bf16[512,1280]{1,0:T(8,128)(2,1)}, u32[]{:S(2)}, u32[]{:S(2)}) collective-permute-start(bf16[512,1280]{1,0:T(8,128)(2,1)} %collective-permute-done.4.r_1_), channel_id=1, source_target_pairs={{0,2},{1,3},{2,4},{3,5},{4,6},{5,7},{6,0},{7,1},{8,10},{9,11},{10,... | collective-permute-start | bytes 3932168 | tf_op jit(solution)/shard_map/ppermute | solution.py:621
  104.1 59.3 %collective-permute-start.7 = (bf16[512,1280]{1,0:T(8,128)(2,1)}, bf16[512,1280]{1,0:T(8,128)(2,1)}, u32[]{:S(2)}, u32[]{:S(2)}) collective-permute-start(bf16[512,1280]{1,0:T(8,128)(2,1)} %get-tuple-element.232), channel_id=1, source_target_pairs={{0,1},{1,0},{2,3},{3,2},{4,5},{5,4},{6,7},{7,6},{8,9},{9,8},{10,11... | collective-permute-start | bytes 3932168 | tf_op jit(solution)/shard_map/ppermute | solution.py:616
  105.5 58.0 %copy-start.35 = (bf16[640,2688]{1,0:T(8,128)(2,1)S(1)}, bf16[640,2688]{1,0:T(8,128)(2,1)}, u32[]{:S(2)}) copy-start(bf16[640,2688]{1,0:T(8,128)(2,1)} %get-tuple-element.235) | copy-start | bytes 10321924
  166.7 4.4 collective-permute-start.12
  166.7 6.0 %collective-permute-start.17 = (bf16[512,1280]{1,0:T(8,128)(2,1)S(1)}, bf16[512,1280]{1,0:T(8,128)(2,1)}, u32[]{:S(2)}, u32[]{:S(2)}) collective-permute-start(bf16[512,1280]{1,0:T(8,128)(2,1)S(1)} %copy-done.65), channel_id=1, source_target_pairs={{0,1},{1,0},{2,3},{3,2},{4,5},{5,4},{6,7},{7,6},{8,9},{9,8},{10,11... | collective-permute-start | bytes 3932168 | tf_op jit(solution)/shard_map/ppermute | solution.py:616
  167.2 52.7 %collective-permute-start.9 = (bf16[2,2,2,40,2688]{4,3,2,1,0:T(8,128)(2,1)}, bf16[2,2,2,40,2688]{4,3,2,1,0:T(8,128)(2,1)}, u32[]{:S(2)}, u32[]{:S(2)}) collective-permute-start(bf16[2,2,2,40,2688]{4,3,2,1,0:T(8,128)(2,1)} %fusion.2), channel_id=1, source_target_pairs={{0,8},{8,0},{16,24},{24,16},{1,9},{9,1},{17,25},{25,17},{2,10},{10... | collective-permute-start | bytes 5160968 | tf_op jit(solution)/shard_map/ppermute | solution.py:662
  168.8 7.1 %collective-permute-start.14 = (bf16[528,1280]{1,0:T(8,128)(2,1)}, bf16[528,1280]{1,0:T(8,128)(2,1)}, u32[]{:S(2)}, u32[]{:S(2)}) collective-permute-start(bf16[528,1280]{1,0:T(8,128)(2,1)} %collective-permute-done.3.r_3_), channel_id=1, source_target_pairs={{0,1},{1,0},{2,3},{3,2},{4,5},{5,4},{6,7},{7,6},{8,9},{9,8},{10,11... | collective-permute-start | bytes 4055048 | tf_op jit(solution)/shard_map/ppermute | solution.py:616
  168.8 51.1 %collective-permute-start.16 = (bf16[512,1280]{1,0:T(8,128)(2,1)}, bf16[512,1280]{1,0:T(8,128)(2,1)}, u32[]{:S(2)}, u32[]{:S(2)}) collective-permute-start(bf16[512,1280]{1,0:T(8,128)(2,1)} %collective-permute-done.10.r_1_), channel_id=1, source_target_pairs={{0,2},{1,3},{2,4},{3,5},{4,6},{5,7},{6,0},{7,1},{8,10},{9,11},{10,... | collective-permute-start | bytes 3932168 | tf_op jit(solution)/shard_map/ppermute | solution.py:621
  171.1 4.8 collective-permute-start.13
  172.7 59.3 %collective-permute-start.18 = (bf16[544,1280]{1,0:T(8,128)(2,1)}, bf16[544,1280]{1,0:T(8,128)(2,1)}, u32[]{:S(2)}, u32[]{:S(2)}) collective-permute-start(bf16[544,1280]{1,0:T(8,128)(2,1)} %add_convert_fusion.3), channel_id=1, source_target_pairs={{0,2},{1,3},{2,4},{3,5},{4,6},{5,7},{6,0},{7,1},{8,10},{9,11},{10,... | collective-permute-start | bytes 4177928 | tf_op jit(solution)/shard_map/ppermute | solution.py:621
  232.0 3.2 collective-permute-start.19
  237.1 36.9 %collective-permute-start.23 = (bf16[544,1280]{1,0:T(8,128)(2,1)S(1)}, bf16[544,1280]{1,0:T(8,128)(2,1)S(1)}, u32[]{:S(2)}, u32[]{:S(2)}) collective-permute-start(bf16[544,1280]{1,0:T(8,128)(2,1)S(1)} %add_convert_fusion.2), channel_id=1, source_target_pairs={{0,2},{1,3},{2,4},{3,5},{4,6},{5,7},{6,0},{7,1},{8,10},{9,11},{10,... | collective-permute-start | bytes 4177928 | tf_op jit(solution)/shard_map/ppermute | solution.py:621
  237.1 3.7 collective-permute-start.21
  237.3 5.0 collective-permute-start.20
  237.7 36.3 %collective-permute-start.22 = (bf16[512,1280]{1,0:T(8,128)(2,1)}, bf16[512,1280]{1,0:T(8,128)(2,1)S(1)}, u32[]{:S(2)}, u32[]{:S(2)}) collective-permute-start(bf16[512,1280]{1,0:T(8,128)(2,1)} %get-tuple-element.283), channel_id=1, source_target_pairs={{0,1},{1,0},{2,3},{3,2},{4,5},{5,4},{6,7},{7,6},{8,9},{9,8},{10,11... | collective-permute-start | bytes 3932168 | tf_op jit(solution)/shard_map/ppermute | solution.py:616
  237.9 36.1 %collective-permute-start.15 = (bf16[2,2,40,2688]{3,2,1,0:T(8,128)(2,1)S(1)}, bf16[2,2,40,2688]{3,2,1,0:T(8,128)(2,1)S(1)}, u32[]{:S(2)}, u32[]{:S(2)}) collective-permute-start(bf16[2,2,40,2688]{3,2,1,0:T(8,128)(2,1)S(1)} %fusion.3), channel_id=1, source_target_pairs={{0,16},{8,24},{16,0},{24,8},{1,17},{9,25},{17,1},{25,9},{2,18},{10... | collective-permute-start | bytes 2580488 | tf_op jit(solution)/shard_map/ppermute | solution.py:662
  274.0 3.4 collective-permute-start.24
  279.4 55.2 %collective-permute-start.25 = (bf16[544,1280]{1,0:T(8,128)(2,1)}, bf16[544,1280]{1,0:T(8,128)(2,1)S(1)}, u32[]{:S(2)}, u32[]{:S(2)}) collective-permute-start(bf16[544,1280]{1,0:T(8,128)(2,1)} %get-tuple-element.287), channel_id=1, source_target_pairs={{0,1},{1,0},{2,3},{3,2},{4,5},{5,4},{6,7},{7,6},{8,9},{9,8},{10,11... | collective-permute-start | bytes 4177928 | tf_op jit(solution)/shard_map/ppermute | solution.py:616
  279.6 55.0 %collective-permute-start.26 = (bf16[544,1280]{1,0:T(8,128)(2,1)S(1)}, bf16[544,1280]{1,0:T(8,128)(2,1)S(1)}, u32[]{:S(2)}, u32[]{:S(2)}) collective-permute-start(bf16[544,1280]{1,0:T(8,128)(2,1)S(1)} %add_convert_fusion.1), channel_id=1, source_target_pairs={{0,2},{1,3},{2,4},{3,5},{4,6},{5,7},{6,0},{7,1},{8,10},{9,11},{10,... | collective-permute-start | bytes 4177928 | tf_op jit(solution)/shard_map/ppermute | solution.py:621
  279.6 55.0 %collective-permute-start.29 = (bf16[512,1280]{1,0:T(8,128)(2,1)}, bf16[512,1280]{1,0:T(8,128)(2,1)S(1)}, u32[]{:S(2)}, u32[]{:S(2)}) collective-permute-start(bf16[512,1280]{1,0:T(8,128)(2,1)} %get-tuple-element.305), channel_id=1, source_target_pairs={{0,1},{1,0},{2,3},{3,2},{4,5},{5,4},{6,7},{7,6},{8,9},{9,8},{10,11... | collective-permute-start | bytes 3932168 | tf_op jit(solution)/shard_map/ppermute | solution.py:616
  288.7 50.4 %copy-start.23 = (bf16[448,1280]{1,0:T(8,128)(2,1)}, bf16[448,1280]{1,0:T(8,128)(2,1)S(1)}, u32[]{:S(2)}) copy-start(bf16[448,1280]{1,0:T(8,128)(2,1)S(1)} %get-tuple-element.291) | copy-start | bytes 3440644
  298.5 36.1 %collective-permute-start.27 = (bf16[448,1280]{1,0:T(8,128)(2,1)S(1)}, bf16[448,1280]{1,0:T(8,128)(2,1)}, u32[]{:S(2)}, u32[]{:S(2)}) collective-permute-start(bf16[448,1280]{1,0:T(8,128)(2,1)S(1)} %get-tuple-element.295), channel_id=1, source_target_pairs={{0,16},{8,24},{16,0},{24,8},{1,17},{9,25},{17,1},{25,9},{2,18},{10... | collective-permute-start | bytes 3440648 | tf_op jit(solution)/shard_map/ppermute | solution.py:822
  300.0 34.6 %collective-permute-start.28 = (bf16[448,1280]{1,0:T(8,128)(2,1)S(1)}, bf16[448,1280]{1,0:T(8,128)(2,1)}, u32[]{:S(2)}, u32[]{:S(2)}) collective-permute-start(bf16[448,1280]{1,0:T(8,128)(2,1)S(1)} %get-tuple-element.292), channel_id=1, source_target_pairs={{0,8},{8,0},{16,24},{24,16},{1,9},{9,1},{17,25},{25,17},{2,10},{10... | collective-permute-start | bytes 3440648 | tf_op jit(solution)/shard_map/ppermute | solution.py:822
  334.6 33.5 %collective-permute-start.30 = (bf16[512,1280]{1,0:T(8,128)(2,1)}, bf16[512,1280]{1,0:T(8,128)(2,1)}, u32[]{:S(2)}, u32[]{:S(2)}) collective-permute-start(bf16[512,1280]{1,0:T(8,128)(2,1)} %add_convert_fusion.8), channel_id=1, source_target_pairs={{0,2},{1,3},{2,4},{3,5},{4,6},{5,7},{6,0},{7,1},{8,10},{9,11},{10,... | collective-permute-start | bytes 3932168 | tf_op jit(solution)/shard_map/ppermute | solution.py:621
  337.1 72.4 %collective-permute-start.32 = (bf16[640,1792]{1,0:T(8,128)(2,1)}, bf16[640,1792]{1,0:T(8,128)(2,1)}, u32[]{:S(2)}, u32[]{:S(2)}) collective-permute-start(bf16[640,1792]{1,0:T(8,128)(2,1)} %copy-done.32), channel_id=1, source_target_pairs={{0,8},{8,0},{16,24},{24,16},{1,9},{9,1},{17,25},{25,17},{2,10},{10... | collective-permute-start | bytes 6881288 | tf_op jit(solution)/shard_map/ppermute | solution.py:822
  338.6 70.9 %collective-permute-start.33 = (bf16[640,1792]{1,0:T(8,128)(2,1)}, bf16[640,1792]{1,0:T(8,128)(2,1)}, u32[]{:S(2)}, u32[]{:S(2)}) collective-permute-start(bf16[640,1792]{1,0:T(8,128)(2,1)} %copy-done.33), channel_id=1, source_target_pairs={{0,16},{8,24},{16,0},{24,8},{1,17},{9,25},{17,1},{25,9},{2,18},{10... | collective-permute-start | bytes 6881288 | tf_op jit(solution)/shard_map/ppermute | solution.py:822
  370.0 39.5 %collective-permute-start.31 = (bf16[512,1280]{1,0:T(8,128)(2,1)S(1)}, bf16[512,1280]{1,0:T(8,128)(2,1)}, u32[]{:S(2)}, u32[]{:S(2)}) collective-permute-start(bf16[512,1280]{1,0:T(8,128)(2,1)S(1)} %add_convert_fusion.7), channel_id=1, source_target_pairs={{0,2},{1,3},{2,4},{3,5},{4,6},{5,7},{6,0},{7,1},{8,10},{9,11},{10,... | collective-permute-start | bytes 3932168 | tf_op jit(solution)/shard_map/ppermute | solution.py:621
  372.8 36.6 %collective-permute-start.35 = (bf16[224,1280]{1,0:T(8,128)(2,1)S(1)}, bf16[224,1280]{1,0:T(8,128)(2,1)S(1)}, u32[]{:S(2)}, u32[]{:S(2)}) collective-permute-start(bf16[224,1280]{1,0:T(8,128)(2,1)S(1)} %fusion.18), channel_id=1, source_target_pairs={{0,8},{8,0},{16,24},{24,16},{1,9},{9,1},{17,25},{25,17},{2,10},{10... | collective-permute-start | bytes 1720328 | tf_op jit(solution)/shard_map/ppermute | solution.py:662
  373.3 36.2 %collective-permute-start.34 = (bf16[224,1280]{1,0:T(8,128)(2,1)S(1)}, bf16[224,1280]{1,0:T(8,128)(2,1)S(1)}, u32[]{:S(2)}, u32[]{:S(2)}) collective-permute-start(bf16[224,1280]{1,0:T(8,128)(2,1)S(1)} %fusion.17), channel_id=1, source_target_pairs={{0,16},{8,24},{16,0},{24,8},{1,17},{9,25},{17,1},{25,9},{2,18},{10... | collective-permute-start | bytes 1720328 | tf_op jit(solution)/shard_map/ppermute | solution.py:662
  410.5 5.3 collective-permute-start.38
  410.5 9.0 %collective-permute-start.37 = (bf16[640,2048]{1,0:T(8,128)(2,1)}, bf16[640,2048]{1,0:T(8,128)(2,1)}, u32[]{:S(2)}, u32[]{:S(2)}) collective-permute-start(bf16[640,2048]{1,0:T(8,128)(2,1)} %get-tuple-element.344), channel_id=1, source_target_pairs={{0,1},{1,0},{2,3},{3,2},{4,5},{5,4},{6,7},{7,6},{8,9},{9,8},{10,11... | collective-permute-start | bytes 7864328 | tf_op jit(solution)/shard_map/ppermute | solution.py:616
  411.0 14.9 %collective-permute-start.36 = (bf16[640,1152]{1,0:T(8,128)(2,1)}, bf16[640,1152]{1,0:T(8,128)(2,1)}, u32[]{:S(2)}, u32[]{:S(2)}) collective-permute-start(bf16[640,1152]{1,0:T(8,128)(2,1)} %get-tuple-element.339), channel_id=1, source_target_pairs={{0,1},{1,0},{2,3},{3,2},{4,5},{5,4},{6,7},{7,6},{8,9},{9,8},{10,11... | collective-permute-start | bytes 4423688 | tf_op jit(solution)/shard_map/ppermute | solution.py:616
  417.7 31.7 %collective-permute-start.42 = (bf16[2,2,2,40,2048]{4,3,2,1,0:T(8,128)(2,1)S(1)}, bf16[2,2,2,40,2048]{4,3,2,1,0:T(8,128)(2,1)S(1)}, u32[]{:S(2)}, u32[]{:S(2)}) collective-permute-start(bf16[2,2,2,40,2048]{4,3,2,1,0:T(8,128)(2,1)S(1)} %fusion.4), channel_id=1, source_target_pairs={{0,8},{8,0},{16,24},{24,16},{1,9},{9,1},{17,25},{25,17},{2,10},{10... | collective-permute-start | bytes 3932168 | tf_op jit(solution)/shard_map/ppermute | solution.py:662
  421.4 30.9 %collective-permute-start.41 = (bf16[2,2,2,40,2048]{4,3,2,1,0:T(8,128)(2,1)S(1)}, bf16[2,2,2,40,2048]{4,3,2,1,0:T(8,128)(2,1)S(1)}, u32[]{:S(2)}, u32[]{:S(2)}) collective-permute-start(bf16[2,2,2,40,2048]{4,3,2,1,0:T(8,128)(2,1)S(1)} %fusion.5), channel_id=1, source_target_pairs={{0,16},{8,24},{16,0},{24,8},{1,17},{9,25},{17,1},{25,9},{2,18},{10... | collective-permute-start | bytes 3932168 | tf_op jit(solution)/shard_map/ppermute | solution.py:662
  423.8 45.7 %collective-permute-start.43 = (bf16[512,1280]{1,0:T(8,128)(2,1)S(1)}, bf16[512,1280]{1,0:T(8,128)(2,1)S(1)}, u32[]{:S(2)}, u32[]{:S(2)}) collective-permute-start(bf16[512,1280]{1,0:T(8,128)(2,1)S(1)} %convert_add_fusion.1), channel_id=1, source_target_pairs={{0,2},{1,3},{2,4},{3,5},{4,6},{5,7},{6,0},{7,1},{8,10},{9,11},{10,... | collective-permute-start | bytes 3932168 | tf_op jit(solution)/shard_map/ppermute | solution.py:621
  427.2 37.9 %collective-permute-start.40 = (bf16[2,2,2,40,1152]{4,3,2,1,0:T(8,128)(2,1)S(1)}, bf16[2,2,2,40,1152]{4,3,2,1,0:T(8,128)(2,1)S(1)}, u32[]{:S(2)}, u32[]{:S(2)}) collective-permute-start(bf16[2,2,2,40,1152]{4,3,2,1,0:T(8,128)(2,1)S(1)} %fusion.13), channel_id=1, source_target_pairs={{0,8},{8,0},{16,24},{24,16},{1,9},{9,1},{17,25},{25,17},{2,10},{10... | collective-permute-start | bytes 2211848 | tf_op jit(solution)/shard_map/ppermute | solution.py:662
  430.4 36.3 %collective-permute-start.39 = (bf16[2,40,2688]{2,1,0:T(8,128)(2,1)S(1)}, bf16[2,40,2688]{2,1,0:T(8,128)(2,1)S(1)}, u32[]{:S(2)}, u32[]{:S(2)}) collective-permute-start(bf16[2,40,2688]{2,1,0:T(8,128)(2,1)S(1)} %fusion.12), channel_id=1, source_target_pairs={{0,2},{1,3},{2,0},{3,1},{4,6},{5,7},{6,4},{7,5},{8,10},{9,11},{10,... | collective-permute-start | bytes 1290248 | tf_op jit(solution)/shard_map/ppermute | solution.py:662
  449.4 40.9 %copy-start.48 = (bf16[2,2,2,40,2048]{4,3,2,1,0:T(8,128)(2,1)}, bf16[2,2,2,40,2048]{4,3,2,1,0:T(8,128)(2,1)S(1)}, u32[]{:S(2)}) copy-start(bf16[2,2,2,40,2048]{4,3,2,1,0:T(8,128)(2,1)S(1)} %collective-permute-done.42) | copy-start | bytes 3932164
  451.3 21.6 %collective-permute-start.46 = (bf16[2,2,40,2048]{3,2,1,0:T(8,128)(2,1)S(1)}, bf16[2,2,40,2048]{3,2,1,0:T(8,128)(2,1)S(1)}, u32[]{:S(2)}, u32[]{:S(2)}) collective-permute-start(bf16[2,2,40,2048]{3,2,1,0:T(8,128)(2,1)S(1)} %fusion.7), channel_id=1, source_target_pairs={{0,16},{8,24},{16,0},{24,8},{1,17},{9,25},{17,1},{25,9},{2,18},{10... | collective-permute-start | bytes 1966088 | tf_op jit(solution)/shard_map/ppermute | solution.py:662
  452.3 41.7 %copy-start.49 = (bf16[2,2,2,40,2048]{4,3,2,1,0:T(8,128)(2,1)}, bf16[2,2,2,40,2048]{4,3,2,1,0:T(8,128)(2,1)S(1)}, u32[]{:S(2)}) copy-start(bf16[2,2,2,40,2048]{4,3,2,1,0:T(8,128)(2,1)S(1)} %collective-permute-done.41) | copy-start | bytes 3932164
  454.2 24.2 %collective-permute-start.45 = (bf16[2,2,40,2048]{3,2,1,0:T(8,128)(2,1)S(1)}, bf16[2,2,40,2048]{3,2,1,0:T(8,128)(2,1)S(1)}, u32[]{:S(2)}, u32[]{:S(2)}) collective-permute-start(bf16[2,2,40,2048]{3,2,1,0:T(8,128)(2,1)S(1)} %fusion.6), channel_id=1, source_target_pairs={{0,8},{8,0},{16,24},{24,16},{1,9},{9,1},{17,25},{25,17},{2,10},{10... | collective-permute-start | bytes 1966088 | tf_op jit(solution)/shard_map/ppermute | solution.py:662
  466.3 15.3 %collective-permute-start.44 = (bf16[2,2,40,1152]{3,2,1,0:T(8,128)(2,1)S(1)}, bf16[2,2,40,1152]{3,2,1,0:T(8,128)(2,1)S(1)}, u32[]{:S(2)}, u32[]{:S(2)}) collective-permute-start(bf16[2,2,40,1152]{3,2,1,0:T(8,128)(2,1)S(1)} %fusion.14), channel_id=1, source_target_pairs={{0,16},{8,24},{16,0},{24,8},{1,17},{9,25},{17,1},{25,9},{2,18},{10... | collective-permute-start | bytes 1105928 | tf_op jit(solution)/shard_map/ppermute | solution.py:662
  468.0 30.3 %collective-permute-start.53 = (bf16[40,2688]{1,0:T(8,128)(2,1)S(1)}, bf16[40,2688]{1,0:T(8,128)(2,1)S(1)}, u32[]{:S(2)}, u32[]{:S(2)}) collective-permute-start(bf16[40,2688]{1,0:T(8,128)(2,1)S(1)} %fusion.20), channel_id=1, source_target_pairs={{0,4},{1,5},{2,6},{3,7},{4,0},{5,1},{6,2},{7,3},{8,12},{9,13},{10,... | collective-permute-start | bytes 645128 | tf_op jit(solution)/shard_map/ppermute | solution.py:662
  474.0 14.7 %collective-permute-start.49 = (bf16[2,40,2048]{2,1,0:T(8,128)(2,1)S(1)}, bf16[2,40,2048]{2,1,0:T(8,128)(2,1)S(1)}, u32[]{:S(2)}, u32[]{:S(2)}) collective-permute-start(bf16[2,40,2048]{2,1,0:T(8,128)(2,1)S(1)} %fusion.16), channel_id=1, source_target_pairs={{0,2},{1,3},{2,0},{3,1},{4,6},{5,7},{6,4},{7,5},{8,10},{9,11},{10,... | collective-permute-start | bytes 983048 | tf_op jit(solution)/shard_map/ppermute | solution.py:662
  479.8 14.2 %collective-permute-start.48 = (bf16[2,40,2048]{2,1,0:T(8,128)(2,1)S(1)}, bf16[2,40,2048]{2,1,0:T(8,128)(2,1)S(1)}, u32[]{:S(2)}, u32[]{:S(2)}) collective-permute-start(bf16[2,40,2048]{2,1,0:T(8,128)(2,1)S(1)} %fusion.15), channel_id=1, source_target_pairs={{0,2},{1,3},{2,0},{3,1},{4,6},{5,7},{6,4},{7,5},{8,10},{9,11},{10,... | collective-permute-start | bytes 983048 | tf_op jit(solution)/shard_map/ppermute | solution.py:662
  482.6 13.8 %collective-permute-start.47 = (bf16[2,40,1152]{2,1,0:T(8,128)(2,1)S(1)}, bf16[2,40,1152]{2,1,0:T(8,128)(2,1)S(1)}, u32[]{:S(2)}, u32[]{:S(2)}) collective-permute-start(bf16[2,40,1152]{2,1,0:T(8,128)(2,1)S(1)} %fusion.21), channel_id=1, source_target_pairs={{0,2},{1,3},{2,0},{3,1},{4,6},{5,7},{6,4},{7,5},{8,10},{9,11},{10,... | collective-permute-start | bytes 552968 | tf_op jit(solution)/shard_map/ppermute | solution.py:662
  485.7 36.9 %collective-permute-start.54 = (bf16[320,1792]{1,0:T(8,128)(2,1)}, bf16[320,1792]{1,0:T(8,128)(2,1)}, u32[]{:S(2)}, u32[]{:S(2)}) collective-permute-start(bf16[320,1792]{1,0:T(8,128)(2,1)} %fusion.8), channel_id=1, source_target_pairs={{0,16},{8,24},{16,0},{24,8},{1,17},{9,25},{17,1},{25,9},{2,18},{10... | collective-permute-start | bytes 3440648 | tf_op jit(solution)/shard_map/ppermute | solution.py:662
  488.7 34.0 %collective-permute-start.55 = (bf16[320,1792]{1,0:T(8,128)(2,1)}, bf16[320,1792]{1,0:T(8,128)(2,1)}, u32[]{:S(2)}, u32[]{:S(2)}) collective-permute-start(bf16[320,1792]{1,0:T(8,128)(2,1)} %fusion.9), channel_id=1, source_target_pairs={{0,8},{8,0},{16,24},{24,16},{1,9},{9,1},{17,25},{25,17},{2,10},{10... | collective-permute-start | bytes 3440648 | tf_op jit(solution)/shard_map/ppermute | solution.py:662
  497.3 6.8 %collective-permute-start.50 = (bf16[40,1152]{1,0:T(8,128)(2,1)S(1)}, bf16[40,1152]{1,0:T(8,128)(2,1)S(1)}, u32[]{:S(2)}, u32[]{:S(2)}) collective-permute-start(bf16[40,1152]{1,0:T(8,128)(2,1)S(1)} %fusion.28), channel_id=1, source_target_pairs={{0,4},{1,5},{2,6},{3,7},{4,0},{5,1},{6,2},{7,3},{8,12},{9,13},{10,... | collective-permute-start | bytes 276488 | tf_op jit(solution)/shard_map/ppermute | solution.py:662
  501.0 15.3 %collective-permute-start.52 = (bf16[40,2048]{1,0:T(8,128)(2,1)}, bf16[40,2048]{1,0:T(8,128)(2,1)}, u32[]{:S(2)}, u32[]{:S(2)}) collective-permute-start(bf16[40,2048]{1,0:T(8,128)(2,1)} %fusion.24), channel_id=1, source_target_pairs={{0,4},{1,5},{2,6},{3,7},{4,0},{5,1},{6,2},{7,3},{8,12},{9,13},{10,... | collective-permute-start | bytes 491528 | tf_op jit(solution)/shard_map/ppermute | solution.py:662
  503.1 15.6 %collective-permute-start.51 = (bf16[40,2048]{1,0:T(8,128)(2,1)}, bf16[40,2048]{1,0:T(8,128)(2,1)}, u32[]{:S(2)}, u32[]{:S(2)}) collective-permute-start(bf16[40,2048]{1,0:T(8,128)(2,1)} %fusion.25), channel_id=1, source_target_pairs={{0,4},{1,5},{2,6},{3,7},{4,0},{5,1},{6,2},{7,3},{8,12},{9,13},{10,... | collective-permute-start | bytes 491528 | tf_op jit(solution)/shard_map/ppermute | solution.py:662
  (58 other events, 327.2 us)

commit v7 on v6

--- a/solution.py
+++ b/solution.py
@@ -605,7 +605,7 @@
 
 def expert_sums(scatters):
     flat = lambda term: term.reshape(-1, term.shape[-1])
-    if True or any(len(scatter.choices[0]) != 1 for scatter in scatters):
+    if any(len(scatter.choices[0]) != 1 for scatter in scatters):
         return jnp.stack([scatter.finish() for scatter in scatters])
     chosen = jnp.stack([scatter.choices[0][0][1] for scatter in scatters]).astype(jnp.int32)
     return final_sums(chosen, [[flat(term) for term in scatter.terms] for scatter in scatters])

time: 537 us -> 538 us (level)
  other arithmetic: 69.5 us -> 57.8 us
  Pallas kernels: 300 us -> 310 us
    another operation x6 -> x1, other arithmetic: 11.2 us -> 0.07 us  [expert_sums(): jnp.stack([scatter.choices[0][0][1] for scatter in scatters])]
    pallas_call x0 -> x2, Pallas kernels: none -> 9.73 us  [final_sums(): pl.pallas_call(final_kernel, grid_spec=pltpu.PrefetchScalarGridSpec(num_s...]
    unnamed x135 -> x145, local copies, waits for them, and re-layouts: 20.5 us -> 23.6 us
  transfers between devices with their start and end apart: 56 -> 56, of which waited for: 21 -> 21; matrix products, arithmetic and copies ran while one was open for 11% -> 10% of each run, Pallas kernels for 56% -> 57%
where the time goes in v7:
time: 538 us; the launch traced here: 531 us
  Pallas kernels  310 us (58%)
  waiting for transfers between devices  89 us (17%)
  other arithmetic  57.8 us (11%)
  starting transfers between devices  44.8 us (8%)
  local copies, waits for them, and re-layouts  26.9 us (5%)
    pallas_call x4, Pallas kernels, expert_step(): pl.pallas_call(lambda *r: expert_kernel(cap, tokens, hidden, step in (0,...  151 us
    pallas_call x3, Pallas kernels, attention_backward(): pl.pallas_call(lambda *r: attention_back_kernel(rows, extra, carried, *r)...  49 us
    pallas_call x4, Pallas kernels, weight_grad(): pl.pallas_call(lambda *r: weight_grad_kernel(parts, bit, *r), grid=(n //...  45.5 us
    ppermute x20, waiting for transfers between devices, advance(): lax.ppermute(away, name, [(i, i ^ 1 << bit) for i in range(lax.axis_size(...  37.8 us
    convert_element_type x20, other arithmetic, advance(): away = sum_terms([picked(term, made + [(dim, 1 - mine)]) for term, made i...  33.6 us
    ppermute x12, waiting for transfers between devices, next_chip(): lax.ppermute(values_in, 'expert', [(i, (i + 2) % owners) for i in range(o...  32.3 us
    unnamed x145, local copies, waits for them, and re-layouts  23.6 us
    pallas_call x1, Pallas kernels, attention_forward(): pl.pallas_call(attention_kernel, grid=(pairs,), in_specs=[pl.BlockSpec(me...  23.1 us
  transfers between devices with their start and end apart: 56, of which 21 were waited for; matrix products, arithmetic and copies ran while one was open for 10% of the time, Pallas kernels for 57%

profile of v7, /device:TPU:0, one launch (start us, length us, event | category | flops | bytes accessed | tf_op | source)
XLA Modules:
  0.0 531.1 jit_solution(10957643257304899798)
XLA Ops:
  1.3 1.6 copy.72.ids
  2.9 3.5 token_rows.1.r_3_.r_2_
  6.8 2.6 collective-permute-start
  10.8 23.1 %attention_forward.1 = (bf16[512,1280]{1,0:T(8,128)(2,1)}, bf16[512,1280]{1,0:T(8,128)(2,1)}, bf16[512,1280]{1,0:T(8,128)(2,1)}, bf16[512,1280]{1,0:T(8,128)(2,1...) custom-call(s32[1]{0:T(128)} %copy.133.length_ref.r_0_, ...), custom_call_target="tpu_custom_call" | custom-call | tf_op jit(solution)/shard_map/attention_forward/pallas_call | solution.py:80
  34.1 1.6 collective-permute-start.4
  35.7 6.6 %collective-permute-done.r_3_ = bf16[528,1280]{1,0:T(8,128)(2,1)} collective-permute-done((bf16[528,1280]{1,0:T(8,128)(2,1)}, bf16[528,1280]{1,0:T(8,128)(2,1)}, u32[]{:S(2)}, u32[]{:S(2)}) %collective-permute-start) | collective-permute-done | bytes 1351712 | tf_op jit(solution)/shard_map/ppermute | solution.py:621
  47.4 31.3 %expert_step.4 = (bf16[544,1280]{1,0:T(8,128)(2,1)}, bf16[544,1280]{1,0:T(8,128)(2,1)}, bf16[512,1280]{1,0:T(8,128)(2,1)}, bf16[512,1280]{1,0:T(8,128)(2,1)}, bf...) custom-call(s32[1]{0:T(128)} %bitcast.2.r_0_, ...), custom_call_target="tpu_custom_call" | custom-call | tf_op jit(solution)/shard_map/expert_step/pallas_call | solution.py:332
  78.7 17.4 %shared_expert.1 = (f32[512,1280]{1,0:T(8,128)}, f32[512,1280]{1,0:T(8,128)}, f32[512,128]{1,0:T(8,128)S(1)}, bf16[640,2688]{1,0:T(8,128)(2,1)}, bf16[640,2688]{1,0:T(8,128)(2,1)}) custom-call(s32[1]{0:T(128)} %bitcast.1.r_0_.r_1_, bf16[512,1280]{1,0:T(8,128)(2,1)S(1)} %copy-done.3, bf16[528,1280]{1,0:T(8,128)(2,1)S(1)} %copy-done.2, ...), custom_call_target="tpu_custom_call" | custom-call | tf_op jit(solution)/shard_map/shared_expert/pallas_call | solution.py:449
  97.3 2.9 collective-permute-done.5.r_2_
  102.8 1.6 collective-permute-start.10
  105.8 44.0 %expert_step.5 = (bf16[544,1280]{1,0:T(8,128)(2,1)}, bf16[544,1280]{1,0:T(8,128)(2,1)}, bf16[512,1280]{1,0:T(8,128)(2,1)}, bf16[512,1280]{1,0:T(8,128)(2,1)}, bf...) custom-call(s32[1]{0:T(128)} %bitcast.2.r_0_, ...), custom_call_target="tpu_custom_call", output_to_operand_aliasing={{4}: (8, {}), {5}: (9, {}), {6}: (10, {}), {7}: (11, {})} | custom-call | tf_op jit(solution)/shard_map/expert_step/pallas_call | solution.py:332
  149.8 13.9 %collective-permute-done.10.r_1_ = bf16[512,1280]{1,0:T(8,128)(2,1)} collective-permute-done((bf16[512,1280]{1,0:T(8,128)(2,1)}, bf16[512,1280]{1,0:T(8,128)(2,1)}, u32[]{:S(2)}, u32[]{:S(2)}) %collective-permute-start.10) | collective-permute-done | bytes 1310752 | tf_op jit(solution)/shard_map/ppermute | solution.py:621
  163.7 3.3 fusion
  167.5 1.6 collective-permute-start.9
  169.1 2.3 collective-permute-done.12
  173.1 3.1 add_convert_fusion.8
  176.2 44.0 %expert_step.6 = (bf16[544,1280]{1,0:T(8,128)(2,1)}, bf16[544,1280]{1,0:T(8,128)(2,1)}, bf16[512,1280]{1,0:T(8,128)(2,1)}, bf16[512,1280]{1,0:T(8,128)(2,1)}, bf...) custom-call(s32[1]{0:T(128)} %bitcast.2.r_0_, ...), custom_call_target="tpu_custom_call", output_to_operand_aliasing={{4}: (8, {}), {5}: (9, {}), {6}: (10, {}), {7}: (11, {})} | custom-call | tf_op jit(solution)/shard_map/expert_step/pallas_call | solution.py:332
  220.3 2.1 fusion.1
  222.4 9.8 %collective-permute-done.18 = bf16[544,1280]{1,0:T(8,128)(2,1)} collective-permute-done((bf16[544,1280]{1,0:T(8,128)(2,1)}, bf16[544,1280]{1,0:T(8,128)(2,1)}, u32[]{:S(2)}, u32[]{:S(2)}) %collective-permute-start.18) | collective-permute-done | bytes 1392672 | tf_op jit(solution)/shard_map/ppermute | solution.py:621
  232.3 3.1 collective-permute-done.19
  235.4 1.9 add_convert_fusion.2
  238.1 1.6 collective-permute-start.15
  242.7 31.8 %expert_step.7 = (bf16[544,1280]{1,0:T(8,128)(2,1)}, bf16[544,1280]{1,0:T(8,128)(2,1)}, bf16[512,1280]{1,0:T(8,128)(2,1)}, bf16[512,1280]{1,0:T(8,128)(2,1)}, bf...) custom-call(s32[1]{0:T(128)} %bitcast.2.r_0_, ...), custom_call_target="tpu_custom_call", output_to_operand_aliasing={{4}: (8, {}), {5}: (9, {}), {6}: (10, {}), {7}: (11, {})} | custom-call | tf_op jit(solution)/shard_map/expert_step/pallas_call | solution.py:332
  274.7 3.2 collective-permute-done.24
  278.0 1.9 add_convert_fusion.1
  280.5 8.5 %weight_grad.4 = (bf16[448,1280]{1,0:T(8,128)(2,1)S(1)}, bf16[448,1280]{1,0:T(8,128)(2,1)S(1)}) custom-call(s32[1]{0:T(128)} %bitcast.9.r_0_, bf16[2,1920,896]{2,1,0:T(8,128)(2,1)} %get-tuple-element.293.r_1_, bf16[2,1920,1280]{2,1,0:T(8,128)(2,1)} %get-tuple-element.290.r_2_), custom_call_target="tpu_custom_call" | custom-call | tf_op jit(solution)/shard_map/weight_grad/pallas_call | solution.py:527
  289.0 8.7 %weight_grad.5 = (bf16[448,1280]{1,0:T(8,128)(2,1)S(1)}, bf16[448,1280]{1,0:T(8,128)(2,1)S(1)}) custom-call(s32[1]{0:T(128)} %bitcast.9.r_0_, bf16[2,1920,896]{2,1,0:T(8,128)(2,1)} %get-tuple-element.293.r_1_, bf16[2,1920,1280]{2,1,0:T(8,128)(2,1)} %get-tuple-element.290.r_2_), custom_call_target="tpu_custom_call" | custom-call | tf_op jit(solution)/shard_map/weight_grad/pallas_call | solution.py:527
  298.8 1.6 collective-permute-start.27
  300.9 14.2 %weight_grad.6 = (bf16[640,1792]{1,0:T(8,128)(2,1)S(1)}, bf16[640,1792]{1,0:T(8,128)(2,1)S(1)}) custom-call(s32[1]{0:T(128)} %bitcast.9.r_0_, bf16[2,1920,1280]{2,1,0:T(8,128)(2,1)} %get-tuple-element.301.r_1_, bf16[2,1920,1792]{2,1,0:T(8,128)(2,1)} %get-tuple-element.298.r_2_), custom_call_target="tpu_custom_call" | custom-call | tf_op jit(solution)/shard_map/weight_grad/pallas_call | solution.py:527
  317.8 14.2 %weight_grad.7 = (bf16[640,1792]{1,0:T(8,128)(2,1)S(1)}, bf16[640,1792]{1,0:T(8,128)(2,1)S(1)}) custom-call(s32[1]{0:T(128)} %bitcast.9.r_0_, bf16[2,1920,1280]{2,1,0:T(8,128)(2,1)} %get-tuple-element.301.r_1_, bf16[2,1920,1792]{2,1,0:T(8,128)(2,1)} %get-tuple-element.298.r_2_), custom_call_target="tpu_custom_call" | custom-call | tf_op jit(solution)/shard_map/weight_grad/pallas_call | solution.py:527
  334.9 1.7 collective-permute-start.30
  340.8 8.7 %middle_back.1 = (f32[512,1280]{1,0:T(8,128)}, bf16[512,1280]{1,0:T(8,128)(2,1)S(1)}, f32[1280,128]{1,0:T(8,128)S(1)}) custom-call(s32[1]{0:T(128)} %copy.133.length_ref.r_0_, bf16[544,1280]{1,0:T(8,128)(2,1)} %get-tuple-element.310.r_1_, bf16[544,1280]{1,0:T(8,128)(2,1)} %copy-done.45, bf16[544,1280]{1,0:T(8,128)(2,1)} %copy-done.46, ...), custom_call_target="tpu_custom_call" | custom-call | tf_op jit(solution)/shard_map/middle_back/pallas_call | solution.py:495
  349.5 17.0 %attention_backward.3 = (bf16[640,2048]{1,0:T(8,128)(2,1)S(1)}, bf16[640,2048]{1,0:T(8,128)(2,1)}, f32[512,1280]{1,0:T(8,128)}) custom-call(s32[2]{0:T(128)S(1)} %pad_add_fusion.2.r_0_, s32[1]{0:T(128)} %bitcast.1.r_0_.r_1_, bf16[512,1280]{1,0:T(8,128)(2,1)S(1)} %get-tuple-element.330.r_2_, bf16[1280,1280]{1,0:T(8,128)(2,1)} %r_3_.7, ...), custom_call_target="tpu_custom_call" | custom-call | tf_op jit(solution)/shard_map/attention_backward/pallas_call | solution.py:190
  366.5 1.9 collective-permute-done.30
  368.4 1.8 add_convert_fusion.7
  370.2 2.8 collective-permute-start.31
  375.2 17.9 %attention_backward.4 = (bf16[640,2048]{1,0:T(8,128)(2,1)S(1)}, bf16[640,2048]{1,0:T(8,128)(2,1)}, f32[512,1280]{1,0:T(8,128)}) custom-call(s32[2]{0:T(128)S(1)} %get-tuple-element.476.r_0_, s32[1]{0:T(128)} %bitcast.1.r_0_.r_1_, bf16[512,1280]{1,0:T(8,128)(2,1)S(1)} %get-tuple-element.330.r_2_, bf16[1280,1280]{1,0:T(8,128)(2,1)} %r_3_.7, ...), custom_call_target="tpu_custom_call" | custom-call | tf_op jit(solution)/shard_map/attention_backward/pallas_call | solution.py:190
  394.7 14.0 %attention_backward.5 = (bf16[640,1152]{1,0:T(8,128)(2,1)S(1)}, bf16[640,1152]{1,0:T(8,128)(2,1)}, f32[512,1280]{1,0:T(8,128)}) custom-call(s32[2]{0:T(128)S(1)} %get-tuple-element.475.r_0_, s32[1]{0:T(128)} %bitcast.1.r_0_.r_1_, bf16[512,1280]{1,0:T(8,128)(2,1)S(1)} %get-tuple-element.330.r_2_, bf16[1280,1280]{1,0:T(8,128)(2,1)} %r_3_.7, ...), custom_call_target="tpu_custom_call" | custom-call | tf_op jit(solution)/shard_map/attention_backward/pallas_call | solution.py:190
  412.7 4.2 collective-permute-done.38
  416.9 1.9 fusion.2
  420.6 1.9 fusion.3
  423.3 2.0 convert_add_fusion.1
  425.2 1.7 collective-permute-start.43
  431.8 4.4 final_sums.2
  436.2 14.3 %collective-permute-done.42 = bf16[2,2,2,40,2048]{4,3,2,1,0:T(8,128)(2,1)S(1)} collective-permute-done((bf16[2,2,2,40,2048]{4,3,2,1,0:T(8,128)(2,1)S(1)}, bf16[2,2,2,40,2048]{4,3,2,1,0:T(8,128)(2,1)S(1)}, u32[]{:S(2)}, u32[]{:S(2)}) %collective-permute-start.42) | collective-permute-done | bytes 1310752 | tf_op jit(solution)/shard_map/ppermute | solution.py:662
  450.5 1.9 fusion.5
  453.5 1.9 fusion.4
  455.4 1.5 collective-permute-start.45
  457.0 9.3 %collective-permute-done.40 = bf16[2,2,2,40,1152]{4,3,2,1,0:T(8,128)(2,1)S(1)} collective-permute-done((bf16[2,2,2,40,1152]{4,3,2,1,0:T(8,128)(2,1)S(1)}, bf16[2,2,2,40,1152]{4,3,2,1,0:T(8,128)(2,1)S(1)}, u32[]{:S(2)}, u32[]{:S(2)}) %collective-permute-start.40) | collective-permute-done | bytes 737312 | tf_op jit(solution)/shard_map/ppermute | solution.py:662
  470.9 3.3 add_convert_fusion.4
  476.7 2.9 collective-permute-done.45
  480.9 1.8 collective-permute-start.48
  484.1 2.7 fusion.6
  487.4 2.6 fusion.7
  491.4 1.8 fusion.21
  493.2 1.9 collective-permute-done.48
  495.1 1.8 fusion.20
  502.1 2.3 collective-permute-start.52
  509.7 7.8 %collective-permute-done.52 = bf16[40,2048]{1,0:T(8,128)(2,1)} collective-permute-done((bf16[40,2048]{1,0:T(8,128)(2,1)}, bf16[40,2048]{1,0:T(8,128)(2,1)}, u32[]{:S(2)}, u32[]{:S(2)}) %collective-permute-start.52) | collective-permute-done | bytes 163872 | tf_op jit(solution)/shard_map/ppermute | solution.py:662
  517.5 2.1 fusion.18.r_1_
  519.7 2.1 fusion.19.r_0_
  521.8 2.1 assemble.1
  523.9 1.6 copy-done.14
  525.6 5.4 %final_sums.3 = f32[2,320,1792]{2,1,0:T(8,128)} custom-call(s32[2]{0:T(128)S(1)} %pad_add_fusion.3.chosen_ref, bf16[640,1792]{1,0:T(8,128)(2,1)S(1)} %copy-done.11, bf16[640,1792]{1,0:T(8,128)(2,1)} %bitcast.90.refs_1_, bf16[320,1792]{1,0:T(8,128)(2,1)S(1)} %collective-permute-done.54.refs_2_, bf16[640,1792]{1,0:T(8,128)(2,1)S(1)} %copy-done.14, ...), custom_call_target="tpu_custom_call" | custom-call | tf_op jit(solution)/shard_map/final_sums/pallas_call | solution.py:591
  (264 shorter events, 68.3 us)
Async XLA Ops:
  6.4 37.6 %collective-permute-start.2 = (bf16[528,1280]{1,0:T(8,128)(2,1)}, bf16[528,1280]{1,0:T(8,128)(2,1)}, u32[]{:S(2)}, u32[]{:S(2)}) collective-permute-start(bf16[528,1280]{1,0:T(8,128)(2,1)} %token_rows.1.r_3_.r_2_), channel_id=1, source_target_pairs={{0,1},{1,0},{2,3},{3,2},{4,5},{5,4},{6,7},{7,6},{8,9},{9,8},{10,11... | collective-permute-start | bytes 4055048 | tf_op jit(solution)/shard_map/ppermute | solution.py:616
  6.8 35.5 %collective-permute-start = (bf16[528,1280]{1,0:T(8,128)(2,1)}, bf16[528,1280]{1,0:T(8,128)(2,1)}, u32[]{:S(2)}, u32[]{:S(2)}) collective-permute-start(bf16[528,1280]{1,0:T(8,128)(2,1)} %token_rows.1.r_3_.r_2_), channel_id=1, source_target_pairs={{0,2},{1,3},{2,4},{3,5},{4,6},{5,7},{6,0},{7,1},{8,10},{9,11},{10,... | collective-permute-start | bytes 4055048 | tf_op jit(solution)/shard_map/ppermute | solution.py:621
  33.9 10.0 %collective-permute-start.1 = (bf16[512,1280]{1,0:T(8,128)(2,1)}, bf16[512,1280]{1,0:T(8,128)(2,1)S(1)}, u32[]{:S(2)}, u32[]{:S(2)}) collective-permute-start(bf16[512,1280]{1,0:T(8,128)(2,1)} %get-tuple-element.227.r_1_.r_6_), channel_id=1, source_target_pairs={{0,1},{1,0},{2,3},{3,2},{4,5},{5,4},{6,7},{7,6},{8,9},{9,8},{10,11... | collective-permute-start | bytes 3932168 | tf_op jit(solution)/shard_map/ppermute | solution.py:616
  34.1 62.7 %collective-permute-start.4 = (bf16[512,1280]{1,0:T(8,128)(2,1)}, bf16[512,1280]{1,0:T(8,128)(2,1)}, u32[]{:S(2)}, u32[]{:S(2)}) collective-permute-start(bf16[512,1280]{1,0:T(8,128)(2,1)} %get-tuple-element.227.r_1_.r_6_), channel_id=1, source_target_pairs={{0,2},{1,3},{2,4},{3,5},{4,6},{5,7},{6,0},{7,1},{8,10},{9,11},{10,... | collective-permute-start | bytes 3932168 | tf_op jit(solution)/shard_map/ppermute | solution.py:621
  42.3 58.9 %collective-permute-start.6 = (bf16[528,1280]{1,0:T(8,128)(2,1)}, bf16[528,1280]{1,0:T(8,128)(2,1)}, u32[]{:S(2)}, u32[]{:S(2)}) collective-permute-start(bf16[528,1280]{1,0:T(8,128)(2,1)} %collective-permute-done.r_3_), channel_id=1, source_target_pairs={{0,1},{1,0},{2,3},{3,2},{4,5},{5,4},{6,7},{7,6},{8,9},{9,8},{10,11... | collective-permute-start | bytes 4055048 | tf_op jit(solution)/shard_map/ppermute | solution.py:616
  42.3 58.9 %collective-permute-start.3 = (bf16[528,1280]{1,0:T(8,128)(2,1)}, bf16[528,1280]{1,0:T(8,128)(2,1)}, u32[]{:S(2)}, u32[]{:S(2)}) collective-permute-start(bf16[528,1280]{1,0:T(8,128)(2,1)} %collective-permute-done.r_3_), channel_id=1, source_target_pairs={{0,2},{1,3},{2,4},{3,5},{4,6},{5,7},{6,0},{7,1},{8,10},{9,11},{10,... | collective-permute-start | bytes 4055048 | tf_op jit(solution)/shard_map/ppermute | solution.py:621
  47.4 31.3 %copy-start.2 = (bf16[528,1280]{1,0:T(8,128)(2,1)S(1)}, bf16[528,1280]{1,0:T(8,128)(2,1)}, u32[]{:S(2)}) copy-start(bf16[528,1280]{1,0:T(8,128)(2,1)} %token_rows.1.r_3_.r_2_) | copy-start | bytes 4055044
  47.4 31.3 %copy-start.27 = (bf16[896,1280]{1,0:T(8,128)(2,1)S(1)}, bf16[896,1280]{1,0:T(8,128)(2,1)}, u32[]{:S(2)}) copy-start(bf16[896,1280]{1,0:T(8,128)(2,1)} %r_4_.1) | copy-start | bytes 6881284
  78.7 25.8 %copy-start.33 = (bf16[1280,16]{0,1:T(8,128)(2,1)S(1)}, bf16[1280,16]{0,1:T(8,128)(2,1)}, u32[]{:S(2)}) copy-start(bf16[1280,16]{0,1:T(8,128)(2,1)} %param.20) | copy-start | bytes 122884
  96.8 3.4 collective-permute-start.5
  101.3 62.4 %collective-permute-start.8 = (bf16[640,2688]{1,0:T(8,128)(2,1)}, bf16[640,2688]{1,0:T(8,128)(2,1)}, u32[]{:S(2)}, u32[]{:S(2)}) collective-permute-start(bf16[640,2688]{1,0:T(8,128)(2,1)} %get-tuple-element.236), channel_id=1, source_target_pairs={{0,1},{1,0},{2,3},{3,2},{4,5},{5,4},{6,7},{7,6},{8,9},{9,8},{10,11... | collective-permute-start | bytes 10321928 | tf_op jit(solution)/shard_map/ppermute | solution.py:616
  101.6 62.0 %collective-permute-start.11 = (bf16[528,1280]{1,0:T(8,128)(2,1)}, bf16[528,1280]{1,0:T(8,128)(2,1)S(1)}, u32[]{:S(2)}, u32[]{:S(2)}) collective-permute-start(bf16[528,1280]{1,0:T(8,128)(2,1)} %collective-permute-done.3.r_3_), channel_id=1, source_target_pairs={{0,2},{1,3},{2,4},{3,5},{4,6},{5,7},{6,0},{7,1},{8,10},{9,11},{10,... | collective-permute-start | bytes 4055048 | tf_op jit(solution)/shard_map/ppermute | solution.py:621
  102.8 60.8 %collective-permute-start.10 = (bf16[512,1280]{1,0:T(8,128)(2,1)}, bf16[512,1280]{1,0:T(8,128)(2,1)}, u32[]{:S(2)}, u32[]{:S(2)}) collective-permute-start(bf16[512,1280]{1,0:T(8,128)(2,1)} %collective-permute-done.4.r_1_), channel_id=1, source_target_pairs={{0,2},{1,3},{2,4},{3,5},{4,6},{5,7},{6,0},{7,1},{8,10},{9,11},{10,... | collective-permute-start | bytes 3932168 | tf_op jit(solution)/shard_map/ppermute | solution.py:621
  104.4 59.2 %collective-permute-start.7 = (bf16[512,1280]{1,0:T(8,128)(2,1)}, bf16[512,1280]{1,0:T(8,128)(2,1)}, u32[]{:S(2)}, u32[]{:S(2)}) collective-permute-start(bf16[512,1280]{1,0:T(8,128)(2,1)} %get-tuple-element.232), channel_id=1, source_target_pairs={{0,1},{1,0},{2,3},{3,2},{4,5},{5,4},{6,7},{7,6},{8,9},{9,8},{10,11... | collective-permute-start | bytes 3932168 | tf_op jit(solution)/shard_map/ppermute | solution.py:616
  105.8 57.9 %copy-start.43 = (bf16[640,2688]{1,0:T(8,128)(2,1)S(1)}, bf16[640,2688]{1,0:T(8,128)(2,1)}, u32[]{:S(2)}) copy-start(bf16[640,2688]{1,0:T(8,128)(2,1)} %get-tuple-element.235) | copy-start | bytes 10321924
  167.0 4.4 collective-permute-start.12
  167.0 6.0 %collective-permute-start.17 = (bf16[512,1280]{1,0:T(8,128)(2,1)S(1)}, bf16[512,1280]{1,0:T(8,128)(2,1)}, u32[]{:S(2)}, u32[]{:S(2)}) collective-permute-start(bf16[512,1280]{1,0:T(8,128)(2,1)S(1)} %copy-done.70), channel_id=1, source_target_pairs={{0,1},{1,0},{2,3},{3,2},{4,5},{5,4},{6,7},{7,6},{8,9},{9,8},{10,11... | collective-permute-start | bytes 3932168 | tf_op jit(solution)/shard_map/ppermute | solution.py:616
  167.5 52.7 %collective-permute-start.9 = (bf16[2,2,2,40,2688]{4,3,2,1,0:T(8,128)(2,1)}, bf16[2,2,2,40,2688]{4,3,2,1,0:T(8,128)(2,1)}, u32[]{:S(2)}, u32[]{:S(2)}) collective-permute-start(bf16[2,2,2,40,2688]{4,3,2,1,0:T(8,128)(2,1)} %fusion), channel_id=1, source_target_pairs={{0,8},{8,0},{16,24},{24,16},{1,9},{9,1},{17,25},{25,17},{2,10},{10... | collective-permute-start | bytes 5160968 | tf_op jit(solution)/shard_map/ppermute | solution.py:662
  169.1 7.1 %collective-permute-start.14 = (bf16[528,1280]{1,0:T(8,128)(2,1)}, bf16[528,1280]{1,0:T(8,128)(2,1)}, u32[]{:S(2)}, u32[]{:S(2)}) collective-permute-start(bf16[528,1280]{1,0:T(8,128)(2,1)} %collective-permute-done.3.r_3_), channel_id=1, source_target_pairs={{0,1},{1,0},{2,3},{3,2},{4,5},{5,4},{6,7},{7,6},{8,9},{9,8},{10,11... | collective-permute-start | bytes 4055048 | tf_op jit(solution)/shard_map/ppermute | solution.py:616
  169.1 51.1 %collective-permute-start.16 = (bf16[512,1280]{1,0:T(8,128)(2,1)}, bf16[512,1280]{1,0:T(8,128)(2,1)}, u32[]{:S(2)}, u32[]{:S(2)}) collective-permute-start(bf16[512,1280]{1,0:T(8,128)(2,1)} %collective-permute-done.10.r_1_), channel_id=1, source_target_pairs={{0,2},{1,3},{2,4},{3,5},{4,6},{5,7},{6,0},{7,1},{8,10},{9,11},{10,... | collective-permute-start | bytes 3932168 | tf_op jit(solution)/shard_map/ppermute | solution.py:621
  171.4 4.8 collective-permute-start.13
  173.0 59.3 %collective-permute-start.18 = (bf16[544,1280]{1,0:T(8,128)(2,1)}, bf16[544,1280]{1,0:T(8,128)(2,1)}, u32[]{:S(2)}, u32[]{:S(2)}) collective-permute-start(bf16[544,1280]{1,0:T(8,128)(2,1)} %add_convert_fusion.3), channel_id=1, source_target_pairs={{0,2},{1,3},{2,4},{3,5},{4,6},{5,7},{6,0},{7,1},{8,10},{9,11},{10,... | collective-permute-start | bytes 4177928 | tf_op jit(solution)/shard_map/ppermute | solution.py:621
  232.3 3.2 collective-permute-start.19
  237.3 37.2 %collective-permute-start.23 = (bf16[544,1280]{1,0:T(8,128)(2,1)S(1)}, bf16[544,1280]{1,0:T(8,128)(2,1)S(1)}, u32[]{:S(2)}, u32[]{:S(2)}) collective-permute-start(bf16[544,1280]{1,0:T(8,128)(2,1)S(1)} %add_convert_fusion.2), channel_id=1, source_target_pairs={{0,2},{1,3},{2,4},{3,5},{4,6},{5,7},{6,0},{7,1},{8,10},{9,11},{10,... | collective-permute-start | bytes 4177928 | tf_op jit(solution)/shard_map/ppermute | solution.py:621
  237.4 3.7 collective-permute-start.21
  237.6 5.0 collective-permute-start.20
  238.0 36.5 %collective-permute-start.22 = (bf16[512,1280]{1,0:T(8,128)(2,1)}, bf16[512,1280]{1,0:T(8,128)(2,1)S(1)}, u32[]{:S(2)}, u32[]{:S(2)}) collective-permute-start(bf16[512,1280]{1,0:T(8,128)(2,1)} %get-tuple-element.283), channel_id=1, source_target_pairs={{0,1},{1,0},{2,3},{3,2},{4,5},{5,4},{6,7},{7,6},{8,9},{9,8},{10,11... | collective-permute-start | bytes 3932168 | tf_op jit(solution)/shard_map/ppermute | solution.py:616
  238.1 36.4 %collective-permute-start.15 = (bf16[2,2,40,2688]{3,2,1,0:T(8,128)(2,1)S(1)}, bf16[2,2,40,2688]{3,2,1,0:T(8,128)(2,1)S(1)}, u32[]{:S(2)}, u32[]{:S(2)}) collective-permute-start(bf16[2,2,40,2688]{3,2,1,0:T(8,128)(2,1)S(1)} %fusion.1), channel_id=1, source_target_pairs={{0,16},{8,24},{16,0},{24,8},{1,17},{9,25},{17,1},{25,9},{2,18},{10... | collective-permute-start | bytes 2580488 | tf_op jit(solution)/shard_map/ppermute | solution.py:662
  274.5 3.4 collective-permute-start.24
  279.9 54.9 %collective-permute-start.25 = (bf16[544,1280]{1,0:T(8,128)(2,1)}, bf16[544,1280]{1,0:T(8,128)(2,1)S(1)}, u32[]{:S(2)}, u32[]{:S(2)}) collective-permute-start(bf16[544,1280]{1,0:T(8,128)(2,1)} %get-tuple-element.287), channel_id=1, source_target_pairs={{0,1},{1,0},{2,3},{3,2},{4,5},{5,4},{6,7},{7,6},{8,9},{9,8},{10,11... | collective-permute-start | bytes 4177928 | tf_op jit(solution)/shard_map/ppermute | solution.py:616
  280.1 54.8 %collective-permute-start.26 = (bf16[544,1280]{1,0:T(8,128)(2,1)S(1)}, bf16[544,1280]{1,0:T(8,128)(2,1)S(1)}, u32[]{:S(2)}, u32[]{:S(2)}) collective-permute-start(bf16[544,1280]{1,0:T(8,128)(2,1)S(1)} %add_convert_fusion.1), channel_id=1, source_target_pairs={{0,2},{1,3},{2,4},{3,5},{4,6},{5,7},{6,0},{7,1},{8,10},{9,11},{10,... | collective-permute-start | bytes 4177928 | tf_op jit(solution)/shard_map/ppermute | solution.py:621
  280.1 54.7 %collective-permute-start.29 = (bf16[512,1280]{1,0:T(8,128)(2,1)}, bf16[512,1280]{1,0:T(8,128)(2,1)}, u32[]{:S(2)}, u32[]{:S(2)}) collective-permute-start(bf16[512,1280]{1,0:T(8,128)(2,1)} %get-tuple-element.305), channel_id=1, source_target_pairs={{0,1},{1,0},{2,3},{3,2},{4,5},{5,4},{6,7},{7,6},{8,9},{9,8},{10,11... | collective-permute-start | bytes 3932168 | tf_op jit(solution)/shard_map/ppermute | solution.py:616
  289.0 50.3 %copy-start.18 = (bf16[448,1280]{1,0:T(8,128)(2,1)}, bf16[448,1280]{1,0:T(8,128)(2,1)S(1)}, u32[]{:S(2)}) copy-start(bf16[448,1280]{1,0:T(8,128)(2,1)S(1)} %get-tuple-element.291) | copy-start | bytes 3440644
  298.8 36.1 %collective-permute-start.27 = (bf16[448,1280]{1,0:T(8,128)(2,1)S(1)}, bf16[448,1280]{1,0:T(8,128)(2,1)S(1)}, u32[]{:S(2)}, u32[]{:S(2)}) collective-permute-start(bf16[448,1280]{1,0:T(8,128)(2,1)S(1)} %get-tuple-element.295), channel_id=1, source_target_pairs={{0,16},{8,24},{16,0},{24,8},{1,17},{9,25},{17,1},{25,9},{2,18},{10... | collective-permute-start | bytes 3440648 | tf_op jit(solution)/shard_map/ppermute | solution.py:822
  300.3 34.5 %collective-permute-start.28 = (bf16[448,1280]{1,0:T(8,128)(2,1)S(1)}, bf16[448,1280]{1,0:T(8,128)(2,1)}, u32[]{:S(2)}, u32[]{:S(2)}) collective-permute-start(bf16[448,1280]{1,0:T(8,128)(2,1)S(1)} %get-tuple-element.292), channel_id=1, source_target_pairs={{0,8},{8,0},{16,24},{24,16},{1,9},{9,1},{17,25},{25,17},{2,10},{10... | collective-permute-start | bytes 3440648 | tf_op jit(solution)/shard_map/ppermute | solution.py:822
  334.9 33.5 %collective-permute-start.30 = (bf16[512,1280]{1,0:T(8,128)(2,1)}, bf16[512,1280]{1,0:T(8,128)(2,1)}, u32[]{:S(2)}, u32[]{:S(2)}) collective-permute-start(bf16[512,1280]{1,0:T(8,128)(2,1)} %add_convert_fusion.8), channel_id=1, source_target_pairs={{0,2},{1,3},{2,4},{3,5},{4,6},{5,7},{6,0},{7,1},{8,10},{9,11},{10,... | collective-permute-start | bytes 3932168 | tf_op jit(solution)/shard_map/ppermute | solution.py:621
  337.3 74.2 %collective-permute-start.32 = (bf16[640,1792]{1,0:T(8,128)(2,1)}, bf16[640,1792]{1,0:T(8,128)(2,1)}, u32[]{:S(2)}, u32[]{:S(2)}) collective-permute-start(bf16[640,1792]{1,0:T(8,128)(2,1)} %copy-done.40), channel_id=1, source_target_pairs={{0,8},{8,0},{16,24},{24,16},{1,9},{9,1},{17,25},{25,17},{2,10},{10... | collective-permute-start | bytes 6881288 | tf_op jit(solution)/shard_map/ppermute | solution.py:822
  338.9 72.7 %collective-permute-start.33 = (bf16[640,1792]{1,0:T(8,128)(2,1)}, bf16[640,1792]{1,0:T(8,128)(2,1)}, u32[]{:S(2)}, u32[]{:S(2)}) collective-permute-start(bf16[640,1792]{1,0:T(8,128)(2,1)} %copy-done.41), channel_id=1, source_target_pairs={{0,16},{8,24},{16,0},{24,8},{1,17},{9,25},{17,1},{25,9},{2,18},{10... | collective-permute-start | bytes 6881288 | tf_op jit(solution)/shard_map/ppermute | solution.py:822
  366.5 107.7 %copy-start.15 = (bf16[640,2048]{1,0:T(8,128)(2,1)}, bf16[640,2048]{1,0:T(8,128)(2,1)S(1)}, u32[]{:S(2)}) copy-start(bf16[640,2048]{1,0:T(8,128)(2,1)S(1)} %get-tuple-element.347) | copy-start | bytes 7864324
  370.2 41.3 %collective-permute-start.31 = (bf16[512,1280]{1,0:T(8,128)(2,1)S(1)}, bf16[512,1280]{1,0:T(8,128)(2,1)S(1)}, u32[]{:S(2)}, u32[]{:S(2)}) collective-permute-start(bf16[512,1280]{1,0:T(8,128)(2,1)S(1)} %add_convert_fusion.7), channel_id=1, source_target_pairs={{0,2},{1,3},{2,4},{3,5},{4,6},{5,7},{6,0},{7,1},{8,10},{9,11},{10,... | collective-permute-start | bytes 3932168 | tf_op jit(solution)/shard_map/ppermute | solution.py:621
  373.1 36.8 %collective-permute-start.35 = (bf16[224,1280]{1,0:T(8,128)(2,1)S(1)}, bf16[224,1280]{1,0:T(8,128)(2,1)S(1)}, u32[]{:S(2)}, u32[]{:S(2)}) collective-permute-start(bf16[224,1280]{1,0:T(8,128)(2,1)S(1)} %fusion.14), channel_id=1, source_target_pairs={{0,8},{8,0},{16,24},{24,16},{1,9},{9,1},{17,25},{25,17},{2,10},{10... | collective-permute-start | bytes 1720328 | tf_op jit(solution)/shard_map/ppermute | solution.py:662
  373.7 37.0 %collective-permute-start.34 = (bf16[224,1280]{1,0:T(8,128)(2,1)S(1)}, bf16[224,1280]{1,0:T(8,128)(2,1)S(1)}, u32[]{:S(2)}, u32[]{:S(2)}) collective-permute-start(bf16[224,1280]{1,0:T(8,128)(2,1)S(1)} %fusion.13), channel_id=1, source_target_pairs={{0,16},{8,24},{16,0},{24,8},{1,17},{9,25},{17,1},{25,9},{2,18},{10... | collective-permute-start | bytes 1720328 | tf_op jit(solution)/shard_map/ppermute | solution.py:662
  411.6 5.3 %collective-permute-start.38 = (bf16[640,2048]{1,0:T(8,128)(2,1)}, bf16[640,2048]{1,0:T(8,128)(2,1)}, u32[]{:S(2)}, u32[]{:S(2)}) collective-permute-start(bf16[640,2048]{1,0:T(8,128)(2,1)} %get-tuple-element.348), channel_id=1, source_target_pairs={{0,1},{1,0},{2,3},{3,2},{4,5},{5,4},{6,7},{7,6},{8,9},{9,8},{10,11... | collective-permute-start | bytes 7864328 | tf_op jit(solution)/shard_map/ppermute | solution.py:616
  411.6 9.0 %collective-permute-start.37 = (bf16[640,2048]{1,0:T(8,128)(2,1)}, bf16[640,2048]{1,0:T(8,128)(2,1)}, u32[]{:S(2)}, u32[]{:S(2)}) collective-permute-start(bf16[640,2048]{1,0:T(8,128)(2,1)} %get-tuple-element.344), channel_id=1, source_target_pairs={{0,1},{1,0},{2,3},{3,2},{4,5},{5,4},{6,7},{7,6},{8,9},{9,8},{10,11... | collective-permute-start | bytes 7864328 | tf_op jit(solution)/shard_map/ppermute | solution.py:616
  412.1 14.8 %collective-permute-start.36 = (bf16[640,1152]{1,0:T(8,128)(2,1)}, bf16[640,1152]{1,0:T(8,128)(2,1)}, u32[]{:S(2)}, u32[]{:S(2)}) collective-permute-start(bf16[640,1152]{1,0:T(8,128)(2,1)} %get-tuple-element.339), channel_id=1, source_target_pairs={{0,1},{1,0},{2,3},{3,2},{4,5},{5,4},{6,7},{7,6},{8,9},{9,8},{10,11... | collective-permute-start | bytes 4423688 | tf_op jit(solution)/shard_map/ppermute | solution.py:616
  418.8 31.7 %collective-permute-start.42 = (bf16[2,2,2,40,2048]{4,3,2,1,0:T(8,128)(2,1)S(1)}, bf16[2,2,2,40,2048]{4,3,2,1,0:T(8,128)(2,1)S(1)}, u32[]{:S(2)}, u32[]{:S(2)}) collective-permute-start(bf16[2,2,2,40,2048]{4,3,2,1,0:T(8,128)(2,1)S(1)} %fusion.2), channel_id=1, source_target_pairs={{0,8},{8,0},{16,24},{24,16},{1,9},{9,1},{17,25},{25,17},{2,10},{10... | collective-permute-start | bytes 3932168 | tf_op jit(solution)/shard_map/ppermute | solution.py:662
  422.6 30.9 %collective-permute-start.41 = (bf16[2,2,2,40,2048]{4,3,2,1,0:T(8,128)(2,1)S(1)}, bf16[2,2,2,40,2048]{4,3,2,1,0:T(8,128)(2,1)S(1)}, u32[]{:S(2)}, u32[]{:S(2)}) collective-permute-start(bf16[2,2,2,40,2048]{4,3,2,1,0:T(8,128)(2,1)S(1)} %fusion.3), channel_id=1, source_target_pairs={{0,16},{8,24},{16,0},{24,8},{1,17},{9,25},{17,1},{25,9},{2,18},{10... | collective-permute-start | bytes 3932168 | tf_op jit(solution)/shard_map/ppermute | solution.py:662
  425.2 45.6 %collective-permute-start.43 = (bf16[512,1280]{1,0:T(8,128)(2,1)S(1)}, bf16[512,1280]{1,0:T(8,128)(2,1)S(1)}, u32[]{:S(2)}, u32[]{:S(2)}) collective-permute-start(bf16[512,1280]{1,0:T(8,128)(2,1)S(1)} %convert_add_fusion.1), channel_id=1, source_target_pairs={{0,2},{1,3},{2,4},{3,5},{4,6},{5,7},{6,0},{7,1},{8,10},{9,11},{10,... | collective-permute-start | bytes 3932168 | tf_op jit(solution)/shard_map/ppermute | solution.py:621
  428.5 37.8 %collective-permute-start.40 = (bf16[2,2,2,40,1152]{4,3,2,1,0:T(8,128)(2,1)S(1)}, bf16[2,2,2,40,1152]{4,3,2,1,0:T(8,128)(2,1)S(1)}, u32[]{:S(2)}, u32[]{:S(2)}) collective-permute-start(bf16[2,2,2,40,1152]{4,3,2,1,0:T(8,128)(2,1)S(1)} %fusion.9), channel_id=1, source_target_pairs={{0,8},{8,0},{16,24},{24,16},{1,9},{9,1},{17,25},{25,17},{2,10},{10... | collective-permute-start | bytes 2211848 | tf_op jit(solution)/shard_map/ppermute | solution.py:662
  431.5 36.7 %collective-permute-start.39 = (bf16[2,40,2688]{2,1,0:T(8,128)(2,1)S(1)}, bf16[2,40,2688]{2,1,0:T(8,128)(2,1)S(1)}, u32[]{:S(2)}, u32[]{:S(2)}) collective-permute-start(bf16[2,40,2688]{2,1,0:T(8,128)(2,1)S(1)} %fusion.8), channel_id=1, source_target_pairs={{0,2},{1,3},{2,0},{3,1},{4,6},{5,7},{6,4},{7,5},{8,10},{9,11},{10,... | collective-permute-start | bytes 1290248 | tf_op jit(solution)/shard_map/ppermute | solution.py:662
  450.5 40.9 %copy-start.56 = (bf16[2,2,2,40,2048]{4,3,2,1,0:T(8,128)(2,1)}, bf16[2,2,2,40,2048]{4,3,2,1,0:T(8,128)(2,1)S(1)}, u32[]{:S(2)}) copy-start(bf16[2,2,2,40,2048]{4,3,2,1,0:T(8,128)(2,1)S(1)} %collective-permute-done.42) | copy-start | bytes 3932164
  452.4 21.8 %collective-permute-start.46 = (bf16[2,2,40,2048]{3,2,1,0:T(8,128)(2,1)S(1)}, bf16[2,2,40,2048]{3,2,1,0:T(8,128)(2,1)S(1)}, u32[]{:S(2)}, u32[]{:S(2)}) collective-permute-start(bf16[2,2,40,2048]{3,2,1,0:T(8,128)(2,1)S(1)} %fusion.5), channel_id=1, source_target_pairs={{0,16},{8,24},{16,0},{24,8},{1,17},{9,25},{17,1},{25,9},{2,18},{10... | collective-permute-start | bytes 1966088 | tf_op jit(solution)/shard_map/ppermute | solution.py:662
  453.5 41.7 %copy-start.57 = (bf16[2,2,2,40,2048]{4,3,2,1,0:T(8,128)(2,1)}, bf16[2,2,2,40,2048]{4,3,2,1,0:T(8,128)(2,1)S(1)}, u32[]{:S(2)}) copy-start(bf16[2,2,2,40,2048]{4,3,2,1,0:T(8,128)(2,1)S(1)} %collective-permute-done.41) | copy-start | bytes 3932164
  455.4 24.1 %collective-permute-start.45 = (bf16[2,2,40,2048]{3,2,1,0:T(8,128)(2,1)S(1)}, bf16[2,2,40,2048]{3,2,1,0:T(8,128)(2,1)S(1)}, u32[]{:S(2)}, u32[]{:S(2)}) collective-permute-start(bf16[2,2,40,2048]{3,2,1,0:T(8,128)(2,1)S(1)} %fusion.4), channel_id=1, source_target_pairs={{0,8},{8,0},{16,24},{24,16},{1,9},{9,1},{17,25},{25,17},{2,10},{10... | collective-permute-start | bytes 1966088 | tf_op jit(solution)/shard_map/ppermute | solution.py:662
  467.5 15.2 %collective-permute-start.44 = (bf16[2,2,40,1152]{3,2,1,0:T(8,128)(2,1)S(1)}, bf16[2,2,40,1152]{3,2,1,0:T(8,128)(2,1)S(1)}, u32[]{:S(2)}, u32[]{:S(2)}) collective-permute-start(bf16[2,2,40,1152]{3,2,1,0:T(8,128)(2,1)S(1)} %fusion.10), channel_id=1, source_target_pairs={{0,16},{8,24},{16,0},{24,8},{1,17},{9,25},{17,1},{25,9},{2,18},{10... | collective-permute-start | bytes 1105928 | tf_op jit(solution)/shard_map/ppermute | solution.py:662
  469.4 30.0 %collective-permute-start.53 = (bf16[40,2688]{1,0:T(8,128)(2,1)S(1)}, bf16[40,2688]{1,0:T(8,128)(2,1)S(1)}, u32[]{:S(2)}, u32[]{:S(2)}) collective-permute-start(bf16[40,2688]{1,0:T(8,128)(2,1)S(1)} %fusion.16), channel_id=1, source_target_pairs={{0,4},{1,5},{2,6},{3,7},{4,0},{5,1},{6,2},{7,3},{8,12},{9,13},{10,... | collective-permute-start | bytes 645128 | tf_op jit(solution)/shard_map/ppermute | solution.py:662
  475.6 14.4 %collective-permute-start.49 = (bf16[2,40,2048]{2,1,0:T(8,128)(2,1)S(1)}, bf16[2,40,2048]{2,1,0:T(8,128)(2,1)S(1)}, u32[]{:S(2)}, u32[]{:S(2)}) collective-permute-start(bf16[2,40,2048]{2,1,0:T(8,128)(2,1)S(1)} %fusion.12), channel_id=1, source_target_pairs={{0,2},{1,3},{2,0},{3,1},{4,6},{5,7},{6,4},{7,5},{8,10},{9,11},{10,... | collective-permute-start | bytes 983048 | tf_op jit(solution)/shard_map/ppermute | solution.py:662
  480.9 14.2 %collective-permute-start.48 = (bf16[2,40,2048]{2,1,0:T(8,128)(2,1)S(1)}, bf16[2,40,2048]{2,1,0:T(8,128)(2,1)S(1)}, u32[]{:S(2)}, u32[]{:S(2)}) collective-permute-start(bf16[2,40,2048]{2,1,0:T(8,128)(2,1)S(1)} %fusion.11), channel_id=1, source_target_pairs={{0,2},{1,3},{2,0},{3,1},{4,6},{5,7},{6,4},{7,5},{8,10},{9,11},{10,... | collective-permute-start | bytes 983048 | tf_op jit(solution)/shard_map/ppermute | solution.py:662
  483.7 14.1 %collective-permute-start.47 = (bf16[2,40,1152]{2,1,0:T(8,128)(2,1)S(1)}, bf16[2,40,1152]{2,1,0:T(8,128)(2,1)S(1)}, u32[]{:S(2)}, u32[]{:S(2)}) collective-permute-start(bf16[2,40,1152]{2,1,0:T(8,128)(2,1)S(1)} %fusion.17), channel_id=1, source_target_pairs={{0,2},{1,3},{2,0},{3,1},{4,6},{5,7},{6,4},{7,5},{8,10},{9,11},{10,... | collective-permute-start | bytes 552968 | tf_op jit(solution)/shard_map/ppermute | solution.py:662
  486.8 37.1 %collective-permute-start.54 = (bf16[320,1792]{1,0:T(8,128)(2,1)}, bf16[320,1792]{1,0:T(8,128)(2,1)S(1)}, u32[]{:S(2)}, u32[]{:S(2)}) collective-permute-start(bf16[320,1792]{1,0:T(8,128)(2,1)} %fusion.6), channel_id=1, source_target_pairs={{0,16},{8,24},{16,0},{24,8},{1,17},{9,25},{17,1},{25,9},{2,18},{10... | collective-permute-start | bytes 3440648 | tf_op jit(solution)/shard_map/ppermute | solution.py:662
  490.0 33.9 %collective-permute-start.55 = (bf16[320,1792]{1,0:T(8,128)(2,1)}, bf16[320,1792]{1,0:T(8,128)(2,1)}, u32[]{:S(2)}, u32[]{:S(2)}) collective-permute-start(bf16[320,1792]{1,0:T(8,128)(2,1)} %fusion.7), channel_id=1, source_target_pairs={{0,8},{8,0},{16,24},{24,16},{1,9},{9,1},{17,25},{25,17},{2,10},{10... | collective-permute-start | bytes 3440648 | tf_op jit(solution)/shard_map/ppermute | solution.py:662
  498.7 6.5 %collective-permute-start.50 = (bf16[40,1152]{1,0:T(8,128)(2,1)S(1)}, bf16[40,1152]{1,0:T(8,128)(2,1)S(1)}, u32[]{:S(2)}, u32[]{:S(2)}) collective-permute-start(bf16[40,1152]{1,0:T(8,128)(2,1)S(1)} %fusion.24), channel_id=1, source_target_pairs={{0,4},{1,5},{2,6},{3,7},{4,0},{5,1},{6,2},{7,3},{8,12},{9,13},{10,... | collective-permute-start | bytes 276488 | tf_op jit(solution)/shard_map/ppermute | solution.py:662
  502.1 15.3 %collective-permute-start.52 = (bf16[40,2048]{1,0:T(8,128)(2,1)}, bf16[40,2048]{1,0:T(8,128)(2,1)}, u32[]{:S(2)}, u32[]{:S(2)}) collective-permute-start(bf16[40,2048]{1,0:T(8,128)(2,1)} %fusion.20), channel_id=1, source_target_pairs={{0,4},{1,5},{2,6},{3,7},{4,0},{5,1},{6,2},{7,3},{8,12},{9,13},{10,... | collective-permute-start | bytes 491528 | tf_op jit(solution)/shard_map/ppermute | solution.py:662
  504.5 15.2 %collective-permute-start.51 = (bf16[40,2048]{1,0:T(8,128)(2,1)}, bf16[40,2048]{1,0:T(8,128)(2,1)}, u32[]{:S(2)}, u32[]{:S(2)}) collective-permute-start(bf16[40,2048]{1,0:T(8,128)(2,1)} %fusion.21), channel_id=1, source_target_pairs={{0,4},{1,5},{2,6},{3,7},{4,0},{5,1},{6,2},{7,3},{8,12},{9,13},{10,... | collective-permute-start | bytes 491528 | tf_op jit(solution)/shard_map/ppermute | solution.py:662
  (63 other events, 373.2 us)
